TPU v7x, 128 devices: a whole 4x4x4 slice. The times are simulated.
128 devices in a mesh: ctx: 32 (over y, x, core), head: 4 (over z).
Axes of the slice: x: 4, y: 4, z: 4, core: 2. Of those that a mesh axis runs over, the one named last changes fastest.
Arguments:
- tokens: bfloat16 [4096, 4096], P('ctx'), may hold values from -8 to 8
- w_query: bfloat16 [4096, 4096], P(None, 'head'), may hold values from -1 to 1
- w_key: bfloat16 [4096, 1024], P(None, 'head'), may hold values from -1 to 1
- w_value: bfloat16 [4096, 1024], P(None, 'head'), may hold values from -0.09375 to 0.09375
- w_out: bfloat16 [4096, 4096], P('head'), may hold values from -0.09375 to 0.09375
- doc_ids: int32 [4096], P('ctx'), may hold values from 0 to 31, never falling along the last dimension, each value on 1 to 2176 neighbouring positions
Outputs:
- mixed: bfloat16 [4096, 4096], P('ctx', 'head')
Inputs may be any that keep to these rules, and one draw needn't show every extreme that they name: doc_ids never fall along the context; each document has 1 to 2176 tokens and one has exactly 2176.
All inputs are finite; a program needn't handle non-finite values.
Results may differ from a plain program's by a relative error of at most 0.011.
Values may be sent and summed in bfloat16 or wider, within the bound.
No kernel may reach another device: no remote copies, remote signals or barrier semaphores. Data moves between devices by JAX's collectives and lax.ppermute only.
A program may use at most 128 MiB of HBM per device.

v0:
```python
import math

import jax
import jax.numpy as jnp
from jax import lax
from jax.sharding import PartitionSpec as P

HD = 128


def joined_along(pieces, dim):
    pieces = jnp.moveaxis(pieces, 0, dim)
    dims = pieces.shape
    return pieces.reshape(*dims[:dim], dims[dim] * dims[dim + 1], *dims[dim + 2 :])


def copy_for_each(value, axis):
    peers = lax.axis_size(axis)
    return lax.all_to_all(
        jnp.broadcast_to(value[None], (peers, *value.shape)), axis, 0, 0, tiled=True
    )


def gather_directly(value, axis, dim):
    return joined_along(copy_for_each(value, axis), dim)


def cut_along(value, dim, peers):
    before, after = (value.shape[:dim], value.shape[dim + 1 :])
    return jnp.moveaxis(value.reshape(*before, peers, -1, *after), dim, 0)


def summed_on_arrival(value, axis, dim):
    peers = lax.axis_size(axis)
    pieces = lax.all_to_all(cut_along(value, dim, peers), axis, 0, 0, tiled=True)
    return jnp.sum(pieces.astype(jnp.float32), axis=0)


def rotate(vectors, places):
    half_dim = vectors.shape[-1] // 2
    freqs = 500000.0 ** (-2.0 * jnp.arange(half_dim, dtype=jnp.float32) / vectors.shape[-1])
    angles = places.astype(jnp.float32)[:, None] * freqs[None, :]
    cosine = jnp.cos(angles)[:, None, :]
    sine = jnp.sin(angles)[:, None, :]
    first_half = vectors[..., :half_dim]
    second_half = vectors[..., half_dim:]
    return jnp.concatenate(
        [first_half * cosine - second_half * sine, second_half * cosine + first_half * sine],
        axis=-1,
    )


def shards(tokens, w_query, w_key, w_value, w_out, doc_ids):
    tok_rows = tokens.shape[0]
    my_index = lax.axis_index("ctx")
    first_row = my_index * tok_rows
    places = first_row + jnp.arange(tok_rows, dtype=jnp.int32)
    query_heads = w_query.shape[1] // HD
    kv_heads = w_key.shape[1] // HD
    group_size = query_heads // kv_heads
    queries = rotate(
        jnp.dot(tokens, w_query, preferred_element_type=jnp.float32).reshape(
            tok_rows, query_heads, HD
        ),
        places,
    ).astype(jnp.bfloat16)
    queries = queries.reshape(tok_rows, kv_heads, group_size, HD)
    keys_here = rotate(
        jnp.dot(tokens, w_key, preferred_element_type=jnp.float32).reshape(tok_rows, kv_heads, HD),
        places,
    ).astype(jnp.bfloat16)
    values_here = jnp.dot(tokens, w_value, preferred_element_type=jnp.float32).astype(jnp.bfloat16)
    kv_width = kv_heads * HD
    packed = jnp.concatenate([keys_here.reshape(tok_rows, kv_width), values_here], axis=1)
    all_docs = gather_directly(doc_ids, "ctx", 0)
    query_low = jnp.min(doc_ids)
    query_high = jnp.max(doc_ids)
    query_last = first_row + tok_rows - 1
    score_scale = 1.0 / math.sqrt(HD)
    initial = (
        jnp.full((kv_heads, group_size, tok_rows), -1e30, jnp.float32),
        jnp.zeros((kv_heads, group_size, tok_rows), jnp.float32),
        jnp.zeros((kv_heads, group_size, tok_rows, HD), jnp.float32),
    )
    block_kv = lax.all_gather(packed, "ctx", axis=0, tiled=True)
    key_start = jnp.int32(0)
    key_count = block_kv.shape[0]
    key_start = jnp.asarray(key_start, jnp.int32)
    key_index = jnp.arange(key_count, dtype=jnp.int32)

    def accumulate(inner):
        run_max, run_sum, run_acc = inner
        block_keys = block_kv[:, :kv_width].reshape(key_count, kv_heads, HD)
        block_values = block_kv[:, kv_width:].reshape(key_count, kv_heads, HD)
        allowed = (all_docs[None, :] == doc_ids[:, None]) & (key_index[None, :] <= places[:, None])
        scores = (
            jnp.einsum("tjgd,njd->jgtn", queries, block_keys, preferred_element_type=jnp.float32)
            * score_scale
        )
        scores = jnp.where(allowed, scores, -1e30)
        new_max = jnp.maximum(run_max, jnp.max(scores, axis=-1))
        weights = jnp.exp(scores - new_max[..., None]) * allowed.astype(jnp.float32)
        new_sum = jnp.sum(weights, axis=-1)
        summed = jnp.einsum(
            "jgtn,njd->jgtd",
            weights.astype(jnp.bfloat16),
            block_values,
            preferred_element_type=jnp.float32,
        )
        return (new_max, new_sum, summed)

    touches = (
        (jnp.max(all_docs) >= query_low)
        & (jnp.min(all_docs) <= query_high)
        & (key_start <= query_last)
        & (key_start >= 0)
    )
    state = lax.cond(touches, accumulate, lambda inner: inner, initial)
    run_max, run_sum, run_acc = state
    result = run_acc / run_sum[..., None]
    attended = (
        jnp.transpose(result, (2, 0, 1, 3)).reshape(tok_rows, query_heads * HD).astype(jnp.bfloat16)
    )
    partial_value = jnp.dot(attended, w_out, preferred_element_type=jnp.float32)
    return summed_on_arrival(partial_value.astype(jnp.bfloat16), "head", 1).astype(jnp.bfloat16)


def solution(mesh):
    return jax.shard_map(
        shards,
        mesh=mesh,
        in_specs=(
            P("ctx", None),
            P(None, "head"),
            P(None, "head"),
            P(None, "head"),
            P("head", None),
            P("ctx"),
        ),
        out_specs=P("ctx", "head"),
        check_vma=False,
    )
```

profile of v0, /device:TPU:0, one launch (start us, length us, event | category | flops | bytes accessed | tf_op | source)
XLA Modules:
  0.0 124.6 jit_solution(13467767419816730099)
XLA Ops:
  6.6 1.6 %copy-done = bf16[4096,256]{1,0:T(8,128)(2,1)S(1)} copy-done((bf16[4096,256]{1,0:T(8,128)(2,1)S(1)}, bf16[4096,256]{1,0:T(8,128)(2,1)}, u32[]{:S(2)}) %copy-start) | copy-done | bytes 2097176
  8.1 1.7 %convolution_convert_fusion.1 = bf16[128,256]{1,0:T(8,128)(2,1)S(1)} fusion(bf16[128,4096]{1,0:T(8,128)(2,1)} %param.8, bf16[4096,256]{1,0:T(8,128)(2,1)S(1)} %copy-done), kind=kOutput, calls=%fused_computation.15 | convolution fusion | flops 268468224 | bytes 3211264 | tf_op jit(solution)/shard_map/dot_general | solution.py:72
  9.8 2.4 %fusion.12 = f32[128,256]{1,0:T(8,128)S(1)} fusion(bf16[128,4096]{1,0:T(8,128)(2,1)} %param.8, bf16[4096,256]{1,0:T(8,128)(2,1)} %param.10), kind=kOutput, calls=%fused_computation.33 | convolution fusion | flops 268435456 | bytes 3276800 | tf_op jit(solution)/shard_map/dot_general | solution.py:69
  12.2 0.3 multiply_cosine_fusion
  13.1 0.7 pad_maximum_fusion.1
  13.7 1.3 %broadcast_in_dim.16 = s32[32,1,128]{2,1,0:T(1,128)} broadcast(s32[128]{0:T(128)} %param.13), dimensions={2} | broadcast | bytes 16896 | tf_op jit(solution)/shard_map/broadcast_in_dim | solution.py:20
  15.0 7.4 %all-to-all-start = ((s32[32,1,128]{2,1,0:T(1,128)}), s32[32,1,128]{2,1,0:T(1,128)S(1)}, u32[]{:S(2)}, u32[]{:S(2)}) async-start(s32[32,1,128]{2,1,0:T(1,128)} %broadcast_in_dim.16), calls=%async_computation | async-start | bytes 32768 | tf_op jit(solution)/shard_map/all_to_all | solution.py:19
  22.4 4.7 %convolution_bitcast_fusion = f32[16,8,8,128]{3,1,2,0:T(8,128)S(1)} fusion(bf16[128,4096]{1,0:T(8,128)(2,1)S(1)} %copy-done.1, bf16[4096,1024]{1,0:T(8,128)(2,1)} %param.9), kind=kOutput, calls=%fused_computation.14 | convolution fusion | flops 1073741824 | bytes 9961472 | tf_op jit(solution)/shard_map/dot_general | solution.py:62
  27.6 0.9 pad_maximum_fusion
  28.4 0.6 fusion.10
  29.1 0.7 all-to-all-done
  29.8 0.7 fusion.9
  33.0 29.3 %all-gather.2.cloned.1.call-done = bf16[4096,512]{1,0:T(8,128)(2,1)} async-done(((bf16[128,512]{1,0:T(8,128)(2,1)}), bf16[4096,512]{1,0:T(8,128)(2,1)}) %all-gather.2.cloned.1.call-update) | async-done | bytes 4194320 | tf_op jit(solution)/shard_map/all_gather | solution.py:85
  62.3 28.9 %conditional.1 = (f32[2,4,128]{2,1,0:T(4,128)S(1)}, f32[2,4,128,128]{2,3,1,0:T(8,128)}) conditional(s32[]{:T(128)} %convert_element_type.45, () %tuple.13, (s32[32,1,128]{2,1,0:T(1,128)S(1)}, s32[128]{0:T(128)S(1)}, s32[4096]{0:T(1024)S(1)}, s32[]{:T(128)}, s32[128]{0:T(128)S(1)}, /*index=5*/bf16[4096,512]{1,0:T(8,128)(2,1)}, ...), branch_computations={%region_4.0_spmd, %region_5.8_spmd} | conditional | flops 2204105728 | bytes 81586224 | solution.py:118
  62.3 2.7 %compare_and_fusion = (pred[128,4096]{0,1:T(8,128)(4,1)S(1)}, f32[128,4096]{0,1:T(8,128)}) fusion(s32[128]{0:T(128)S(1)} %broadcast_add_fusion, s32[128]{0:T(128)S(1)} %get-tuple-element.23, s32[4096]{0:T(1024)S(1)} %get-tuple-element.24, s32[4096]{0:T(1024)S(1)} %bitcast.62), kind=kLoop, calls=%fused_computation.7 | loop fusion | flops 2097152 | bytes 2655232 | tf_op jit(solution)/shard_map/cond/branch_1_fun/and | solution.py:95
  65.0 6.5 %copy.22 = bf16[4096,512]{0,1:T(8,128)(2,1)} copy(bf16[4096,512]{1,0:T(8,128)(2,1)} %get-tuple-element.45) | data formatting | bytes 8388608 | tf_op jit(solution)/shard_map
  71.5 4.1 %fusion.11 = (bf16[4096,256]{0,1:T(8,128)(2,1)}, bf16[4096,256]{0,1:T(8,128)(2,1)S(1)}) fusion(bf16[4096,512]{0,1:T(8,128)(2,1)} %copy.22), kind=kLoop, calls=%fused_computation.32 | loop fusion | bytes 8388608 | tf_op jit(solution)/shard_map/cond/branch_1_fun/slice | solution.py:94
  75.5 2.8 %fusion = (f32[2,4,128]{2,1,0:T(4,128)S(1)}, f32[2,4096,128,4]{2,1,3,0:T(8,128)S(1)}) fusion(pred[128,4096]{0,1:T(8,128)(4,1)S(1)} %get-tuple-element.54, bf16[4096,2,128,1]{0,2,3,1:T(8,128)(2,1)S(1)} %bitcast.52, bf16[128,2,4,128]{3,0,2,1:T(8,128)(2,1)S(1)} %copy-done.2), kind=kOutput, calls=%fused_computation.2 | convolution fusion | flops 1086323712 | bytes 19664896 | tf_op jit(solution)/shard_map/cond/branch_1_fun/tjgd,njd->jgtn/dot_general | solution.py:97
  78.3 7.8 %fusion.3 = f32[2,4,128,128]{2,3,1,0:T(8,128)} fusion(bf16[4096,2,128,1]{0,2,3,1:T(8,128)(2,1)} %bitcast.56, f32[2,4096,128,4]{2,1,3,0:T(8,128)S(1)} %get-tuple-element.57, f32[128,4096]{0,1:T(8,128)} %get-tuple-element.55, f32[2,4,128]{2,1,0:T(4,128)S(1)} %broadcast_maximum_fusion, pred[128,4096]{0,1:T(8,128)(4,1)S(1)} %get-tuple-element.54), kind=kOutput, calls=%fused_computation.5 | convolution fusion | flops 1094713344 | bytes 22024192 | tf_op jit(solution)/shard_map/cond | solution.py:118
  86.1 5.1 %fusion.2 = f32[2,4,128]{2,1,0:T(4,128)S(1)} fusion(f32[2,4096,128,4]{2,1,3,0:T(8,128)S(1)} %get-tuple-element.57, f32[128,4096]{0,1:T(8,128)} %get-tuple-element.55, f32[2,4,128]{2,1,0:T(4,128)S(1)} %broadcast_maximum_fusion, pred[128,4096]{0,1:T(8,128)(4,1)S(1)} %get-tuple-element.54), kind=kLoop, calls=%fused_computation.4 | loop fusion | flops 20970496 | bytes 19406848 | tf_op jit(solution)/shard_map/cond/branch_1_fun/reduce_sum | solution.py:103
  91.2 1.1 divide_convert_fusion
  92.3 4.7 %convolution_convert_fusion = bf16[128,4096]{1,0:T(8,128)(2,1)S(1)} fusion(bf16[128,1024]{0,1:T(8,128)(2,1)S(1)} %bitcast.57, bf16[1024,4096]{1,0:T(8,128)(2,1)} %param.12), kind=kOutput, calls=%fused_computation.13 | convolution fusion | flops 1074266112 | bytes 9699328 | tf_op jit(solution)/shard_map/dot_general | solution.py:124
  97.1 19.7 %all_to_all.11 = bf16[4,128,1024]{2,1,0:T(8,128)(2,1)S(1)} all-to-all(bf16[4,128,1024]{2,1,0:T(8,128)(2,1)S(1)} %bitcast.54), channel_id=1, replica_groups=mesh['ctx'=32,'head'=4] {'head'}, dimensions={0} | all-to-all | bytes 2097152 | tf_op jit(solution)/shard_map/all_to_all | solution.py:35
  116.8 0.9 reduce_sum.21
  (24 shorter events, 1.1 us)
Async XLA Ops:
  6.5 1.6 %copy-start = (bf16[4096,256]{1,0:T(8,128)(2,1)S(1)}, bf16[4096,256]{1,0:T(8,128)(2,1)}, u32[]{:S(2)}) copy-start(bf16[4096,256]{1,0:T(8,128)(2,1)} %param.11) | copy-start | bytes 6291460
  6.5 15.9 %copy-start.1 = (bf16[128,4096]{1,0:T(8,128)(2,1)S(1)}, bf16[128,4096]{1,0:T(8,128)(2,1)}, u32[]{:S(2)}) copy-start(bf16[128,4096]{1,0:T(8,128)(2,1)} %param.8) | copy-start | bytes 3145732
  6.5 55.8 %all-gather.2.cloned.1.call-start = ((), (), s32[]{:S(2)}) async-start(), calls=%async_computation.2 | async-start | bytes 4325376 | tf_op jit(solution)/shard_map/all_gather | solution.py:85
  15.0 14.8 %all-to-all-start = ((s32[32,1,128]{2,1,0:T(1,128)}), s32[32,1,128]{2,1,0:T(1,128)S(1)}, u32[]{:S(2)}, u32[]{:S(2)}) async-start(s32[32,1,128]{2,1,0:T(1,128)} %broadcast_in_dim.16), calls=%async_computation | async-start | bytes 32768 | tf_op jit(solution)/shard_map/all_to_all | solution.py:19
  22.4 6.0 %copy-start.3 = (s32[128]{0:T(128)S(1)}, s32[128]{0:T(128)}, u32[]{:S(2)}) copy-start(s32[128]{0:T(128)} %param.13) | copy-start | bytes 1540
  71.5 4.1 %copy-start.2 = (bf16[128,2,4,128]{3,0,2,1:T(8,128)(2,1)S(1)}, bf16[128,2,4,128]{3,0,2,1:T(8,128)(2,1)}, u32[]{:S(2)}) copy-start(bf16[128,2,4,128]{3,0,2,1:T(8,128)(2,1)} %get-tuple-element.28) | copy-start | bytes 786436 | tf_op jit(solution)/shard_map/cond
Sparse Core Ops, SparseCore 0:
  13.9 48.3 all-gather.1
where the time goes:
time: 125 us
  waiting for transfers between devices  30.1 us (24%)
  matrix products  24 us (19%)
  blocking collectives  19.7 us (16%)
  between operations  16 us (13%)
  other arithmetic  13.8 us (11%)
  local copies, waits for them, and re-layouts  13.7 us (11%)
  starting transfers between devices  7.4 us (6%)
    all_gather x1, waiting for transfers between devices, shards(): block_kv = lax.all_gather(packed, 'ctx', axis=0, tiled=True)  29.3 us
    all_to_all x1, blocking collectives, summed_on_arrival(): lax.all_to_all(cut_along(value, dim, peers), axis, 0, 0, tiled=True)  19.7 us
    cond x1, matrix products, shards(): state = lax.cond(touches, accumulate, lambda inner: inner, initial)  7.79 us
    all_to_all x1, starting transfers between devices, copy_for_each(): lax.all_to_all(jnp.broadcast_to(value[None], (peers, *value.shape)), axis...  7.4 us
    another operation x3, local copies, waits for them, and re-layouts  6.52 us
    reduce_sum x1, other arithmetic, accumulate(): new_sum = jnp.sum(weights, axis=-1)  5.1 us
    dot_general x1, matrix products, shards(): partial_value = jnp.dot(attended, w_out, preferred_element_type=jnp.float32)  4.68 us
    dot_general x1, matrix products, shards(): jnp.dot(tokens, w_query, preferred_element_type=jnp.float32)  4.66 us
  transfers between devices with their start and end apart: 2, of which 2 were waited for; matrix products, arithmetic and copies ran while one was open for 7% of the time, Pallas kernels for 0%

commit v1 on v0

v1 whole, which is shorter than its diff:
```python
import math

import jax
import jax.numpy as jnp
import numpy as np
from jax import lax
from jax.experimental import pallas as pl
from jax.experimental.pallas import tpu as pltpu
from jax.sharding import PartitionSpec as P

HD = 128
ROWS = 128
UNIT = 264
F32 = jnp.float32
BF16 = jnp.bfloat16
MIB = 1 << 20
SCALE = math.log2(math.e) / math.sqrt(HD)


def rope_table(count):
    half = HD // 2
    freqs = 500000.0 ** (-2.0 * np.arange(half, dtype=np.float64) / HD)
    angles = np.arange(count, dtype=np.float64)[:, None] * freqs[None, :]
    return np.concatenate([np.cos(angles), np.sin(angles)], axis=1).astype(np.float32)


def rotation(table):
    half = HD // 2
    cosine, sine = table[:, :half], table[:, half:]
    cosine = jnp.concatenate([cosine, cosine], axis=1)
    sine = jnp.concatenate([-sine, sine], axis=1)
    return lambda t: t * cosine + pltpu.roll(t, half, 1) * sine


SMEM = pl.BlockSpec(memory_space=pltpu.SMEM)
VMEM = pl.BlockSpec(memory_space=pltpu.VMEM)
HBM = pl.BlockSpec(memory_space=pltpu.HBM)


def like(*dims, dtype=BF16):
    return jax.ShapeDtypeStruct(dims, dtype)


def call(body, name, out, ins, outs, scratch=(), limit=4, flops=0, moved=1, exps=0):
    return pl.pallas_call(
        body,
        out_shape=out,
        in_specs=ins,
        out_specs=outs,
        scratch_shapes=list(scratch),
        name=name,
        cost_estimate=pl.CostEstimate(
            flops=flops, bytes_accessed=moved * MIB, transcendentals=exps
        ),
        compiler_params=pltpu.CompilerParams(vmem_limit_bytes=limit * MIB),
    )


def core_index():
    return lax.rem(lax.axis_index("ctx"), 2)


def table_rows(table):
    return table.at[pl.ds(pl.multiple_of(lax.axis_index("ctx") * ROWS, ROWS), ROWS), :]


def started(copies):
    for copy in copies:
        copy.start()
    return copies


KV_PARTS = 4


def kv_body(tok, wk, wv, docs, table, mine, send, tok_s, wk_s, wv_s, docs_s, table_s, acc, sems):
    part = tok.shape[1] // KV_PARTS
    copies = []
    for i in range(KV_PARTS):
        cut = pl.ds(i * part, part)
        copies.append(
            started([
                pltpu.make_async_copy(tok.at[:, cut], tok_s.at[:, cut], sems.at[3 * i]),
                pltpu.make_async_copy(wk.at[cut, :], wk_s.at[cut, :], sems.at[3 * i + 1]),
                pltpu.make_async_copy(wv.at[cut, :], wv_s.at[cut, :], sems.at[3 * i + 2]),
            ])
        )
    small = started([
        pltpu.make_async_copy(docs, docs_s, sems.at[3 * KV_PARTS]),
        pltpu.make_async_copy(table_rows(table), table_s, sems.at[3 * KV_PARTS + 1]),
    ])
    for i, group in enumerate(copies):
        for copy in group:
            copy.wait()
        cut = slice(i * part, (i + 1) * part)
        keys = jnp.dot(tok_s[:, cut], wk_s[cut, :], preferred_element_type=F32)
        values = jnp.dot(tok_s[:, cut], wv_s[cut, :], preferred_element_type=F32)
        if i == 0:
            acc[:, : 2 * HD] = keys
            acc[:, 2 * HD :] = values
        else:
            acc[:, : 2 * HD] += keys
            acc[:, 2 * HD :] += values
    for copy in small:
        copy.wait()
    first = core_index() == 0
    rot = rotation(table_s[...])
    keys = [rot(acc[:, h * HD : (h + 1) * HD]).astype(BF16) for h in (0, 1)]
    values = [acc[:, (2 + h) * HD : (3 + h) * HD].astype(BF16) for h in (0, 1)]
    tags = jnp.broadcast_to((docs_s[...] + 1).astype(F32), (8, ROWS)).astype(BF16)
    for out, kept in ((mine, first), (send, jnp.logical_not(first))):
        out[:ROWS, :HD] = jnp.where(kept, keys[0], keys[1])
        out[:ROWS, HD:] = jnp.where(kept, values[0], values[1])
        out[ROWS:, :HD] = tags
        out[ROWS:, HD:] = tags


def project_kv(tokens, w_key, w_value, docs, table):
    depth = tokens.shape[1]
    half = like(ROWS + 8, 2 * HD)
    return call(
        kv_body, "project_kv", (half, half), [HBM] * 5, (VMEM, VMEM),
        [
            pltpu.VMEM((ROWS, depth), BF16),
            pltpu.VMEM((depth, 2 * HD), BF16),
            pltpu.VMEM((depth, 2 * HD), BF16),
            pltpu.VMEM((1, ROWS), jnp.int32),
            pltpu.VMEM((ROWS, HD), F32),
            pltpu.VMEM((ROWS, 4 * HD), F32),
            pltpu.SemaphoreType.DMA((3 * KV_PARTS + 2,)),
        ],
        limit=8, flops=2 * ROWS * depth * 4 * HD, moved=5,
    )(tokens, w_key, w_value, docs, table)


def merge_body(mine, came, unit):
    first = core_index() == 0
    a, b = mine[...], came[...]
    unit[:ROWS, :] = jnp.where(first, a[:ROWS], b[:ROWS])
    unit[ROWS : 2 * ROWS, :] = jnp.where(first, b[:ROWS], a[:ROWS])
    unit[2 * ROWS :, :HD] = jnp.where(first, a[ROWS:, :HD], b[ROWS:, :HD])
    unit[2 * ROWS :, HD:] = jnp.where(first, b[ROWS:, :HD], a[ROWS:, :HD])


def merge(mine, came):
    return call(merge_body, "merge", like(UNIT, 2 * HD), [VMEM] * 2, VMEM, limit=1)(mine, came)


Q_PARTS = 2


def q_body(tok, wq, table, mine, send, tok_s, wq_s, table_s, sems):
    half = wq.shape[1] // 2
    part = wq.shape[0] // Q_PARTS
    core = core_index()
    small = started([
        pltpu.make_async_copy(tok, tok_s, sems.at[0]),
        pltpu.make_async_copy(table_rows(table), table_s, sems.at[1]),
    ])
    copies = []
    for side, at in ((0, 1 - core), (1, core)):
        cols = pl.ds(pl.multiple_of(at * half, half), half)
        for i in range(Q_PARTS):
            rows = pl.ds(i * part, part)
            copies += started([
                pltpu.make_async_copy(
                    wq.at[rows, cols], wq_s.at[side, rows, :], sems.at[2 + side * Q_PARTS + i]
                )
            ])
    for copy in small:
        copy.wait()
    rot = rotation(table_s[...])
    for side, out in ((0, send), (1, mine)):
        got = None
        for i in range(Q_PARTS):
            copies[side * Q_PARTS + i].wait()
            rows = slice(i * part, (i + 1) * part)
            more = jnp.dot(tok_s[:, rows], wq_s[side, rows, :], preferred_element_type=F32)
            got = more if got is None else got + more
        for h in range(half // HD):
            cols = slice(h * HD, (h + 1) * HD)
            out[:, cols] = rot(got[:, cols]).astype(BF16)


def project_q(tokens, w_query, table):
    depth, width = w_query.shape
    half = like(ROWS, width // 2)
    return call(
        q_body, "project_q", (half, half), [HBM] * 3, (VMEM, VMEM),
        [
            pltpu.VMEM((ROWS, depth), BF16),
            pltpu.VMEM((2, depth, width // 2), BF16),
            pltpu.VMEM((ROWS, HD), F32),
            pltpu.SemaphoreType.DMA((2 + 2 * Q_PARTS,)),
        ],
        limit=12, flops=2 * ROWS * depth * width, moved=9,
    )(tokens, w_query, table)


def bundle_body(unit, r1, r2, r3, out_a, out_b, out_c, slots):
    place = lax.axis_index("ctx")
    odd = lax.rem(place, 2)
    column = lax.rem(lax.div(place, 2), 4)
    for i, src in enumerate((unit, r1, r2, r3, unit)):
        slots[i] = src[...]

    def fill(out, count, late):
        skip = jnp.where((odd == 1) & (column >= late), 1, 0)
        for i in range(count):
            out[i * UNIT : (i + 1) * UNIT, :] = slots[skip + i]

    fill(out_a, 4, 3)
    fill(out_b, 2, 2)
    fill(out_c, 2, 1)


def bundle(unit, r1, r2, r3):
    return call(
        bundle_body, "bundle",
        (like(4 * UNIT, 2 * HD), like(2 * UNIT, 2 * HD), like(2 * UNIT, 2 * HD)),
        [VMEM] * 4, (VMEM,) * 3, [pltpu.VMEM((5, UNIT, 2 * HD), BF16)], limit=2,
    )(unit, r1, r2, r3)


COUNT = 2 * ROWS
CONTRACT = (((1,), (1,)), ((), ()))


def add_unit(qs, src, base, q_tag, q_first, state, allow=True):
    m_s, l_s, acc = state
    k_tag = src[pl.ds(base + COUNT, 8), :].astype(F32)

    @pl.when((jnp.max(k_tag) >= q_first) & allow)
    def _():
        bias = jnp.where(k_tag[0:1, :] == q_tag, 0.0, -1e30)
        keys = src[pl.ds(base, COUNT), :HD]
        values = src[pl.ds(base, COUNT), HD:]
        for h in range(qs.shape[0]):
            s = lax.dot_general(qs[h], keys, CONTRACT, preferred_element_type=F32)
            s = s * SCALE + bias
            old = m_s[h]
            top = jnp.maximum(old, jnp.max(s, axis=1, keepdims=True))
            fade = jnp.exp2(old - top)
            w = jnp.exp2(s - jnp.concatenate([top, top], axis=1))
            m_s[h] = top
            l_s[h] = fade * l_s[h] + jnp.sum(w, axis=1, keepdims=True)
            acc[h] = fade * acc[h] + jnp.dot(w.astype(BF16), values, preferred_element_type=F32)


def tags_of(unit):
    tags = unit[COUNT:UNIT, :].astype(F32)
    return tags, jnp.transpose(tags, (1, 0))[:, 0:1], jnp.min(tags)


def spans():
    core = core_index()
    own = pl.ds(pl.multiple_of(core * ROWS, ROWS), ROWS)
    other = pl.ds(pl.multiple_of((1 - core) * ROWS, ROWS), ROWS)
    return own, other


def near_body(qm, qr, unit, r1, r2, r3, qs, m_s, l_s, acc):
    heads = qs.shape[0]
    own, other = spans()
    for h in range(heads):
        qs[h, own, :] = qm[:, h * HD : (h + 1) * HD]
        qs[h, other, :] = qr[:, h * HD : (h + 1) * HD]
    tags, q_tag, q_first = tags_of(unit)
    rows = lax.broadcasted_iota(jnp.int32, (COUNT, COUNT), 0)
    cols = lax.broadcasted_iota(jnp.int32, (COUNT, COUNT), 1)
    bias = jnp.where((tags[0:1, :] == q_tag) & (cols <= rows), 0.0, -1e30)
    keys, values = unit[:COUNT, :HD], unit[:COUNT, HD:]
    for h in range(heads):
        s = lax.dot_general(qs[h], keys, CONTRACT, preferred_element_type=F32)
        s = s * SCALE + bias
        top = jnp.max(s, axis=1, keepdims=True)
        w = jnp.exp2(s - top)
        m_s[h] = jnp.broadcast_to(top, (COUNT, HD))
        l_s[h] = jnp.broadcast_to(jnp.sum(w, axis=1, keepdims=True), (COUNT, HD))
        acc[h] = jnp.dot(w.astype(BF16), values, preferred_element_type=F32)
    for src in (r1, r2, r3):
        add_unit(qs, src, 0, q_tag, q_first, (m_s, l_s, acc))


def attend_near(qm, qr, unit, r1, r2, r3):
    heads = qm.shape[1] // HD
    state = like(heads, COUNT, HD, dtype=F32)
    return call(
        near_body, "attend_near", (like(heads, COUNT, HD), state, state, state),
        [VMEM] * 6, (VMEM,) * 4, limit=4,
        flops=4 * heads * COUNT * 4 * COUNT * HD, exps=heads * COUNT * 4 * COUNT,
    )(qm, qr, unit, r1, r2, r3)


def far_body(qs, m_in, l_in, acc_in, unit, far_a, far_b, far_c, mine, send, m_s, l_s, acc):
    heads = qs.shape[0]
    state = (m_s, l_s, acc)
    for new, old in zip(state, (m_in, l_in, acc_in)):
        new[...] = old[...]
    _, q_tag, q_first = tags_of(unit)
    even = core_index() == 0
    for src, count in ((far_b, 2), (far_c, 2), (far_a, 4)):

        def step(i, carry):
            base = pl.multiple_of(i * UNIT, 8)
            add_unit(qs, src, base, q_tag, q_first, state, even | (i < 3))
            return carry

        lax.fori_loop(0, count, step, 0)
    own, other = spans()
    for h in range(heads):
        cols = slice(h * HD, (h + 1) * HD)
        mine[:, cols] = (acc[h, own, :] / l_s[h, own, :]).astype(BF16)
        send[:, cols] = (acc[h, other, :] / l_s[h, other, :]).astype(BF16)


def attend_far(qs, m_in, l_in, acc_in, unit, far_a, far_b, far_c):
    heads = qs.shape[0]
    half = like(ROWS, heads * HD)
    state = pltpu.VMEM((heads, COUNT, HD), F32)
    return call(
        far_body, "attend_far", (half, half), [VMEM] * 8, (VMEM,) * 2, [state] * 3, limit=6,
        flops=4 * heads * COUNT * 7 * COUNT * HD, exps=heads * COUNT * 7 * COUNT,
    )(qs, m_in, l_in, acc_in, unit, far_a, far_b, far_c)


def project_out(xm, xr, w_out, shift, groups):
    depth = xm.shape[1]
    width = w_out.shape[1] // groups

    def body(xm, xr, w, out):
        core = core_index()
        group = lax.rem(lax.axis_index("head") + shift, groups)
        cols = pl.ds(pl.multiple_of(group * width, width), width)
        own = pl.ds(pl.multiple_of(core * depth, depth), depth)
        other = pl.ds(pl.multiple_of((1 - core) * depth, depth), depth)
        got = jnp.dot(xm[...], w[own, cols], preferred_element_type=F32)
        got += jnp.dot(xr[...], w[other, cols], preferred_element_type=F32)
        out[...] = got.astype(BF16)

    return call(
        body, "project_out", like(ROWS, width), [VMEM] * 3, VMEM, limit=4,
        flops=2 * ROWS * 2 * depth * width, moved=3,
    )(xm, xr, w_out)


def shards(tokens, w_query, w_key, w_value, w_out, doc_ids):
    ranks = lax.axis_size("ctx")
    groups = lax.axis_size("head")
    table = jnp.asarray(rope_table(ranks * ROWS))

    def swap(value):
        return lax.ppermute(value, "ctx", [(r, r ^ 1) for r in range(ranks)])

    def along(value, even, odd):
        moves = []
        for r in range(ranks):
            chip = (odd if r % 2 else even)(r // 2)
            if chip is not None and chip < ranks // 2:
                moves.append((r, 2 * chip + r % 2))
        return lax.ppermute(value, "ctx", moves)

    def ahead(step):
        return lambda chip: chip + step

    def in_row(step):
        return lambda chip: chip // 4 * 4 + (chip + step) % 4

    def nowhere(chip):
        return None

    tokens, w_key, w_value, w_query, table, docs = (
        pltpu.with_memory_space_constraint(a, pltpu.HBM)
        for a in (tokens, w_key, w_value, w_query, table, doc_ids.reshape(1, -1))
    )
    mine, send = project_kv(tokens, w_key, w_value, docs, table)
    unit = merge(mine, swap(send))
    r1 = along(unit, ahead(1), ahead(4))
    r2 = along(unit, ahead(2), ahead(8))
    r3 = along(unit, ahead(3), lambda chip: 15 if chip == 3 else None)
    qm, qs = project_q(tokens, w_query, table)
    r1, r2, r3, qm, qs = lax.optimization_barrier((r1, r2, r3, qm, qs))
    qr = swap(qs)
    out_a, out_b, out_c = bundle(unit, r1, r2, r3)
    far_a = along(out_a, ahead(4), in_row(1))
    far_b = along(out_b, ahead(8), in_row(2))
    far_c = along(out_c, nowhere, in_row(3))
    state = attend_near(qm, qr, unit, r1, r2, r3)
    xm, xs = attend_far(*state, unit, far_a, far_b, far_c)
    xr = swap(xs)
    came = []
    for shift in (2, 1, 3):
        partial = project_out(xm, xr, w_out, shift, groups)
        came.append(
            lax.ppermute(partial, "head", [(g, (g + shift) % groups) for g in range(groups)])
        )
    total = project_out(xm, xr, w_out, 0, groups).astype(F32)
    for partial in came:
        total = total + partial.astype(F32)
    return total.astype(BF16)


def solution(mesh):
    return jax.shard_map(
        shards,
        mesh=mesh,
        in_specs=(
            P("ctx", None),
            P(None, "head"),
            P(None, "head"),
            P(None, "head"),
            P("head", None),
            P("ctx"),
        ),
        out_specs=P("ctx", "head"),
        check_vma=False,
    )
```

time: 125 us -> 63.1 us (0.50)
  the two profiles are of different devices: /device:TPU:0 before, /device:TPU:16 now
where the time goes in v1:
time: 63.1 us; the launch traced here: 64 us
  starting transfers between devices  23 us (36%)
  waiting for transfers between devices  20.8 us (33%)
  Pallas kernels  19.1 us (30%)
  other arithmetic  0.87 us (1%)
    ppermute x6, starting transfers between devices, along(): return lax.ppermute(value, 'ctx', moves)  16.5 us
    ppermute x3, waiting for transfers between devices, shards(): lax.ppermute(partial, 'head', [(g, (g + shift) % groups) for g in range(g...  12 us
    ppermute x3, starting transfers between devices, shards(): lax.ppermute(partial, 'head', [(g, (g + shift) % groups) for g in range(g...  6.09 us
    pallas_call x1, Pallas kernels, attend_far(): call(far_body, 'attend_far', (half, half), [VMEM] * 8, (VMEM,) * 2, [stat...  5.71 us
    ppermute x6, waiting for transfers between devices, along(): return lax.ppermute(value, 'ctx', moves)  4.98 us
    pallas_call x1, Pallas kernels, project_q(): call(q_body, 'project_q', (half, half), [HBM] * 3, (VMEM, VMEM), [pltpu.V...  4.68 us
    ppermute x3, waiting for transfers between devices, swap(): return lax.ppermute(value, 'ctx', [(r, r ^ 1) for r in range(ranks)])  3.77 us
    pallas_call x1, Pallas kernels, attend_near(): call(near_body, 'attend_near', (like(heads, COUNT, HD), state, state, sta...  3.73 us
  transfers between devices with their start and end apart: 12, of which 6 were waited for; matrix products, arithmetic and copies ran while one was open for 0% of the time, Pallas kernels for 15%

profile of v1, /device:TPU:16, one launch (start us, length us, event | category | flops | bytes accessed | tf_op | source)
XLA Modules:
  0.0 64.0 jit_solution(3804328348045890915)
XLA Ops:
  0.0 3.0 %project_kv.1 = (bf16[136,256]{1,0:T(8,128)(2,1)S(1)}, bf16[136,256]{1,0:T(8,128)(2,1)S(1)}) custom-call(bf16[128,4096]{1,0:T(8,128)(2,1)} %tok.3, bf16[4096,256]{1,0:T(8,128)(2,1)} %wk.1, bf16[4096,256]{1,0:T(8,128)(2,1)} %wv.1, s32[1,128]{1,0:T(1,128)} %bitcast.3, f32[4096,128]{1,0:T(8,128)} %constant.2.clone.table), custom_call_target="tpu_custom_call" | custom-call | flops 536870912 | bytes 5242880 | tf_op jit(solution)/shard_map/project_kv/pallas_call | solution.py:121
  3.1 1.2 %collective-permute-done.came = bf16[136,256]{1,0:T(8,128)(2,1)S(1)} collective-permute-done((bf16[136,256]{1,0:T(8,128)(2,1)S(1)}, bf16[136,256]{1,0:T(8,128)(2,1)S(1)}, u32[]{:S(2)}, u32[]{:S(2)}) %collective-permute-start) | collective-permute-done | bytes 69664 | tf_op jit(solution)/shard_map/ppermute | solution.py:353
  4.4 3.7 %collective-permute-start.1 = (bf16[264,256]{1,0:T(8,128)(2,1)S(1)}, bf16[264,256]{1,0:T(8,128)(2,1)S(1)}, u32[]{:S(2)}, u32[]{:S(2)}) collective-permute-start(bf16[264,256]{1,0:T(8,128)(2,1)S(1)} %merge.1.unit), channel_id=1, source_target_pairs={{0,8},{4,36},{8,16},{12,44},{16,24},{20,52},{24,32},{28,60},{32,40... | collective-permute-start | bytes 405512 | tf_op jit(solution)/shard_map/ppermute | solution.py:361
  8.1 4.6 %collective-permute-start.2 = (bf16[264,256]{1,0:T(8,128)(2,1)S(1)}, bf16[264,256]{1,0:T(8,128)(2,1)S(1)}, u32[]{:S(2)}, u32[]{:S(2)}) collective-permute-start(bf16[264,256]{1,0:T(8,128)(2,1)S(1)} %merge.1.unit), channel_id=1, source_target_pairs={{0,16},{4,68},{8,24},{12,76},{16,32},{20,84},{24,40},{28,92},{32,4... | collective-permute-start | bytes 405512 | tf_op jit(solution)/shard_map/ppermute | solution.py:361
  12.7 4.1 %collective-permute-start.3 = (bf16[264,256]{1,0:T(8,128)(2,1)S(1)}, bf16[264,256]{1,0:T(8,128)(2,1)S(1)}, u32[]{:S(2)}, u32[]{:S(2)}) collective-permute-start(bf16[264,256]{1,0:T(8,128)(2,1)S(1)} %merge.1.unit), channel_id=1, source_target_pairs={{0,24},{8,32},{16,40},{24,48},{28,124},{32,56},{40,64},{48,72},{56... | collective-permute-start | bytes 405512 | tf_op jit(solution)/shard_map/ppermute | solution.py:361
  16.8 4.7 %project_q.1 = (bf16[128,512]{1,0:T(8,128)(2,1)S(1)}, bf16[128,512]{1,0:T(8,128)(2,1)S(1)}) custom-call(bf16[128,4096]{1,0:T(8,128)(2,1)} %tok.3, bf16[4096,1024]{1,0:T(8,128)(2,1)} %wq.1, f32[4096,128]{1,0:T(8,128)} %constant.2.clone.table), custom_call_target="tpu_custom_call" | custom-call | flops 1073741824 | bytes 9437184 | tf_op jit(solution)/shard_map/project_q/pallas_call | solution.py:188
  21.7 2.2 %collective-permute-start.5 = (bf16[1056,256]{1,0:T(8,128)(2,1)S(1)}, bf16[1056,256]{1,0:T(8,128)(2,1)S(1)}, u32[]{:S(2)}, u32[]{:S(2)}) collective-permute-start(bf16[1056,256]{1,0:T(8,128)(2,1)S(1)} %get-tuple-element.36), channel_id=1, source_target_pairs={{0,32},{4,12},{8,40},{12,20},{16,48},{20,28},{24,56},{28,4},{32,64... | collective-permute-start | bytes 1622024 | tf_op jit(solution)/shard_map/ppermute | solution.py:361
  23.9 1.3 %collective-permute-start.6 = (bf16[528,256]{1,0:T(8,128)(2,1)S(1)}, bf16[528,256]{1,0:T(8,128)(2,1)S(1)}, u32[]{:S(2)}, u32[]{:S(2)}) collective-permute-start(bf16[528,256]{1,0:T(8,128)(2,1)S(1)} %get-tuple-element.37), channel_id=1, source_target_pairs={{0,64},{4,20},{8,72},{12,28},{16,80},{20,4},{24,88},{28,12},{32,96... | collective-permute-start | bytes 811016 | tf_op jit(solution)/shard_map/ppermute | solution.py:361
  25.2 0.7 %collective-permute-start.7 = (bf16[528,256]{1,0:T(8,128)(2,1)S(1)}, bf16[528,256]{1,0:T(8,128)(2,1)S(1)}, u32[]{:S(2)}, u32[]{:S(2)}) collective-permute-start(bf16[528,256]{1,0:T(8,128)(2,1)S(1)} %get-tuple-element.38), channel_id=1, source_target_pairs={{4,28},{12,4},{20,12},{28,20},{36,60},{44,36},{52,44},{60,52},{68,... | collective-permute-start | bytes 811016 | tf_op jit(solution)/shard_map/ppermute | solution.py:361
  25.9 0.2 collective-permute-start.4
  26.1 1.2 %collective-permute-done.4.qr = bf16[128,512]{1,0:T(8,128)(2,1)S(1)} collective-permute-done((bf16[128,512]{1,0:T(8,128)(2,1)S(1)}, bf16[128,512]{1,0:T(8,128)(2,1)S(1)}, u32[]{:S(2)}, u32[]{:S(2)}) %collective-permute-start.4) | collective-permute-done | bytes 131104 | tf_op jit(solution)/shard_map/ppermute | solution.py:353
  27.3 3.7 %attend_near.1 = (bf16[4,256,128]{2,1,0:T(8,128)(2,1)S(1)}, f32[4,256,128]{2,1,0:T(8,128)S(1)}, f32[4,256,128]{2,1,0:T(8,128)S(1)}, f32[4,256,128]{2,1,0:T(8,128)S(1)}) custom-call(bf16[128,512]{1,0:T(8,128)(2,1)S(1)} %get-tuple-element.27.qm, bf16[128,512]{1,0:T(8,128)(2,1)S(1)} %collective-permute-done.4.qr, bf16[264,256]{1,0:T(8,128)(2,1)S(1)} %merge.1.unit, ...), custom_call_target="tpu_custom_call" | custom-call | flops 536870912 | bytes 1048576 | tf_op jit(solution)/shard_map/attend_near/pallas_call | solution.py:288
  31.0 5.0 %collective-permute-done.6.far_b = bf16[528,256]{1,0:T(8,128)(2,1)S(1)} collective-permute-done((bf16[528,256]{1,0:T(8,128)(2,1)S(1)}, bf16[528,256]{1,0:T(8,128)(2,1)S(1)}, u32[]{:S(2)}, u32[]{:S(2)}) %collective-permute-start.6) | collective-permute-done | bytes 270368 | tf_op jit(solution)/shard_map/ppermute | solution.py:361
  36.0 5.7 %attend_far.1 = (bf16[128,512]{1,0:T(8,128)(2,1)S(1)}, bf16[128,512]{1,0:T(8,128)(2,1)S(1)}) custom-call(bf16[4,256,128]{2,1,0:T(8,128)(2,1)S(1)} %get-tuple-element.32.qs, f32[4,256,128]{2,1,0:T(8,128)S(1)} %get-tuple-element.33.m_in, f32[4,256,128]{2,1,0:T(8,128)S(1)} %get-tuple-element.34.l_in, f32[4,256,128]{2,1,0:T(8,128)S(1)} %get-tuple-element.35.acc_in, ...), custom_call_target="tpu_custom_call" | custom-call | flops 939524096 | bytes 1048576 | tf_op jit(solution)/shard_map/attend_far/pallas_call | solution.py:321
  41.8 1.3 %collective-permute-done.8.xr = bf16[128,512]{1,0:T(8,128)(2,1)S(1)} collective-permute-done((bf16[128,512]{1,0:T(8,128)(2,1)S(1)}, bf16[128,512]{1,0:T(8,128)(2,1)S(1)}, u32[]{:S(2)}, u32[]{:S(2)}) %collective-permute-start.8) | collective-permute-done | bytes 131104 | tf_op jit(solution)/shard_map/ppermute | solution.py:353
  43.2 0.5 project_out.7
  43.6 4.1 %collective-permute-start.11 = (bf16[128,1024]{1,0:T(8,128)(2,1)S(1)}, bf16[128,1024]{1,0:T(8,128)(2,1)S(1)}, u32[]{:S(2)}, u32[]{:S(2)}) collective-permute-start(bf16[128,1024]{1,0:T(8,128)(2,1)S(1)} %project_out.7), channel_id=1, source_target_pairs={{0,3},{1,0},{2,1},{3,2},{4,7},{5,4},{6,5},{7,6},{8,11},{9,8},{10,9... | collective-permute-start | bytes 786440 | tf_op jit(solution)/shard_map/ppermute | solution.py:395
  47.7 0.4 project_out.6
  48.3 0.5 project_out.5
  48.7 1.9 %collective-permute-start.9 = (bf16[128,1024]{1,0:T(8,128)(2,1)S(1)}, bf16[128,1024]{1,0:T(8,128)(2,1)S(1)}, u32[]{:S(2)}, u32[]{:S(2)}) collective-permute-start(bf16[128,1024]{1,0:T(8,128)(2,1)S(1)} %project_out.5), channel_id=1, source_target_pairs={{0,2},{1,3},{2,0},{3,1},{4,6},{5,7},{6,4},{7,5},{8,10},{9,11},{10,... | collective-permute-start | bytes 786440 | tf_op jit(solution)/shard_map/ppermute | solution.py:395
  50.6 0.5 project_out.4
  51.1 8.1 %collective-permute-done.11 = bf16[128,1024]{1,0:T(8,128)(2,1)S(1)} collective-permute-done((bf16[128,1024]{1,0:T(8,128)(2,1)S(1)}, bf16[128,1024]{1,0:T(8,128)(2,1)S(1)}, u32[]{:S(2)}, u32[]{:S(2)}) %collective-permute-start.11) | collective-permute-done | bytes 262176 | tf_op jit(solution)/shard_map/ppermute | solution.py:395
  59.2 3.9 %collective-permute-done.10 = bf16[128,1024]{1,0:T(8,128)(2,1)S(1)} collective-permute-done((bf16[128,1024]{1,0:T(8,128)(2,1)S(1)}, bf16[128,1024]{1,0:T(8,128)(2,1)S(1)}, u32[]{:S(2)}, u32[]{:S(2)}) %collective-permute-start.10) | collective-permute-done | bytes 262176 | tf_op jit(solution)/shard_map/ppermute | solution.py:395
  63.1 0.9 %add_convert_fusion = bf16[128,1024]{1,0:T(8,128)(2,1)} fusion(bf16[128,1024]{1,0:T(8,128)(2,1)S(1)} %collective-permute-done.11, bf16[128,1024]{1,0:T(8,128)(2,1)S(1)} %collective-permute-done.10, bf16[128,1024]{1,0:T(8,128)(2,1)S(1)} %collective-permute-done.9, bf16[128,1024]{1,0:T(8,128)(2,1)S(1)} %project_out.4), kind=kLoop, calls=%fused_computation | loop fusion | flops 1048576 | bytes 1310720 | tf_op jit(solution)/shard_map/convert_element_type | solution.py:400
  (16 shorter events, 0.4 us)
Async XLA Ops:
  3.0 1.3 %collective-permute-start = (bf16[136,256]{1,0:T(8,128)(2,1)S(1)}, bf16[136,256]{1,0:T(8,128)(2,1)S(1)}, u32[]{:S(2)}, u32[]{:S(2)}) collective-permute-start(bf16[136,256]{1,0:T(8,128)(2,1)S(1)} %get-tuple-element.24), channel_id=1, source_target_pairs={{0,4},{4,0},{8,12},{12,8},{16,20},{20,16},{24,28},{28,24},{32,36},... | collective-permute-start | bytes 208904 | tf_op jit(solution)/shard_map/ppermute | solution.py:353
  4.4 38.8 %slice-start = ((s8[8388608]{0:T(1024)(128)(4,1)}), s8[4194304]{0:T(1024)(128)(4,1)S(1)}, s32[]{:S(2)}) async-start(s8[8388608]{0:T(1024)(128)(4,1)} %bitcast.1), calls=%async_computation | async-start | bytes 8388608
  4.4 38.7 %slice-start.1 = ((s8[8388608]{0:T(1024)(128)(4,1)}), s8[4194304]{0:T(1024)(128)(4,1)S(1)}, s32[]{:S(2)}) async-start(s8[8388608]{0:T(1024)(128)(4,1)} %bitcast.1), calls=%async_computation.1 | async-start | bytes 8388608
  4.4 17.1 %collective-permute-start.1 = (bf16[264,256]{1,0:T(8,128)(2,1)S(1)}, bf16[264,256]{1,0:T(8,128)(2,1)S(1)}, u32[]{:S(2)}, u32[]{:S(2)}) collective-permute-start(bf16[264,256]{1,0:T(8,128)(2,1)S(1)} %merge.1.unit), channel_id=1, source_target_pairs={{0,8},{4,36},{8,16},{12,44},{16,24},{20,52},{24,32},{28,60},{32,40... | collective-permute-start | bytes 405512 | tf_op jit(solution)/shard_map/ppermute | solution.py:361
  8.1 13.4 %collective-permute-start.2 = (bf16[264,256]{1,0:T(8,128)(2,1)S(1)}, bf16[264,256]{1,0:T(8,128)(2,1)S(1)}, u32[]{:S(2)}, u32[]{:S(2)}) collective-permute-start(bf16[264,256]{1,0:T(8,128)(2,1)S(1)} %merge.1.unit), channel_id=1, source_target_pairs={{0,16},{4,68},{8,24},{12,76},{16,32},{20,84},{24,40},{28,92},{32,4... | collective-permute-start | bytes 405512 | tf_op jit(solution)/shard_map/ppermute | solution.py:361
  12.7 8.8 %collective-permute-start.3 = (bf16[264,256]{1,0:T(8,128)(2,1)S(1)}, bf16[264,256]{1,0:T(8,128)(2,1)S(1)}, u32[]{:S(2)}, u32[]{:S(2)}) collective-permute-start(bf16[264,256]{1,0:T(8,128)(2,1)S(1)} %merge.1.unit), channel_id=1, source_target_pairs={{0,24},{8,32},{16,40},{24,48},{28,124},{32,56},{40,64},{48,72},{56... | collective-permute-start | bytes 405512 | tf_op jit(solution)/shard_map/ppermute | solution.py:361
  21.7 14.3 %collective-permute-start.5 = (bf16[1056,256]{1,0:T(8,128)(2,1)S(1)}, bf16[1056,256]{1,0:T(8,128)(2,1)S(1)}, u32[]{:S(2)}, u32[]{:S(2)}) collective-permute-start(bf16[1056,256]{1,0:T(8,128)(2,1)S(1)} %get-tuple-element.36), channel_id=1, source_target_pairs={{0,32},{4,12},{8,40},{12,20},{16,48},{20,28},{24,56},{28,4},{32,64... | collective-permute-start | bytes 1622024 | tf_op jit(solution)/shard_map/ppermute | solution.py:361
  23.9 12.1 %collective-permute-start.6 = (bf16[528,256]{1,0:T(8,128)(2,1)S(1)}, bf16[528,256]{1,0:T(8,128)(2,1)S(1)}, u32[]{:S(2)}, u32[]{:S(2)}) collective-permute-start(bf16[528,256]{1,0:T(8,128)(2,1)S(1)} %get-tuple-element.37), channel_id=1, source_target_pairs={{0,64},{4,20},{8,72},{12,28},{16,80},{20,4},{24,88},{28,12},{32,96... | collective-permute-start | bytes 811016 | tf_op jit(solution)/shard_map/ppermute | solution.py:361
  25.2 10.8 %collective-permute-start.7 = (bf16[528,256]{1,0:T(8,128)(2,1)S(1)}, bf16[528,256]{1,0:T(8,128)(2,1)S(1)}, u32[]{:S(2)}, u32[]{:S(2)}) collective-permute-start(bf16[528,256]{1,0:T(8,128)(2,1)S(1)} %get-tuple-element.38), channel_id=1, source_target_pairs={{4,28},{12,4},{20,12},{28,20},{36,60},{44,36},{52,44},{60,52},{68,... | collective-permute-start | bytes 811016 | tf_op jit(solution)/shard_map/ppermute | solution.py:361
  25.9 1.4 %collective-permute-start.4 = (bf16[128,512]{1,0:T(8,128)(2,1)S(1)}, bf16[128,512]{1,0:T(8,128)(2,1)S(1)}, u32[]{:S(2)}, u32[]{:S(2)}) collective-permute-start(bf16[128,512]{1,0:T(8,128)(2,1)S(1)} %get-tuple-element.28), channel_id=1, source_target_pairs={{0,4},{4,0},{8,12},{12,8},{16,20},{20,16},{24,28},{28,24},{32,36},... | collective-permute-start | bytes 393224 | tf_op jit(solution)/shard_map/ppermute | solution.py:353
  41.7 1.4 %collective-permute-start.8 = (bf16[128,512]{1,0:T(8,128)(2,1)S(1)}, bf16[128,512]{1,0:T(8,128)(2,1)S(1)}, u32[]{:S(2)}, u32[]{:S(2)}) collective-permute-start(bf16[128,512]{1,0:T(8,128)(2,1)S(1)} %get-tuple-element.40), channel_id=1, source_target_pairs={{0,4},{4,0},{8,12},{12,8},{16,20},{20,16},{24,28},{28,24},{32,36},... | collective-permute-start | bytes 393224 | tf_op jit(solution)/shard_map/ppermute | solution.py:353
  43.6 15.6 %collective-permute-start.11 = (bf16[128,1024]{1,0:T(8,128)(2,1)S(1)}, bf16[128,1024]{1,0:T(8,128)(2,1)S(1)}, u32[]{:S(2)}, u32[]{:S(2)}) collective-permute-start(bf16[128,1024]{1,0:T(8,128)(2,1)S(1)} %project_out.7), channel_id=1, source_target_pairs={{0,3},{1,0},{2,1},{3,2},{4,7},{5,4},{6,5},{7,6},{8,11},{9,8},{10,9... | collective-permute-start | bytes 786440 | tf_op jit(solution)/shard_map/ppermute | solution.py:395
  48.2 15.0 %collective-permute-start.10 = (bf16[128,1024]{1,0:T(8,128)(2,1)S(1)}, bf16[128,1024]{1,0:T(8,128)(2,1)S(1)}, u32[]{:S(2)}, u32[]{:S(2)}) collective-permute-start(bf16[128,1024]{1,0:T(8,128)(2,1)S(1)} %project_out.6), channel_id=1, source_target_pairs={{0,1},{1,2},{2,3},{3,0},{4,5},{5,6},{6,7},{7,4},{8,9},{9,10},{10,1... | collective-permute-start | bytes 786440 | tf_op jit(solution)/shard_map/ppermute | solution.py:395
  48.7 14.4 %collective-permute-start.9 = (bf16[128,1024]{1,0:T(8,128)(2,1)S(1)}, bf16[128,1024]{1,0:T(8,128)(2,1)S(1)}, u32[]{:S(2)}, u32[]{:S(2)}) collective-permute-start(bf16[128,1024]{1,0:T(8,128)(2,1)S(1)} %project_out.5), channel_id=1, source_target_pairs={{0,2},{1,3},{2,0},{3,1},{4,6},{5,7},{6,4},{7,5},{8,10},{9,11},{10,... | collective-permute-start | bytes 786440 | tf_op jit(solution)/shard_map/ppermute | solution.py:395

commit v2 on v1

--- a/solution.py
+++ b/solution.py
@@ -179,7 +179,7 @@
             got = more if got is None else got + more
         for h in range(half // HD):
             cols = slice(h * HD, (h + 1) * HD)
-            out[:, cols] = rot(got[:, cols]).astype(BF16)
+            out[:, cols] = (rot(got[:, cols]) * SCALE).astype(BF16)
 
 
 def project_q(tokens, w_query, table):
@@ -197,28 +197,35 @@
     )(tokens, w_query, table)
 
 
+NONE = 99
+NEAR = ((1, 2, 3), (4, 8, NONE))
+FAR_A = ((4, 5, 6), (1, 5, 9))
+FAR_B = ((8, 9), (2, 6))
+FAR_C = ((7, NONE), (3, 7))
+
+
 def bundle_body(unit, r1, r2, r3, out_a, out_b, out_c, slots):
     place = lax.axis_index("ctx")
-    odd = lax.rem(place, 2)
+    odd = lax.rem(place, 2) == 1
     column = lax.rem(lax.div(place, 2), 4)
-    for i, src in enumerate((unit, r1, r2, r3, unit)):
+    for i, src in enumerate((unit, r1, r2, r3)):
         slots[i] = src[...]
 
-    def fill(out, count, late):
-        skip = jnp.where((odd == 1) & (column >= late), 1, 0)
-        for i in range(count):
-            out[i * UNIT : (i + 1) * UNIT, :] = slots[skip + i]
-
-    fill(out_a, 4, 3)
-    fill(out_b, 2, 2)
-    fill(out_c, 2, 1)
+    def fill(out, even, late):
+        skip = jnp.where(column >= late, 1, 0)
+        for i, at in enumerate(even):
+            out[i * UNIT : (i + 1) * UNIT, :] = slots[jnp.where(odd, skip + i, at)]
+
+    fill(out_a, (0, 1, 2), 3)
+    fill(out_b, (0, 1), 2)
+    fill(out_c, (3, 3), 1)
 
 
 def bundle(unit, r1, r2, r3):
     return call(
         bundle_body, "bundle",
-        (like(4 * UNIT, 2 * HD), like(2 * UNIT, 2 * HD), like(2 * UNIT, 2 * HD)),
-        [VMEM] * 4, (VMEM,) * 3, [pltpu.VMEM((5, UNIT, 2 * HD), BF16)], limit=2,
+        (like(3 * UNIT, 2 * HD), like(2 * UNIT, 2 * HD), like(2 * UNIT, 2 * HD)),
+        [VMEM] * 4, (VMEM,) * 3, [pltpu.VMEM((4, UNIT, 2 * HD), BF16)], limit=2,
     )(unit, r1, r2, r3)
 
 
@@ -226,30 +233,9 @@
 CONTRACT = (((1,), (1,)), ((), ()))
 
 
-def add_unit(qs, src, base, q_tag, q_first, state, allow=True):
-    m_s, l_s, acc = state
-    k_tag = src[pl.ds(base + COUNT, 8), :].astype(F32)
-
-    @pl.when((jnp.max(k_tag) >= q_first) & allow)
-    def _():
-        bias = jnp.where(k_tag[0:1, :] == q_tag, 0.0, -1e30)
-        keys = src[pl.ds(base, COUNT), :HD]
-        values = src[pl.ds(base, COUNT), HD:]
-        for h in range(qs.shape[0]):
-            s = lax.dot_general(qs[h], keys, CONTRACT, preferred_element_type=F32)
-            s = s * SCALE + bias
-            old = m_s[h]
-            top = jnp.maximum(old, jnp.max(s, axis=1, keepdims=True))
-            fade = jnp.exp2(old - top)
-            w = jnp.exp2(s - jnp.concatenate([top, top], axis=1))
-            m_s[h] = top
-            l_s[h] = fade * l_s[h] + jnp.sum(w, axis=1, keepdims=True)
-            acc[h] = fade * acc[h] + jnp.dot(w.astype(BF16), values, preferred_element_type=F32)
-
-
 def tags_of(unit):
     tags = unit[COUNT:UNIT, :].astype(F32)
-    return tags, jnp.transpose(tags, (1, 0))[:, 0:1], jnp.min(tags)
+    return tags, jnp.transpose(tags, (1, 0))[:, 0:1]
 
 
 def spans():
@@ -257,6 +243,35 @@
     own = pl.ds(pl.multiple_of(core * ROWS, ROWS), ROWS)
     other = pl.ds(pl.multiple_of((1 - core) * ROWS, ROWS), ROWS)
     return own, other
+
+
+def with_ones(values):
+    return jnp.concatenate([values, jnp.ones((COUNT, HD), BF16)], axis=1)
+
+
+def add_units(qs, pieces, q_tag, state):
+    m_s, l_s, acc = state
+    place = lax.axis_index("ctx")
+    odd = lax.rem(place, 2) == 1
+    chip = lax.div(place, 2)
+    for src, distances in pieces:
+        for i, (even_step, odd_step) in enumerate(zip(*distances)):
+            base = i * UNIT
+            valid = chip >= jnp.where(odd, odd_step, even_step)
+            k_tag = src[base + COUNT : base + UNIT, :].astype(F32)[0:1, :]
+            bias = jnp.where((k_tag == q_tag) & valid, 0.0, -1e30)
+            keys = src[base : base + COUNT, :HD]
+            values = with_ones(src[base : base + COUNT, HD:])
+            for h in range(qs.shape[0]):
+                s = lax.dot_general(qs[h], keys, CONTRACT, preferred_element_type=F32) + bias
+                old = m_s[h]
+                top = jnp.maximum(old, jnp.max(s, axis=1, keepdims=True))
+                fade = jnp.exp2(old - top)
+                w = jnp.exp2(s - jnp.concatenate([top, top], axis=1)).astype(BF16)
+                got = jnp.dot(w, values, preferred_element_type=F32)
+                m_s[h] = top
+                l_s[h] = fade * l_s[h] + got[:, HD:]
+                acc[h] = fade * acc[h] + got[:, :HD]
 
 
 def near_body(qm, qr, unit, r1, r2, r3, qs, m_s, l_s, acc):
@@ -265,21 +280,22 @@
     for h in range(heads):
         qs[h, own, :] = qm[:, h * HD : (h + 1) * HD]
         qs[h, other, :] = qr[:, h * HD : (h + 1) * HD]
-    tags, q_tag, q_first = tags_of(unit)
+    tags, q_tag = tags_of(unit)
     rows = lax.broadcasted_iota(jnp.int32, (COUNT, COUNT), 0)
     cols = lax.broadcasted_iota(jnp.int32, (COUNT, COUNT), 1)
     bias = jnp.where((tags[0:1, :] == q_tag) & (cols <= rows), 0.0, -1e30)
-    keys, values = unit[:COUNT, :HD], unit[:COUNT, HD:]
+    keys, values = unit[:COUNT, :HD], with_ones(unit[:COUNT, HD:])
     for h in range(heads):
-        s = lax.dot_general(qs[h], keys, CONTRACT, preferred_element_type=F32)
-        s = s * SCALE + bias
+        s = lax.dot_general(qs[h], keys, CONTRACT, preferred_element_type=F32) + bias
         top = jnp.max(s, axis=1, keepdims=True)
-        w = jnp.exp2(s - top)
+        got = jnp.dot(jnp.exp2(s - top).astype(BF16), values, preferred_element_type=F32)
         m_s[h] = jnp.broadcast_to(top, (COUNT, HD))
-        l_s[h] = jnp.broadcast_to(jnp.sum(w, axis=1, keepdims=True), (COUNT, HD))
-        acc[h] = jnp.dot(w.astype(BF16), values, preferred_element_type=F32)
-    for src in (r1, r2, r3):
-        add_unit(qs, src, 0, q_tag, q_first, (m_s, l_s, acc))
+        l_s[h] = got[:, HD:]
+        acc[h] = got[:, :HD]
+    pieces = [
+        (src, ((even,), (odd,))) for src, even, odd in zip((r1, r2, r3), NEAR[0], NEAR[1])
+    ]
+    add_units(qs, pieces, q_tag, (m_s, l_s, acc))
 
 
 def attend_near(qm, qr, unit, r1, r2, r3):
@@ -287,61 +303,77 @@
     state = like(heads, COUNT, HD, dtype=F32)
     return call(
         near_body, "attend_near", (like(heads, COUNT, HD), state, state, state),
-        [VMEM] * 6, (VMEM,) * 4, limit=4,
+        [VMEM] * 6, (VMEM,) * 4, limit=8,
         flops=4 * heads * COUNT * 4 * COUNT * HD, exps=heads * COUNT * 4 * COUNT,
     )(qm, qr, unit, r1, r2, r3)
 
 
-def far_body(qs, m_in, l_in, acc_in, unit, far_a, far_b, far_c, mine, send, m_s, l_s, acc):
+def attend_far(side, qs, m_in, l_in, acc_in, unit, far_a, far_b, far_c):
     heads = qs.shape[0]
-    state = (m_s, l_s, acc)
-    for new, old in zip(state, (m_in, l_in, acc_in)):
-        new[...] = old[...]
-    _, q_tag, q_first = tags_of(unit)
-    even = core_index() == 0
-    for src, count in ((far_b, 2), (far_c, 2), (far_a, 4)):
-
-        def step(i, carry):
-            base = pl.multiple_of(i * UNIT, 8)
-            add_unit(qs, src, base, q_tag, q_first, state, even | (i < 3))
-            return carry
-
-        lax.fori_loop(0, count, step, 0)
-    own, other = spans()
-    for h in range(heads):
-        cols = slice(h * HD, (h + 1) * HD)
-        mine[:, cols] = (acc[h, own, :] / l_s[h, own, :]).astype(BF16)
-        send[:, cols] = (acc[h, other, :] / l_s[h, other, :]).astype(BF16)
-
-
-def attend_far(qs, m_in, l_in, acc_in, unit, far_a, far_b, far_c):
-    heads = qs.shape[0]
-    half = like(ROWS, heads * HD)
-    state = pltpu.VMEM((heads, COUNT, HD), F32)
-    return call(
-        far_body, "attend_far", (half, half), [VMEM] * 8, (VMEM,) * 2, [state] * 3, limit=6,
-        flops=4 * heads * COUNT * 7 * COUNT * HD, exps=heads * COUNT * 7 * COUNT,
+
+    def body(q_in, m_in, l_in, acc_in, unit, far_a, far_b, far_c, out, qs, tag_s, m_s, l_s, acc):
+        rows = spans()[side]
+        state = (m_s, l_s, acc)
+        for new, old in zip((qs, *state), (q_in, m_in, l_in, acc_in)):
+            for h in range(heads):
+                new[h] = old[h, rows, :]
+        tag_s[...] = jnp.broadcast_to(tags_of(unit)[1], (COUNT, HD))
+        pieces = ((far_b, FAR_B), (far_c, FAR_C), (far_a, FAR_A))
+        add_units(qs, pieces, tag_s[rows, :][:, 0:1], state)
+        for h in range(heads):
+            out[:, h * HD : (h + 1) * HD] = (acc[h] / l_s[h]).astype(BF16)
+
+    state = pltpu.VMEM((heads, ROWS, HD), F32)
+    return call(
+        body, "attend_far", like(ROWS, heads * HD), [VMEM] * 8, VMEM,
+        [pltpu.VMEM((heads, ROWS, HD), BF16), pltpu.VMEM((COUNT, HD), F32), state, state, state],
+        limit=8, flops=4 * heads * ROWS * 7 * COUNT * HD, exps=heads * ROWS * 7 * COUNT,
     )(qs, m_in, l_in, acc_in, unit, far_a, far_b, far_c)
 
 
-def project_out(xm, xr, w_out, shift, groups):
+def project_out(xm, xr, w_out, groups, parts, dtype):
     depth = xm.shape[1]
     width = w_out.shape[1] // groups
-
-    def body(xm, xr, w, out):
+    half = width // 2
+
+    def body(xm, xr, w, *outs):
         core = core_index()
-        group = lax.rem(lax.axis_index("head") + shift, groups)
-        cols = pl.ds(pl.multiple_of(group * width, width), width)
         own = pl.ds(pl.multiple_of(core * depth, depth), depth)
         other = pl.ds(pl.multiple_of((1 - core) * depth, depth), depth)
-        got = jnp.dot(xm[...], w[own, cols], preferred_element_type=F32)
-        got += jnp.dot(xr[...], w[other, cols], preferred_element_type=F32)
-        out[...] = got.astype(BF16)
-
-    return call(
-        body, "project_out", like(ROWS, width), [VMEM] * 3, VMEM, limit=4,
-        flops=2 * ROWS * 2 * depth * width, moved=3,
+        for (shift, side), out in zip(parts, outs):
+            group = lax.rem(lax.axis_index("head") + shift, groups)
+            cols = pl.ds(pl.multiple_of(group * width + side * half, half), half)
+            got = jnp.dot(xm[...], w[own, cols], preferred_element_type=F32)
+            got += jnp.dot(xr[...], w[other, cols], preferred_element_type=F32)
+            out[...] = got.astype(dtype)
+
+    return call(
+        body, "project_out", (like(ROWS, half, dtype=dtype),) * len(parts), [VMEM] * 3,
+        (VMEM,) * len(parts), limit=4,
+        flops=2 * ROWS * 2 * depth * half * len(parts), moved=len(parts),
     )(xm, xr, w_out)
+
+
+def add_body(a, b, p, q, out_a, out_b):
+    out_a[...] = (a[...] + p[...].astype(F32)).astype(BF16)
+    out_b[...] = (b[...] + q[...].astype(F32)).astype(BF16)
+
+
+def add_passing(a, b, p, q):
+    out = like(*p.shape)
+    return call(add_body, "add_passing", (out, out), [VMEM] * 4, (VMEM,) * 2, limit=2)(a, b, p, q)
+
+
+def total_body(own_a, own_b, left_a, left_b, right_a, right_b, out):
+    half = own_a.shape[1]
+    for at, pieces in ((0, (own_a, left_a, right_a)), (half, (own_b, left_b, right_b))):
+        total = pieces[0][...] + pieces[1][...].astype(F32) + pieces[2][...].astype(F32)
+        out[:, at : at + half] = total.astype(BF16)
+
+
+def add_total(*pieces):
+    rows, half = pieces[0].shape
+    return call(total_body, "add_total", like(rows, 2 * half), [VMEM] * 6, VMEM, limit=2)(*pieces)
 
 
 def shards(tokens, w_query, w_key, w_value, w_out, doc_ids):
@@ -353,21 +385,14 @@
         return lax.ppermute(value, "ctx", [(r, r ^ 1) for r in range(ranks)])
 
     def along(value, even, odd):
-        moves = []
-        for r in range(ranks):
-            chip = (odd if r % 2 else even)(r // 2)
-            if chip is not None and chip < ranks // 2:
-                moves.append((r, 2 * chip + r % 2))
+        moves = [(r, 2 * (odd if r % 2 else even)(r // 2) + r % 2) for r in range(ranks)]
         return lax.ppermute(value, "ctx", moves)
 
     def ahead(step):
-        return lambda chip: chip + step
+        return lambda chip: (chip + step) % (ranks // 2)
 
     def in_row(step):
         return lambda chip: chip // 4 * 4 + (chip + step) % 4
-
-    def nowhere(chip):
-        return None
 
     tokens, w_key, w_value, w_query, table, docs = (
         pltpu.with_memory_space_constraint(a, pltpu.HBM)
@@ -377,27 +402,30 @@
     unit = merge(mine, swap(send))
     r1 = along(unit, ahead(1), ahead(4))
     r2 = along(unit, ahead(2), ahead(8))
-    r3 = along(unit, ahead(3), lambda chip: 15 if chip == 3 else None)
+    r3 = along(unit, ahead(3), ahead(12))
     qm, qs = project_q(tokens, w_query, table)
     r1, r2, r3, qm, qs = lax.optimization_barrier((r1, r2, r3, qm, qs))
     qr = swap(qs)
     out_a, out_b, out_c = bundle(unit, r1, r2, r3)
     far_a = along(out_a, ahead(4), in_row(1))
     far_b = along(out_b, ahead(8), in_row(2))
-    far_c = along(out_c, nowhere, in_row(3))
+    far_c = along(out_c, ahead(4), in_row(3))
     state = attend_near(qm, qr, unit, r1, r2, r3)
-    xm, xs = attend_far(*state, unit, far_a, far_b, far_c)
-    xr = swap(xs)
-    came = []
-    for shift in (2, 1, 3):
-        partial = project_out(xm, xr, w_out, shift, groups)
-        came.append(
-            lax.ppermute(partial, "head", [(g, (g + shift) % groups) for g in range(groups)])
-        )
-    total = project_out(xm, xr, w_out, 0, groups).astype(F32)
-    for partial in came:
-        total = total + partial.astype(F32)
-    return total.astype(BF16)
+    far = (*state, unit, far_a, far_b, far_c)
+    xr = swap(attend_far(1, *far))
+    xm = attend_far(0, *far)
+
+    def shift(value, step):
+        return lax.ppermute(value, "head", [(g, (g + step) % groups) for g in range(groups)])
+
+    a2, b2 = project_out(xm, xr, w_out, groups, ((2, 0), (2, 1)), BF16)
+    pass_a, pass_b = shift(a2, 1), shift(b2, -1)
+    b1, a3 = project_out(xm, xr, w_out, groups, ((1, 1), (3, 0)), BF16)
+    left_b, right_a = shift(b1, 1), shift(a3, -1)
+    a1, b3, a0, b0 = project_out(xm, xr, w_out, groups, ((1, 0), (3, 1), (0, 0), (0, 1)), F32)
+    a1, b3 = add_passing(a1, b3, pass_a, pass_b)
+    left_a, right_b = shift(a1, 1), shift(b3, -1)
+    return add_total(a0, b0, left_a, left_b, right_a, right_b)
 
 
 def solution(mesh):

time: 63.1 us -> 52.3 us (0.83)
  the two profiles are of different devices: /device:TPU:16 before, /device:TPU:0 now
where the time goes in v2:
time: 52.3 us; the launch traced here: 52.2 us
  starting transfers between devices  22.1 us (42%)
  Pallas kernels  15.4 us (29%)
  waiting for transfers between devices  14.5 us (28%)
    ppermute x6, starting transfers between devices, along(): return lax.ppermute(value, 'ctx', moves)  11 us
    ppermute x6, starting transfers between devices, shift(): lax.ppermute(value, 'head', [(g, (g + step) % groups) for g in range(grou...  10.9 us
    ppermute x6, waiting for transfers between devices, along(): return lax.ppermute(value, 'ctx', moves)  8.82 us
    pallas_call x1, Pallas kernels, project_q(): call(q_body, 'project_q', (half, half), [HBM] * 3, (VMEM, VMEM), [pltpu.V...  4.67 us
    pallas_call x2, Pallas kernels, attend_far(): call(body, 'attend_far', like(ROWS, heads * HD), [VMEM] * 8, VMEM, [pltpu...  3.27 us
    ppermute x6, waiting for transfers between devices, shift(): lax.ppermute(value, 'head', [(g, (g + step) % groups) for g in range(grou...  3.08 us
    pallas_call x1, Pallas kernels, project_kv(): call(kv_body, 'project_kv', (half, half), [HBM] * 5, (VMEM, VMEM), [pltpu...  3.04 us
    ppermute x3, waiting for transfers between devices, swap(): return lax.ppermute(value, 'ctx', [(r, r ^ 1) for r in range(ranks)])  2.59 us
  transfers between devices with their start and end apart: 15, of which 7 were waited for; matrix products, arithmetic and copies ran while one was open for 0% of the time, Pallas kernels for 18%

profile of v2, /device:TPU:0, one launch (start us, length us, event | category | flops | bytes accessed | tf_op | source)
XLA Modules:
  0.0 52.2 jit_solution(219798941136218146)
XLA Ops:
  0.0 3.0 %project_kv.1 = (bf16[136,256]{1,0:T(8,128)(2,1)S(1)}, bf16[136,256]{1,0:T(8,128)(2,1)S(1)}) custom-call(bf16[128,4096]{1,0:T(8,128)(2,1)} %tok.3, bf16[4096,256]{1,0:T(8,128)(2,1)} %wk.1, bf16[4096,256]{1,0:T(8,128)(2,1)} %wv.1, s32[1,128]{1,0:T(1,128)} %bitcast.3, f32[4096,128]{1,0:T(8,128)} %constant.2.clone.table), custom_call_target="tpu_custom_call" | custom-call | flops 536870912 | bytes 5242880 | tf_op jit(solution)/shard_map/project_kv/pallas_call | solution.py:121
  3.2 1.2 %collective-permute-done.came = bf16[136,256]{1,0:T(8,128)(2,1)S(1)} collective-permute-done((bf16[136,256]{1,0:T(8,128)(2,1)S(1)}, bf16[136,256]{1,0:T(8,128)(2,1)S(1)}, u32[]{:S(2)}, u32[]{:S(2)}) %collective-permute-start) | collective-permute-done | bytes 69664 | tf_op jit(solution)/shard_map/ppermute | solution.py:385
  4.4 1.6 %collective-permute-start.1 = (bf16[264,256]{1,0:T(8,128)(2,1)S(1)}, bf16[264,256]{1,0:T(8,128)(2,1)S(1)}, u32[]{:S(2)}, u32[]{:S(2)}) collective-permute-start(bf16[264,256]{1,0:T(8,128)(2,1)S(1)} %merge.1.unit), channel_id=1, source_target_pairs={{0,8},{4,36},{8,16},{12,44},{16,24},{20,52},{24,32},{28,60},{32,40... | collective-permute-start | bytes 405512 | tf_op jit(solution)/shard_map/ppermute | solution.py:389
  6.1 2.7 %collective-permute-start.2 = (bf16[264,256]{1,0:T(8,128)(2,1)S(1)}, bf16[264,256]{1,0:T(8,128)(2,1)S(1)}, u32[]{:S(2)}, u32[]{:S(2)}) collective-permute-start(bf16[264,256]{1,0:T(8,128)(2,1)S(1)} %merge.1.unit), channel_id=1, source_target_pairs={{0,16},{4,68},{8,24},{12,76},{16,32},{20,84},{24,40},{28,92},{32,4... | collective-permute-start | bytes 405512 | tf_op jit(solution)/shard_map/ppermute | solution.py:389
  8.8 2.4 %collective-permute-start.3 = (bf16[264,256]{1,0:T(8,128)(2,1)S(1)}, bf16[264,256]{1,0:T(8,128)(2,1)S(1)}, u32[]{:S(2)}, u32[]{:S(2)}) collective-permute-start(bf16[264,256]{1,0:T(8,128)(2,1)S(1)} %merge.1.unit), channel_id=1, source_target_pairs={{0,24},{4,100},{8,32},{12,108},{16,40},{20,116},{24,48},{28,124},{... | collective-permute-start | bytes 405512 | tf_op jit(solution)/shard_map/ppermute | solution.py:389
  11.3 4.7 %project_q.1 = (bf16[128,512]{1,0:T(8,128)(2,1)S(1)}, bf16[128,512]{1,0:T(8,128)(2,1)S(1)}) custom-call(bf16[128,4096]{1,0:T(8,128)(2,1)} %tok.3, bf16[4096,1024]{1,0:T(8,128)(2,1)} %wq.1, f32[4096,128]{1,0:T(8,128)} %constant.2.clone.table), custom_call_target="tpu_custom_call" | custom-call | flops 1073741824 | bytes 9437184 | tf_op jit(solution)/shard_map/project_q/pallas_call | solution.py:188
  15.9 0.9 %collective-permute-done.2.r2 = bf16[264,256]{1,0:T(8,128)(2,1)S(1)} collective-permute-done((bf16[264,256]{1,0:T(8,128)(2,1)S(1)}, bf16[264,256]{1,0:T(8,128)(2,1)S(1)}, u32[]{:S(2)}, u32[]{:S(2)}) %collective-permute-start.2) | collective-permute-done | bytes 135200 | tf_op jit(solution)/shard_map/ppermute | solution.py:389
  17.7 1.9 %collective-permute-start.6 = (bf16[528,256]{1,0:T(8,128)(2,1)S(1)}, bf16[528,256]{1,0:T(8,128)(2,1)S(1)}, u32[]{:S(2)}, u32[]{:S(2)}) collective-permute-start(bf16[528,256]{1,0:T(8,128)(2,1)S(1)} %get-tuple-element.45), channel_id=1, source_target_pairs={{0,64},{4,20},{8,72},{12,28},{16,80},{20,4},{24,88},{28,12},{32,96... | collective-permute-start | bytes 811016 | tf_op jit(solution)/shard_map/ppermute | solution.py:389
  19.6 1.9 %collective-permute-start.7 = (bf16[528,256]{1,0:T(8,128)(2,1)S(1)}, bf16[528,256]{1,0:T(8,128)(2,1)S(1)}, u32[]{:S(2)}, u32[]{:S(2)}) collective-permute-start(bf16[528,256]{1,0:T(8,128)(2,1)S(1)} %get-tuple-element.46), channel_id=1, source_target_pairs={{0,32},{4,28},{8,40},{12,4},{16,48},{20,12},{24,56},{28,20},{32,64... | collective-permute-start | bytes 811016 | tf_op jit(solution)/shard_map/ppermute | solution.py:389
  21.4 1.3 %collective-permute-done.4.qr = bf16[128,512]{1,0:T(8,128)(2,1)S(1)} collective-permute-done((bf16[128,512]{1,0:T(8,128)(2,1)S(1)}, bf16[128,512]{1,0:T(8,128)(2,1)S(1)}, u32[]{:S(2)}, u32[]{:S(2)}) %collective-permute-start.4) | collective-permute-done | bytes 131104 | tf_op jit(solution)/shard_map/ppermute | solution.py:385
  22.8 1.9 %attend_near.1 = (bf16[4,256,128]{2,1,0:T(8,128)(2,1)S(1)}, f32[4,256,128]{2,1,0:T(8,128)S(1)}, f32[4,256,128]{2,1,0:T(8,128)S(1)}, f32[4,256,128]{2,1,0:T(8,128)S(1)}) custom-call(bf16[128,512]{1,0:T(8,128)(2,1)S(1)} %get-tuple-element.35.qm, bf16[128,512]{1,0:T(8,128)(2,1)S(1)} %collective-permute-done.4.qr, bf16[264,256]{1,0:T(8,128)(2,1)S(1)} %merge.1.unit, ...), custom_call_target="tpu_custom_call" | custom-call | flops 536870912 | bytes 1048576 | tf_op jit(solution)/shard_map/attend_near/pallas_call | solution.py:304
  24.7 3.8 %collective-permute-done.6.far_b = bf16[528,256]{1,0:T(8,128)(2,1)S(1)} collective-permute-done((bf16[528,256]{1,0:T(8,128)(2,1)S(1)}, bf16[528,256]{1,0:T(8,128)(2,1)S(1)}, u32[]{:S(2)}, u32[]{:S(2)}) %collective-permute-start.6) | collective-permute-done | bytes 270368 | tf_op jit(solution)/shard_map/ppermute | solution.py:389
  28.5 3.8 %collective-permute-done.7.far_c = bf16[528,256]{1,0:T(8,128)(2,1)S(1)} collective-permute-done((bf16[528,256]{1,0:T(8,128)(2,1)S(1)}, bf16[528,256]{1,0:T(8,128)(2,1)S(1)}, u32[]{:S(2)}, u32[]{:S(2)}) %collective-permute-start.7) | collective-permute-done | bytes 270368 | tf_op jit(solution)/shard_map/ppermute | solution.py:389
  32.3 1.6 %attend_far.3 = bf16[128,512]{1,0:T(8,128)(2,1)S(1)} custom-call(bf16[4,256,128]{2,1,0:T(8,128)(2,1)S(1)} %get-tuple-element.40.q_in, f32[4,256,128]{2,1,0:T(8,128)S(1)} %get-tuple-element.41.m_in, f32[4,256,128]{2,1,0:T(8,128)S(1)} %get-tuple-element.42.l_in, f32[4,256,128]{2,1,0:T(8,128)S(1)} %get-tuple-element.43.acc_in, bf16[264,256]{1,0:T(8,128)(2,1)S(1)} %merge.1.unit, ...), custom_call_target="tpu_custom_call" | custom-call | flops 469762048 | bytes 1048576 | tf_op jit(solution)/shard_map/attend_far/pallas_call | solution.py:327
  34.0 1.6 %attend_far.2.xm = bf16[128,512]{1,0:T(8,128)(2,1)S(1)} custom-call(bf16[4,256,128]{2,1,0:T(8,128)(2,1)S(1)} %get-tuple-element.40.q_in, f32[4,256,128]{2,1,0:T(8,128)S(1)} %get-tuple-element.41.m_in, f32[4,256,128]{2,1,0:T(8,128)S(1)} %get-tuple-element.42.l_in, f32[4,256,128]{2,1,0:T(8,128)S(1)} %get-tuple-element.43.acc_in, ...), custom_call_target="tpu_custom_call" | custom-call | flops 469762048 | bytes 1048576 | tf_op jit(solution)/shard_map/attend_far/pallas_call | solution.py:327
  35.7 0.5 project_out.4
  36.2 2.0 %collective-permute-start.9 = (bf16[128,512]{1,0:T(8,128)(2,1)S(1)}, bf16[128,512]{1,0:T(8,128)(2,1)S(1)}, u32[]{:S(2)}, u32[]{:S(2)}) collective-permute-start(bf16[128,512]{1,0:T(8,128)(2,1)S(1)} %get-tuple-element.51), channel_id=1, source_target_pairs={{0,1},{1,2},{2,3},{3,0},{4,5},{5,6},{6,7},{7,4},{8,9},{9,10},{10,1... | collective-permute-start | bytes 393224 | tf_op jit(solution)/shard_map/ppermute | solution.py:419
  38.1 2.4 %collective-permute-start.10 = (bf16[128,512]{1,0:T(8,128)(2,1)S(1)}, bf16[128,512]{1,0:T(8,128)(2,1)S(1)}, u32[]{:S(2)}, u32[]{:S(2)}) collective-permute-start(bf16[128,512]{1,0:T(8,128)(2,1)S(1)} %get-tuple-element.52), channel_id=1, source_target_pairs={{0,3},{1,0},{2,1},{3,2},{4,7},{5,4},{6,5},{7,6},{8,11},{9,8},{10,9... | collective-permute-start | bytes 393224 | tf_op jit(solution)/shard_map/ppermute | solution.py:419
  41.0 3.2 %collective-permute-start.13 = (bf16[128,512]{1,0:T(8,128)(2,1)S(1)}, bf16[128,512]{1,0:T(8,128)(2,1)S(1)}, u32[]{:S(2)}, u32[]{:S(2)}) collective-permute-start(bf16[128,512]{1,0:T(8,128)(2,1)S(1)} %get-tuple-element.55), channel_id=1, source_target_pairs={{0,3},{1,0},{2,1},{3,2},{4,7},{5,4},{6,5},{7,6},{8,11},{9,8},{10,9... | collective-permute-start | bytes 393224 | tf_op jit(solution)/shard_map/ppermute | solution.py:419
  44.3 0.7 %project_out.3 = (f32[128,512]{1,0:T(8,128)S(1)}, f32[128,512]{1,0:T(8,128)S(1)}, f32[128,512]{1,0:T(8,128)S(1)}, f32[128,512]{1,0:T(8,128)S(1)}) custom-call(bf16[128,512]{1,0:T(8,128)(2,1)S(1)} %attend_far.2.xm, bf16[128,512]{1,0:T(8,128)(2,1)S(1)} %collective-permute-done.8.xr, bf16[1024,4096]{1,0:T(8,128)(2,1)S(1)} %bitcast.2), custom_call_target="tpu_custom_call" | custom-call | flops 536870912 | bytes 4194304 | tf_op jit(solution)/shard_map/project_out/pallas_call | solution.py:350
  45.1 1.4 %collective-permute-start.11 = (bf16[128,512]{1,0:T(8,128)(2,1)S(1)}, bf16[128,512]{1,0:T(8,128)(2,1)S(1)}, u32[]{:S(2)}, u32[]{:S(2)}) collective-permute-start(bf16[128,512]{1,0:T(8,128)(2,1)S(1)} %get-tuple-element.53), channel_id=1, source_target_pairs={{0,1},{1,2},{2,3},{3,0},{4,5},{5,6},{6,7},{7,4},{8,9},{9,10},{10,1... | collective-permute-start | bytes 393224 | tf_op jit(solution)/shard_map/ppermute | solution.py:419
  46.5 1.9 %collective-permute-start.14 = (bf16[128,512]{1,0:T(8,128)(2,1)S(1)}, bf16[128,512]{1,0:T(8,128)(2,1)S(1)}, u32[]{:S(2)}, u32[]{:S(2)}) collective-permute-start(bf16[128,512]{1,0:T(8,128)(2,1)S(1)} %get-tuple-element.56), channel_id=1, source_target_pairs={{0,3},{1,0},{2,1},{3,2},{4,7},{5,4},{6,5},{7,6},{8,11},{9,8},{10,9... | collective-permute-start | bytes 393224 | tf_op jit(solution)/shard_map/ppermute | solution.py:419
  48.4 3.0 %collective-permute-done.11.left_a = bf16[128,512]{1,0:T(8,128)(2,1)S(1)} collective-permute-done((bf16[128,512]{1,0:T(8,128)(2,1)S(1)}, bf16[128,512]{1,0:T(8,128)(2,1)S(1)}, u32[]{:S(2)}, u32[]{:S(2)}) %collective-permute-start.11) | collective-permute-done | bytes 131104 | tf_op jit(solution)/shard_map/ppermute | solution.py:419
  51.4 0.8 %add_total.1 = bf16[128,1024]{1,0:T(8,128)(2,1)} custom-call(f32[128,512]{1,0:T(8,128)S(1)} %get-tuple-element.47.own_a, f32[128,512]{1,0:T(8,128)S(1)} %get-tuple-element.48.own_b, bf16[128,512]{1,0:T(8,128)(2,1)S(1)} %collective-permute-done.11.left_a, bf16[128,512]{1,0:T(8,128)(2,1)S(1)} %collective-permute-done.12.left_b, ...), custom_call_target="tpu_custom_call" | custom-call | bytes 1048576 | tf_op jit(solution)/shard_map/add_total/pallas_call | solution.py:376
  (23 shorter events, 1.7 us)
Async XLA Ops:
  3.0 32.6 %slice-start = ((s8[8388608]{0:T(1024)(128)(4,1)}), s8[4194304]{0:T(1024)(128)(4,1)S(1)}, s32[]{:S(2)}) async-start(s8[8388608]{0:T(1024)(128)(4,1)} %bitcast.1), calls=%async_computation | async-start | bytes 8388608
  3.1 1.3 %collective-permute-start = (bf16[136,256]{1,0:T(8,128)(2,1)S(1)}, bf16[136,256]{1,0:T(8,128)(2,1)S(1)}, u32[]{:S(2)}, u32[]{:S(2)}) collective-permute-start(bf16[136,256]{1,0:T(8,128)(2,1)S(1)} %get-tuple-element.32), channel_id=1, source_target_pairs={{0,4},{4,0},{8,12},{12,8},{16,20},{20,16},{24,28},{28,24},{32,36},... | collective-permute-start | bytes 208904 | tf_op jit(solution)/shard_map/ppermute | solution.py:385
  4.4 31.2 %slice-start.1 = ((s8[8388608]{0:T(1024)(128)(4,1)}), s8[4194304]{0:T(1024)(128)(4,1)S(1)}, s32[]{:S(2)}) async-start(s8[8388608]{0:T(1024)(128)(4,1)} %bitcast.1), calls=%async_computation.1 | async-start | bytes 8388608
  4.4 11.5 %collective-permute-start.1 = (bf16[264,256]{1,0:T(8,128)(2,1)S(1)}, bf16[264,256]{1,0:T(8,128)(2,1)S(1)}, u32[]{:S(2)}, u32[]{:S(2)}) collective-permute-start(bf16[264,256]{1,0:T(8,128)(2,1)S(1)} %merge.1.unit), channel_id=1, source_target_pairs={{0,8},{4,36},{8,16},{12,44},{16,24},{20,52},{24,32},{28,60},{32,40... | collective-permute-start | bytes 405512 | tf_op jit(solution)/shard_map/ppermute | solution.py:389
  6.1 10.7 %collective-permute-start.2 = (bf16[264,256]{1,0:T(8,128)(2,1)S(1)}, bf16[264,256]{1,0:T(8,128)(2,1)S(1)}, u32[]{:S(2)}, u32[]{:S(2)}) collective-permute-start(bf16[264,256]{1,0:T(8,128)(2,1)S(1)} %merge.1.unit), channel_id=1, source_target_pairs={{0,16},{4,68},{8,24},{12,76},{16,32},{20,84},{24,40},{28,92},{32,4... | collective-permute-start | bytes 405512 | tf_op jit(solution)/shard_map/ppermute | solution.py:389
  8.8 8.4 %collective-permute-start.3 = (bf16[264,256]{1,0:T(8,128)(2,1)S(1)}, bf16[264,256]{1,0:T(8,128)(2,1)S(1)}, u32[]{:S(2)}, u32[]{:S(2)}) collective-permute-start(bf16[264,256]{1,0:T(8,128)(2,1)S(1)} %merge.1.unit), channel_id=1, source_target_pairs={{0,24},{4,100},{8,32},{12,108},{16,40},{20,116},{24,48},{28,124},{... | collective-permute-start | bytes 405512 | tf_op jit(solution)/shard_map/ppermute | solution.py:389
  17.3 15.0 %collective-permute-start.5 = (bf16[792,256]{1,0:T(8,128)(2,1)S(1)}, bf16[792,256]{1,0:T(8,128)(2,1)S(1)}, u32[]{:S(2)}, u32[]{:S(2)}) collective-permute-start(bf16[792,256]{1,0:T(8,128)(2,1)S(1)} %get-tuple-element.44), channel_id=1, source_target_pairs={{0,32},{4,12},{8,40},{12,20},{16,48},{20,28},{24,56},{28,4},{32,64... | collective-permute-start | bytes 1216520 | tf_op jit(solution)/shard_map/ppermute | solution.py:389
  17.7 10.8 %collective-permute-start.6 = (bf16[528,256]{1,0:T(8,128)(2,1)S(1)}, bf16[528,256]{1,0:T(8,128)(2,1)S(1)}, u32[]{:S(2)}, u32[]{:S(2)}) collective-permute-start(bf16[528,256]{1,0:T(8,128)(2,1)S(1)} %get-tuple-element.45), channel_id=1, source_target_pairs={{0,64},{4,20},{8,72},{12,28},{16,80},{20,4},{24,88},{28,12},{32,96... | collective-permute-start | bytes 811016 | tf_op jit(solution)/shard_map/ppermute | solution.py:389
  19.6 12.7 %collective-permute-start.7 = (bf16[528,256]{1,0:T(8,128)(2,1)S(1)}, bf16[528,256]{1,0:T(8,128)(2,1)S(1)}, u32[]{:S(2)}, u32[]{:S(2)}) collective-permute-start(bf16[528,256]{1,0:T(8,128)(2,1)S(1)} %get-tuple-element.46), channel_id=1, source_target_pairs={{0,32},{4,28},{8,40},{12,4},{16,48},{20,12},{24,56},{28,20},{32,64... | collective-permute-start | bytes 811016 | tf_op jit(solution)/shard_map/ppermute | solution.py:389
  21.4 1.3 %collective-permute-start.4 = (bf16[128,512]{1,0:T(8,128)(2,1)S(1)}, bf16[128,512]{1,0:T(8,128)(2,1)S(1)}, u32[]{:S(2)}, u32[]{:S(2)}) collective-permute-start(bf16[128,512]{1,0:T(8,128)(2,1)S(1)} %get-tuple-element.36), channel_id=1, source_target_pairs={{0,4},{4,0},{8,12},{12,8},{16,20},{20,16},{24,28},{28,24},{32,36},... | collective-permute-start | bytes 393224 | tf_op jit(solution)/shard_map/ppermute | solution.py:385
  33.9 1.7 %collective-permute-start.8 = (bf16[128,512]{1,0:T(8,128)(2,1)S(1)}, bf16[128,512]{1,0:T(8,128)(2,1)S(1)}, u32[]{:S(2)}, u32[]{:S(2)}) collective-permute-start(bf16[128,512]{1,0:T(8,128)(2,1)S(1)} %attend_far.3), channel_id=1, source_target_pairs={{0,4},{4,0},{8,12},{12,8},{16,20},{20,16},{24,28},{28,24},{32,36},... | collective-permute-start | bytes 393224 | tf_op jit(solution)/shard_map/ppermute | solution.py:385
  36.2 8.8 %collective-permute-start.9 = (bf16[128,512]{1,0:T(8,128)(2,1)S(1)}, bf16[128,512]{1,0:T(8,128)(2,1)S(1)}, u32[]{:S(2)}, u32[]{:S(2)}) collective-permute-start(bf16[128,512]{1,0:T(8,128)(2,1)S(1)} %get-tuple-element.51), channel_id=1, source_target_pairs={{0,1},{1,2},{2,3},{3,0},{4,5},{5,6},{6,7},{7,4},{8,9},{9,10},{10,1... | collective-permute-start | bytes 393224 | tf_op jit(solution)/shard_map/ppermute | solution.py:419
  38.1 6.9 %collective-permute-start.10 = (bf16[128,512]{1,0:T(8,128)(2,1)S(1)}, bf16[128,512]{1,0:T(8,128)(2,1)S(1)}, u32[]{:S(2)}, u32[]{:S(2)}) collective-permute-start(bf16[128,512]{1,0:T(8,128)(2,1)S(1)} %get-tuple-element.52), channel_id=1, source_target_pairs={{0,3},{1,0},{2,1},{3,2},{4,7},{5,4},{6,5},{7,6},{8,11},{9,8},{10,9... | collective-permute-start | bytes 393224 | tf_op jit(solution)/shard_map/ppermute | solution.py:419
  40.9 7.4 %collective-permute-start.12 = (bf16[128,512]{1,0:T(8,128)(2,1)S(1)}, bf16[128,512]{1,0:T(8,128)(2,1)S(1)}, u32[]{:S(2)}, u32[]{:S(2)}) collective-permute-start(bf16[128,512]{1,0:T(8,128)(2,1)S(1)} %get-tuple-element.54), channel_id=1, source_target_pairs={{0,1},{1,2},{2,3},{3,0},{4,5},{5,6},{6,7},{7,4},{8,9},{9,10},{10,1... | collective-permute-start | bytes 393224 | tf_op jit(solution)/shard_map/ppermute | solution.py:419
  41.0 7.3 %collective-permute-start.13 = (bf16[128,512]{1,0:T(8,128)(2,1)S(1)}, bf16[128,512]{1,0:T(8,128)(2,1)S(1)}, u32[]{:S(2)}, u32[]{:S(2)}) collective-permute-start(bf16[128,512]{1,0:T(8,128)(2,1)S(1)} %get-tuple-element.55), channel_id=1, source_target_pairs={{0,3},{1,0},{2,1},{3,2},{4,7},{5,4},{6,5},{7,6},{8,11},{9,8},{10,9... | collective-permute-start | bytes 393224 | tf_op jit(solution)/shard_map/ppermute | solution.py:419
  45.1 6.3 %collective-permute-start.11 = (bf16[128,512]{1,0:T(8,128)(2,1)S(1)}, bf16[128,512]{1,0:T(8,128)(2,1)S(1)}, u32[]{:S(2)}, u32[]{:S(2)}) collective-permute-start(bf16[128,512]{1,0:T(8,128)(2,1)S(1)} %get-tuple-element.53), channel_id=1, source_target_pairs={{0,1},{1,2},{2,3},{3,0},{4,5},{5,6},{6,7},{7,4},{8,9},{9,10},{10,1... | collective-permute-start | bytes 393224 | tf_op jit(solution)/shard_map/ppermute | solution.py:419
  46.5 5.0 %collective-permute-start.14 = (bf16[128,512]{1,0:T(8,128)(2,1)S(1)}, bf16[128,512]{1,0:T(8,128)(2,1)S(1)}, u32[]{:S(2)}, u32[]{:S(2)}) collective-permute-start(bf16[128,512]{1,0:T(8,128)(2,1)S(1)} %get-tuple-element.56), channel_id=1, source_target_pairs={{0,3},{1,0},{2,1},{3,2},{4,7},{5,4},{6,5},{7,6},{8,11},{9,8},{10,9... | collective-permute-start | bytes 393224 | tf_op jit(solution)/shard_map/ppermute | solution.py:419

commit v3 on v2

v3 whole, which is shorter than its diff:
```python
import math

import jax
import jax.numpy as jnp
import numpy as np
from jax import lax
from jax.experimental import pallas as pl
from jax.experimental.pallas import tpu as pltpu
from jax.sharding import PartitionSpec as P

HD = 128
ROWS = 128
UNIT = 264
F32 = jnp.float32
BF16 = jnp.bfloat16
MIB = 1 << 20
SCALE = math.log2(math.e) / math.sqrt(HD)


def rope_table(count):
    half = HD // 2
    freqs = 500000.0 ** (-2.0 * np.arange(half, dtype=np.float64) / HD)
    angles = np.arange(count, dtype=np.float64)[:, None] * freqs[None, :]
    return np.concatenate([np.cos(angles), np.sin(angles)], axis=1).astype(np.float32)


def rotation(table):
    half = HD // 2
    cosine, sine = table[:, :half], table[:, half:]
    cosine = jnp.concatenate([cosine, cosine], axis=1)
    sine = jnp.concatenate([-sine, sine], axis=1)
    return lambda t: t * cosine + pltpu.roll(t, half, 1) * sine


SMEM = pl.BlockSpec(memory_space=pltpu.SMEM)
VMEM = pl.BlockSpec(memory_space=pltpu.VMEM)
HBM = pl.BlockSpec(memory_space=pltpu.HBM)


def like(*dims, dtype=BF16):
    return jax.ShapeDtypeStruct(dims, dtype)


def call(body, name, out, ins, outs, scratch=(), limit=4, flops=0, moved=1, exps=0):
    return pl.pallas_call(
        body,
        out_shape=out,
        in_specs=ins,
        out_specs=outs,
        scratch_shapes=list(scratch),
        name=name,
        cost_estimate=pl.CostEstimate(
            flops=flops, bytes_accessed=moved * MIB, transcendentals=exps
        ),
        compiler_params=pltpu.CompilerParams(vmem_limit_bytes=limit * MIB),
    )


def core_index():
    return lax.rem(lax.axis_index("ctx"), 2)


def table_rows(table):
    return table.at[pl.ds(pl.multiple_of(lax.axis_index("ctx") * ROWS, ROWS), ROWS), :]


def started(copies):
    for copy in copies:
        copy.start()
    return copies


KV_PARTS = 4
CHIP = 2 * ROWS


def halves():
    core = core_index()
    own = pl.ds(pl.multiple_of(core * ROWS, ROWS), ROWS)
    other = pl.ds(pl.multiple_of((1 - core) * ROWS, ROWS), ROWS)
    return own, other


def own_body(tok, wk, wv, docs, table, half, tok_s, w_s, docs_s, table_s, acc, sems):
    part = tok.shape[1] // KV_PARTS
    cols = pl.ds(pl.multiple_of(core_index() * HD, HD), HD)
    copies = []
    for i in range(KV_PARTS):
        cut = pl.ds(i * part, part)
        copies.append(
            started([
                pltpu.make_async_copy(tok.at[:, cut], tok_s.at[:, cut], sems.at[3 * i]),
                pltpu.make_async_copy(
                    wk.at[cut, cols], w_s.at[cut, pl.ds(0, HD)], sems.at[3 * i + 1]
                ),
                pltpu.make_async_copy(
                    wv.at[cut, cols], w_s.at[cut, pl.ds(HD, HD)], sems.at[3 * i + 2]
                ),
            ])
        )
    first = pl.multiple_of(lax.div(lax.axis_index("ctx"), 2) * CHIP, CHIP)
    small = started([
        pltpu.make_async_copy(docs, docs_s, sems.at[3 * KV_PARTS]),
        pltpu.make_async_copy(table.at[pl.ds(first, CHIP), :], table_s, sems.at[3 * KV_PARTS + 1]),
    ])
    for i, group in enumerate(copies):
        for copy in group:
            copy.wait()
        cut = slice(i * part, (i + 1) * part)
        more = jnp.dot(tok_s[:, cut], w_s[cut, :], preferred_element_type=F32)
        if i == 0:
            acc[...] = more
        else:
            acc[...] += more
    for copy in small:
        copy.wait()
    rot = rotation(table_s[halves()[0], :])
    half[:, :HD] = rot(acc[:, :HD]).astype(BF16)
    half[:, HD:] = acc[:, HD:].astype(BF16)


def project_own(tokens, w_key, w_value, docs, table):
    depth = tokens.shape[1]
    return call(
        own_body, "project_own",
        (
            like(ROWS, 2 * HD),
            like(ROWS, depth),
            like(depth, 2 * HD),
            like(1, ROWS, dtype=jnp.int32),
            like(CHIP, HD, dtype=F32),
        ),
        [HBM] * 5, (VMEM,) * 5,
        [pltpu.VMEM((ROWS, 2 * HD), F32), pltpu.SemaphoreType.DMA((3 * KV_PARTS + 2,))],
        limit=6, flops=2 * ROWS * depth * 2 * HD, moved=3,
    )(tokens, w_key, w_value, docs, table)


def unit_body(half, came, w, docs, docs_came, table, unit):
    own, other = halves()
    got = jnp.dot(came[...], w[...], preferred_element_type=F32)
    unit[own, :] = half[...]
    unit[other, :HD] = rotation(table[other, :])(got[:, :HD]).astype(BF16)
    unit[other, HD:] = got[:, HD:].astype(BF16)
    first = core_index() == 0
    a, b = docs[...], docs_came[...]
    tags = jnp.concatenate([jnp.where(first, a, b), jnp.where(first, b, a)], axis=1)
    tags = (tags + 1).astype(F32)
    unit[CHIP:, :] = jnp.broadcast_to(tags, (8, CHIP)).astype(BF16)


def project_unit(half, came, w, docs, docs_came, table):
    return call(
        unit_body, "project_unit", like(UNIT, 2 * HD), [VMEM] * 6, VMEM, limit=2,
        flops=2 * ROWS * w.shape[0] * 2 * HD,
    )(half, came, w, docs, docs_came, table)


Q_PARTS = 4


def q_body(tok, came, wq, table, out, wq_s, sems):
    half = wq.shape[1] // 2
    part = wq.shape[0] // Q_PARTS
    cols = pl.ds(pl.multiple_of(core_index() * half, half), half)
    copies = []
    for i in range(Q_PARTS):
        rows = pl.ds(i * part, part)
        copies += started([
            pltpu.make_async_copy(wq.at[rows, cols], wq_s.at[rows, :], sems.at[i])
        ])
    got = [None, None]
    for i in range(Q_PARTS):
        copies[i].wait()
        rows = slice(i * part, (i + 1) * part)
        for side, src in enumerate((tok, came)):
            more = jnp.dot(src[:, rows], wq_s[rows, :], preferred_element_type=F32)
            got[side] = more if i == 0 else got[side] + more
    for side, span in enumerate(halves()):
        rot = rotation(table[span, :])
        for h in range(half // HD):
            out[h, span, :] = rot(got[side][:, h * HD : (h + 1) * HD]).astype(BF16)


def project_q(tokens, came, w_query, table):
    depth, width = w_query.shape
    return call(
        q_body, "project_q", like(width // 2 // HD, CHIP, HD), [VMEM, VMEM, HBM, VMEM], VMEM,
        [pltpu.VMEM((depth, width // 2), BF16), pltpu.SemaphoreType.DMA((Q_PARTS,))],
        limit=8, flops=2 * CHIP * depth * width // 2, moved=6,
    )(tokens, came, w_query, table)


NONE = 99
NEAR = ((1, 2, 3), (4, 8, NONE))
FAR = ((4, 5, 6, 8, 9, 7, NONE), (1, 5, 9, 2, 6, 3, 7))


def bundle_body(unit, r1, r2, r3, out_a, out_b, out_c, slots):
    place = lax.axis_index("ctx")
    odd = lax.rem(place, 2) == 1
    column = lax.rem(lax.div(place, 2), 4)
    for i, src in enumerate((unit, r1, r2, r3)):
        slots[i] = src[...]

    def fill(out, even, late):
        skip = jnp.where(column >= late, 1, 0)
        for i, at in enumerate(even):
            out[i * UNIT : (i + 1) * UNIT, :] = slots[jnp.where(odd, jnp.minimum(skip + i, 3), at)]

    fill(out_a, (0, 1, 2, 3), 3)
    fill(out_b, (0, 1), 2)
    fill(out_c, (0, 1), 1)


def bundle(unit, r1, r2, r3):
    return call(
        bundle_body, "bundle",
        (like(4 * UNIT, 2 * HD), like(2 * UNIT, 2 * HD), like(2 * UNIT, 2 * HD)),
        [VMEM] * 4, (VMEM,) * 3, [pltpu.VMEM((4, UNIT, 2 * HD), BF16)], limit=2,
    )(unit, r1, r2, r3)


CONTRACT = (((1,), (1,)), ((), ()))


def tags_of(unit):
    tags = unit[CHIP:UNIT, :].astype(F32)
    return tags, jnp.transpose(tags, (1, 0))[:, 0:1]


def with_ones(values):
    return jnp.concatenate([values, jnp.ones((CHIP, HD), BF16)], axis=1)


def add_units(qs, units, steps, q_tag, state):
    m_s, l_s, acc = state
    place = lax.axis_index("ctx")
    odd = lax.rem(place, 2) == 1
    chip = lax.div(place, 2)
    for unit, even_step, odd_step in zip(units, *steps):
        block = unit()
        valid = chip >= jnp.where(odd, odd_step, even_step)
        k_tag = block[CHIP:, :].astype(F32)[0:1, :]
        bias = jnp.where((k_tag == q_tag) & valid, 0.0, -1e30)
        keys = block[:CHIP, :HD]
        values = with_ones(block[:CHIP, HD:])
        for h in range(qs.shape[0]):
            s = lax.dot_general(qs[h], keys, CONTRACT, preferred_element_type=F32)
            s = s * SCALE + bias
            old = m_s[h]
            top = jnp.maximum(old, jnp.max(s, axis=1, keepdims=True))
            fade = jnp.exp2(old - top)
            w = jnp.exp2(s - jnp.concatenate([top, top], axis=1)).astype(BF16)
            got = jnp.dot(w, values, preferred_element_type=F32)
            m_s[h] = top
            l_s[h] = fade * l_s[h] + got[:, HD:]
            acc[h] = fade * acc[h] + got[:, :HD]


def near_body(qs, unit, r1, r2, r3, m_s, l_s, acc):
    tags, q_tag = tags_of(unit)
    rows = lax.broadcasted_iota(jnp.int32, (CHIP, CHIP), 0)
    cols = lax.broadcasted_iota(jnp.int32, (CHIP, CHIP), 1)
    bias = jnp.where((tags[0:1, :] == q_tag) & (cols <= rows), 0.0, -1e30)
    keys, values = unit[:CHIP, :HD], with_ones(unit[:CHIP, HD:])
    for h in range(qs.shape[0]):
        s = lax.dot_general(qs[h], keys, CONTRACT, preferred_element_type=F32)
        s = s * SCALE + bias
        top = jnp.max(s, axis=1, keepdims=True)
        got = jnp.dot(jnp.exp2(s - top).astype(BF16), values, preferred_element_type=F32)
        m_s[h] = jnp.broadcast_to(top, (CHIP, HD))
        l_s[h] = got[:, HD:]
        acc[h] = got[:, :HD]
    units = [lambda src=src: src[...] for src in (r1, r2, r3)]
    add_units(qs, units, NEAR, q_tag, (m_s, l_s, acc))


def attend_near(qs, unit, r1, r2, r3):
    heads = qs.shape[0]
    state = like(heads, CHIP, HD, dtype=F32)
    return call(
        near_body, "attend_near", (state, state, state), [VMEM] * 5, (VMEM,) * 3, limit=8,
        flops=4 * heads * CHIP * 4 * CHIP * HD, exps=heads * CHIP * 4 * CHIP,
    )(qs, unit, r1, r2, r3)


def attend_far(side, qs, m_in, l_in, acc_in, unit, far_a, far_b, far_c):
    heads = qs.shape[0]

    def body(q_in, m_in, l_in, acc_in, unit, far_a, far_b, far_c, out, qs, tag_s, m_s, l_s, acc):
        rows = halves()[side]
        state = (m_s, l_s, acc)
        for new, old in zip((qs, *state), (q_in, m_in, l_in, acc_in)):
            for h in range(heads):
                new[h] = old[h, rows, :]
        tag_s[...] = jnp.broadcast_to(tags_of(unit)[1], (CHIP, HD))
        odd = core_index() == 1

        def at(src, i):
            return lambda: src[i * UNIT : (i + 1) * UNIT, :]

        units = [at(far_a, 0), at(far_a, 1), at(far_a, 2), at(far_b, 0), at(far_b, 1)]
        units.append(lambda: jnp.where(odd, at(far_c, 0)(), at(far_a, 3)()))
        units.append(at(far_c, 1))
        add_units(qs, units, FAR, tag_s[rows, :][:, 0:1], state)
        for h in range(heads):
            out[:, h * HD : (h + 1) * HD] = (acc[h] / l_s[h]).astype(BF16)

    state = pltpu.VMEM((heads, ROWS, HD), F32)
    return call(
        body, "attend_far", like(ROWS, heads * HD), [VMEM] * 8, VMEM,
        [pltpu.VMEM((heads, ROWS, HD), BF16), pltpu.VMEM((CHIP, HD), F32), state, state, state],
        limit=8, flops=4 * heads * ROWS * 7 * CHIP * HD, exps=heads * ROWS * 7 * CHIP,
    )(qs, m_in, l_in, acc_in, unit, far_a, far_b, far_c)


def project_out(xm, xr, w_out, groups, parts, dtype):
    depth = xm.shape[1]
    width = w_out.shape[1] // groups
    half = width // 2

    def body(xm, xr, w, *outs):
        core = core_index()
        own = pl.ds(pl.multiple_of(core * depth, depth), depth)
        other = pl.ds(pl.multiple_of((1 - core) * depth, depth), depth)
        for (shift, side), out in zip(parts, outs):
            group = lax.rem(lax.axis_index("head") + shift, groups)
            cols = pl.ds(pl.multiple_of(group * width + side * half, half), half)
            got = jnp.dot(xm[...], w[own, cols], preferred_element_type=F32)
            got += jnp.dot(xr[...], w[other, cols], preferred_element_type=F32)
            out[...] = got.astype(dtype)

    return call(
        body, "project_out", (like(ROWS, half, dtype=dtype),) * len(parts), [VMEM] * 3,
        (VMEM,) * len(parts), limit=4,
        flops=2 * ROWS * 2 * depth * half * len(parts), moved=len(parts),
    )(xm, xr, w_out)


def add_body(a, b, p, q, out_a, out_b):
    out_a[...] = (a[...] + p[...].astype(F32)).astype(BF16)
    out_b[...] = (b[...] + q[...].astype(F32)).astype(BF16)


def add_passing(a, b, p, q):
    out = like(*p.shape)
    return call(add_body, "add_passing", (out, out), [VMEM] * 4, (VMEM,) * 2, limit=2)(a, b, p, q)


def total_body(own_a, own_b, left_a, left_b, right_a, right_b, out):
    half = own_a.shape[1]
    for at, pieces in ((0, (own_a, left_a, right_a)), (half, (own_b, left_b, right_b))):
        total = pieces[0][...] + pieces[1][...].astype(F32) + pieces[2][...].astype(F32)
        out[:, at : at + half] = total.astype(BF16)


def add_total(*pieces):
    rows, half = pieces[0].shape
    return call(total_body, "add_total", like(rows, 2 * half), [VMEM] * 6, VMEM, limit=2)(*pieces)


def shards(tokens, w_query, w_key, w_value, w_out, doc_ids):
    ranks = lax.axis_size("ctx")
    groups = lax.axis_size("head")
    table = jnp.asarray(rope_table(ranks * ROWS))

    def swap(value):
        return lax.ppermute(value, "ctx", [(r, r ^ 1) for r in range(ranks)])

    def along(value, even, odd):
        moves = [(r, 2 * (odd if r % 2 else even)(r // 2) + r % 2) for r in range(ranks)]
        return lax.ppermute(value, "ctx", moves)

    def ahead(step):
        return lambda chip: (chip + step) % (ranks // 2)

    def in_row(step):
        return lambda chip: chip // 4 * 4 + (chip + step) % 4

    docs = doc_ids.reshape(1, -1)
    came, docs_came = swap(tokens), swap(docs)
    tokens, w_key, w_value, w_query, table, docs = (
        pltpu.with_memory_space_constraint(a, pltpu.HBM)
        for a in (tokens, w_key, w_value, w_query, table, docs)
    )
    half, tokens, w_kv, docs, table = project_own(tokens, w_key, w_value, docs, table)
    unit = project_unit(half, came, w_kv, docs, docs_came, table)
    r1 = along(unit, ahead(1), ahead(4))
    r2 = along(unit, ahead(2), ahead(8))
    r3 = along(unit, ahead(3), ahead(12))
    r1, r2, r3, came = lax.optimization_barrier((r1, r2, r3, came))
    out_a, out_b, out_c = bundle(unit, r1, r2, r3)
    far_a = along(out_a, ahead(4), in_row(1))
    far_b = along(out_b, ahead(8), in_row(2))
    far_c = along(out_c, ahead(12), in_row(3))
    qs = project_q(tokens, came, w_query, table)
    state = attend_near(qs, unit, r1, r2, r3)
    far = (qs, *state, unit, far_a, far_b, far_c)
    xr = swap(attend_far(1, *far))
    xm = attend_far(0, *far)

    def shift(value, step):
        return lax.ppermute(value, "head", [(g, (g + step) % groups) for g in range(groups)])

    a2, b2 = project_out(xm, xr, w_out, groups, ((2, 0), (2, 1)), BF16)
    pass_a, pass_b = shift(a2, 1), shift(b2, -1)
    b1, a3 = project_out(xm, xr, w_out, groups, ((1, 1), (3, 0)), BF16)
    left_b, right_a = shift(b1, 1), shift(a3, -1)
    a1, b3, a0, b0 = project_out(xm, xr, w_out, groups, ((1, 0), (3, 1), (0, 0), (0, 1)), F32)
    a1, b3 = add_passing(a1, b3, pass_a, pass_b)
    left_a, right_b = shift(a1, 1), shift(b3, -1)
    return add_total(a0, b0, left_a, left_b, right_a, right_b)


def solution(mesh):
    return jax.shard_map(
        shards,
        mesh=mesh,
        in_specs=(
            P("ctx", None),
            P(None, "head"),
            P(None, "head"),
            P(None, "head"),
            P("head", None),
            P("ctx"),
        ),
        out_specs=P("ctx", "head"),
        check_vma=False,
    )
```

time: 52.3 us -> 50.8 us (0.971)
  Pallas kernels: 15.4 us -> 14.6 us
    ppermute x3, waiting for transfers between devices: 2.59 us -> 0.01 us  [swap(): return lax.ppermute(value, 'ctx', [(r, r ^ 1) for r in range(ranks)])]
    ppermute x6, waiting for transfers between devices: 8.82 us -> 11.1 us  [along(): return lax.ppermute(value, 'ctx', moves)]
    pallas_call x5, Pallas kernels: 9.7 us -> 8.24 us  [the longest x1 3.22 us: project_q(): call(q_body, 'project_q', like(width // 2 // HD, CHIP, HD), [VMEM, VMEM,...]
    ppermute x6, starting transfers between devices: 11 us -> 10.3 us  [along(): return lax.ppermute(value, 'ctx', moves)]
  transfers between devices with their start and end apart: 15 -> 15, of which waited for: 7 -> 5; matrix products, arithmetic and copies ran while one was open for 0% -> 0% of each run, Pallas kernels for 18% -> 21%
where the time goes in v3:
time: 50.8 us; the launch traced here: 50.7 us
  starting transfers between devices  21.9 us (43%)
  Pallas kernels  14.6 us (29%)
  waiting for transfers between devices  14.1 us (28%)
    ppermute x6, waiting for transfers between devices, along(): return lax.ppermute(value, 'ctx', moves)  11.1 us
    ppermute x6, starting transfers between devices, shift(): lax.ppermute(value, 'head', [(g, (g + step) % groups) for g in range(grou...  11 us
    ppermute x6, starting transfers between devices, along(): return lax.ppermute(value, 'ctx', moves)  10.3 us
    pallas_call x2, Pallas kernels, attend_far(): call(body, 'attend_far', like(ROWS, heads * HD), [VMEM] * 8, VMEM, [pltpu...  3.77 us
    pallas_call x1, Pallas kernels, project_q(): call(q_body, 'project_q', like(width // 2 // HD, CHIP, HD), [VMEM, VMEM,...  3.22 us
    ppermute x6, waiting for transfers between devices, shift(): lax.ppermute(value, 'head', [(g, (g + step) % groups) for g in range(grou...  3.04 us
    pallas_call x1, Pallas kernels, project_own(): call(own_body, 'project_own', (like(ROWS, 2 * HD), like(ROWS, depth), lik...  2.35 us
    pallas_call x1, Pallas kernels, attend_near(): call(near_body, 'attend_near', (state, state, state), [VMEM] * 5, (VMEM,)...  2.04 us
  transfers between devices with their start and end apart: 15, of which 5 were waited for; matrix products, arithmetic and copies ran while one was open for 0% of the time, Pallas kernels for 21%

profile of v3, /device:TPU:0, one launch (start us, length us, event | category | flops | bytes accessed | tf_op | source)
XLA Modules:
  0.0 50.7 jit_solution(11627759744797954768)
XLA Ops:
  0.0 0.5 %collective-permute-start.1 = (s32[1,128]{1,0:T(1,128)}, s32[1,128]{1,0:T(1,128)S(1)}, u32[]{:S(2)}, u32[]{:S(2)}) collective-permute-start(s32[1,128]{1,0:T(1,128)} %bitcast.3), channel_id=1, source_target_pairs={{0,4},{4,0},{8,12},{12,8},{16,20},{20,16},{24,28},{28,24},{32,36},... | collective-permute-start | bytes 1544 | tf_op jit(solution)/shard_map/ppermute | solution.py:369
  0.5 2.3 %project_own.1 = (bf16[128,256]{1,0:T(8,128)(2,1)S(1)}, bf16[128,4096]{1,0:T(8,128)(2,1)S(1)}, bf16[4096,256]{1,0:T(8,128)(2,1)S(1)}, s32[1,128]{1,0:T(1,128)S(1)}, f32[256,128]{1,0:T(8,128)S(1)}) custom-call(bf16[128,4096]{1,0:T(8,128)(2,1)} %tok.1, bf16[4096,256]{1,0:T(8,128)(2,1)} %wk.1, bf16[4096,256]{1,0:T(8,128)(2,1)} %wv.1, s32[1,128]{1,0:T(1,128)} %bitcast.4, ...), custom_call_target="tpu_custom_call" | custom-call | flops 268435456 | bytes 3145728 | tf_op jit(solution)/shard_map/project_own/pallas_call | solution.py:124
  2.9 0.5 %project_unit.1.unit = bf16[264,256]{1,0:T(8,128)(2,1)S(1)} custom-call(bf16[128,256]{1,0:T(8,128)(2,1)S(1)} %get-tuple-element.31.half, bf16[128,4096]{1,0:T(8,128)(2,1)S(1)} %collective-permute-done.came, bf16[4096,256]{1,0:T(8,128)(2,1)S(1)} %get-tuple-element.32.w, s32[1,128]{1,0:T(1,128)S(1)} %get-tuple-element.33.docs, ...), custom_call_target="tpu_custom_call" | custom-call | flops 268435456 | bytes 1048576 | tf_op jit(solution)/shard_map/project_unit/pallas_call | solution.py:153
  3.4 2.9 %collective-permute-start.4 = (bf16[264,256]{1,0:T(8,128)(2,1)S(1)}, bf16[264,256]{1,0:T(8,128)(2,1)S(1)}, u32[]{:S(2)}, u32[]{:S(2)}) collective-permute-start(bf16[264,256]{1,0:T(8,128)(2,1)S(1)} %project_unit.1.unit), channel_id=1, source_target_pairs={{0,24},{4,100},{8,32},{12,108},{16,40},{20,116},{24,48},{28,124},{... | collective-permute-start | bytes 405512 | tf_op jit(solution)/shard_map/ppermute | solution.py:373
  6.3 1.8 %collective-permute-start.3 = (bf16[264,256]{1,0:T(8,128)(2,1)S(1)}, bf16[264,256]{1,0:T(8,128)(2,1)S(1)}, u32[]{:S(2)}, u32[]{:S(2)}) collective-permute-start(bf16[264,256]{1,0:T(8,128)(2,1)S(1)} %project_unit.1.unit), channel_id=1, source_target_pairs={{0,16},{4,68},{8,24},{12,76},{16,32},{20,84},{24,40},{28,92},{32,4... | collective-permute-start | bytes 405512 | tf_op jit(solution)/shard_map/ppermute | solution.py:373
  8.1 0.9 %collective-permute-start.2 = (bf16[264,256]{1,0:T(8,128)(2,1)S(1)}, bf16[264,256]{1,0:T(8,128)(2,1)S(1)}, u32[]{:S(2)}, u32[]{:S(2)}) collective-permute-start(bf16[264,256]{1,0:T(8,128)(2,1)S(1)} %project_unit.1.unit), channel_id=1, source_target_pairs={{0,8},{4,36},{8,16},{12,44},{16,24},{20,52},{24,32},{28,60},{32,40... | collective-permute-start | bytes 405512 | tf_op jit(solution)/shard_map/ppermute | solution.py:373
  9.0 1.6 %collective-permute-done.4.r3 = bf16[264,256]{1,0:T(8,128)(2,1)S(1)} collective-permute-done((bf16[264,256]{1,0:T(8,128)(2,1)S(1)}, bf16[264,256]{1,0:T(8,128)(2,1)S(1)}, u32[]{:S(2)}, u32[]{:S(2)}) %collective-permute-start.4) | collective-permute-done | bytes 135200 | tf_op jit(solution)/shard_map/ppermute | solution.py:373
  10.6 4.3 %collective-permute-done.3.r2 = bf16[264,256]{1,0:T(8,128)(2,1)S(1)} collective-permute-done((bf16[264,256]{1,0:T(8,128)(2,1)S(1)}, bf16[264,256]{1,0:T(8,128)(2,1)S(1)}, u32[]{:S(2)}, u32[]{:S(2)}) %collective-permute-start.3) | collective-permute-done | bytes 135200 | tf_op jit(solution)/shard_map/ppermute | solution.py:373
  14.9 1.5 %collective-permute-done.2.r1 = bf16[264,256]{1,0:T(8,128)(2,1)S(1)} collective-permute-done((bf16[264,256]{1,0:T(8,128)(2,1)S(1)}, bf16[264,256]{1,0:T(8,128)(2,1)S(1)}, u32[]{:S(2)}, u32[]{:S(2)}) %collective-permute-start.2) | collective-permute-done | bytes 135200 | tf_op jit(solution)/shard_map/ppermute | solution.py:373
  17.1 2.9 %collective-permute-start.6 = (bf16[528,256]{1,0:T(8,128)(2,1)S(1)}, bf16[528,256]{1,0:T(8,128)(2,1)S(1)}, u32[]{:S(2)}, u32[]{:S(2)}) collective-permute-start(bf16[528,256]{1,0:T(8,128)(2,1)S(1)} %get-tuple-element.43), channel_id=1, source_target_pairs={{0,64},{4,20},{8,72},{12,28},{16,80},{20,4},{24,88},{28,12},{32,96... | collective-permute-start | bytes 811016 | tf_op jit(solution)/shard_map/ppermute | solution.py:373
  19.9 1.3 %collective-permute-start.7 = (bf16[528,256]{1,0:T(8,128)(2,1)S(1)}, bf16[528,256]{1,0:T(8,128)(2,1)S(1)}, u32[]{:S(2)}, u32[]{:S(2)}) collective-permute-start(bf16[528,256]{1,0:T(8,128)(2,1)S(1)} %get-tuple-element.44), channel_id=1, source_target_pairs={{0,96},{4,28},{8,104},{12,4},{16,112},{20,12},{24,120},{28,20},{32... | collective-permute-start | bytes 811016 | tf_op jit(solution)/shard_map/ppermute | solution.py:373
  21.3 3.2 %project_q.1.qs.q_in = bf16[4,256,128]{2,1,0:T(8,128)(2,1)S(1)} custom-call(bf16[128,4096]{1,0:T(8,128)(2,1)S(1)} %get-tuple-element.30.tok, bf16[128,4096]{1,0:T(8,128)(2,1)S(1)} %collective-permute-done.came, bf16[4096,1024]{1,0:T(8,128)(2,1)} %wq.1, f32[256,128]{1,0:T(8,128)S(1)} %get-tuple-element.34.table), custom_call_target="tpu_custom_call" | custom-call | flops 1073741824 | bytes 6291456 | tf_op jit(solution)/shard_map/project_q/pallas_call | solution.py:187
  24.5 2.0 %attend_near.1 = (f32[4,256,128]{2,1,0:T(8,128)S(1)}, f32[4,256,128]{2,1,0:T(8,128)S(1)}, f32[4,256,128]{2,1,0:T(8,128)S(1)}) custom-call(bf16[4,256,128]{2,1,0:T(8,128)(2,1)S(1)} %project_q.1.qs.q_in, bf16[264,256]{1,0:T(8,128)(2,1)S(1)} %project_unit.1.unit, bf16[264,256]{1,0:T(8,128)(2,1)S(1)} %collective-permute-done.2.r1, ...), custom_call_target="tpu_custom_call" | custom-call | flops 536870912 | bytes 1048576 | tf_op jit(solution)/shard_map/attend_near/pallas_call | solution.py:282
  26.6 3.6 %collective-permute-done.6.far_b = bf16[528,256]{1,0:T(8,128)(2,1)S(1)} collective-permute-done((bf16[528,256]{1,0:T(8,128)(2,1)S(1)}, bf16[528,256]{1,0:T(8,128)(2,1)S(1)}, u32[]{:S(2)}, u32[]{:S(2)}) %collective-permute-start.6) | collective-permute-done | bytes 270368 | tf_op jit(solution)/shard_map/ppermute | solution.py:373
  30.2 1.9 %attend_far.3 = bf16[128,512]{1,0:T(8,128)(2,1)S(1)} custom-call(bf16[4,256,128]{2,1,0:T(8,128)(2,1)S(1)} %project_q.1.qs.q_in, f32[4,256,128]{2,1,0:T(8,128)S(1)} %get-tuple-element.39.m_in, f32[4,256,128]{2,1,0:T(8,128)S(1)} %get-tuple-element.40.l_in, f32[4,256,128]{2,1,0:T(8,128)S(1)} %get-tuple-element.41.acc_in, ...), custom_call_target="tpu_custom_call" | custom-call | flops 469762048 | bytes 1048576 | tf_op jit(solution)/shard_map/attend_far/pallas_call | solution.py:311
  32.1 1.9 %attend_far.2.xm = bf16[128,512]{1,0:T(8,128)(2,1)S(1)} custom-call(bf16[4,256,128]{2,1,0:T(8,128)(2,1)S(1)} %project_q.1.qs.q_in, f32[4,256,128]{2,1,0:T(8,128)S(1)} %get-tuple-element.39.m_in, f32[4,256,128]{2,1,0:T(8,128)S(1)} %get-tuple-element.40.l_in, f32[4,256,128]{2,1,0:T(8,128)S(1)} %get-tuple-element.41.acc_in, ...), custom_call_target="tpu_custom_call" | custom-call | flops 469762048 | bytes 1048576 | tf_op jit(solution)/shard_map/attend_far/pallas_call | solution.py:311
  34.6 2.0 %collective-permute-start.9 = (bf16[128,512]{1,0:T(8,128)(2,1)S(1)}, bf16[128,512]{1,0:T(8,128)(2,1)S(1)}, u32[]{:S(2)}, u32[]{:S(2)}) collective-permute-start(bf16[128,512]{1,0:T(8,128)(2,1)S(1)} %get-tuple-element.49), channel_id=1, source_target_pairs={{0,1},{1,2},{2,3},{3,0},{4,5},{5,6},{6,7},{7,4},{8,9},{9,10},{10,1... | collective-permute-start | bytes 393224 | tf_op jit(solution)/shard_map/ppermute | solution.py:404
  36.5 2.4 %collective-permute-start.10 = (bf16[128,512]{1,0:T(8,128)(2,1)S(1)}, bf16[128,512]{1,0:T(8,128)(2,1)S(1)}, u32[]{:S(2)}, u32[]{:S(2)}) collective-permute-start(bf16[128,512]{1,0:T(8,128)(2,1)S(1)} %get-tuple-element.50), channel_id=1, source_target_pairs={{0,3},{1,0},{2,1},{3,2},{4,7},{5,4},{6,5},{7,6},{8,11},{9,8},{10,9... | collective-permute-start | bytes 393224 | tf_op jit(solution)/shard_map/ppermute | solution.py:404
  39.5 3.2 %collective-permute-start.13 = (bf16[128,512]{1,0:T(8,128)(2,1)S(1)}, bf16[128,512]{1,0:T(8,128)(2,1)S(1)}, u32[]{:S(2)}, u32[]{:S(2)}) collective-permute-start(bf16[128,512]{1,0:T(8,128)(2,1)S(1)} %get-tuple-element.53), channel_id=1, source_target_pairs={{0,3},{1,0},{2,1},{3,2},{4,7},{5,4},{6,5},{7,6},{8,11},{9,8},{10,9... | collective-permute-start | bytes 393224 | tf_op jit(solution)/shard_map/ppermute | solution.py:404
  42.7 0.8 %project_out.3 = (f32[128,512]{1,0:T(8,128)S(1)}, f32[128,512]{1,0:T(8,128)S(1)}, f32[128,512]{1,0:T(8,128)S(1)}, f32[128,512]{1,0:T(8,128)S(1)}) custom-call(bf16[128,512]{1,0:T(8,128)(2,1)S(1)} %attend_far.2.xm, bf16[128,512]{1,0:T(8,128)(2,1)S(1)} %collective-permute-done.8.xr, bf16[1024,4096]{1,0:T(8,128)(2,1)S(1)} %bitcast.2), custom_call_target="tpu_custom_call" | custom-call | flops 536870912 | bytes 4194304 | tf_op jit(solution)/shard_map/project_out/pallas_call | solution.py:334
  43.6 1.4 %collective-permute-start.11 = (bf16[128,512]{1,0:T(8,128)(2,1)S(1)}, bf16[128,512]{1,0:T(8,128)(2,1)S(1)}, u32[]{:S(2)}, u32[]{:S(2)}) collective-permute-start(bf16[128,512]{1,0:T(8,128)(2,1)S(1)} %get-tuple-element.51), channel_id=1, source_target_pairs={{0,1},{1,2},{2,3},{3,0},{4,5},{5,6},{6,7},{7,4},{8,9},{9,10},{10,1... | collective-permute-start | bytes 393224 | tf_op jit(solution)/shard_map/ppermute | solution.py:404
  44.9 2.0 %collective-permute-start.14 = (bf16[128,512]{1,0:T(8,128)(2,1)S(1)}, bf16[128,512]{1,0:T(8,128)(2,1)S(1)}, u32[]{:S(2)}, u32[]{:S(2)}) collective-permute-start(bf16[128,512]{1,0:T(8,128)(2,1)S(1)} %get-tuple-element.54), channel_id=1, source_target_pairs={{0,3},{1,0},{2,1},{3,2},{4,7},{5,4},{6,5},{7,6},{8,11},{9,8},{10,9... | collective-permute-start | bytes 393224 | tf_op jit(solution)/shard_map/ppermute | solution.py:404
  46.9 3.0 %collective-permute-done.11.left_a = bf16[128,512]{1,0:T(8,128)(2,1)S(1)} collective-permute-done((bf16[128,512]{1,0:T(8,128)(2,1)S(1)}, bf16[128,512]{1,0:T(8,128)(2,1)S(1)}, u32[]{:S(2)}, u32[]{:S(2)}) %collective-permute-start.11) | collective-permute-done | bytes 131104 | tf_op jit(solution)/shard_map/ppermute | solution.py:404
  49.9 0.8 %add_total.1 = bf16[128,1024]{1,0:T(8,128)(2,1)} custom-call(f32[128,512]{1,0:T(8,128)S(1)} %get-tuple-element.45.own_a, f32[128,512]{1,0:T(8,128)S(1)} %get-tuple-element.46.own_b, bf16[128,512]{1,0:T(8,128)(2,1)S(1)} %collective-permute-done.11.left_a, bf16[128,512]{1,0:T(8,128)(2,1)S(1)} %collective-permute-done.12.left_b, ...), custom_call_target="tpu_custom_call" | custom-call | bytes 1048576 | tf_op jit(solution)/shard_map/add_total/pallas_call | solution.py:360
  (23 shorter events, 1.8 us)
Async XLA Ops:
  0.0 2.9 %collective-permute-start = (bf16[128,4096]{1,0:T(8,128)(2,1)}, bf16[128,4096]{1,0:T(8,128)(2,1)S(1)}, u32[]{:S(2)}, u32[]{:S(2)}) collective-permute-start(bf16[128,4096]{1,0:T(8,128)(2,1)} %tok.1), channel_id=1, source_target_pairs={{0,4},{4,0},{8,12},{12,8},{16,20},{20,16},{24,28},{28,24},{32,36},... | collective-permute-start | bytes 3145736 | tf_op jit(solution)/shard_map/ppermute | solution.py:369
  0.0 2.9 %collective-permute-start.1 = (s32[1,128]{1,0:T(1,128)}, s32[1,128]{1,0:T(1,128)S(1)}, u32[]{:S(2)}, u32[]{:S(2)}) collective-permute-start(s32[1,128]{1,0:T(1,128)} %bitcast.3), channel_id=1, source_target_pairs={{0,4},{4,0},{8,12},{12,8},{16,20},{20,16},{24,28},{28,24},{32,36},... | collective-permute-start | bytes 1544 | tf_op jit(solution)/shard_map/ppermute | solution.py:369
  3.4 7.2 %collective-permute-start.4 = (bf16[264,256]{1,0:T(8,128)(2,1)S(1)}, bf16[264,256]{1,0:T(8,128)(2,1)S(1)}, u32[]{:S(2)}, u32[]{:S(2)}) collective-permute-start(bf16[264,256]{1,0:T(8,128)(2,1)S(1)} %project_unit.1.unit), channel_id=1, source_target_pairs={{0,24},{4,100},{8,32},{12,108},{16,40},{20,116},{24,48},{28,124},{... | collective-permute-start | bytes 405512 | tf_op jit(solution)/shard_map/ppermute | solution.py:373
  6.3 8.6 %collective-permute-start.3 = (bf16[264,256]{1,0:T(8,128)(2,1)S(1)}, bf16[264,256]{1,0:T(8,128)(2,1)S(1)}, u32[]{:S(2)}, u32[]{:S(2)}) collective-permute-start(bf16[264,256]{1,0:T(8,128)(2,1)S(1)} %project_unit.1.unit), channel_id=1, source_target_pairs={{0,16},{4,68},{8,24},{12,76},{16,32},{20,84},{24,40},{28,92},{32,4... | collective-permute-start | bytes 405512 | tf_op jit(solution)/shard_map/ppermute | solution.py:373
  8.1 8.3 %collective-permute-start.2 = (bf16[264,256]{1,0:T(8,128)(2,1)S(1)}, bf16[264,256]{1,0:T(8,128)(2,1)S(1)}, u32[]{:S(2)}, u32[]{:S(2)}) collective-permute-start(bf16[264,256]{1,0:T(8,128)(2,1)S(1)} %project_unit.1.unit), channel_id=1, source_target_pairs={{0,8},{4,36},{8,16},{12,44},{16,24},{20,52},{24,32},{28,60},{32,40... | collective-permute-start | bytes 405512 | tf_op jit(solution)/shard_map/ppermute | solution.py:373
  16.5 17.6 %slice-start = ((s8[8388608]{0:T(1024)(128)(4,1)}), s8[4194304]{0:T(1024)(128)(4,1)S(1)}, s32[]{:S(2)}) async-start(s8[8388608]{0:T(1024)(128)(4,1)} %bitcast.1), calls=%async_computation | async-start | bytes 8388608
  16.6 13.6 %collective-permute-start.5 = (bf16[1056,256]{1,0:T(8,128)(2,1)S(1)}, bf16[1056,256]{1,0:T(8,128)(2,1)S(1)}, u32[]{:S(2)}, u32[]{:S(2)}) collective-permute-start(bf16[1056,256]{1,0:T(8,128)(2,1)S(1)} %get-tuple-element.42), channel_id=1, source_target_pairs={{0,32},{4,12},{8,40},{12,20},{16,48},{20,28},{24,56},{28,4},{32,64... | collective-permute-start | bytes 1622024 | tf_op jit(solution)/shard_map/ppermute | solution.py:373
  17.1 13.1 %collective-permute-start.6 = (bf16[528,256]{1,0:T(8,128)(2,1)S(1)}, bf16[528,256]{1,0:T(8,128)(2,1)S(1)}, u32[]{:S(2)}, u32[]{:S(2)}) collective-permute-start(bf16[528,256]{1,0:T(8,128)(2,1)S(1)} %get-tuple-element.43), channel_id=1, source_target_pairs={{0,64},{4,20},{8,72},{12,28},{16,80},{20,4},{24,88},{28,12},{32,96... | collective-permute-start | bytes 811016 | tf_op jit(solution)/shard_map/ppermute | solution.py:373
  19.9 10.2 %collective-permute-start.7 = (bf16[528,256]{1,0:T(8,128)(2,1)S(1)}, bf16[528,256]{1,0:T(8,128)(2,1)S(1)}, u32[]{:S(2)}, u32[]{:S(2)}) collective-permute-start(bf16[528,256]{1,0:T(8,128)(2,1)S(1)} %get-tuple-element.44), channel_id=1, source_target_pairs={{0,96},{4,28},{8,104},{12,4},{16,112},{20,12},{24,120},{28,20},{32... | collective-permute-start | bytes 811016 | tf_op jit(solution)/shard_map/ppermute | solution.py:373
  21.3 12.8 %slice-start.1 = ((s8[8388608]{0:T(1024)(128)(4,1)}), s8[4194304]{0:T(1024)(128)(4,1)S(1)}, s32[]{:S(2)}) async-start(s8[8388608]{0:T(1024)(128)(4,1)} %bitcast.1), calls=%async_computation.1 | async-start | bytes 8388608
  32.1 2.0 %collective-permute-start.8 = (bf16[128,512]{1,0:T(8,128)(2,1)S(1)}, bf16[128,512]{1,0:T(8,128)(2,1)S(1)}, u32[]{:S(2)}, u32[]{:S(2)}) collective-permute-start(bf16[128,512]{1,0:T(8,128)(2,1)S(1)} %attend_far.3), channel_id=1, source_target_pairs={{0,4},{4,0},{8,12},{12,8},{16,20},{20,16},{24,28},{28,24},{32,36},... | collective-permute-start | bytes 393224 | tf_op jit(solution)/shard_map/ppermute | solution.py:369
  34.6 8.9 %collective-permute-start.9 = (bf16[128,512]{1,0:T(8,128)(2,1)S(1)}, bf16[128,512]{1,0:T(8,128)(2,1)S(1)}, u32[]{:S(2)}, u32[]{:S(2)}) collective-permute-start(bf16[128,512]{1,0:T(8,128)(2,1)S(1)} %get-tuple-element.49), channel_id=1, source_target_pairs={{0,1},{1,2},{2,3},{3,0},{4,5},{5,6},{6,7},{7,4},{8,9},{9,10},{10,1... | collective-permute-start | bytes 393224 | tf_op jit(solution)/shard_map/ppermute | solution.py:404
  36.5 7.0 %collective-permute-start.10 = (bf16[128,512]{1,0:T(8,128)(2,1)S(1)}, bf16[128,512]{1,0:T(8,128)(2,1)S(1)}, u32[]{:S(2)}, u32[]{:S(2)}) collective-permute-start(bf16[128,512]{1,0:T(8,128)(2,1)S(1)} %get-tuple-element.50), channel_id=1, source_target_pairs={{0,3},{1,0},{2,1},{3,2},{4,7},{5,4},{6,5},{7,6},{8,11},{9,8},{10,9... | collective-permute-start | bytes 393224 | tf_op jit(solution)/shard_map/ppermute | solution.py:404
  39.4 7.5 %collective-permute-start.12 = (bf16[128,512]{1,0:T(8,128)(2,1)S(1)}, bf16[128,512]{1,0:T(8,128)(2,1)S(1)}, u32[]{:S(2)}, u32[]{:S(2)}) collective-permute-start(bf16[128,512]{1,0:T(8,128)(2,1)S(1)} %get-tuple-element.52), channel_id=1, source_target_pairs={{0,1},{1,2},{2,3},{3,0},{4,5},{5,6},{6,7},{7,4},{8,9},{9,10},{10,1... | collective-permute-start | bytes 393224 | tf_op jit(solution)/shard_map/ppermute | solution.py:404
  39.5 7.4 %collective-permute-start.13 = (bf16[128,512]{1,0:T(8,128)(2,1)S(1)}, bf16[128,512]{1,0:T(8,128)(2,1)S(1)}, u32[]{:S(2)}, u32[]{:S(2)}) collective-permute-start(bf16[128,512]{1,0:T(8,128)(2,1)S(1)} %get-tuple-element.53), channel_id=1, source_target_pairs={{0,3},{1,0},{2,1},{3,2},{4,7},{5,4},{6,5},{7,6},{8,11},{9,8},{10,9... | collective-permute-start | bytes 393224 | tf_op jit(solution)/shard_map/ppermute | solution.py:404
  43.6 6.3 %collective-permute-start.11 = (bf16[128,512]{1,0:T(8,128)(2,1)S(1)}, bf16[128,512]{1,0:T(8,128)(2,1)S(1)}, u32[]{:S(2)}, u32[]{:S(2)}) collective-permute-start(bf16[128,512]{1,0:T(8,128)(2,1)S(1)} %get-tuple-element.51), channel_id=1, source_target_pairs={{0,1},{1,2},{2,3},{3,0},{4,5},{5,6},{6,7},{7,4},{8,9},{9,10},{10,1... | collective-permute-start | bytes 393224 | tf_op jit(solution)/shard_map/ppermute | solution.py:404
  44.9 5.0 %collective-permute-start.14 = (bf16[128,512]{1,0:T(8,128)(2,1)S(1)}, bf16[128,512]{1,0:T(8,128)(2,1)S(1)}, u32[]{:S(2)}, u32[]{:S(2)}) collective-permute-start(bf16[128,512]{1,0:T(8,128)(2,1)S(1)} %get-tuple-element.54), channel_id=1, source_target_pairs={{0,3},{1,0},{2,1},{3,2},{4,7},{5,4},{6,5},{7,6},{8,11},{9,8},{10,9... | collective-permute-start | bytes 393224 | tf_op jit(solution)/shard_map/ppermute | solution.py:404

commit v4 on v3

--- a/solution.py
+++ b/solution.py
@@ -193,32 +193,44 @@
 
 NONE = 99
 NEAR = ((1, 2, 3), (4, 8, NONE))
-FAR = ((4, 5, 6, 8, 9, 7, NONE), (1, 5, 9, 2, 6, 3, 7))
-
-
-def bundle_body(unit, r1, r2, r3, out_a, out_b, out_c, slots):
+MIDDLE = ((8, 9, NONE, NONE), (2, 6, 3, 7))
+LAST = ((4, 5, 6, 7), (1, 5, 9, NONE))
+
+
+def fill(out, slots, late):
     place = lax.axis_index("ctx")
-    odd = lax.rem(place, 2) == 1
     column = lax.rem(lax.div(place, 2), 4)
+    skip = jnp.where((lax.rem(place, 2) == 1) & (column >= late), 1, 0)
+    for i in range(out.shape[0] // UNIT):
+        out[i * UNIT : (i + 1) * UNIT, :] = slots[jnp.minimum(skip + i, 3)]
+
+
+def pairs_body(unit, r1, r2, out_b, out_c, slots):
+    for i, src in enumerate((unit, r1, r2)):
+        slots[i] = src[...]
+    fill(out_b, slots, 2)
+    fill(out_c, slots, 1)
+
+
+def bundle_pairs(unit, r1, r2):
+    pair = like(2 * UNIT, 2 * HD)
+    return call(
+        pairs_body, "bundle_pairs", (pair, pair), [VMEM] * 3, (VMEM,) * 2,
+        [pltpu.VMEM((3, UNIT, 2 * HD), BF16)], limit=2,
+    )(unit, r1, r2)
+
+
+def row_body(unit, r1, r2, r3, after, out_a, slots):
     for i, src in enumerate((unit, r1, r2, r3)):
         slots[i] = src[...]
-
-    def fill(out, even, late):
-        skip = jnp.where(column >= late, 1, 0)
-        for i, at in enumerate(even):
-            out[i * UNIT : (i + 1) * UNIT, :] = slots[jnp.where(odd, jnp.minimum(skip + i, 3), at)]
-
-    fill(out_a, (0, 1, 2, 3), 3)
-    fill(out_b, (0, 1), 2)
-    fill(out_c, (0, 1), 1)
-
-
-def bundle(unit, r1, r2, r3):
-    return call(
-        bundle_body, "bundle",
-        (like(4 * UNIT, 2 * HD), like(2 * UNIT, 2 * HD), like(2 * UNIT, 2 * HD)),
-        [VMEM] * 4, (VMEM,) * 3, [pltpu.VMEM((4, UNIT, 2 * HD), BF16)], limit=2,
-    )(unit, r1, r2, r3)
+    fill(out_a, slots, 3)
+
+
+def bundle_row(unit, r1, r2, r3, after):
+    return call(
+        row_body, "bundle_row", like(4 * UNIT, 2 * HD), [VMEM] * 5, VMEM,
+        [pltpu.VMEM((4, UNIT, 2 * HD), BF16)], limit=2,
+    )(unit, r1, r2, r3, after)
 
 
 CONTRACT = (((1,), (1,)), ((), ()))
@@ -233,29 +245,34 @@
     return jnp.concatenate([values, jnp.ones((CHIP, HD), BF16)], axis=1)
 
 
-def add_units(qs, units, steps, q_tag, state):
-    m_s, l_s, acc = state
+def add_units(queries, units, steps, q_tag, before, after):
     place = lax.axis_index("ctx")
     odd = lax.rem(place, 2) == 1
     chip = lax.div(place, 2)
-    for unit, even_step, odd_step in zip(units, *steps):
-        block = unit()
+    for i, (block, even_step, odd_step) in enumerate(zip(units, *steps)):
         valid = chip >= jnp.where(odd, odd_step, even_step)
         k_tag = block[CHIP:, :].astype(F32)[0:1, :]
         bias = jnp.where((k_tag == q_tag) & valid, 0.0, -1e30)
         keys = block[:CHIP, :HD]
         values = with_ones(block[:CHIP, HD:])
-        for h in range(qs.shape[0]):
-            s = lax.dot_general(qs[h], keys, CONTRACT, preferred_element_type=F32)
+        for h in range(after[0].shape[0]):
+            s = lax.dot_general(queries(h), keys, CONTRACT, preferred_element_type=F32)
             s = s * SCALE + bias
-            old = m_s[h]
+            if i == 0:
+                old, old_sum, old_acc = before(h)
+            else:
+                old, old_sum, old_acc = (ref[h] for ref in after)
             top = jnp.maximum(old, jnp.max(s, axis=1, keepdims=True))
             fade = jnp.exp2(old - top)
             w = jnp.exp2(s - jnp.concatenate([top, top], axis=1)).astype(BF16)
             got = jnp.dot(w, values, preferred_element_type=F32)
-            m_s[h] = top
-            l_s[h] = fade * l_s[h] + got[:, HD:]
-            acc[h] = fade * acc[h] + got[:, :HD]
+            after[0][h] = top
+            after[1][h] = fade * old_sum + got[:, HD:]
+            after[2][h] = fade * old_acc + got[:, :HD]
+
+
+def parts(src):
+    return [src[i * UNIT : (i + 1) * UNIT, :] for i in range(src.shape[0] // UNIT)]
 
 
 def near_body(qs, unit, r1, r2, r3, m_s, l_s, acc):
@@ -272,8 +289,9 @@
         m_s[h] = jnp.broadcast_to(top, (CHIP, HD))
         l_s[h] = got[:, HD:]
         acc[h] = got[:, :HD]
-    units = [lambda src=src: src[...] for src in (r1, r2, r3)]
-    add_units(qs, units, NEAR, q_tag, (m_s, l_s, acc))
+    state = (m_s, l_s, acc)
+    units = [src[...] for src in (r1, r2, r3)]
+    add_units(lambda h: qs[h], units, NEAR, q_tag, lambda h: [ref[h] for ref in state], state)
 
 
 def attend_near(qs, unit, r1, r2, r3):
@@ -285,79 +303,84 @@
     )(qs, unit, r1, r2, r3)
 
 
-def attend_far(side, qs, m_in, l_in, acc_in, unit, far_a, far_b, far_c):
+def middle_body(qs, m_in, l_in, acc_in, unit, far_b, far_c, m_s, l_s, acc):
+    before = (m_in, l_in, acc_in)
+    add_units(
+        lambda h: qs[h], parts(far_b) + parts(far_c), MIDDLE, tags_of(unit)[1],
+        lambda h: [ref[h] for ref in before], (m_s, l_s, acc),
+    )
+
+
+def attend_middle(qs, m_in, l_in, acc_in, unit, far_b, far_c):
     heads = qs.shape[0]
-
-    def body(q_in, m_in, l_in, acc_in, unit, far_a, far_b, far_c, out, qs, tag_s, m_s, l_s, acc):
+    state = like(heads, CHIP, HD, dtype=F32)
+    return call(
+        middle_body, "attend_middle", (state,) * 3, [VMEM] * 7, (VMEM,) * 3, limit=8,
+        flops=4 * heads * CHIP * 4 * CHIP * HD, exps=heads * CHIP * 4 * CHIP,
+    )(qs, m_in, l_in, acc_in, unit, far_b, far_c)
+
+
+def attend_last(side, qs, m_in, l_in, acc_in, unit, far_a):
+    heads = qs.shape[0]
+
+    def body(qs, m_in, l_in, acc_in, unit, far_a, out, tag_s, m_s, l_s, acc):
         rows = halves()[side]
-        state = (m_s, l_s, acc)
-        for new, old in zip((qs, *state), (q_in, m_in, l_in, acc_in)):
-            for h in range(heads):
-                new[h] = old[h, rows, :]
+        before = (m_in, l_in, acc_in)
         tag_s[...] = jnp.broadcast_to(tags_of(unit)[1], (CHIP, HD))
-        odd = core_index() == 1
-
-        def at(src, i):
-            return lambda: src[i * UNIT : (i + 1) * UNIT, :]
-
-        units = [at(far_a, 0), at(far_a, 1), at(far_a, 2), at(far_b, 0), at(far_b, 1)]
-        units.append(lambda: jnp.where(odd, at(far_c, 0)(), at(far_a, 3)()))
-        units.append(at(far_c, 1))
-        add_units(qs, units, FAR, tag_s[rows, :][:, 0:1], state)
+        add_units(
+            lambda h: qs[h, rows, :], parts(far_a), LAST, tag_s[rows, :][:, 0:1],
+            lambda h: [ref[h, rows, :] for ref in before], (m_s, l_s, acc),
+        )
         for h in range(heads):
             out[:, h * HD : (h + 1) * HD] = (acc[h] / l_s[h]).astype(BF16)
 
     state = pltpu.VMEM((heads, ROWS, HD), F32)
     return call(
-        body, "attend_far", like(ROWS, heads * HD), [VMEM] * 8, VMEM,
-        [pltpu.VMEM((heads, ROWS, HD), BF16), pltpu.VMEM((CHIP, HD), F32), state, state, state],
-        limit=8, flops=4 * heads * ROWS * 7 * CHIP * HD, exps=heads * ROWS * 7 * CHIP,
-    )(qs, m_in, l_in, acc_in, unit, far_a, far_b, far_c)
-
-
-def project_out(xm, xr, w_out, groups, parts, dtype):
+        body, "attend_last", like(ROWS, heads * HD), [VMEM] * 6, VMEM,
+        [pltpu.VMEM((CHIP, HD), F32), state, state, state],
+        limit=8, flops=4 * heads * ROWS * 4 * CHIP * HD, exps=heads * ROWS * 4 * CHIP,
+    )(qs, m_in, l_in, acc_in, unit, far_a)
+
+
+def project_out(xm, xr, w_out, groups, shifts, dtypes):
     depth = xm.shape[1]
     width = w_out.shape[1] // groups
-    half = width // 2
 
     def body(xm, xr, w, *outs):
         core = core_index()
         own = pl.ds(pl.multiple_of(core * depth, depth), depth)
         other = pl.ds(pl.multiple_of((1 - core) * depth, depth), depth)
-        for (shift, side), out in zip(parts, outs):
+        for (even, odd), out in zip(shifts, outs):
+            shift = jnp.where(core == 0, even, odd)
             group = lax.rem(lax.axis_index("head") + shift, groups)
-            cols = pl.ds(pl.multiple_of(group * width + side * half, half), half)
+            cols = pl.ds(pl.multiple_of(group * width, width), width)
             got = jnp.dot(xm[...], w[own, cols], preferred_element_type=F32)
             got += jnp.dot(xr[...], w[other, cols], preferred_element_type=F32)
-            out[...] = got.astype(dtype)
-
-    return call(
-        body, "project_out", (like(ROWS, half, dtype=dtype),) * len(parts), [VMEM] * 3,
-        (VMEM,) * len(parts), limit=4,
-        flops=2 * ROWS * 2 * depth * half * len(parts), moved=len(parts),
+            out[...] = got.astype(out.dtype)
+
+    return call(
+        body, "project_out", tuple(like(ROWS, width, dtype=d) for d in dtypes), [VMEM] * 3,
+        (VMEM,) * len(shifts), limit=4,
+        flops=2 * ROWS * 2 * depth * width * len(shifts), moved=2 * len(shifts),
     )(xm, xr, w_out)
 
 
-def add_body(a, b, p, q, out_a, out_b):
-    out_a[...] = (a[...] + p[...].astype(F32)).astype(BF16)
-    out_b[...] = (b[...] + q[...].astype(F32)).astype(BF16)
-
-
-def add_passing(a, b, p, q):
-    out = like(*p.shape)
-    return call(add_body, "add_passing", (out, out), [VMEM] * 4, (VMEM,) * 2, limit=2)(a, b, p, q)
-
-
-def total_body(own_a, own_b, left_a, left_b, right_a, right_b, out):
-    half = own_a.shape[1]
-    for at, pieces in ((0, (own_a, left_a, right_a)), (half, (own_b, left_b, right_b))):
-        total = pieces[0][...] + pieces[1][...].astype(F32) + pieces[2][...].astype(F32)
-        out[:, at : at + half] = total.astype(BF16)
-
-
-def add_total(*pieces):
-    rows, half = pieces[0].shape
-    return call(total_body, "add_total", like(rows, 2 * half), [VMEM] * 6, VMEM, limit=2)(*pieces)
+def passing_body(own, came, out):
+    out[...] = (own[...] + came[...].astype(F32)).astype(BF16)
+
+
+def add_passing(own, came):
+    return call(passing_body, "add_passing", like(*own.shape), [VMEM] * 2, VMEM, limit=2)(own, came)
+
+
+def total_body(own, first, second, out):
+    out[...] = (own[...] + first[...].astype(F32) + second[...].astype(F32)).astype(BF16)
+
+
+def add_total(own, first, second):
+    return call(total_body, "add_total", like(*own.shape), [VMEM] * 3, VMEM, limit=2)(
+        own, first, second
+    )
 
 
 def shards(tokens, w_query, w_key, w_value, w_out, doc_ids):
@@ -390,27 +413,32 @@
     r2 = along(unit, ahead(2), ahead(8))
     r3 = along(unit, ahead(3), ahead(12))
     r1, r2, r3, came = lax.optimization_barrier((r1, r2, r3, came))
-    out_a, out_b, out_c = bundle(unit, r1, r2, r3)
-    far_a = along(out_a, ahead(4), in_row(1))
+    out_b, out_c = bundle_pairs(unit, r1, r2)
     far_b = along(out_b, ahead(8), in_row(2))
     far_c = along(out_c, ahead(12), in_row(3))
+    far_a = along(bundle_row(unit, r1, r2, r3, out_c), ahead(4), in_row(1))
     qs = project_q(tokens, came, w_query, table)
     state = attend_near(qs, unit, r1, r2, r3)
-    far = (qs, *state, unit, far_a, far_b, far_c)
-    xr = swap(attend_far(1, *far))
-    xm = attend_far(0, *far)
-
-    def shift(value, step):
-        return lax.ppermute(value, "head", [(g, (g + step) % groups) for g in range(groups)])
-
-    a2, b2 = project_out(xm, xr, w_out, groups, ((2, 0), (2, 1)), BF16)
-    pass_a, pass_b = shift(a2, 1), shift(b2, -1)
-    b1, a3 = project_out(xm, xr, w_out, groups, ((1, 1), (3, 0)), BF16)
-    left_b, right_a = shift(b1, 1), shift(a3, -1)
-    a1, b3, a0, b0 = project_out(xm, xr, w_out, groups, ((1, 0), (3, 1), (0, 0), (0, 1)), F32)
-    a1, b3 = add_passing(a1, b3, pass_a, pass_b)
-    left_a, right_b = shift(a1, 1), shift(b3, -1)
-    return add_total(a0, b0, left_a, left_b, right_a, right_b)
+    state = attend_middle(qs, *state, unit, far_b, far_c)
+    xr = swap(attend_last(1, qs, *state, unit, far_a))
+    xm = attend_last(0, qs, *state, unit, far_a)
+
+    def across(value, even, odd):
+        moves = []
+        for r in range(ranks):
+            for g in range(groups):
+                to = (g + (odd if r % 2 else even)) % groups
+                moves.append((r * groups + g, r * groups + to))
+        return lax.ppermute(value, ("ctx", "head"), moves)
+
+    (opposite,) = project_out(xm, xr, w_out, groups, ((2, 2),), (BF16,))
+    passing = across(opposite, 1, 3)
+    direct, onward, total = project_out(
+        xm, xr, w_out, groups, ((3, 1), (1, 3), (0, 0)), (BF16, F32, F32)
+    )
+    direct = across(direct, 3, 1)
+    onward = across(add_passing(onward, passing), 1, 3)
+    return add_total(total, direct, onward)
 
 
 def solution(mesh):

time: 50.8 us -> 53.6 us (1.055)
  waiting for transfers between devices: 14.1 us -> 21.4 us
  starting transfers between devices: 21.9 us -> 16.8 us
  Pallas kernels: 14.6 us -> 15.2 us
    ppermute x6 -> x3, waiting for transfers between devices: 3.04 us -> 10.2 us  [across(): return lax.ppermute(value, ('ctx', 'head'), moves)]
    ppermute x6 -> x3, starting transfers between devices: 11 us -> 5.88 us  [across(): return lax.ppermute(value, ('ctx', 'head'), moves)]
    pallas_call x8 -> x9, Pallas kernels: 6.46 us -> 7.05 us  [the longest x2 2.36 us: attend_last(): call(body, 'attend_last', like(ROWS, heads * HD), [VMEM] * 6, VMEM, [pltp...]
  transfers between devices with their start and end apart: 15 -> 12, of which waited for: 5 -> 7; matrix products, arithmetic and copies ran while one was open for 0% -> 0% of each run, Pallas kernels for 21% -> 23%
where the time goes in v4:
time: 53.6 us; the launch traced here: 53.5 us
  waiting for transfers between devices  21.4 us (40%)
  starting transfers between devices  16.8 us (31%)
  Pallas kernels  15.2 us (28%)
    ppermute x6, waiting for transfers between devices, along(): return lax.ppermute(value, 'ctx', moves)  11.1 us
    ppermute x6, starting transfers between devices, along(): return lax.ppermute(value, 'ctx', moves)  10.3 us
    ppermute x3, waiting for transfers between devices, across(): return lax.ppermute(value, ('ctx', 'head'), moves)  10.2 us
    ppermute x3, starting transfers between devices, across(): return lax.ppermute(value, ('ctx', 'head'), moves)  5.88 us
    pallas_call x1, Pallas kernels, project_q(): call(q_body, 'project_q', like(width // 2 // HD, CHIP, HD), [VMEM, VMEM,...  3.25 us
    pallas_call x2, Pallas kernels, attend_last(): call(body, 'attend_last', like(ROWS, heads * HD), [VMEM] * 6, VMEM, [pltp...  2.36 us
    pallas_call x1, Pallas kernels, project_own(): call(own_body, 'project_own', (like(ROWS, 2 * HD), like(ROWS, depth), lik...  2.35 us
    pallas_call x1, Pallas kernels, attend_middle(): call(middle_body, 'attend_middle', (state,) * 3, [VMEM] * 7, (VMEM,) * 3,...  2.19 us
  transfers between devices with their start and end apart: 12, of which 7 were waited for; matrix products, arithmetic and copies ran while one was open for 0% of the time, Pallas kernels for 23%

profile of v4, /device:TPU:0, one launch (start us, length us, event | category | flops | bytes accessed | tf_op | source)
XLA Modules:
  0.0 53.5 jit_solution(15170803759907506558)
XLA Ops:
  0.0 0.5 collective-permute-start.1
  0.5 2.3 %project_own.1 = (bf16[128,256]{1,0:T(8,128)(2,1)S(1)}, bf16[128,4096]{1,0:T(8,128)(2,1)S(1)}, bf16[4096,256]{1,0:T(8,128)(2,1)S(1)}, s32[1,128]{1,0:T(1,128)S(1)}, f32[256,128]{1,0:T(8,128)S(1)}) custom-call(bf16[128,4096]{1,0:T(8,128)(2,1)} %tok.1, bf16[4096,256]{1,0:T(8,128)(2,1)} %wk.1, bf16[4096,256]{1,0:T(8,128)(2,1)} %wv.1, s32[1,128]{1,0:T(1,128)} %bitcast.4, ...), custom_call_target="tpu_custom_call" | custom-call | flops 268435456 | bytes 3145728 | tf_op jit(solution)/shard_map/project_own/pallas_call | solution.py:124
  2.9 0.6 %project_unit.1.unit = bf16[264,256]{1,0:T(8,128)(2,1)S(1)} custom-call(bf16[128,256]{1,0:T(8,128)(2,1)S(1)} %get-tuple-element.26.half, bf16[128,4096]{1,0:T(8,128)(2,1)S(1)} %collective-permute-done.came, bf16[4096,256]{1,0:T(8,128)(2,1)S(1)} %get-tuple-element.27.w, s32[1,128]{1,0:T(1,128)S(1)} %get-tuple-element.28.docs, ...), custom_call_target="tpu_custom_call" | custom-call | flops 268435456 | bytes 1048576 | tf_op jit(solution)/shard_map/project_unit/pallas_call | solution.py:153
  3.4 2.9 %collective-permute-start.4 = (bf16[264,256]{1,0:T(8,128)(2,1)S(1)}, bf16[264,256]{1,0:T(8,128)(2,1)S(1)}, u32[]{:S(2)}, u32[]{:S(2)}) collective-permute-start(bf16[264,256]{1,0:T(8,128)(2,1)S(1)} %project_unit.1.unit), channel_id=1, source_target_pairs={{0,24},{4,100},{8,32},{12,108},{16,40},{20,116},{24,48},{28,124},{... | collective-permute-start | bytes 405512 | tf_op jit(solution)/shard_map/ppermute | solution.py:396
  6.4 1.8 %collective-permute-start.3 = (bf16[264,256]{1,0:T(8,128)(2,1)S(1)}, bf16[264,256]{1,0:T(8,128)(2,1)S(1)}, u32[]{:S(2)}, u32[]{:S(2)}) collective-permute-start(bf16[264,256]{1,0:T(8,128)(2,1)S(1)} %project_unit.1.unit), channel_id=1, source_target_pairs={{0,16},{4,68},{8,24},{12,76},{16,32},{20,84},{24,40},{28,92},{32,4... | collective-permute-start | bytes 405512 | tf_op jit(solution)/shard_map/ppermute | solution.py:396
  8.2 0.9 %collective-permute-start.2 = (bf16[264,256]{1,0:T(8,128)(2,1)S(1)}, bf16[264,256]{1,0:T(8,128)(2,1)S(1)}, u32[]{:S(2)}, u32[]{:S(2)}) collective-permute-start(bf16[264,256]{1,0:T(8,128)(2,1)S(1)} %project_unit.1.unit), channel_id=1, source_target_pairs={{0,8},{4,36},{8,16},{12,44},{16,24},{20,52},{24,32},{28,60},{32,40... | collective-permute-start | bytes 405512 | tf_op jit(solution)/shard_map/ppermute | solution.py:396
  9.1 1.6 %collective-permute-done.4.r3 = bf16[264,256]{1,0:T(8,128)(2,1)S(1)} collective-permute-done((bf16[264,256]{1,0:T(8,128)(2,1)S(1)}, bf16[264,256]{1,0:T(8,128)(2,1)S(1)}, u32[]{:S(2)}, u32[]{:S(2)}) %collective-permute-start.4) | collective-permute-done | bytes 135200 | tf_op jit(solution)/shard_map/ppermute | solution.py:396
  10.6 4.3 %collective-permute-done.3.r2 = bf16[264,256]{1,0:T(8,128)(2,1)S(1)} collective-permute-done((bf16[264,256]{1,0:T(8,128)(2,1)S(1)}, bf16[264,256]{1,0:T(8,128)(2,1)S(1)}, u32[]{:S(2)}, u32[]{:S(2)}) %collective-permute-start.3) | collective-permute-done | bytes 135200 | tf_op jit(solution)/shard_map/ppermute | solution.py:396
  15.0 1.5 %collective-permute-done.2.r1 = bf16[264,256]{1,0:T(8,128)(2,1)S(1)} collective-permute-done((bf16[264,256]{1,0:T(8,128)(2,1)S(1)}, bf16[264,256]{1,0:T(8,128)(2,1)S(1)}, u32[]{:S(2)}, u32[]{:S(2)}) %collective-permute-start.2) | collective-permute-done | bytes 135200 | tf_op jit(solution)/shard_map/ppermute | solution.py:396
  17.2 2.9 %collective-permute-start.5 = (bf16[528,256]{1,0:T(8,128)(2,1)S(1)}, bf16[528,256]{1,0:T(8,128)(2,1)S(1)}, u32[]{:S(2)}, u32[]{:S(2)}) collective-permute-start(bf16[528,256]{1,0:T(8,128)(2,1)S(1)} %get-tuple-element.37), channel_id=1, source_target_pairs={{0,64},{4,20},{8,72},{12,28},{16,80},{20,4},{24,88},{28,12},{32,96... | collective-permute-start | bytes 811016 | tf_op jit(solution)/shard_map/ppermute | solution.py:396
  20.0 1.3 %collective-permute-start.6 = (bf16[528,256]{1,0:T(8,128)(2,1)S(1)}, bf16[528,256]{1,0:T(8,128)(2,1)S(1)}, u32[]{:S(2)}, u32[]{:S(2)}) collective-permute-start(bf16[528,256]{1,0:T(8,128)(2,1)S(1)} %get-tuple-element.38.after), channel_id=1, source_target_pairs={{0,96},{4,28},{8,104},{12,4},{16,112},{20,12},{24,120},{28,20},{32... | collective-permute-start | bytes 811016 | tf_op jit(solution)/shard_map/ppermute | solution.py:396
  21.4 3.3 %project_q.1.qs = bf16[4,256,128]{2,1,0:T(8,128)(2,1)S(1)} custom-call(bf16[128,4096]{1,0:T(8,128)(2,1)S(1)} %get-tuple-element.25.tok, bf16[128,4096]{1,0:T(8,128)(2,1)S(1)} %collective-permute-done.came, bf16[4096,1024]{1,0:T(8,128)(2,1)} %wq.1, f32[256,128]{1,0:T(8,128)S(1)} %get-tuple-element.29.table), custom_call_target="tpu_custom_call" | custom-call | flops 1073741824 | bytes 6291456 | tf_op jit(solution)/shard_map/project_q/pallas_call | solution.py:187
  24.6 2.0 %attend_near.1 = (f32[4,256,128]{2,1,0:T(8,128)S(1)}, f32[4,256,128]{2,1,0:T(8,128)S(1)}, f32[4,256,128]{2,1,0:T(8,128)S(1)}) custom-call(bf16[4,256,128]{2,1,0:T(8,128)(2,1)S(1)} %project_q.1.qs, bf16[264,256]{1,0:T(8,128)(2,1)S(1)} %project_unit.1.unit, bf16[264,256]{1,0:T(8,128)(2,1)S(1)} %collective-permute-done.2.r1, ...), custom_call_target="tpu_custom_call" | custom-call | flops 536870912 | bytes 1048576 | tf_op jit(solution)/shard_map/attend_near/pallas_call | solution.py:300
  26.6 3.6 %collective-permute-done.5.far_b = bf16[528,256]{1,0:T(8,128)(2,1)S(1)} collective-permute-done((bf16[528,256]{1,0:T(8,128)(2,1)S(1)}, bf16[528,256]{1,0:T(8,128)(2,1)S(1)}, u32[]{:S(2)}, u32[]{:S(2)}) %collective-permute-start.5) | collective-permute-done | bytes 270368 | tf_op jit(solution)/shard_map/ppermute | solution.py:396
  30.2 2.2 %attend_middle.1 = (f32[4,256,128]{2,1,0:T(8,128)S(1)}, f32[4,256,128]{2,1,0:T(8,128)S(1)}, f32[4,256,128]{2,1,0:T(8,128)S(1)}) custom-call(bf16[4,256,128]{2,1,0:T(8,128)(2,1)S(1)} %project_q.1.qs, f32[4,256,128]{2,1,0:T(8,128)S(1)} %get-tuple-element.34.m_in, f32[4,256,128]{2,1,0:T(8,128)S(1)} %get-tuple-element.35.l_in, ...), custom_call_target="tpu_custom_call" | custom-call | flops 536870912 | bytes 1048576 | tf_op jit(solution)/shard_map/attend_middle/pallas_call | solution.py:317
  32.4 1.2 %attend_last.3 = bf16[128,512]{1,0:T(8,128)(2,1)S(1)} custom-call(bf16[4,256,128]{2,1,0:T(8,128)(2,1)S(1)} %project_q.1.qs, f32[4,256,128]{2,1,0:T(8,128)S(1)} %get-tuple-element.39.m_in, f32[4,256,128]{2,1,0:T(8,128)S(1)} %get-tuple-element.40.l_in, f32[4,256,128]{2,1,0:T(8,128)S(1)} %get-tuple-element.41.acc_in, bf16[264,256]{1,0:T(8,128)(2,1)S(1)} %project_unit.1.unit, ...), custom_call_target="tpu_custom_call" | custom-call | flops 268435456 | bytes 1048576 | tf_op jit(solution)/shard_map/attend_last/pallas_call | solution.py:338
  33.7 1.2 %attend_last.2.xm = bf16[128,512]{1,0:T(8,128)(2,1)S(1)} custom-call(bf16[4,256,128]{2,1,0:T(8,128)(2,1)S(1)} %project_q.1.qs, f32[4,256,128]{2,1,0:T(8,128)S(1)} %get-tuple-element.39.m_in, f32[4,256,128]{2,1,0:T(8,128)S(1)} %get-tuple-element.40.l_in, f32[4,256,128]{2,1,0:T(8,128)S(1)} %get-tuple-element.41.acc_in, bf16[264,256]{1,0:T(8,128)(2,1)S(1)} %project_unit.1.unit, ...), custom_call_target="tpu_custom_call" | custom-call | flops 268435456 | bytes 1048576 | tf_op jit(solution)/shard_map/attend_last/pallas_call | solution.py:338
  35.5 2.0 %collective-permute-start.10 = (bf16[128,1024]{1,0:T(8,128)(2,1)S(1)}, bf16[128,1024]{1,0:T(8,128)(2,1)S(1)}, u32[]{:S(2)}, u32[]{:S(2)}) collective-permute-start(bf16[128,1024]{1,0:T(8,128)(2,1)S(1)} %project_out.3), channel_id=1, source_target_pairs={{0,1},{1,2},{2,3},{3,0},{4,7},{5,4},{6,5},{7,6},{8,9},{9,10},{10,1... | collective-permute-start | bytes 786440 | tf_op jit(solution)/shard_map/ppermute | solution.py:432
  37.5 1.0 %project_out.2 = (bf16[128,1024]{1,0:T(8,128)(2,1)S(1)}, f32[128,1024]{1,0:T(8,128)S(1)}, f32[128,1024]{1,0:T(8,128)S(1)}) custom-call(bf16[128,512]{1,0:T(8,128)(2,1)S(1)} %attend_last.2.xm, bf16[128,512]{1,0:T(8,128)(2,1)S(1)} %collective-permute-done.8.xr, bf16[1024,4096]{1,0:T(8,128)(2,1)S(1)} %bitcast.2), custom_call_target="tpu_custom_call" | custom-call | flops 805306368 | bytes 6291456 | tf_op jit(solution)/shard_map/project_out/pallas_call | solution.py:361
  38.6 2.2 %collective-permute-start.9 = (bf16[128,1024]{1,0:T(8,128)(2,1)S(1)}, bf16[128,1024]{1,0:T(8,128)(2,1)S(1)}, u32[]{:S(2)}, u32[]{:S(2)}) collective-permute-start(bf16[128,1024]{1,0:T(8,128)(2,1)S(1)} %get-tuple-element.43), channel_id=1, source_target_pairs={{0,3},{1,0},{2,1},{3,2},{4,5},{5,6},{6,7},{7,4},{8,11},{9,8},{10,9... | collective-permute-start | bytes 786440 | tf_op jit(solution)/shard_map/ppermute | solution.py:432
  40.8 3.2 %collective-permute-done.10.came = bf16[128,1024]{1,0:T(8,128)(2,1)S(1)} collective-permute-done((bf16[128,1024]{1,0:T(8,128)(2,1)S(1)}, bf16[128,1024]{1,0:T(8,128)(2,1)S(1)}, u32[]{:S(2)}, u32[]{:S(2)}) %collective-permute-start.10) | collective-permute-done | bytes 262176 | tf_op jit(solution)/shard_map/ppermute | solution.py:432
  44.1 1.7 %collective-permute-start.11 = (bf16[128,1024]{1,0:T(8,128)(2,1)S(1)}, bf16[128,1024]{1,0:T(8,128)(2,1)S(1)}, u32[]{:S(2)}, u32[]{:S(2)}) collective-permute-start(bf16[128,1024]{1,0:T(8,128)(2,1)S(1)} %add_passing.1), channel_id=1, source_target_pairs={{0,1},{1,2},{2,3},{3,0},{4,7},{5,4},{6,5},{7,6},{8,9},{9,10},{10,1... | collective-permute-start | bytes 786440 | tf_op jit(solution)/shard_map/ppermute | solution.py:432
  45.8 6.9 %collective-permute-done.11.second = bf16[128,1024]{1,0:T(8,128)(2,1)S(1)} collective-permute-done((bf16[128,1024]{1,0:T(8,128)(2,1)S(1)}, bf16[128,1024]{1,0:T(8,128)(2,1)S(1)}, u32[]{:S(2)}, u32[]{:S(2)}) %collective-permute-start.11) | collective-permute-done | bytes 262176 | tf_op jit(solution)/shard_map/ppermute | solution.py:432
  52.7 0.8 %add_total.1 = bf16[128,1024]{1,0:T(8,128)(2,1)} custom-call(f32[128,1024]{1,0:T(8,128)S(1)} %get-tuple-element.42.own, bf16[128,1024]{1,0:T(8,128)(2,1)S(1)} %collective-permute-done.9.first, bf16[128,1024]{1,0:T(8,128)(2,1)S(1)} %collective-permute-done.11.second), custom_call_target="tpu_custom_call" | custom-call | bytes 1048576 | tf_op jit(solution)/shard_map/add_total/pallas_call | solution.py:381
  (18 shorter events, 1.4 us)
Async XLA Ops:
  0.0 2.9 %collective-permute-start = (bf16[128,4096]{1,0:T(8,128)(2,1)}, bf16[128,4096]{1,0:T(8,128)(2,1)S(1)}, u32[]{:S(2)}, u32[]{:S(2)}) collective-permute-start(bf16[128,4096]{1,0:T(8,128)(2,1)} %tok.1), channel_id=1, source_target_pairs={{0,4},{4,0},{8,12},{12,8},{16,20},{20,16},{24,28},{28,24},{32,36},... | collective-permute-start | bytes 3145736 | tf_op jit(solution)/shard_map/ppermute | solution.py:392
  0.0 2.9 %collective-permute-start.1 = (s32[1,128]{1,0:T(1,128)}, s32[1,128]{1,0:T(1,128)S(1)}, u32[]{:S(2)}, u32[]{:S(2)}) collective-permute-start(s32[1,128]{1,0:T(1,128)} %bitcast.3), channel_id=1, source_target_pairs={{0,4},{4,0},{8,12},{12,8},{16,20},{20,16},{24,28},{28,24},{32,36},... | collective-permute-start | bytes 1544 | tf_op jit(solution)/shard_map/ppermute | solution.py:392
  3.4 7.2 %collective-permute-start.4 = (bf16[264,256]{1,0:T(8,128)(2,1)S(1)}, bf16[264,256]{1,0:T(8,128)(2,1)S(1)}, u32[]{:S(2)}, u32[]{:S(2)}) collective-permute-start(bf16[264,256]{1,0:T(8,128)(2,1)S(1)} %project_unit.1.unit), channel_id=1, source_target_pairs={{0,24},{4,100},{8,32},{12,108},{16,40},{20,116},{24,48},{28,124},{... | collective-permute-start | bytes 405512 | tf_op jit(solution)/shard_map/ppermute | solution.py:396
  6.4 8.6 %collective-permute-start.3 = (bf16[264,256]{1,0:T(8,128)(2,1)S(1)}, bf16[264,256]{1,0:T(8,128)(2,1)S(1)}, u32[]{:S(2)}, u32[]{:S(2)}) collective-permute-start(bf16[264,256]{1,0:T(8,128)(2,1)S(1)} %project_unit.1.unit), channel_id=1, source_target_pairs={{0,16},{4,68},{8,24},{12,76},{16,32},{20,84},{24,40},{28,92},{32,4... | collective-permute-start | bytes 405512 | tf_op jit(solution)/shard_map/ppermute | solution.py:396
  8.2 8.3 %collective-permute-start.2 = (bf16[264,256]{1,0:T(8,128)(2,1)S(1)}, bf16[264,256]{1,0:T(8,128)(2,1)S(1)}, u32[]{:S(2)}, u32[]{:S(2)}) collective-permute-start(bf16[264,256]{1,0:T(8,128)(2,1)S(1)} %project_unit.1.unit), channel_id=1, source_target_pairs={{0,8},{4,36},{8,16},{12,44},{16,24},{20,52},{24,32},{28,60},{32,40... | collective-permute-start | bytes 405512 | tf_op jit(solution)/shard_map/ppermute | solution.py:396
  16.6 18.5 %slice-start = ((s8[8388608]{0:T(1024)(128)(4,1)}), s8[4194304]{0:T(1024)(128)(4,1)S(1)}, s32[]{:S(2)}) async-start(s8[8388608]{0:T(1024)(128)(4,1)} %bitcast.1), calls=%async_computation | async-start | bytes 8388608
  16.7 15.8 %collective-permute-start.7 = (bf16[1056,256]{1,0:T(8,128)(2,1)S(1)}, bf16[1056,256]{1,0:T(8,128)(2,1)S(1)}, u32[]{:S(2)}, u32[]{:S(2)}) collective-permute-start(bf16[1056,256]{1,0:T(8,128)(2,1)S(1)} %bundle_row.1), channel_id=1, source_target_pairs={{0,32},{4,12},{8,40},{12,20},{16,48},{20,28},{24,56},{28,4},{32,64... | collective-permute-start | bytes 1622024 | tf_op jit(solution)/shard_map/ppermute | solution.py:396
  17.2 13.1 %collective-permute-start.5 = (bf16[528,256]{1,0:T(8,128)(2,1)S(1)}, bf16[528,256]{1,0:T(8,128)(2,1)S(1)}, u32[]{:S(2)}, u32[]{:S(2)}) collective-permute-start(bf16[528,256]{1,0:T(8,128)(2,1)S(1)} %get-tuple-element.37), channel_id=1, source_target_pairs={{0,64},{4,20},{8,72},{12,28},{16,80},{20,4},{24,88},{28,12},{32,96... | collective-permute-start | bytes 811016 | tf_op jit(solution)/shard_map/ppermute | solution.py:396
  20.0 10.2 %collective-permute-start.6 = (bf16[528,256]{1,0:T(8,128)(2,1)S(1)}, bf16[528,256]{1,0:T(8,128)(2,1)S(1)}, u32[]{:S(2)}, u32[]{:S(2)}) collective-permute-start(bf16[528,256]{1,0:T(8,128)(2,1)S(1)} %get-tuple-element.38.after), channel_id=1, source_target_pairs={{0,96},{4,28},{8,104},{12,4},{16,112},{20,12},{24,120},{28,20},{32... | collective-permute-start | bytes 811016 | tf_op jit(solution)/shard_map/ppermute | solution.py:396
  21.4 13.7 %slice-start.1 = ((s8[8388608]{0:T(1024)(128)(4,1)}), s8[4194304]{0:T(1024)(128)(4,1)S(1)}, s32[]{:S(2)}) async-start(s8[8388608]{0:T(1024)(128)(4,1)} %bitcast.1), calls=%async_computation.1 | async-start | bytes 8388608
  33.6 1.4 %collective-permute-start.8 = (bf16[128,512]{1,0:T(8,128)(2,1)S(1)}, bf16[128,512]{1,0:T(8,128)(2,1)S(1)}, u32[]{:S(2)}, u32[]{:S(2)}) collective-permute-start(bf16[128,512]{1,0:T(8,128)(2,1)S(1)} %attend_last.3), channel_id=1, source_target_pairs={{0,4},{4,0},{8,12},{12,8},{16,20},{20,16},{24,28},{28,24},{32,36},... | collective-permute-start | bytes 393224 | tf_op jit(solution)/shard_map/ppermute | solution.py:392
  35.5 8.5 %collective-permute-start.10 = (bf16[128,1024]{1,0:T(8,128)(2,1)S(1)}, bf16[128,1024]{1,0:T(8,128)(2,1)S(1)}, u32[]{:S(2)}, u32[]{:S(2)}) collective-permute-start(bf16[128,1024]{1,0:T(8,128)(2,1)S(1)} %project_out.3), channel_id=1, source_target_pairs={{0,1},{1,2},{2,3},{3,0},{4,7},{5,4},{6,5},{7,6},{8,9},{9,10},{10,1... | collective-permute-start | bytes 786440 | tf_op jit(solution)/shard_map/ppermute | solution.py:432
  38.6 7.2 %collective-permute-start.9 = (bf16[128,1024]{1,0:T(8,128)(2,1)S(1)}, bf16[128,1024]{1,0:T(8,128)(2,1)S(1)}, u32[]{:S(2)}, u32[]{:S(2)}) collective-permute-start(bf16[128,1024]{1,0:T(8,128)(2,1)S(1)} %get-tuple-element.43), channel_id=1, source_target_pairs={{0,3},{1,0},{2,1},{3,2},{4,5},{5,6},{6,7},{7,4},{8,11},{9,8},{10,9... | collective-permute-start | bytes 786440 | tf_op jit(solution)/shard_map/ppermute | solution.py:432
  44.1 8.6 %collective-permute-start.11 = (bf16[128,1024]{1,0:T(8,128)(2,1)S(1)}, bf16[128,1024]{1,0:T(8,128)(2,1)S(1)}, u32[]{:S(2)}, u32[]{:S(2)}) collective-permute-start(bf16[128,1024]{1,0:T(8,128)(2,1)S(1)} %add_passing.1), channel_id=1, source_target_pairs={{0,1},{1,2},{2,3},{3,0},{4,7},{5,4},{6,5},{7,6},{8,9},{9,10},{10,1... | collective-permute-start | bytes 786440 | tf_op jit(solution)/shard_map/ppermute | solution.py:432

commit v5 on v4

--- a/solution.py
+++ b/solution.py
@@ -316,7 +316,7 @@
     state = like(heads, CHIP, HD, dtype=F32)
     return call(
         middle_body, "attend_middle", (state,) * 3, [VMEM] * 7, (VMEM,) * 3, limit=8,
-        flops=4 * heads * CHIP * 4 * CHIP * HD, exps=heads * CHIP * 4 * CHIP,
+        flops=32 * heads * CHIP * 4 * CHIP * HD, exps=heads * CHIP * 4 * CHIP,
     )(qs, m_in, l_in, acc_in, unit, far_b, far_c)
 
 
@@ -342,45 +342,49 @@
     )(qs, m_in, l_in, acc_in, unit, far_a)
 
 
-def project_out(xm, xr, w_out, groups, shifts, dtypes):
+def project_out(xm, xr, w_out, groups, parts, dtype):
     depth = xm.shape[1]
     width = w_out.shape[1] // groups
+    half = width // 2
 
     def body(xm, xr, w, *outs):
         core = core_index()
         own = pl.ds(pl.multiple_of(core * depth, depth), depth)
         other = pl.ds(pl.multiple_of((1 - core) * depth, depth), depth)
-        for (even, odd), out in zip(shifts, outs):
-            shift = jnp.where(core == 0, even, odd)
+        for (shift, side), out in zip(parts, outs):
             group = lax.rem(lax.axis_index("head") + shift, groups)
-            cols = pl.ds(pl.multiple_of(group * width, width), width)
+            cols = pl.ds(pl.multiple_of(group * width + side * half, half), half)
             got = jnp.dot(xm[...], w[own, cols], preferred_element_type=F32)
             got += jnp.dot(xr[...], w[other, cols], preferred_element_type=F32)
-            out[...] = got.astype(out.dtype)
-
-    return call(
-        body, "project_out", tuple(like(ROWS, width, dtype=d) for d in dtypes), [VMEM] * 3,
-        (VMEM,) * len(shifts), limit=4,
-        flops=2 * ROWS * 2 * depth * width * len(shifts), moved=2 * len(shifts),
+            out[...] = got.astype(dtype)
+
+    return call(
+        body, "project_out", (like(ROWS, half, dtype=dtype),) * len(parts), [VMEM] * 3,
+        (VMEM,) * len(parts), limit=4,
+        flops=2 * ROWS * 2 * depth * half * len(parts), moved=len(parts),
     )(xm, xr, w_out)
 
 
-def passing_body(own, came, out):
-    out[...] = (own[...] + came[...].astype(F32)).astype(BF16)
-
-
-def add_passing(own, came):
-    return call(passing_body, "add_passing", like(*own.shape), [VMEM] * 2, VMEM, limit=2)(own, came)
-
-
-def total_body(own, first, second, out):
-    out[...] = (own[...] + first[...].astype(F32) + second[...].astype(F32)).astype(BF16)
-
-
-def add_total(own, first, second):
-    return call(total_body, "add_total", like(*own.shape), [VMEM] * 3, VMEM, limit=2)(
-        own, first, second
-    )
+def add_body(a, b, p, q, out_a, out_b):
+    out_a[...] = (a[...] + p[...].astype(F32)).astype(BF16)
+    out_b[...] = (b[...] + q[...].astype(F32)).astype(BF16)
+
+
+def add_passing(a, b, p, q):
+    out = like(*p.shape)
+    return call(add_body, "add_passing", (out, out), [VMEM] * 4, (VMEM,) * 2, limit=2)(a, b, p, q)
+
+
+def total_body(own_a, own_b, left_a, left_b, right_a, right_b, out):
+    half = own_a.shape[1]
+    for at, pieces in ((0, (own_a, left_a, right_a)), (half, (own_b, left_b, right_b))):
+        total = pieces[0][...] + pieces[1][...].astype(F32) + pieces[2][...].astype(F32)
+        out[:, at : at + half] = total.astype(BF16)
+
+
+def add_total(*pieces):
+    rows, half = pieces[0].shape
+    return call(total_body, "add_total", like(rows, 2 * half), [VMEM] * 6, VMEM, limit=2)(*pieces)
 
 
 def shards(tokens, w_query, w_key, w_value, w_out, doc_ids):
@@ -412,7 +416,7 @@
     r1 = along(unit, ahead(1), ahead(4))
     r2 = along(unit, ahead(2), ahead(8))
     r3 = along(unit, ahead(3), ahead(12))
-    r1, r2, r3, came = lax.optimization_barrier((r1, r2, r3, came))
+    r1, r2, came = lax.optimization_barrier((r1, r2, came))
     out_b, out_c = bundle_pairs(unit, r1, r2)
     far_b = along(out_b, ahead(8), in_row(2))
     far_c = along(out_c, ahead(12), in_row(3))
@@ -423,22 +427,17 @@
     xr = swap(attend_last(1, qs, *state, unit, far_a))
     xm = attend_last(0, qs, *state, unit, far_a)
 
-    def across(value, even, odd):
-        moves = []
-        for r in range(ranks):
-            for g in range(groups):
-                to = (g + (odd if r % 2 else even)) % groups
-                moves.append((r * groups + g, r * groups + to))
-        return lax.ppermute(value, ("ctx", "head"), moves)
-
-    (opposite,) = project_out(xm, xr, w_out, groups, ((2, 2),), (BF16,))
-    passing = across(opposite, 1, 3)
-    direct, onward, total = project_out(
-        xm, xr, w_out, groups, ((3, 1), (1, 3), (0, 0)), (BF16, F32, F32)
-    )
-    direct = across(direct, 3, 1)
-    onward = across(add_passing(onward, passing), 1, 3)
-    return add_total(total, direct, onward)
+    def shift(value, step):
+        return lax.ppermute(value, "head", [(g, (g + step) % groups) for g in range(groups)])
+
+    a2, b2 = project_out(xm, xr, w_out, groups, ((2, 0), (2, 1)), BF16)
+    pass_a, pass_b = shift(a2, 1), shift(b2, -1)
+    b1, a3 = project_out(xm, xr, w_out, groups, ((1, 1), (3, 0)), BF16)
+    left_b, right_a = shift(b1, 1), shift(a3, -1)
+    a1, b3, a0, b0 = project_out(xm, xr, w_out, groups, ((1, 0), (3, 1), (0, 0), (0, 1)), F32)
+    a1, b3 = add_passing(a1, b3, pass_a, pass_b)
+    left_a, right_b = shift(a1, 1), shift(b3, -1)
+    return add_total(a0, b0, left_a, left_b, right_a, right_b)
 
 
 def solution(mesh):

time: 53.6 us -> 49.4 us (0.922)
  waiting for transfers between devices: 21.4 us -> 10.6 us
  starting transfers between devices: 16.8 us -> 23.1 us
    ppermute x3 -> x6, waiting for transfers between devices: 10.2 us -> 3.19 us  [shift(): lax.ppermute(value, 'head', [(g, (g + step) % groups) for g in range(grou...]
    ppermute x3 -> x6, starting transfers between devices: 5.88 us -> 11 us  [shift(): lax.ppermute(value, 'head', [(g, (g + step) % groups) for g in range(grou...]
    ppermute x6, waiting for transfers between devices: 11.1 us -> 7.31 us  [along(): return lax.ppermute(value, 'ctx', moves)]
    ppermute x6, starting transfers between devices: 10.3 us -> 11.5 us  [along(): return lax.ppermute(value, 'ctx', moves)]
    pallas_call x4 -> x5, Pallas kernels: 2.36 us -> 2.58 us  [the longest x3 1.73 us: project_out(): call(body, 'project_out', (like(ROWS, half, dtype=dtype),) * len(parts),...]
  transfers between devices with their start and end apart: 12 -> 15, of which waited for: 7 -> 7; matrix products, arithmetic and copies ran while one was open for 0% -> 0% of each run, Pallas kernels for 23% -> 25%
where the time goes in v5:
time: 49.4 us; the launch traced here: 49.2 us
  starting transfers between devices  23.1 us (47%)
  Pallas kernels  15.4 us (31%)
  waiting for transfers between devices  10.6 us (21%)
    ppermute x6, starting transfers between devices, along(): return lax.ppermute(value, 'ctx', moves)  11.5 us
    ppermute x6, starting transfers between devices, shift(): lax.ppermute(value, 'head', [(g, (g + step) % groups) for g in range(grou...  11 us
    ppermute x6, waiting for transfers between devices, along(): return lax.ppermute(value, 'ctx', moves)  7.31 us
    ppermute x6, waiting for transfers between devices, shift(): lax.ppermute(value, 'head', [(g, (g + step) % groups) for g in range(grou...  3.19 us
    pallas_call x1, Pallas kernels, project_q(): call(q_body, 'project_q', like(width // 2 // HD, CHIP, HD), [VMEM, VMEM,...  3.09 us
    pallas_call x2, Pallas kernels, attend_last(): call(body, 'attend_last', like(ROWS, heads * HD), [VMEM] * 6, VMEM, [pltp...  2.45 us
    pallas_call x1, Pallas kernels, project_own(): call(own_body, 'project_own', (like(ROWS, 2 * HD), like(ROWS, depth), lik...  2.35 us
    pallas_call x1, Pallas kernels, attend_middle(): call(middle_body, 'attend_middle', (state,) * 3, [VMEM] * 7, (VMEM,) * 3,...  2.16 us
  transfers between devices with their start and end apart: 15, of which 7 were waited for; matrix products, arithmetic and copies ran while one was open for 0% of the time, Pallas kernels for 25%

profile of v5, /device:TPU:0, one launch (start us, length us, event | category | flops | bytes accessed | tf_op | source)
XLA Modules:
  0.0 49.2 jit_solution(2831220195305958620)
XLA Ops:
  0.5 2.3 %project_own.1 = (bf16[128,256]{1,0:T(8,128)(2,1)S(1)}, bf16[128,4096]{1,0:T(8,128)(2,1)S(1)}, bf16[4096,256]{1,0:T(8,128)(2,1)S(1)}, s32[1,128]{1,0:T(1,128)S(1)}, f32[256,128]{1,0:T(8,128)S(1)}) custom-call(bf16[128,4096]{1,0:T(8,128)(2,1)} %tok.1, bf16[4096,256]{1,0:T(8,128)(2,1)} %wk.1, bf16[4096,256]{1,0:T(8,128)(2,1)} %wv.1, s32[1,128]{1,0:T(1,128)} %bitcast.4, ...), custom_call_target="tpu_custom_call" | custom-call | flops 268435456 | bytes 3145728 | tf_op jit(solution)/shard_map/project_own/pallas_call | solution.py:124
  3.4 3.2 %collective-permute-start.3 = (bf16[264,256]{1,0:T(8,128)(2,1)S(1)}, bf16[264,256]{1,0:T(8,128)(2,1)S(1)}, u32[]{:S(2)}, u32[]{:S(2)}) collective-permute-start(bf16[264,256]{1,0:T(8,128)(2,1)S(1)} %project_unit.1.unit), channel_id=1, source_target_pairs={{0,16},{4,68},{8,24},{12,76},{16,32},{20,84},{24,40},{28,92},{32,4... | collective-permute-start | bytes 405512 | tf_op jit(solution)/shard_map/ppermute | solution.py:400
  6.6 0.6 %collective-permute-start.2 = (bf16[264,256]{1,0:T(8,128)(2,1)S(1)}, bf16[264,256]{1,0:T(8,128)(2,1)S(1)}, u32[]{:S(2)}, u32[]{:S(2)}) collective-permute-start(bf16[264,256]{1,0:T(8,128)(2,1)S(1)} %project_unit.1.unit), channel_id=1, source_target_pairs={{0,8},{4,36},{8,16},{12,44},{16,24},{20,52},{24,32},{28,60},{32,40... | collective-permute-start | bytes 405512 | tf_op jit(solution)/shard_map/ppermute | solution.py:400
  7.2 3.7 %collective-permute-start.4 = (bf16[264,256]{1,0:T(8,128)(2,1)S(1)}, bf16[264,256]{1,0:T(8,128)(2,1)S(1)}, u32[]{:S(2)}, u32[]{:S(2)}) collective-permute-start(bf16[264,256]{1,0:T(8,128)(2,1)S(1)} %project_unit.1.unit), channel_id=1, source_target_pairs={{0,24},{4,100},{8,32},{12,108},{16,40},{20,116},{24,48},{28,124},{... | collective-permute-start | bytes 405512 | tf_op jit(solution)/shard_map/ppermute | solution.py:400
  10.8 1.4 %collective-permute-done.3.r2 = bf16[264,256]{1,0:T(8,128)(2,1)S(1)} collective-permute-done((bf16[264,256]{1,0:T(8,128)(2,1)S(1)}, bf16[264,256]{1,0:T(8,128)(2,1)S(1)}, u32[]{:S(2)}, u32[]{:S(2)}) %collective-permute-start.3) | collective-permute-done | bytes 135200 | tf_op jit(solution)/shard_map/ppermute | solution.py:400
  12.2 3.6 %collective-permute-done.2.r1 = bf16[264,256]{1,0:T(8,128)(2,1)S(1)} collective-permute-done((bf16[264,256]{1,0:T(8,128)(2,1)S(1)}, bf16[264,256]{1,0:T(8,128)(2,1)S(1)}, u32[]{:S(2)}, u32[]{:S(2)}) %collective-permute-start.2) | collective-permute-done | bytes 135200 | tf_op jit(solution)/shard_map/ppermute | solution.py:400
  15.9 2.0 %collective-permute-start.5 = (bf16[528,256]{1,0:T(8,128)(2,1)S(1)}, bf16[528,256]{1,0:T(8,128)(2,1)S(1)}, u32[]{:S(2)}, u32[]{:S(2)}) collective-permute-start(bf16[528,256]{1,0:T(8,128)(2,1)S(1)} %get-tuple-element.42), channel_id=1, source_target_pairs={{0,64},{4,20},{8,72},{12,28},{16,80},{20,4},{24,88},{28,12},{32,96... | collective-permute-start | bytes 811016 | tf_op jit(solution)/shard_map/ppermute | solution.py:400
  17.9 1.2 %collective-permute-start.6 = (bf16[528,256]{1,0:T(8,128)(2,1)S(1)}, bf16[528,256]{1,0:T(8,128)(2,1)S(1)}, u32[]{:S(2)}, u32[]{:S(2)}) collective-permute-start(bf16[528,256]{1,0:T(8,128)(2,1)S(1)} %get-tuple-element.43.after), channel_id=1, source_target_pairs={{0,96},{4,28},{8,104},{12,4},{16,112},{20,12},{24,120},{28,20},{32... | collective-permute-start | bytes 811016 | tf_op jit(solution)/shard_map/ppermute | solution.py:400
  19.1 0.9 %collective-permute-start.7 = (bf16[1056,256]{1,0:T(8,128)(2,1)S(1)}, bf16[1056,256]{1,0:T(8,128)(2,1)S(1)}, u32[]{:S(2)}, u32[]{:S(2)}) collective-permute-start(bf16[1056,256]{1,0:T(8,128)(2,1)S(1)} %bundle_row.1), channel_id=1, source_target_pairs={{0,32},{4,12},{8,40},{12,20},{16,48},{20,28},{24,56},{28,4},{32,64... | collective-permute-start | bytes 1622024 | tf_op jit(solution)/shard_map/ppermute | solution.py:400
  20.1 3.1 %project_q.1.qs = bf16[4,256,128]{2,1,0:T(8,128)(2,1)S(1)} custom-call(bf16[128,4096]{1,0:T(8,128)(2,1)S(1)} %get-tuple-element.31.tok, bf16[128,4096]{1,0:T(8,128)(2,1)S(1)} %collective-permute-done.came, bf16[4096,1024]{1,0:T(8,128)(2,1)} %wq.1, f32[256,128]{1,0:T(8,128)S(1)} %get-tuple-element.35.table), custom_call_target="tpu_custom_call" | custom-call | flops 1073741824 | bytes 6291456 | tf_op jit(solution)/shard_map/project_q/pallas_call | solution.py:187
  23.2 2.1 %attend_near.1 = (f32[4,256,128]{2,1,0:T(8,128)S(1)}, f32[4,256,128]{2,1,0:T(8,128)S(1)}, f32[4,256,128]{2,1,0:T(8,128)S(1)}) custom-call(bf16[4,256,128]{2,1,0:T(8,128)(2,1)S(1)} %project_q.1.qs, bf16[264,256]{1,0:T(8,128)(2,1)S(1)} %project_unit.1.unit, bf16[264,256]{1,0:T(8,128)(2,1)S(1)} %collective-permute-done.2.r1, ...), custom_call_target="tpu_custom_call" | custom-call | flops 536870912 | bytes 1048576 | tf_op jit(solution)/shard_map/attend_near/pallas_call | solution.py:300
  25.3 0.7 %collective-permute-done.6.far_c = bf16[528,256]{1,0:T(8,128)(2,1)S(1)} collective-permute-done((bf16[528,256]{1,0:T(8,128)(2,1)S(1)}, bf16[528,256]{1,0:T(8,128)(2,1)S(1)}, u32[]{:S(2)}, u32[]{:S(2)}) %collective-permute-start.6) | collective-permute-done | bytes 270368 | tf_op jit(solution)/shard_map/ppermute | solution.py:400
  25.9 2.2 %attend_middle.1 = (f32[4,256,128]{2,1,0:T(8,128)S(1)}, f32[4,256,128]{2,1,0:T(8,128)S(1)}, f32[4,256,128]{2,1,0:T(8,128)S(1)}) custom-call(bf16[4,256,128]{2,1,0:T(8,128)(2,1)S(1)} %project_q.1.qs, f32[4,256,128]{2,1,0:T(8,128)S(1)} %get-tuple-element.39.m_in, f32[4,256,128]{2,1,0:T(8,128)S(1)} %get-tuple-element.40.l_in, ...), custom_call_target="tpu_custom_call" | custom-call | flops 4294967296 | bytes 1048576 | tf_op jit(solution)/shard_map/attend_middle/pallas_call | solution.py:317
  28.1 1.7 %collective-permute-done.7.far_a = bf16[1056,256]{1,0:T(8,128)(2,1)S(1)} collective-permute-done((bf16[1056,256]{1,0:T(8,128)(2,1)S(1)}, bf16[1056,256]{1,0:T(8,128)(2,1)S(1)}, u32[]{:S(2)}, u32[]{:S(2)}) %collective-permute-start.7) | collective-permute-done | bytes 540704 | tf_op jit(solution)/shard_map/ppermute | solution.py:400
  29.8 1.2 %attend_last.3 = bf16[128,512]{1,0:T(8,128)(2,1)S(1)} custom-call(bf16[4,256,128]{2,1,0:T(8,128)(2,1)S(1)} %project_q.1.qs, f32[4,256,128]{2,1,0:T(8,128)S(1)} %get-tuple-element.44.m_in, f32[4,256,128]{2,1,0:T(8,128)S(1)} %get-tuple-element.45.l_in, f32[4,256,128]{2,1,0:T(8,128)S(1)} %get-tuple-element.46.acc_in, bf16[264,256]{1,0:T(8,128)(2,1)S(1)} %project_unit.1.unit, ...), custom_call_target="tpu_custom_call" | custom-call | flops 268435456 | bytes 1048576 | tf_op jit(solution)/shard_map/attend_last/pallas_call | solution.py:338
  31.1 1.2 %attend_last.2.xm = bf16[128,512]{1,0:T(8,128)(2,1)S(1)} custom-call(bf16[4,256,128]{2,1,0:T(8,128)(2,1)S(1)} %project_q.1.qs, f32[4,256,128]{2,1,0:T(8,128)S(1)} %get-tuple-element.44.m_in, f32[4,256,128]{2,1,0:T(8,128)S(1)} %get-tuple-element.45.l_in, f32[4,256,128]{2,1,0:T(8,128)S(1)} %get-tuple-element.46.acc_in, bf16[264,256]{1,0:T(8,128)(2,1)S(1)} %project_unit.1.unit, ...), custom_call_target="tpu_custom_call" | custom-call | flops 268435456 | bytes 1048576 | tf_op jit(solution)/shard_map/attend_last/pallas_call | solution.py:338
  32.9 2.2 %collective-permute-start.9 = (bf16[128,512]{1,0:T(8,128)(2,1)S(1)}, bf16[128,512]{1,0:T(8,128)(2,1)S(1)}, u32[]{:S(2)}, u32[]{:S(2)}) collective-permute-start(bf16[128,512]{1,0:T(8,128)(2,1)S(1)} %get-tuple-element.51), channel_id=1, source_target_pairs={{0,1},{1,2},{2,3},{3,0},{4,5},{5,6},{6,7},{7,4},{8,9},{9,10},{10,1... | collective-permute-start | bytes 393224 | tf_op jit(solution)/shard_map/ppermute | solution.py:431
  35.1 2.2 %collective-permute-start.10 = (bf16[128,512]{1,0:T(8,128)(2,1)S(1)}, bf16[128,512]{1,0:T(8,128)(2,1)S(1)}, u32[]{:S(2)}, u32[]{:S(2)}) collective-permute-start(bf16[128,512]{1,0:T(8,128)(2,1)S(1)} %get-tuple-element.52), channel_id=1, source_target_pairs={{0,3},{1,0},{2,1},{3,2},{4,7},{5,4},{6,5},{7,6},{8,11},{9,8},{10,9... | collective-permute-start | bytes 393224 | tf_op jit(solution)/shard_map/ppermute | solution.py:431
  37.9 3.2 %collective-permute-start.13 = (bf16[128,512]{1,0:T(8,128)(2,1)S(1)}, bf16[128,512]{1,0:T(8,128)(2,1)S(1)}, u32[]{:S(2)}, u32[]{:S(2)}) collective-permute-start(bf16[128,512]{1,0:T(8,128)(2,1)S(1)} %get-tuple-element.55), channel_id=1, source_target_pairs={{0,3},{1,0},{2,1},{3,2},{4,7},{5,4},{6,5},{7,6},{8,11},{9,8},{10,9... | collective-permute-start | bytes 393224 | tf_op jit(solution)/shard_map/ppermute | solution.py:431
  41.1 0.8 %project_out.3 = (f32[128,512]{1,0:T(8,128)S(1)}, f32[128,512]{1,0:T(8,128)S(1)}, f32[128,512]{1,0:T(8,128)S(1)}, f32[128,512]{1,0:T(8,128)S(1)}) custom-call(bf16[128,512]{1,0:T(8,128)(2,1)S(1)} %attend_last.2.xm, bf16[128,512]{1,0:T(8,128)(2,1)S(1)} %collective-permute-done.8.xr, bf16[1024,4096]{1,0:T(8,128)(2,1)S(1)} %bitcast.2), custom_call_target="tpu_custom_call" | custom-call | flops 536870912 | bytes 4194304 | tf_op jit(solution)/shard_map/project_out/pallas_call | solution.py:361
  41.9 1.5 %collective-permute-start.11 = (bf16[128,512]{1,0:T(8,128)(2,1)S(1)}, bf16[128,512]{1,0:T(8,128)(2,1)S(1)}, u32[]{:S(2)}, u32[]{:S(2)}) collective-permute-start(bf16[128,512]{1,0:T(8,128)(2,1)S(1)} %get-tuple-element.53), channel_id=1, source_target_pairs={{0,1},{1,2},{2,3},{3,0},{4,5},{5,6},{6,7},{7,4},{8,9},{9,10},{10,1... | collective-permute-start | bytes 393224 | tf_op jit(solution)/shard_map/ppermute | solution.py:431
  43.5 1.8 %collective-permute-start.14 = (bf16[128,512]{1,0:T(8,128)(2,1)S(1)}, bf16[128,512]{1,0:T(8,128)(2,1)S(1)}, u32[]{:S(2)}, u32[]{:S(2)}) collective-permute-start(bf16[128,512]{1,0:T(8,128)(2,1)S(1)} %get-tuple-element.56), channel_id=1, source_target_pairs={{0,3},{1,0},{2,1},{3,2},{4,7},{5,4},{6,5},{7,6},{8,11},{9,8},{10,9... | collective-permute-start | bytes 393224 | tf_op jit(solution)/shard_map/ppermute | solution.py:431
  45.3 3.0 %collective-permute-done.11.left_a = bf16[128,512]{1,0:T(8,128)(2,1)S(1)} collective-permute-done((bf16[128,512]{1,0:T(8,128)(2,1)S(1)}, bf16[128,512]{1,0:T(8,128)(2,1)S(1)}, u32[]{:S(2)}, u32[]{:S(2)}) %collective-permute-start.11) | collective-permute-done | bytes 131104 | tf_op jit(solution)/shard_map/ppermute | solution.py:431
  48.4 0.8 %add_total.1 = bf16[128,1024]{1,0:T(8,128)(2,1)} custom-call(f32[128,512]{1,0:T(8,128)S(1)} %get-tuple-element.47.own_a, f32[128,512]{1,0:T(8,128)S(1)} %get-tuple-element.48.own_b, bf16[128,512]{1,0:T(8,128)(2,1)S(1)} %collective-permute-done.11.left_a, bf16[128,512]{1,0:T(8,128)(2,1)S(1)} %collective-permute-done.12.left_b, ...), custom_call_target="tpu_custom_call" | custom-call | bytes 1048576 | tf_op jit(solution)/shard_map/add_total/pallas_call | solution.py:387
  (25 shorter events, 2.7 us)
Async XLA Ops:
  0.0 2.9 %collective-permute-start = (bf16[128,4096]{1,0:T(8,128)(2,1)}, bf16[128,4096]{1,0:T(8,128)(2,1)S(1)}, u32[]{:S(2)}, u32[]{:S(2)}) collective-permute-start(bf16[128,4096]{1,0:T(8,128)(2,1)} %tok.1), channel_id=1, source_target_pairs={{0,4},{4,0},{8,12},{12,8},{16,20},{20,16},{24,28},{28,24},{32,36},... | collective-permute-start | bytes 3145736 | tf_op jit(solution)/shard_map/ppermute | solution.py:396
  0.0 2.9 %collective-permute-start.1 = (s32[1,128]{1,0:T(1,128)}, s32[1,128]{1,0:T(1,128)S(1)}, u32[]{:S(2)}, u32[]{:S(2)}) collective-permute-start(s32[1,128]{1,0:T(1,128)} %bitcast.3), channel_id=1, source_target_pairs={{0,4},{4,0},{8,12},{12,8},{16,20},{20,16},{24,28},{28,24},{32,36},... | collective-permute-start | bytes 1544 | tf_op jit(solution)/shard_map/ppermute | solution.py:396
  3.4 8.8 %collective-permute-start.3 = (bf16[264,256]{1,0:T(8,128)(2,1)S(1)}, bf16[264,256]{1,0:T(8,128)(2,1)S(1)}, u32[]{:S(2)}, u32[]{:S(2)}) collective-permute-start(bf16[264,256]{1,0:T(8,128)(2,1)S(1)} %project_unit.1.unit), channel_id=1, source_target_pairs={{0,16},{4,68},{8,24},{12,76},{16,32},{20,84},{24,40},{28,92},{32,4... | collective-permute-start | bytes 405512 | tf_op jit(solution)/shard_map/ppermute | solution.py:400
  6.6 9.2 %collective-permute-start.2 = (bf16[264,256]{1,0:T(8,128)(2,1)S(1)}, bf16[264,256]{1,0:T(8,128)(2,1)S(1)}, u32[]{:S(2)}, u32[]{:S(2)}) collective-permute-start(bf16[264,256]{1,0:T(8,128)(2,1)S(1)} %project_unit.1.unit), channel_id=1, source_target_pairs={{0,8},{4,36},{8,16},{12,44},{16,24},{20,52},{24,32},{28,60},{32,40... | collective-permute-start | bytes 405512 | tf_op jit(solution)/shard_map/ppermute | solution.py:400
  7.2 11.9 %collective-permute-start.4 = (bf16[264,256]{1,0:T(8,128)(2,1)S(1)}, bf16[264,256]{1,0:T(8,128)(2,1)S(1)}, u32[]{:S(2)}, u32[]{:S(2)}) collective-permute-start(bf16[264,256]{1,0:T(8,128)(2,1)S(1)} %project_unit.1.unit), channel_id=1, source_target_pairs={{0,24},{4,100},{8,32},{12,108},{16,40},{20,116},{24,48},{28,124},{... | collective-permute-start | bytes 405512 | tf_op jit(solution)/shard_map/ppermute | solution.py:400
  15.9 9.4 %collective-permute-start.5 = (bf16[528,256]{1,0:T(8,128)(2,1)S(1)}, bf16[528,256]{1,0:T(8,128)(2,1)S(1)}, u32[]{:S(2)}, u32[]{:S(2)}) collective-permute-start(bf16[528,256]{1,0:T(8,128)(2,1)S(1)} %get-tuple-element.42), channel_id=1, source_target_pairs={{0,64},{4,20},{8,72},{12,28},{16,80},{20,4},{24,88},{28,12},{32,96... | collective-permute-start | bytes 811016 | tf_op jit(solution)/shard_map/ppermute | solution.py:400
  17.9 8.0 %collective-permute-start.6 = (bf16[528,256]{1,0:T(8,128)(2,1)S(1)}, bf16[528,256]{1,0:T(8,128)(2,1)S(1)}, u32[]{:S(2)}, u32[]{:S(2)}) collective-permute-start(bf16[528,256]{1,0:T(8,128)(2,1)S(1)} %get-tuple-element.43.after), channel_id=1, source_target_pairs={{0,96},{4,28},{8,104},{12,4},{16,112},{20,12},{24,120},{28,20},{32... | collective-permute-start | bytes 811016 | tf_op jit(solution)/shard_map/ppermute | solution.py:400
  19.1 10.6 %collective-permute-start.7 = (bf16[1056,256]{1,0:T(8,128)(2,1)S(1)}, bf16[1056,256]{1,0:T(8,128)(2,1)S(1)}, u32[]{:S(2)}, u32[]{:S(2)}) collective-permute-start(bf16[1056,256]{1,0:T(8,128)(2,1)S(1)} %bundle_row.1), channel_id=1, source_target_pairs={{0,32},{4,12},{8,40},{12,20},{16,48},{20,28},{24,56},{28,4},{32,64... | collective-permute-start | bytes 1622024 | tf_op jit(solution)/shard_map/ppermute | solution.py:400
  23.2 9.3 %slice-start = ((s8[8388608]{0:T(1024)(128)(4,1)}), s8[4194304]{0:T(1024)(128)(4,1)S(1)}, s32[]{:S(2)}) async-start(s8[8388608]{0:T(1024)(128)(4,1)} %bitcast.1), calls=%async_computation | async-start | bytes 8388608
  25.9 6.5 %slice-start.1 = ((s8[8388608]{0:T(1024)(128)(4,1)}), s8[4194304]{0:T(1024)(128)(4,1)S(1)}, s32[]{:S(2)}) async-start(s8[8388608]{0:T(1024)(128)(4,1)} %bitcast.1), calls=%async_computation.1 | async-start | bytes 8388608
  31.0 1.4 %collective-permute-start.8 = (bf16[128,512]{1,0:T(8,128)(2,1)S(1)}, bf16[128,512]{1,0:T(8,128)(2,1)S(1)}, u32[]{:S(2)}, u32[]{:S(2)}) collective-permute-start(bf16[128,512]{1,0:T(8,128)(2,1)S(1)} %attend_last.3), channel_id=1, source_target_pairs={{0,4},{4,0},{8,12},{12,8},{16,20},{20,16},{24,28},{28,24},{32,36},... | collective-permute-start | bytes 393224 | tf_op jit(solution)/shard_map/ppermute | solution.py:396
  32.9 8.9 %collective-permute-start.9 = (bf16[128,512]{1,0:T(8,128)(2,1)S(1)}, bf16[128,512]{1,0:T(8,128)(2,1)S(1)}, u32[]{:S(2)}, u32[]{:S(2)}) collective-permute-start(bf16[128,512]{1,0:T(8,128)(2,1)S(1)} %get-tuple-element.51), channel_id=1, source_target_pairs={{0,1},{1,2},{2,3},{3,0},{4,5},{5,6},{6,7},{7,4},{8,9},{9,10},{10,1... | collective-permute-start | bytes 393224 | tf_op jit(solution)/shard_map/ppermute | solution.py:431
  35.1 6.8 %collective-permute-start.10 = (bf16[128,512]{1,0:T(8,128)(2,1)S(1)}, bf16[128,512]{1,0:T(8,128)(2,1)S(1)}, u32[]{:S(2)}, u32[]{:S(2)}) collective-permute-start(bf16[128,512]{1,0:T(8,128)(2,1)S(1)} %get-tuple-element.52), channel_id=1, source_target_pairs={{0,3},{1,0},{2,1},{3,2},{4,7},{5,4},{6,5},{7,6},{8,11},{9,8},{10,9... | collective-permute-start | bytes 393224 | tf_op jit(solution)/shard_map/ppermute | solution.py:431
  37.8 7.5 %collective-permute-start.12 = (bf16[128,512]{1,0:T(8,128)(2,1)S(1)}, bf16[128,512]{1,0:T(8,128)(2,1)S(1)}, u32[]{:S(2)}, u32[]{:S(2)}) collective-permute-start(bf16[128,512]{1,0:T(8,128)(2,1)S(1)} %get-tuple-element.54), channel_id=1, source_target_pairs={{0,1},{1,2},{2,3},{3,0},{4,5},{5,6},{6,7},{7,4},{8,9},{9,10},{10,1... | collective-permute-start | bytes 393224 | tf_op jit(solution)/shard_map/ppermute | solution.py:431
  37.9 7.4 %collective-permute-start.13 = (bf16[128,512]{1,0:T(8,128)(2,1)S(1)}, bf16[128,512]{1,0:T(8,128)(2,1)S(1)}, u32[]{:S(2)}, u32[]{:S(2)}) collective-permute-start(bf16[128,512]{1,0:T(8,128)(2,1)S(1)} %get-tuple-element.55), channel_id=1, source_target_pairs={{0,3},{1,0},{2,1},{3,2},{4,7},{5,4},{6,5},{7,6},{8,11},{9,8},{10,9... | collective-permute-start | bytes 393224 | tf_op jit(solution)/shard_map/ppermute | solution.py:431
  41.9 6.3 %collective-permute-start.11 = (bf16[128,512]{1,0:T(8,128)(2,1)S(1)}, bf16[128,512]{1,0:T(8,128)(2,1)S(1)}, u32[]{:S(2)}, u32[]{:S(2)}) collective-permute-start(bf16[128,512]{1,0:T(8,128)(2,1)S(1)} %get-tuple-element.53), channel_id=1, source_target_pairs={{0,1},{1,2},{2,3},{3,0},{4,5},{5,6},{6,7},{7,4},{8,9},{9,10},{10,1... | collective-permute-start | bytes 393224 | tf_op jit(solution)/shard_map/ppermute | solution.py:431
  43.5 5.0 %collective-permute-start.14 = (bf16[128,512]{1,0:T(8,128)(2,1)S(1)}, bf16[128,512]{1,0:T(8,128)(2,1)S(1)}, u32[]{:S(2)}, u32[]{:S(2)}) collective-permute-start(bf16[128,512]{1,0:T(8,128)(2,1)S(1)} %get-tuple-element.56), channel_id=1, source_target_pairs={{0,3},{1,0},{2,1},{3,2},{4,7},{5,4},{6,5},{7,6},{8,11},{9,8},{10,9... | collective-permute-start | bytes 393224 | tf_op jit(solution)/shard_map/ppermute | solution.py:431

commit v6 on v5

--- a/solution.py
+++ b/solution.py
@@ -193,23 +193,23 @@
 
 NONE = 99
 NEAR = ((1, 2, 3), (4, 8, NONE))
-MIDDLE = ((8, 9, NONE, NONE), (2, 6, 3, 7))
-LAST = ((4, 5, 6, 7), (1, 5, 9, NONE))
-
-
-def fill(out, slots, late):
+MIDDLE = ((8, 9, 4, NONE), (2, 6, 3, 7))
+LAST = ((5, 6, 7), (1, 5, 9))
+
+
+def fill(out, slots, late, even):
     place = lax.axis_index("ctx")
     column = lax.rem(lax.div(place, 2), 4)
-    skip = jnp.where((lax.rem(place, 2) == 1) & (column >= late), 1, 0)
+    skip = jnp.where(lax.rem(place, 2) == 0, even, jnp.where(column >= late, 1, 0))
     for i in range(out.shape[0] // UNIT):
-        out[i * UNIT : (i + 1) * UNIT, :] = slots[jnp.minimum(skip + i, 3)]
+        out[i * UNIT : (i + 1) * UNIT, :] = slots[skip + i]
 
 
 def pairs_body(unit, r1, r2, out_b, out_c, slots):
     for i, src in enumerate((unit, r1, r2)):
         slots[i] = src[...]
-    fill(out_b, slots, 2)
-    fill(out_c, slots, 1)
+    fill(out_b, slots, 2, 0)
+    fill(out_c, slots, 1, 0)
 
 
 def bundle_pairs(unit, r1, r2):
@@ -223,12 +223,12 @@
 def row_body(unit, r1, r2, r3, after, out_a, slots):
     for i, src in enumerate((unit, r1, r2, r3)):
         slots[i] = src[...]
-    fill(out_a, slots, 3)
+    fill(out_a, slots, 3, 1)
 
 
 def bundle_row(unit, r1, r2, r3, after):
     return call(
-        row_body, "bundle_row", like(4 * UNIT, 2 * HD), [VMEM] * 5, VMEM,
+        row_body, "bundle_row", like(3 * UNIT, 2 * HD), [VMEM] * 5, VMEM,
         [pltpu.VMEM((4, UNIT, 2 * HD), BF16)], limit=2,
     )(unit, r1, r2, r3, after)
 
@@ -303,21 +303,23 @@
     )(qs, unit, r1, r2, r3)
 
 
-def middle_body(qs, m_in, l_in, acc_in, unit, far_b, far_c, m_s, l_s, acc):
+def middle_body(qs, m_in, l_in, acc_in, unit, r4, far_b, far_c, m_s, l_s, acc):
     before = (m_in, l_in, acc_in)
+    third, fourth = parts(far_c)
+    third = jnp.where(core_index() == 0, r4[...], third)
     add_units(
-        lambda h: qs[h], parts(far_b) + parts(far_c), MIDDLE, tags_of(unit)[1],
+        lambda h: qs[h], parts(far_b) + [third, fourth], MIDDLE, tags_of(unit)[1],
         lambda h: [ref[h] for ref in before], (m_s, l_s, acc),
     )
 
 
-def attend_middle(qs, m_in, l_in, acc_in, unit, far_b, far_c):
+def attend_middle(qs, m_in, l_in, acc_in, unit, r4, far_b, far_c):
     heads = qs.shape[0]
     state = like(heads, CHIP, HD, dtype=F32)
     return call(
-        middle_body, "attend_middle", (state,) * 3, [VMEM] * 7, (VMEM,) * 3, limit=8,
+        middle_body, "attend_middle", (state,) * 3, [VMEM] * 8, (VMEM,) * 3, limit=8,
         flops=32 * heads * CHIP * 4 * CHIP * HD, exps=heads * CHIP * 4 * CHIP,
-    )(qs, m_in, l_in, acc_in, unit, far_b, far_c)
+    )(qs, m_in, l_in, acc_in, unit, r4, far_b, far_c)
 
 
 def attend_last(side, qs, m_in, l_in, acc_in, unit, far_a):
@@ -338,7 +340,7 @@
     return call(
         body, "attend_last", like(ROWS, heads * HD), [VMEM] * 6, VMEM,
         [pltpu.VMEM((CHIP, HD), F32), state, state, state],
-        limit=8, flops=4 * heads * ROWS * 4 * CHIP * HD, exps=heads * ROWS * 4 * CHIP,
+        limit=8, flops=4 * heads * ROWS * 3 * CHIP * HD, exps=heads * ROWS * 3 * CHIP,
     )(qs, m_in, l_in, acc_in, unit, far_a)
 
 
@@ -416,14 +418,15 @@
     r1 = along(unit, ahead(1), ahead(4))
     r2 = along(unit, ahead(2), ahead(8))
     r3 = along(unit, ahead(3), ahead(12))
+    r4 = along(unit, ahead(4), in_row(3))
     r1, r2, came = lax.optimization_barrier((r1, r2, came))
     out_b, out_c = bundle_pairs(unit, r1, r2)
     far_b = along(out_b, ahead(8), in_row(2))
     far_c = along(out_c, ahead(12), in_row(3))
-    far_a = along(bundle_row(unit, r1, r2, r3, out_c), ahead(4), in_row(1))
+    far_a = along(bundle_row(unit, r1, r2, r3, r4), ahead(4), in_row(1))
     qs = project_q(tokens, came, w_query, table)
     state = attend_near(qs, unit, r1, r2, r3)
-    state = attend_middle(qs, *state, unit, far_b, far_c)
+    state = attend_middle(qs, *state, unit, r4, far_b, far_c)
     xr = swap(attend_last(1, qs, *state, unit, far_a))
     xm = attend_last(0, qs, *state, unit, far_a)
 

time: 49.4 us -> 47.6 us (0.964)
  waiting for transfers between devices: 10.6 us -> 7.32 us
  starting transfers between devices: 23.1 us -> 25.2 us
  Pallas kernels: 15.4 us -> 14.7 us
    ppermute x6 -> x7, waiting for transfers between devices: 7.31 us -> 4.07 us  [along(): return lax.ppermute(value, 'ctx', moves)]
    ppermute x6 -> x7, starting transfers between devices: 11.5 us -> 13.5 us  [along(): return lax.ppermute(value, 'ctx', moves)]
  transfers between devices with their start and end apart: 15 -> 16, of which waited for: 7 -> 5; matrix products, arithmetic and copies ran while one was open for 0% -> 0% of each run, Pallas kernels for 25% -> 25%
where the time goes in v6:
time: 47.6 us; the launch traced here: 47.4 us
  starting transfers between devices  25.2 us (53%)
  Pallas kernels  14.7 us (31%)
  waiting for transfers between devices  7.32 us (15%)
    ppermute x7, starting transfers between devices, along(): return lax.ppermute(value, 'ctx', moves)  13.5 us
    ppermute x6, starting transfers between devices, shift(): lax.ppermute(value, 'head', [(g, (g + step) % groups) for g in range(grou...  11 us
    ppermute x7, waiting for transfers between devices, along(): return lax.ppermute(value, 'ctx', moves)  4.07 us
    pallas_call x1, Pallas kernels, project_q(): call(q_body, 'project_q', like(width // 2 // HD, CHIP, HD), [VMEM, VMEM,...  3.09 us
    ppermute x6, waiting for transfers between devices, shift(): lax.ppermute(value, 'head', [(g, (g + step) % groups) for g in range(grou...  3.08 us
    pallas_call x1, Pallas kernels, project_own(): call(own_body, 'project_own', (like(ROWS, 2 * HD), like(ROWS, depth), lik...  2.35 us
    pallas_call x1, Pallas kernels, attend_middle(): call(middle_body, 'attend_middle', (state,) * 3, [VMEM] * 8, (VMEM,) * 3,...  2.17 us
    pallas_call x1, Pallas kernels, attend_near(): call(near_body, 'attend_near', (state, state, state), [VMEM] * 5, (VMEM,)...  2.06 us
  transfers between devices with their start and end apart: 16, of which 5 were waited for; matrix products, arithmetic and copies ran while one was open for 0% of the time, Pallas kernels for 25%

profile of v6, /device:TPU:0, one launch (start us, length us, event | category | flops | bytes accessed | tf_op | source)
XLA Modules:
  0.0 47.4 jit_solution(6574968050147031711)
XLA Ops:
  0.5 2.3 %project_own.1 = (bf16[128,256]{1,0:T(8,128)(2,1)S(1)}, bf16[128,4096]{1,0:T(8,128)(2,1)S(1)}, bf16[4096,256]{1,0:T(8,128)(2,1)S(1)}, s32[1,128]{1,0:T(1,128)S(1)}, f32[256,128]{1,0:T(8,128)S(1)}) custom-call(bf16[128,4096]{1,0:T(8,128)(2,1)} %tok.1, bf16[4096,256]{1,0:T(8,128)(2,1)} %wk.1, bf16[4096,256]{1,0:T(8,128)(2,1)} %wv.1, s32[1,128]{1,0:T(1,128)} %bitcast.4, ...), custom_call_target="tpu_custom_call" | custom-call | flops 268435456 | bytes 3145728 | tf_op jit(solution)/shard_map/project_own/pallas_call | solution.py:124
  2.9 0.5 %project_unit.1.unit = bf16[264,256]{1,0:T(8,128)(2,1)S(1)} custom-call(bf16[128,256]{1,0:T(8,128)(2,1)S(1)} %get-tuple-element.32.half, bf16[128,4096]{1,0:T(8,128)(2,1)S(1)} %collective-permute-done.came, bf16[4096,256]{1,0:T(8,128)(2,1)S(1)} %get-tuple-element.33.w, s32[1,128]{1,0:T(1,128)S(1)} %get-tuple-element.34.docs, ...), custom_call_target="tpu_custom_call" | custom-call | flops 268435456 | bytes 1048576 | tf_op jit(solution)/shard_map/project_unit/pallas_call | solution.py:153
  3.4 3.2 %collective-permute-start.3 = (bf16[264,256]{1,0:T(8,128)(2,1)S(1)}, bf16[264,256]{1,0:T(8,128)(2,1)S(1)}, u32[]{:S(2)}, u32[]{:S(2)}) collective-permute-start(bf16[264,256]{1,0:T(8,128)(2,1)S(1)} %project_unit.1.unit), channel_id=1, source_target_pairs={{0,16},{4,68},{8,24},{12,76},{16,32},{20,84},{24,40},{28,92},{32,4... | collective-permute-start | bytes 405512 | tf_op jit(solution)/shard_map/ppermute | solution.py:402
  6.6 0.6 %collective-permute-start.2 = (bf16[264,256]{1,0:T(8,128)(2,1)S(1)}, bf16[264,256]{1,0:T(8,128)(2,1)S(1)}, u32[]{:S(2)}, u32[]{:S(2)}) collective-permute-start(bf16[264,256]{1,0:T(8,128)(2,1)S(1)} %project_unit.1.unit), channel_id=1, source_target_pairs={{0,8},{4,36},{8,16},{12,44},{16,24},{20,52},{24,32},{28,60},{32,40... | collective-permute-start | bytes 405512 | tf_op jit(solution)/shard_map/ppermute | solution.py:402
  7.2 1.6 %collective-permute-start.5 = (bf16[264,256]{1,0:T(8,128)(2,1)S(1)}, bf16[264,256]{1,0:T(8,128)(2,1)S(1)}, u32[]{:S(2)}, u32[]{:S(2)}) collective-permute-start(bf16[264,256]{1,0:T(8,128)(2,1)S(1)} %project_unit.1.unit), channel_id=1, source_target_pairs={{0,32},{4,28},{8,40},{12,4},{16,48},{20,12},{24,56},{28,20},{32,64... | collective-permute-start | bytes 405512 | tf_op jit(solution)/shard_map/ppermute | solution.py:402
  8.8 3.7 %collective-permute-start.4 = (bf16[264,256]{1,0:T(8,128)(2,1)S(1)}, bf16[264,256]{1,0:T(8,128)(2,1)S(1)}, u32[]{:S(2)}, u32[]{:S(2)}) collective-permute-start(bf16[264,256]{1,0:T(8,128)(2,1)S(1)} %project_unit.1.unit), channel_id=1, source_target_pairs={{0,24},{4,100},{8,32},{12,108},{16,40},{20,116},{24,48},{28,124},{... | collective-permute-start | bytes 405512 | tf_op jit(solution)/shard_map/ppermute | solution.py:402
  12.4 3.1 %collective-permute-done.2.r1 = bf16[264,256]{1,0:T(8,128)(2,1)S(1)} collective-permute-done((bf16[264,256]{1,0:T(8,128)(2,1)S(1)}, bf16[264,256]{1,0:T(8,128)(2,1)S(1)}, u32[]{:S(2)}, u32[]{:S(2)}) %collective-permute-start.2) | collective-permute-done | bytes 135200 | tf_op jit(solution)/shard_map/ppermute | solution.py:402
  15.6 2.4 %collective-permute-start.6 = (bf16[528,256]{1,0:T(8,128)(2,1)S(1)}, bf16[528,256]{1,0:T(8,128)(2,1)S(1)}, u32[]{:S(2)}, u32[]{:S(2)}) collective-permute-start(bf16[528,256]{1,0:T(8,128)(2,1)S(1)} %get-tuple-element.42), channel_id=1, source_target_pairs={{0,64},{4,20},{8,72},{12,28},{16,80},{20,4},{24,88},{28,12},{32,96... | collective-permute-start | bytes 811016 | tf_op jit(solution)/shard_map/ppermute | solution.py:402
  17.9 0.8 %collective-permute-start.7 = (bf16[528,256]{1,0:T(8,128)(2,1)S(1)}, bf16[528,256]{1,0:T(8,128)(2,1)S(1)}, u32[]{:S(2)}, u32[]{:S(2)}) collective-permute-start(bf16[528,256]{1,0:T(8,128)(2,1)S(1)} %get-tuple-element.43), channel_id=1, source_target_pairs={{0,96},{4,28},{8,104},{12,4},{16,112},{20,12},{24,120},{28,20},{32... | collective-permute-start | bytes 811016 | tf_op jit(solution)/shard_map/ppermute | solution.py:402
  18.8 1.3 %collective-permute-start.8 = (bf16[792,256]{1,0:T(8,128)(2,1)S(1)}, bf16[792,256]{1,0:T(8,128)(2,1)S(1)}, u32[]{:S(2)}, u32[]{:S(2)}) collective-permute-start(bf16[792,256]{1,0:T(8,128)(2,1)S(1)} %bundle_row.1), channel_id=1, source_target_pairs={{0,32},{4,12},{8,40},{12,20},{16,48},{20,28},{24,56},{28,4},{32,64... | collective-permute-start | bytes 1216520 | tf_op jit(solution)/shard_map/ppermute | solution.py:402
  20.1 3.1 %project_q.1.qs = bf16[4,256,128]{2,1,0:T(8,128)(2,1)S(1)} custom-call(bf16[128,4096]{1,0:T(8,128)(2,1)S(1)} %get-tuple-element.31.tok, bf16[128,4096]{1,0:T(8,128)(2,1)S(1)} %collective-permute-done.came, bf16[4096,1024]{1,0:T(8,128)(2,1)} %wq.1, f32[256,128]{1,0:T(8,128)S(1)} %get-tuple-element.35.table), custom_call_target="tpu_custom_call" | custom-call | flops 1073741824 | bytes 6291456 | tf_op jit(solution)/shard_map/project_q/pallas_call | solution.py:187
  23.2 2.1 %attend_near.1 = (f32[4,256,128]{2,1,0:T(8,128)S(1)}, f32[4,256,128]{2,1,0:T(8,128)S(1)}, f32[4,256,128]{2,1,0:T(8,128)S(1)}) custom-call(bf16[4,256,128]{2,1,0:T(8,128)(2,1)S(1)} %project_q.1.qs, bf16[264,256]{1,0:T(8,128)(2,1)S(1)} %project_unit.1.unit, bf16[264,256]{1,0:T(8,128)(2,1)S(1)} %collective-permute-done.2.r1, ...), custom_call_target="tpu_custom_call" | custom-call | flops 536870912 | bytes 1048576 | tf_op jit(solution)/shard_map/attend_near/pallas_call | solution.py:300
  25.3 1.0 %collective-permute-done.7.far_c = bf16[528,256]{1,0:T(8,128)(2,1)S(1)} collective-permute-done((bf16[528,256]{1,0:T(8,128)(2,1)S(1)}, bf16[528,256]{1,0:T(8,128)(2,1)S(1)}, u32[]{:S(2)}, u32[]{:S(2)}) %collective-permute-start.7) | collective-permute-done | bytes 270368 | tf_op jit(solution)/shard_map/ppermute | solution.py:402
  26.3 2.2 %attend_middle.1 = (f32[4,256,128]{2,1,0:T(8,128)S(1)}, f32[4,256,128]{2,1,0:T(8,128)S(1)}, f32[4,256,128]{2,1,0:T(8,128)S(1)}) custom-call(bf16[4,256,128]{2,1,0:T(8,128)(2,1)S(1)} %project_q.1.qs, f32[4,256,128]{2,1,0:T(8,128)S(1)} %get-tuple-element.39.m_in, f32[4,256,128]{2,1,0:T(8,128)S(1)} %get-tuple-element.40.l_in, ...), custom_call_target="tpu_custom_call" | custom-call | flops 4294967296 | bytes 1048576 | tf_op jit(solution)/shard_map/attend_middle/pallas_call | solution.py:319
  28.5 1.0 %attend_last.3 = bf16[128,512]{1,0:T(8,128)(2,1)S(1)} custom-call(bf16[4,256,128]{2,1,0:T(8,128)(2,1)S(1)} %project_q.1.qs, f32[4,256,128]{2,1,0:T(8,128)S(1)} %get-tuple-element.44.m_in, f32[4,256,128]{2,1,0:T(8,128)S(1)} %get-tuple-element.45.l_in, f32[4,256,128]{2,1,0:T(8,128)S(1)} %get-tuple-element.46.acc_in, bf16[264,256]{1,0:T(8,128)(2,1)S(1)} %project_unit.1.unit, ...), custom_call_target="tpu_custom_call" | custom-call | flops 201326592 | bytes 1048576 | tf_op jit(solution)/shard_map/attend_last/pallas_call | solution.py:340
  29.7 1.0 %attend_last.2.xm = bf16[128,512]{1,0:T(8,128)(2,1)S(1)} custom-call(bf16[4,256,128]{2,1,0:T(8,128)(2,1)S(1)} %project_q.1.qs, f32[4,256,128]{2,1,0:T(8,128)S(1)} %get-tuple-element.44.m_in, f32[4,256,128]{2,1,0:T(8,128)S(1)} %get-tuple-element.45.l_in, f32[4,256,128]{2,1,0:T(8,128)S(1)} %get-tuple-element.46.acc_in, bf16[264,256]{1,0:T(8,128)(2,1)S(1)} %project_unit.1.unit, ...), custom_call_target="tpu_custom_call" | custom-call | flops 201326592 | bytes 1048576 | tf_op jit(solution)/shard_map/attend_last/pallas_call | solution.py:340
  31.3 2.2 %collective-permute-start.10 = (bf16[128,512]{1,0:T(8,128)(2,1)S(1)}, bf16[128,512]{1,0:T(8,128)(2,1)S(1)}, u32[]{:S(2)}, u32[]{:S(2)}) collective-permute-start(bf16[128,512]{1,0:T(8,128)(2,1)S(1)} %get-tuple-element.51), channel_id=1, source_target_pairs={{0,1},{1,2},{2,3},{3,0},{4,5},{5,6},{6,7},{7,4},{8,9},{9,10},{10,1... | collective-permute-start | bytes 393224 | tf_op jit(solution)/shard_map/ppermute | solution.py:434
  33.5 2.2 %collective-permute-start.11 = (bf16[128,512]{1,0:T(8,128)(2,1)S(1)}, bf16[128,512]{1,0:T(8,128)(2,1)S(1)}, u32[]{:S(2)}, u32[]{:S(2)}) collective-permute-start(bf16[128,512]{1,0:T(8,128)(2,1)S(1)} %get-tuple-element.52), channel_id=1, source_target_pairs={{0,3},{1,0},{2,1},{3,2},{4,7},{5,4},{6,5},{7,6},{8,11},{9,8},{10,9... | collective-permute-start | bytes 393224 | tf_op jit(solution)/shard_map/ppermute | solution.py:434
  36.3 3.2 %collective-permute-start.14 = (bf16[128,512]{1,0:T(8,128)(2,1)S(1)}, bf16[128,512]{1,0:T(8,128)(2,1)S(1)}, u32[]{:S(2)}, u32[]{:S(2)}) collective-permute-start(bf16[128,512]{1,0:T(8,128)(2,1)S(1)} %get-tuple-element.55), channel_id=1, source_target_pairs={{0,3},{1,0},{2,1},{3,2},{4,7},{5,4},{6,5},{7,6},{8,11},{9,8},{10,9... | collective-permute-start | bytes 393224 | tf_op jit(solution)/shard_map/ppermute | solution.py:434
  39.5 0.7 %project_out.3 = (f32[128,512]{1,0:T(8,128)S(1)}, f32[128,512]{1,0:T(8,128)S(1)}, f32[128,512]{1,0:T(8,128)S(1)}, f32[128,512]{1,0:T(8,128)S(1)}) custom-call(bf16[128,512]{1,0:T(8,128)(2,1)S(1)} %attend_last.2.xm, bf16[128,512]{1,0:T(8,128)(2,1)S(1)} %collective-permute-done.9.xr, bf16[1024,4096]{1,0:T(8,128)(2,1)S(1)} %bitcast.2), custom_call_target="tpu_custom_call" | custom-call | flops 536870912 | bytes 4194304 | tf_op jit(solution)/shard_map/project_out/pallas_call | solution.py:363
  40.3 1.4 %collective-permute-start.12 = (bf16[128,512]{1,0:T(8,128)(2,1)S(1)}, bf16[128,512]{1,0:T(8,128)(2,1)S(1)}, u32[]{:S(2)}, u32[]{:S(2)}) collective-permute-start(bf16[128,512]{1,0:T(8,128)(2,1)S(1)} %get-tuple-element.53), channel_id=1, source_target_pairs={{0,1},{1,2},{2,3},{3,0},{4,5},{5,6},{6,7},{7,4},{8,9},{9,10},{10,1... | collective-permute-start | bytes 393224 | tf_op jit(solution)/shard_map/ppermute | solution.py:434
  41.7 1.9 %collective-permute-start.15 = (bf16[128,512]{1,0:T(8,128)(2,1)S(1)}, bf16[128,512]{1,0:T(8,128)(2,1)S(1)}, u32[]{:S(2)}, u32[]{:S(2)}) collective-permute-start(bf16[128,512]{1,0:T(8,128)(2,1)S(1)} %get-tuple-element.56), channel_id=1, source_target_pairs={{0,3},{1,0},{2,1},{3,2},{4,7},{5,4},{6,5},{7,6},{8,11},{9,8},{10,9... | collective-permute-start | bytes 393224 | tf_op jit(solution)/shard_map/ppermute | solution.py:434
  43.6 2.9 %collective-permute-done.12.left_a = bf16[128,512]{1,0:T(8,128)(2,1)S(1)} collective-permute-done((bf16[128,512]{1,0:T(8,128)(2,1)S(1)}, bf16[128,512]{1,0:T(8,128)(2,1)S(1)}, u32[]{:S(2)}, u32[]{:S(2)}) %collective-permute-start.12) | collective-permute-done | bytes 131104 | tf_op jit(solution)/shard_map/ppermute | solution.py:434
  46.7 0.8 %add_total.1 = bf16[128,1024]{1,0:T(8,128)(2,1)} custom-call(f32[128,512]{1,0:T(8,128)S(1)} %get-tuple-element.47.own_a, f32[128,512]{1,0:T(8,128)S(1)} %get-tuple-element.48.own_b, bf16[128,512]{1,0:T(8,128)(2,1)S(1)} %collective-permute-done.12.left_a, bf16[128,512]{1,0:T(8,128)(2,1)S(1)} %collective-permute-done.13.left_b, ...), custom_call_target="tpu_custom_call" | custom-call | bytes 1048576 | tf_op jit(solution)/shard_map/add_total/pallas_call | solution.py:389
  (27 shorter events, 2.3 us)
Async XLA Ops:
  0.0 2.9 %collective-permute-start = (bf16[128,4096]{1,0:T(8,128)(2,1)}, bf16[128,4096]{1,0:T(8,128)(2,1)S(1)}, u32[]{:S(2)}, u32[]{:S(2)}) collective-permute-start(bf16[128,4096]{1,0:T(8,128)(2,1)} %tok.1), channel_id=1, source_target_pairs={{0,4},{4,0},{8,12},{12,8},{16,20},{20,16},{24,28},{28,24},{32,36},... | collective-permute-start | bytes 3145736 | tf_op jit(solution)/shard_map/ppermute | solution.py:398
  0.0 2.9 %collective-permute-start.1 = (s32[1,128]{1,0:T(1,128)}, s32[1,128]{1,0:T(1,128)S(1)}, u32[]{:S(2)}, u32[]{:S(2)}) collective-permute-start(s32[1,128]{1,0:T(1,128)} %bitcast.3), channel_id=1, source_target_pairs={{0,4},{4,0},{8,12},{12,8},{16,20},{20,16},{24,28},{28,24},{32,36},... | collective-permute-start | bytes 1544 | tf_op jit(solution)/shard_map/ppermute | solution.py:398
  3.4 9.0 %collective-permute-start.3 = (bf16[264,256]{1,0:T(8,128)(2,1)S(1)}, bf16[264,256]{1,0:T(8,128)(2,1)S(1)}, u32[]{:S(2)}, u32[]{:S(2)}) collective-permute-start(bf16[264,256]{1,0:T(8,128)(2,1)S(1)} %project_unit.1.unit), channel_id=1, source_target_pairs={{0,16},{4,68},{8,24},{12,76},{16,32},{20,84},{24,40},{28,92},{32,4... | collective-permute-start | bytes 405512 | tf_op jit(solution)/shard_map/ppermute | solution.py:402
  6.6 8.9 %collective-permute-start.2 = (bf16[264,256]{1,0:T(8,128)(2,1)S(1)}, bf16[264,256]{1,0:T(8,128)(2,1)S(1)}, u32[]{:S(2)}, u32[]{:S(2)}) collective-permute-start(bf16[264,256]{1,0:T(8,128)(2,1)S(1)} %project_unit.1.unit), channel_id=1, source_target_pairs={{0,8},{4,36},{8,16},{12,44},{16,24},{20,52},{24,32},{28,60},{32,40... | collective-permute-start | bytes 405512 | tf_op jit(solution)/shard_map/ppermute | solution.py:402
  7.2 11.5 %collective-permute-start.5 = (bf16[264,256]{1,0:T(8,128)(2,1)S(1)}, bf16[264,256]{1,0:T(8,128)(2,1)S(1)}, u32[]{:S(2)}, u32[]{:S(2)}) collective-permute-start(bf16[264,256]{1,0:T(8,128)(2,1)S(1)} %project_unit.1.unit), channel_id=1, source_target_pairs={{0,32},{4,28},{8,40},{12,4},{16,48},{20,12},{24,56},{28,20},{32,64... | collective-permute-start | bytes 405512 | tf_op jit(solution)/shard_map/ppermute | solution.py:402
  8.8 9.9 %collective-permute-start.4 = (bf16[264,256]{1,0:T(8,128)(2,1)S(1)}, bf16[264,256]{1,0:T(8,128)(2,1)S(1)}, u32[]{:S(2)}, u32[]{:S(2)}) collective-permute-start(bf16[264,256]{1,0:T(8,128)(2,1)S(1)} %project_unit.1.unit), channel_id=1, source_target_pairs={{0,24},{4,100},{8,32},{12,108},{16,40},{20,116},{24,48},{28,124},{... | collective-permute-start | bytes 405512 | tf_op jit(solution)/shard_map/ppermute | solution.py:402
  15.6 9.7 %collective-permute-start.6 = (bf16[528,256]{1,0:T(8,128)(2,1)S(1)}, bf16[528,256]{1,0:T(8,128)(2,1)S(1)}, u32[]{:S(2)}, u32[]{:S(2)}) collective-permute-start(bf16[528,256]{1,0:T(8,128)(2,1)S(1)} %get-tuple-element.42), channel_id=1, source_target_pairs={{0,64},{4,20},{8,72},{12,28},{16,80},{20,4},{24,88},{28,12},{32,96... | collective-permute-start | bytes 811016 | tf_op jit(solution)/shard_map/ppermute | solution.py:402
  17.9 8.3 %collective-permute-start.7 = (bf16[528,256]{1,0:T(8,128)(2,1)S(1)}, bf16[528,256]{1,0:T(8,128)(2,1)S(1)}, u32[]{:S(2)}, u32[]{:S(2)}) collective-permute-start(bf16[528,256]{1,0:T(8,128)(2,1)S(1)} %get-tuple-element.43), channel_id=1, source_target_pairs={{0,96},{4,28},{8,104},{12,4},{16,112},{20,12},{24,120},{28,20},{32... | collective-permute-start | bytes 811016 | tf_op jit(solution)/shard_map/ppermute | solution.py:402
  18.8 9.7 %collective-permute-start.8 = (bf16[792,256]{1,0:T(8,128)(2,1)S(1)}, bf16[792,256]{1,0:T(8,128)(2,1)S(1)}, u32[]{:S(2)}, u32[]{:S(2)}) collective-permute-start(bf16[792,256]{1,0:T(8,128)(2,1)S(1)} %bundle_row.1), channel_id=1, source_target_pairs={{0,32},{4,12},{8,40},{12,20},{16,48},{20,28},{24,56},{28,4},{32,64... | collective-permute-start | bytes 1216520 | tf_op jit(solution)/shard_map/ppermute | solution.py:402
  23.2 7.7 %slice-start = ((s8[8388608]{0:T(1024)(128)(4,1)}), s8[4194304]{0:T(1024)(128)(4,1)S(1)}, s32[]{:S(2)}) async-start(s8[8388608]{0:T(1024)(128)(4,1)} %bitcast.1), calls=%async_computation | async-start | bytes 8388608
  26.3 4.6 %slice-start.1 = ((s8[8388608]{0:T(1024)(128)(4,1)}), s8[4194304]{0:T(1024)(128)(4,1)S(1)}, s32[]{:S(2)}) async-start(s8[8388608]{0:T(1024)(128)(4,1)} %bitcast.1), calls=%async_computation.1 | async-start | bytes 8388608
  29.4 1.4 %collective-permute-start.9 = (bf16[128,512]{1,0:T(8,128)(2,1)S(1)}, bf16[128,512]{1,0:T(8,128)(2,1)S(1)}, u32[]{:S(2)}, u32[]{:S(2)}) collective-permute-start(bf16[128,512]{1,0:T(8,128)(2,1)S(1)} %attend_last.3), channel_id=1, source_target_pairs={{0,4},{4,0},{8,12},{12,8},{16,20},{20,16},{24,28},{28,24},{32,36},... | collective-permute-start | bytes 393224 | tf_op jit(solution)/shard_map/ppermute | solution.py:398
  31.3 8.9 %collective-permute-start.10 = (bf16[128,512]{1,0:T(8,128)(2,1)S(1)}, bf16[128,512]{1,0:T(8,128)(2,1)S(1)}, u32[]{:S(2)}, u32[]{:S(2)}) collective-permute-start(bf16[128,512]{1,0:T(8,128)(2,1)S(1)} %get-tuple-element.51), channel_id=1, source_target_pairs={{0,1},{1,2},{2,3},{3,0},{4,5},{5,6},{6,7},{7,4},{8,9},{9,10},{10,1... | collective-permute-start | bytes 393224 | tf_op jit(solution)/shard_map/ppermute | solution.py:434
  33.5 6.7 %collective-permute-start.11 = (bf16[128,512]{1,0:T(8,128)(2,1)S(1)}, bf16[128,512]{1,0:T(8,128)(2,1)S(1)}, u32[]{:S(2)}, u32[]{:S(2)}) collective-permute-start(bf16[128,512]{1,0:T(8,128)(2,1)S(1)} %get-tuple-element.52), channel_id=1, source_target_pairs={{0,3},{1,0},{2,1},{3,2},{4,7},{5,4},{6,5},{7,6},{8,11},{9,8},{10,9... | collective-permute-start | bytes 393224 | tf_op jit(solution)/shard_map/ppermute | solution.py:434
  36.2 7.4 %collective-permute-start.13 = (bf16[128,512]{1,0:T(8,128)(2,1)S(1)}, bf16[128,512]{1,0:T(8,128)(2,1)S(1)}, u32[]{:S(2)}, u32[]{:S(2)}) collective-permute-start(bf16[128,512]{1,0:T(8,128)(2,1)S(1)} %get-tuple-element.54), channel_id=1, source_target_pairs={{0,1},{1,2},{2,3},{3,0},{4,5},{5,6},{6,7},{7,4},{8,9},{9,10},{10,1... | collective-permute-start | bytes 393224 | tf_op jit(solution)/shard_map/ppermute | solution.py:434
  36.3 7.3 %collective-permute-start.14 = (bf16[128,512]{1,0:T(8,128)(2,1)S(1)}, bf16[128,512]{1,0:T(8,128)(2,1)S(1)}, u32[]{:S(2)}, u32[]{:S(2)}) collective-permute-start(bf16[128,512]{1,0:T(8,128)(2,1)S(1)} %get-tuple-element.55), channel_id=1, source_target_pairs={{0,3},{1,0},{2,1},{3,2},{4,7},{5,4},{6,5},{7,6},{8,11},{9,8},{10,9... | collective-permute-start | bytes 393224 | tf_op jit(solution)/shard_map/ppermute | solution.py:434
  40.3 6.2 %collective-permute-start.12 = (bf16[128,512]{1,0:T(8,128)(2,1)S(1)}, bf16[128,512]{1,0:T(8,128)(2,1)S(1)}, u32[]{:S(2)}, u32[]{:S(2)}) collective-permute-start(bf16[128,512]{1,0:T(8,128)(2,1)S(1)} %get-tuple-element.53), channel_id=1, source_target_pairs={{0,1},{1,2},{2,3},{3,0},{4,5},{5,6},{6,7},{7,4},{8,9},{9,10},{10,1... | collective-permute-start | bytes 393224 | tf_op jit(solution)/shard_map/ppermute | solution.py:434
  41.7 5.0 %collective-permute-start.15 = (bf16[128,512]{1,0:T(8,128)(2,1)S(1)}, bf16[128,512]{1,0:T(8,128)(2,1)S(1)}, u32[]{:S(2)}, u32[]{:S(2)}) collective-permute-start(bf16[128,512]{1,0:T(8,128)(2,1)S(1)} %get-tuple-element.56), channel_id=1, source_target_pairs={{0,3},{1,0},{2,1},{3,2},{4,7},{5,4},{6,5},{7,6},{8,11},{9,8},{10,9... | collective-permute-start | bytes 393224 | tf_op jit(solution)/shard_map/ppermute | solution.py:434

commit v7 on v6

--- a/solution.py
+++ b/solution.py
@@ -299,7 +299,7 @@
     state = like(heads, CHIP, HD, dtype=F32)
     return call(
         near_body, "attend_near", (state, state, state), [VMEM] * 5, (VMEM,) * 3, limit=8,
-        flops=4 * heads * CHIP * 4 * CHIP * HD, exps=heads * CHIP * 4 * CHIP,
+        flops=16 * heads * CHIP * 4 * CHIP * HD, exps=heads * CHIP * 4 * CHIP,
     )(qs, unit, r1, r2, r3)
 
 
@@ -419,12 +419,12 @@
     r2 = along(unit, ahead(2), ahead(8))
     r3 = along(unit, ahead(3), ahead(12))
     r4 = along(unit, ahead(4), in_row(3))
-    r1, r2, came = lax.optimization_barrier((r1, r2, came))
+    qs = project_q(tokens, came, w_query, table)
+    r1, r2, qs = lax.optimization_barrier((r1, r2, qs))
     out_b, out_c = bundle_pairs(unit, r1, r2)
     far_b = along(out_b, ahead(8), in_row(2))
     far_c = along(out_c, ahead(12), in_row(3))
     far_a = along(bundle_row(unit, r1, r2, r3, r4), ahead(4), in_row(1))
-    qs = project_q(tokens, came, w_query, table)
     state = attend_near(qs, unit, r1, r2, r3)
     state = attend_middle(qs, *state, unit, r4, far_b, far_c)
     xr = swap(attend_last(1, qs, *state, unit, far_a))

time: 47.6 us -> 48 us (level)
  waiting for transfers between devices: 7.32 us -> 7.97 us
    ppermute x7, waiting for transfers between devices: 4.07 us -> 4.56 us  [along(): return lax.ppermute(value, 'ctx', moves)]
  transfers between devices with their start and end apart: 16 -> 16, of which waited for: 5 -> 6; matrix products, arithmetic and copies ran while one was open for 0% -> 0% of each run, Pallas kernels for 25% -> 25%
where the time goes in v7:
time: 48 us; the launch traced here: 47.9 us
  starting transfers between devices  25 us (52%)
  Pallas kernels  14.7 us (31%)
  waiting for transfers between devices  7.97 us (17%)
    ppermute x7, starting transfers between devices, along(): return lax.ppermute(value, 'ctx', moves)  13.4 us
    ppermute x6, starting transfers between devices, shift(): lax.ppermute(value, 'head', [(g, (g + step) % groups) for g in range(grou...  11 us
    ppermute x7, waiting for transfers between devices, along(): return lax.ppermute(value, 'ctx', moves)  4.56 us
    pallas_call x1, Pallas kernels, project_q(): call(q_body, 'project_q', like(width // 2 // HD, CHIP, HD), [VMEM, VMEM,...  3.09 us
    ppermute x6, waiting for transfers between devices, shift(): lax.ppermute(value, 'head', [(g, (g + step) % groups) for g in range(grou...  3.08 us
    pallas_call x1, Pallas kernels, project_own(): call(own_body, 'project_own', (like(ROWS, 2 * HD), like(ROWS, depth), lik...  2.35 us
    pallas_call x1, Pallas kernels, attend_middle(): call(middle_body, 'attend_middle', (state,) * 3, [VMEM] * 8, (VMEM,) * 3,...  2.17 us
    pallas_call x1, Pallas kernels, attend_near(): call(near_body, 'attend_near', (state, state, state), [VMEM] * 5, (VMEM,)...  2.07 us
  transfers between devices with their start and end apart: 16, of which 6 were waited for; matrix products, arithmetic and copies ran while one was open for 0% of the time, Pallas kernels for 25%

profile of v7, /device:TPU:0, one launch (start us, length us, event | category | flops | bytes accessed | tf_op | source)
XLA Modules:
  0.0 47.9 jit_solution(9423914910163277676)
XLA Ops:
  0.0 0.5 %collective-permute-start.1 = (s32[1,128]{1,0:T(1,128)}, s32[1,128]{1,0:T(1,128)S(1)}, u32[]{:S(2)}, u32[]{:S(2)}) collective-permute-start(s32[1,128]{1,0:T(1,128)} %bitcast.3), channel_id=1, source_target_pairs={{0,4},{4,0},{8,12},{12,8},{16,20},{20,16},{24,28},{28,24},{32,36},... | collective-permute-start | bytes 1544 | tf_op jit(solution)/shard_map/ppermute | solution.py:398
  0.5 2.3 %project_own.1 = (bf16[128,256]{1,0:T(8,128)(2,1)S(1)}, bf16[128,4096]{1,0:T(8,128)(2,1)S(1)}, bf16[4096,256]{1,0:T(8,128)(2,1)S(1)}, s32[1,128]{1,0:T(1,128)S(1)}, f32[256,128]{1,0:T(8,128)S(1)}) custom-call(bf16[128,4096]{1,0:T(8,128)(2,1)} %tok.1, bf16[4096,256]{1,0:T(8,128)(2,1)} %wk.1, bf16[4096,256]{1,0:T(8,128)(2,1)} %wv.1, s32[1,128]{1,0:T(1,128)} %bitcast.4, ...), custom_call_target="tpu_custom_call" | custom-call | flops 268435456 | bytes 3145728 | tf_op jit(solution)/shard_map/project_own/pallas_call | solution.py:124
  2.9 0.5 %project_unit.1.unit = bf16[264,256]{1,0:T(8,128)(2,1)S(1)} custom-call(bf16[128,256]{1,0:T(8,128)(2,1)S(1)} %get-tuple-element.31.half, bf16[128,4096]{1,0:T(8,128)(2,1)S(1)} %collective-permute-done.came, bf16[4096,256]{1,0:T(8,128)(2,1)S(1)} %get-tuple-element.32.w, s32[1,128]{1,0:T(1,128)S(1)} %get-tuple-element.33.docs, ...), custom_call_target="tpu_custom_call" | custom-call | flops 268435456 | bytes 1048576 | tf_op jit(solution)/shard_map/project_unit/pallas_call | solution.py:153
  3.4 3.2 %collective-permute-start.3 = (bf16[264,256]{1,0:T(8,128)(2,1)S(1)}, bf16[264,256]{1,0:T(8,128)(2,1)S(1)}, u32[]{:S(2)}, u32[]{:S(2)}) collective-permute-start(bf16[264,256]{1,0:T(8,128)(2,1)S(1)} %project_unit.1.unit), channel_id=1, source_target_pairs={{0,16},{4,68},{8,24},{12,76},{16,32},{20,84},{24,40},{28,92},{32,4... | collective-permute-start | bytes 405512 | tf_op jit(solution)/shard_map/ppermute | solution.py:402
  6.6 0.6 %collective-permute-start.2 = (bf16[264,256]{1,0:T(8,128)(2,1)S(1)}, bf16[264,256]{1,0:T(8,128)(2,1)S(1)}, u32[]{:S(2)}, u32[]{:S(2)}) collective-permute-start(bf16[264,256]{1,0:T(8,128)(2,1)S(1)} %project_unit.1.unit), channel_id=1, source_target_pairs={{0,8},{4,36},{8,16},{12,44},{16,24},{20,52},{24,32},{28,60},{32,40... | collective-permute-start | bytes 405512 | tf_op jit(solution)/shard_map/ppermute | solution.py:402
  7.2 1.6 %collective-permute-start.5 = (bf16[264,256]{1,0:T(8,128)(2,1)S(1)}, bf16[264,256]{1,0:T(8,128)(2,1)S(1)}, u32[]{:S(2)}, u32[]{:S(2)}) collective-permute-start(bf16[264,256]{1,0:T(8,128)(2,1)S(1)} %project_unit.1.unit), channel_id=1, source_target_pairs={{0,32},{4,28},{8,40},{12,4},{16,48},{20,12},{24,56},{28,20},{32,64... | collective-permute-start | bytes 405512 | tf_op jit(solution)/shard_map/ppermute | solution.py:402
  8.8 3.7 %collective-permute-start.4 = (bf16[264,256]{1,0:T(8,128)(2,1)S(1)}, bf16[264,256]{1,0:T(8,128)(2,1)S(1)}, u32[]{:S(2)}, u32[]{:S(2)}) collective-permute-start(bf16[264,256]{1,0:T(8,128)(2,1)S(1)} %project_unit.1.unit), channel_id=1, source_target_pairs={{0,24},{4,100},{8,32},{12,108},{16,40},{20,116},{24,48},{28,124},{... | collective-permute-start | bytes 405512 | tf_op jit(solution)/shard_map/ppermute | solution.py:402
  12.4 3.1 %project_q.1.qs = bf16[4,256,128]{2,1,0:T(8,128)(2,1)S(1)} custom-call(bf16[128,4096]{1,0:T(8,128)(2,1)S(1)} %get-tuple-element.35.tok, bf16[128,4096]{1,0:T(8,128)(2,1)S(1)} %collective-permute-done.came, bf16[4096,1024]{1,0:T(8,128)(2,1)} %wq.1, f32[256,128]{1,0:T(8,128)S(1)} %get-tuple-element.34.table), custom_call_target="tpu_custom_call" | custom-call | flops 1073741824 | bytes 6291456 | tf_op jit(solution)/shard_map/project_q/pallas_call | solution.py:187
  15.6 2.3 %collective-permute-start.6 = (bf16[528,256]{1,0:T(8,128)(2,1)S(1)}, bf16[528,256]{1,0:T(8,128)(2,1)S(1)}, u32[]{:S(2)}, u32[]{:S(2)}) collective-permute-start(bf16[528,256]{1,0:T(8,128)(2,1)S(1)} %get-tuple-element.42), channel_id=1, source_target_pairs={{0,64},{4,20},{8,72},{12,28},{16,80},{20,4},{24,88},{28,12},{32,96... | collective-permute-start | bytes 811016 | tf_op jit(solution)/shard_map/ppermute | solution.py:402
  17.9 1.7 %collective-permute-start.7 = (bf16[528,256]{1,0:T(8,128)(2,1)S(1)}, bf16[528,256]{1,0:T(8,128)(2,1)S(1)}, u32[]{:S(2)}, u32[]{:S(2)}) collective-permute-start(bf16[528,256]{1,0:T(8,128)(2,1)S(1)} %get-tuple-element.43), channel_id=1, source_target_pairs={{0,96},{4,28},{8,104},{12,4},{16,112},{20,12},{24,120},{28,20},{32... | collective-permute-start | bytes 811016 | tf_op jit(solution)/shard_map/ppermute | solution.py:402
  20.1 2.1 %attend_near.1 = (f32[4,256,128]{2,1,0:T(8,128)S(1)}, f32[4,256,128]{2,1,0:T(8,128)S(1)}, f32[4,256,128]{2,1,0:T(8,128)S(1)}) custom-call(bf16[4,256,128]{2,1,0:T(8,128)(2,1)S(1)} %project_q.1.qs, bf16[264,256]{1,0:T(8,128)(2,1)S(1)} %project_unit.1.unit, bf16[264,256]{1,0:T(8,128)(2,1)S(1)} %collective-permute-done.2.r1, ...), custom_call_target="tpu_custom_call" | custom-call | flops 2147483648 | bytes 1048576 | tf_op jit(solution)/shard_map/attend_near/pallas_call | solution.py:300
  22.2 1.5 %collective-permute-done.6.far_b = bf16[528,256]{1,0:T(8,128)(2,1)S(1)} collective-permute-done((bf16[528,256]{1,0:T(8,128)(2,1)S(1)}, bf16[528,256]{1,0:T(8,128)(2,1)S(1)}, u32[]{:S(2)}, u32[]{:S(2)}) %collective-permute-start.6) | collective-permute-done | bytes 270368 | tf_op jit(solution)/shard_map/ppermute | solution.py:402
  23.6 2.6 %collective-permute-done.7.far_c = bf16[528,256]{1,0:T(8,128)(2,1)S(1)} collective-permute-done((bf16[528,256]{1,0:T(8,128)(2,1)S(1)}, bf16[528,256]{1,0:T(8,128)(2,1)S(1)}, u32[]{:S(2)}, u32[]{:S(2)}) %collective-permute-start.7) | collective-permute-done | bytes 270368 | tf_op jit(solution)/shard_map/ppermute | solution.py:402
  26.2 2.2 %attend_middle.1 = (f32[4,256,128]{2,1,0:T(8,128)S(1)}, f32[4,256,128]{2,1,0:T(8,128)S(1)}, f32[4,256,128]{2,1,0:T(8,128)S(1)}) custom-call(bf16[4,256,128]{2,1,0:T(8,128)(2,1)S(1)} %project_q.1.qs, f32[4,256,128]{2,1,0:T(8,128)S(1)} %get-tuple-element.39.m_in, f32[4,256,128]{2,1,0:T(8,128)S(1)} %get-tuple-element.40.l_in, ...), custom_call_target="tpu_custom_call" | custom-call | flops 4294967296 | bytes 1048576 | tf_op jit(solution)/shard_map/attend_middle/pallas_call | solution.py:319
  28.9 1.0 %attend_last.3 = bf16[128,512]{1,0:T(8,128)(2,1)S(1)} custom-call(bf16[4,256,128]{2,1,0:T(8,128)(2,1)S(1)} %project_q.1.qs, f32[4,256,128]{2,1,0:T(8,128)S(1)} %get-tuple-element.44.m_in, f32[4,256,128]{2,1,0:T(8,128)S(1)} %get-tuple-element.45.l_in, f32[4,256,128]{2,1,0:T(8,128)S(1)} %get-tuple-element.46.acc_in, bf16[264,256]{1,0:T(8,128)(2,1)S(1)} %project_unit.1.unit, ...), custom_call_target="tpu_custom_call" | custom-call | flops 201326592 | bytes 1048576 | tf_op jit(solution)/shard_map/attend_last/pallas_call | solution.py:340
  30.0 1.0 %attend_last.2.xm = bf16[128,512]{1,0:T(8,128)(2,1)S(1)} custom-call(bf16[4,256,128]{2,1,0:T(8,128)(2,1)S(1)} %project_q.1.qs, f32[4,256,128]{2,1,0:T(8,128)S(1)} %get-tuple-element.44.m_in, f32[4,256,128]{2,1,0:T(8,128)S(1)} %get-tuple-element.45.l_in, f32[4,256,128]{2,1,0:T(8,128)S(1)} %get-tuple-element.46.acc_in, bf16[264,256]{1,0:T(8,128)(2,1)S(1)} %project_unit.1.unit, ...), custom_call_target="tpu_custom_call" | custom-call | flops 201326592 | bytes 1048576 | tf_op jit(solution)/shard_map/attend_last/pallas_call | solution.py:340
  31.8 2.2 %collective-permute-start.10 = (bf16[128,512]{1,0:T(8,128)(2,1)S(1)}, bf16[128,512]{1,0:T(8,128)(2,1)S(1)}, u32[]{:S(2)}, u32[]{:S(2)}) collective-permute-start(bf16[128,512]{1,0:T(8,128)(2,1)S(1)} %get-tuple-element.51), channel_id=1, source_target_pairs={{0,1},{1,2},{2,3},{3,0},{4,5},{5,6},{6,7},{7,4},{8,9},{9,10},{10,1... | collective-permute-start | bytes 393224 | tf_op jit(solution)/shard_map/ppermute | solution.py:434
  34.0 2.2 %collective-permute-start.11 = (bf16[128,512]{1,0:T(8,128)(2,1)S(1)}, bf16[128,512]{1,0:T(8,128)(2,1)S(1)}, u32[]{:S(2)}, u32[]{:S(2)}) collective-permute-start(bf16[128,512]{1,0:T(8,128)(2,1)S(1)} %get-tuple-element.52), channel_id=1, source_target_pairs={{0,3},{1,0},{2,1},{3,2},{4,7},{5,4},{6,5},{7,6},{8,11},{9,8},{10,9... | collective-permute-start | bytes 393224 | tf_op jit(solution)/shard_map/ppermute | solution.py:434
  36.7 3.2 %collective-permute-start.14 = (bf16[128,512]{1,0:T(8,128)(2,1)S(1)}, bf16[128,512]{1,0:T(8,128)(2,1)S(1)}, u32[]{:S(2)}, u32[]{:S(2)}) collective-permute-start(bf16[128,512]{1,0:T(8,128)(2,1)S(1)} %get-tuple-element.55), channel_id=1, source_target_pairs={{0,3},{1,0},{2,1},{3,2},{4,7},{5,4},{6,5},{7,6},{8,11},{9,8},{10,9... | collective-permute-start | bytes 393224 | tf_op jit(solution)/shard_map/ppermute | solution.py:434
  39.9 0.7 %project_out.3 = (f32[128,512]{1,0:T(8,128)S(1)}, f32[128,512]{1,0:T(8,128)S(1)}, f32[128,512]{1,0:T(8,128)S(1)}, f32[128,512]{1,0:T(8,128)S(1)}) custom-call(bf16[128,512]{1,0:T(8,128)(2,1)S(1)} %attend_last.2.xm, bf16[128,512]{1,0:T(8,128)(2,1)S(1)} %collective-permute-done.9.xr, bf16[1024,4096]{1,0:T(8,128)(2,1)S(1)} %bitcast.2), custom_call_target="tpu_custom_call" | custom-call | flops 536870912 | bytes 4194304 | tf_op jit(solution)/shard_map/project_out/pallas_call | solution.py:363
  40.7 1.4 %collective-permute-start.12 = (bf16[128,512]{1,0:T(8,128)(2,1)S(1)}, bf16[128,512]{1,0:T(8,128)(2,1)S(1)}, u32[]{:S(2)}, u32[]{:S(2)}) collective-permute-start(bf16[128,512]{1,0:T(8,128)(2,1)S(1)} %get-tuple-element.53), channel_id=1, source_target_pairs={{0,1},{1,2},{2,3},{3,0},{4,5},{5,6},{6,7},{7,4},{8,9},{9,10},{10,1... | collective-permute-start | bytes 393224 | tf_op jit(solution)/shard_map/ppermute | solution.py:434
  42.1 1.9 %collective-permute-start.15 = (bf16[128,512]{1,0:T(8,128)(2,1)S(1)}, bf16[128,512]{1,0:T(8,128)(2,1)S(1)}, u32[]{:S(2)}, u32[]{:S(2)}) collective-permute-start(bf16[128,512]{1,0:T(8,128)(2,1)S(1)} %get-tuple-element.56), channel_id=1, source_target_pairs={{0,3},{1,0},{2,1},{3,2},{4,7},{5,4},{6,5},{7,6},{8,11},{9,8},{10,9... | collective-permute-start | bytes 393224 | tf_op jit(solution)/shard_map/ppermute | solution.py:434
  44.0 2.9 %collective-permute-done.12.left_a = bf16[128,512]{1,0:T(8,128)(2,1)S(1)} collective-permute-done((bf16[128,512]{1,0:T(8,128)(2,1)S(1)}, bf16[128,512]{1,0:T(8,128)(2,1)S(1)}, u32[]{:S(2)}, u32[]{:S(2)}) %collective-permute-start.12) | collective-permute-done | bytes 131104 | tf_op jit(solution)/shard_map/ppermute | solution.py:434
  47.1 0.8 %add_total.1 = bf16[128,1024]{1,0:T(8,128)(2,1)} custom-call(f32[128,512]{1,0:T(8,128)S(1)} %get-tuple-element.47.own_a, f32[128,512]{1,0:T(8,128)S(1)} %get-tuple-element.48.own_b, bf16[128,512]{1,0:T(8,128)(2,1)S(1)} %collective-permute-done.12.left_a, bf16[128,512]{1,0:T(8,128)(2,1)S(1)} %collective-permute-done.13.left_b, ...), custom_call_target="tpu_custom_call" | custom-call | bytes 1048576 | tf_op jit(solution)/shard_map/add_total/pallas_call | solution.py:389
  (27 shorter events, 2.6 us)
Async XLA Ops:
  0.0 2.9 %collective-permute-start = (bf16[128,4096]{1,0:T(8,128)(2,1)}, bf16[128,4096]{1,0:T(8,128)(2,1)S(1)}, u32[]{:S(2)}, u32[]{:S(2)}) collective-permute-start(bf16[128,4096]{1,0:T(8,128)(2,1)} %tok.1), channel_id=1, source_target_pairs={{0,4},{4,0},{8,12},{12,8},{16,20},{20,16},{24,28},{28,24},{32,36},... | collective-permute-start | bytes 3145736 | tf_op jit(solution)/shard_map/ppermute | solution.py:398
  0.0 2.9 %collective-permute-start.1 = (s32[1,128]{1,0:T(1,128)}, s32[1,128]{1,0:T(1,128)S(1)}, u32[]{:S(2)}, u32[]{:S(2)}) collective-permute-start(s32[1,128]{1,0:T(1,128)} %bitcast.3), channel_id=1, source_target_pairs={{0,4},{4,0},{8,12},{12,8},{16,20},{20,16},{24,28},{28,24},{32,36},... | collective-permute-start | bytes 1544 | tf_op jit(solution)/shard_map/ppermute | solution.py:398
  3.4 12.1 %collective-permute-start.3 = (bf16[264,256]{1,0:T(8,128)(2,1)S(1)}, bf16[264,256]{1,0:T(8,128)(2,1)S(1)}, u32[]{:S(2)}, u32[]{:S(2)}) collective-permute-start(bf16[264,256]{1,0:T(8,128)(2,1)S(1)} %project_unit.1.unit), channel_id=1, source_target_pairs={{0,16},{4,68},{8,24},{12,76},{16,32},{20,84},{24,40},{28,92},{32,4... | collective-permute-start | bytes 405512 | tf_op jit(solution)/shard_map/ppermute | solution.py:402
  6.6 8.9 %collective-permute-start.2 = (bf16[264,256]{1,0:T(8,128)(2,1)S(1)}, bf16[264,256]{1,0:T(8,128)(2,1)S(1)}, u32[]{:S(2)}, u32[]{:S(2)}) collective-permute-start(bf16[264,256]{1,0:T(8,128)(2,1)S(1)} %project_unit.1.unit), channel_id=1, source_target_pairs={{0,8},{4,36},{8,16},{12,44},{16,24},{20,52},{24,32},{28,60},{32,40... | collective-permute-start | bytes 405512 | tf_op jit(solution)/shard_map/ppermute | solution.py:402
  7.2 12.5 %collective-permute-start.5 = (bf16[264,256]{1,0:T(8,128)(2,1)S(1)}, bf16[264,256]{1,0:T(8,128)(2,1)S(1)}, u32[]{:S(2)}, u32[]{:S(2)}) collective-permute-start(bf16[264,256]{1,0:T(8,128)(2,1)S(1)} %project_unit.1.unit), channel_id=1, source_target_pairs={{0,32},{4,28},{8,40},{12,4},{16,48},{20,12},{24,56},{28,20},{32,64... | collective-permute-start | bytes 405512 | tf_op jit(solution)/shard_map/ppermute | solution.py:402
  8.8 10.9 %collective-permute-start.4 = (bf16[264,256]{1,0:T(8,128)(2,1)S(1)}, bf16[264,256]{1,0:T(8,128)(2,1)S(1)}, u32[]{:S(2)}, u32[]{:S(2)}) collective-permute-start(bf16[264,256]{1,0:T(8,128)(2,1)S(1)} %project_unit.1.unit), channel_id=1, source_target_pairs={{0,24},{4,100},{8,32},{12,108},{16,40},{20,116},{24,48},{28,124},{... | collective-permute-start | bytes 405512 | tf_op jit(solution)/shard_map/ppermute | solution.py:402
  15.6 8.0 %collective-permute-start.6 = (bf16[528,256]{1,0:T(8,128)(2,1)S(1)}, bf16[528,256]{1,0:T(8,128)(2,1)S(1)}, u32[]{:S(2)}, u32[]{:S(2)}) collective-permute-start(bf16[528,256]{1,0:T(8,128)(2,1)S(1)} %get-tuple-element.42), channel_id=1, source_target_pairs={{0,64},{4,20},{8,72},{12,28},{16,80},{20,4},{24,88},{28,12},{32,96... | collective-permute-start | bytes 811016 | tf_op jit(solution)/shard_map/ppermute | solution.py:402
  17.9 8.3 %collective-permute-start.7 = (bf16[528,256]{1,0:T(8,128)(2,1)S(1)}, bf16[528,256]{1,0:T(8,128)(2,1)S(1)}, u32[]{:S(2)}, u32[]{:S(2)}) collective-permute-start(bf16[528,256]{1,0:T(8,128)(2,1)S(1)} %get-tuple-element.43), channel_id=1, source_target_pairs={{0,96},{4,28},{8,104},{12,4},{16,112},{20,12},{24,120},{28,20},{32... | collective-permute-start | bytes 811016 | tf_op jit(solution)/shard_map/ppermute | solution.py:402
  19.7 9.2 %collective-permute-start.8 = (bf16[792,256]{1,0:T(8,128)(2,1)S(1)}, bf16[792,256]{1,0:T(8,128)(2,1)S(1)}, u32[]{:S(2)}, u32[]{:S(2)}) collective-permute-start(bf16[792,256]{1,0:T(8,128)(2,1)S(1)} %bundle_row.1), channel_id=1, source_target_pairs={{0,32},{4,12},{8,40},{12,20},{16,48},{20,28},{24,56},{28,4},{32,64... | collective-permute-start | bytes 1216520 | tf_op jit(solution)/shard_map/ppermute | solution.py:402
  20.1 11.2 %slice-start = ((s8[8388608]{0:T(1024)(128)(4,1)}), s8[4194304]{0:T(1024)(128)(4,1)S(1)}, s32[]{:S(2)}) async-start(s8[8388608]{0:T(1024)(128)(4,1)} %bitcast.1), calls=%async_computation | async-start | bytes 8388608
  26.2 5.1 %slice-start.1 = ((s8[8388608]{0:T(1024)(128)(4,1)}), s8[4194304]{0:T(1024)(128)(4,1)S(1)}, s32[]{:S(2)}) async-start(s8[8388608]{0:T(1024)(128)(4,1)} %bitcast.1), calls=%async_computation.1 | async-start | bytes 8388608
  29.9 1.4 %collective-permute-start.9 = (bf16[128,512]{1,0:T(8,128)(2,1)S(1)}, bf16[128,512]{1,0:T(8,128)(2,1)S(1)}, u32[]{:S(2)}, u32[]{:S(2)}) collective-permute-start(bf16[128,512]{1,0:T(8,128)(2,1)S(1)} %attend_last.3), channel_id=1, source_target_pairs={{0,4},{4,0},{8,12},{12,8},{16,20},{20,16},{24,28},{28,24},{32,36},... | collective-permute-start | bytes 393224 | tf_op jit(solution)/shard_map/ppermute | solution.py:398
  31.8 8.9 %collective-permute-start.10 = (bf16[128,512]{1,0:T(8,128)(2,1)S(1)}, bf16[128,512]{1,0:T(8,128)(2,1)S(1)}, u32[]{:S(2)}, u32[]{:S(2)}) collective-permute-start(bf16[128,512]{1,0:T(8,128)(2,1)S(1)} %get-tuple-element.51), channel_id=1, source_target_pairs={{0,1},{1,2},{2,3},{3,0},{4,5},{5,6},{6,7},{7,4},{8,9},{9,10},{10,1... | collective-permute-start | bytes 393224 | tf_op jit(solution)/shard_map/ppermute | solution.py:434
  34.0 6.7 %collective-permute-start.11 = (bf16[128,512]{1,0:T(8,128)(2,1)S(1)}, bf16[128,512]{1,0:T(8,128)(2,1)S(1)}, u32[]{:S(2)}, u32[]{:S(2)}) collective-permute-start(bf16[128,512]{1,0:T(8,128)(2,1)S(1)} %get-tuple-element.52), channel_id=1, source_target_pairs={{0,3},{1,0},{2,1},{3,2},{4,7},{5,4},{6,5},{7,6},{8,11},{9,8},{10,9... | collective-permute-start | bytes 393224 | tf_op jit(solution)/shard_map/ppermute | solution.py:434
  36.6 7.4 %collective-permute-start.13 = (bf16[128,512]{1,0:T(8,128)(2,1)S(1)}, bf16[128,512]{1,0:T(8,128)(2,1)S(1)}, u32[]{:S(2)}, u32[]{:S(2)}) collective-permute-start(bf16[128,512]{1,0:T(8,128)(2,1)S(1)} %get-tuple-element.54), channel_id=1, source_target_pairs={{0,1},{1,2},{2,3},{3,0},{4,5},{5,6},{6,7},{7,4},{8,9},{9,10},{10,1... | collective-permute-start | bytes 393224 | tf_op jit(solution)/shard_map/ppermute | solution.py:434
  36.7 7.3 %collective-permute-start.14 = (bf16[128,512]{1,0:T(8,128)(2,1)S(1)}, bf16[128,512]{1,0:T(8,128)(2,1)S(1)}, u32[]{:S(2)}, u32[]{:S(2)}) collective-permute-start(bf16[128,512]{1,0:T(8,128)(2,1)S(1)} %get-tuple-element.55), channel_id=1, source_target_pairs={{0,3},{1,0},{2,1},{3,2},{4,7},{5,4},{6,5},{7,6},{8,11},{9,8},{10,9... | collective-permute-start | bytes 393224 | tf_op jit(solution)/shard_map/ppermute | solution.py:434
  40.7 6.2 %collective-permute-start.12 = (bf16[128,512]{1,0:T(8,128)(2,1)S(1)}, bf16[128,512]{1,0:T(8,128)(2,1)S(1)}, u32[]{:S(2)}, u32[]{:S(2)}) collective-permute-start(bf16[128,512]{1,0:T(8,128)(2,1)S(1)} %get-tuple-element.53), channel_id=1, source_target_pairs={{0,1},{1,2},{2,3},{3,0},{4,5},{5,6},{6,7},{7,4},{8,9},{9,10},{10,1... | collective-permute-start | bytes 393224 | tf_op jit(solution)/shard_map/ppermute | solution.py:434
  42.1 5.0 %collective-permute-start.15 = (bf16[128,512]{1,0:T(8,128)(2,1)S(1)}, bf16[128,512]{1,0:T(8,128)(2,1)S(1)}, u32[]{:S(2)}, u32[]{:S(2)}) collective-permute-start(bf16[128,512]{1,0:T(8,128)(2,1)S(1)} %get-tuple-element.56), channel_id=1, source_target_pairs={{0,3},{1,0},{2,1},{3,2},{4,7},{5,4},{6,5},{7,6},{8,11},{9,8},{10,9... | collective-permute-start | bytes 393224 | tf_op jit(solution)/shard_map/ppermute | solution.py:434

commit v8 on v6

--- a/solution.py
+++ b/solution.py
@@ -192,8 +192,9 @@
 
 
 NONE = 99
-NEAR = ((1, 2, 3), (4, 8, NONE))
-MIDDLE = ((8, 9, 4, NONE), (2, 6, 3, 7))
+NEAR = ((1, 2), (4, 8))
+EARLY = ((8, 9), (2, 6))
+MIDDLE = ((3, 4), (3, 7))
 LAST = ((5, 6, 7), (1, 5, 9))
 
 
@@ -275,7 +276,7 @@
     return [src[i * UNIT : (i + 1) * UNIT, :] for i in range(src.shape[0] // UNIT)]
 
 
-def near_body(qs, unit, r1, r2, r3, m_s, l_s, acc):
+def near_body(qs, unit, r1, r2, m_s, l_s, acc):
     tags, q_tag = tags_of(unit)
     rows = lax.broadcasted_iota(jnp.int32, (CHIP, CHIP), 0)
     cols = lax.broadcasted_iota(jnp.int32, (CHIP, CHIP), 1)
@@ -290,36 +291,54 @@
         l_s[h] = got[:, HD:]
         acc[h] = got[:, :HD]
     state = (m_s, l_s, acc)
-    units = [src[...] for src in (r1, r2, r3)]
+    units = [src[...] for src in (r1, r2)]
     add_units(lambda h: qs[h], units, NEAR, q_tag, lambda h: [ref[h] for ref in state], state)
 
 
-def attend_near(qs, unit, r1, r2, r3):
+def attend_near(qs, unit, r1, r2):
     heads = qs.shape[0]
     state = like(heads, CHIP, HD, dtype=F32)
     return call(
-        near_body, "attend_near", (state, state, state), [VMEM] * 5, (VMEM,) * 3, limit=8,
-        flops=4 * heads * CHIP * 4 * CHIP * HD, exps=heads * CHIP * 4 * CHIP,
-    )(qs, unit, r1, r2, r3)
-
-
-def middle_body(qs, m_in, l_in, acc_in, unit, r4, far_b, far_c, m_s, l_s, acc):
+        near_body, "attend_near", (state, state, state), [VMEM] * 4, (VMEM,) * 3, limit=8,
+        flops=12 * heads * CHIP * CHIP * HD, exps=3 * heads * CHIP * CHIP,
+    )(qs, unit, r1, r2)
+
+
+def early_body(qs, m_in, l_in, acc_in, unit, far_b, m_s, l_s, acc):
     before = (m_in, l_in, acc_in)
-    third, fourth = parts(far_c)
-    third = jnp.where(core_index() == 0, r4[...], third)
     add_units(
-        lambda h: qs[h], parts(far_b) + [third, fourth], MIDDLE, tags_of(unit)[1],
+        lambda h: qs[h], parts(far_b), EARLY, tags_of(unit)[1],
         lambda h: [ref[h] for ref in before], (m_s, l_s, acc),
     )
 
 
-def attend_middle(qs, m_in, l_in, acc_in, unit, r4, far_b, far_c):
+def attend_early(qs, m_in, l_in, acc_in, unit, far_b):
     heads = qs.shape[0]
     state = like(heads, CHIP, HD, dtype=F32)
     return call(
+        early_body, "attend_early", (state,) * 3, [VMEM] * 6, (VMEM,) * 3, limit=8,
+        flops=64 * heads * CHIP * CHIP * HD, exps=2 * heads * CHIP * CHIP,
+    )(qs, m_in, l_in, acc_in, unit, far_b)
+
+
+def middle_body(qs, m_in, l_in, acc_in, unit, r3, r4, far_c, m_s, l_s, acc):
+    before = (m_in, l_in, acc_in)
+    even = core_index() == 0
+    third, fourth = parts(far_c)
+    units = [jnp.where(even, r3[...], third), jnp.where(even, r4[...], fourth)]
+    add_units(
+        lambda h: qs[h], units, MIDDLE, tags_of(unit)[1],
+        lambda h: [ref[h] for ref in before], (m_s, l_s, acc),
+    )
+
+
+def attend_middle(qs, m_in, l_in, acc_in, unit, r3, r4, far_c):
+    heads = qs.shape[0]
+    state = like(heads, CHIP, HD, dtype=F32)
+    return call(
         middle_body, "attend_middle", (state,) * 3, [VMEM] * 8, (VMEM,) * 3, limit=8,
-        flops=32 * heads * CHIP * 4 * CHIP * HD, exps=heads * CHIP * 4 * CHIP,
-    )(qs, m_in, l_in, acc_in, unit, r4, far_b, far_c)
+        flops=64 * heads * CHIP * CHIP * HD, exps=2 * heads * CHIP * CHIP,
+    )(qs, m_in, l_in, acc_in, unit, r3, r4, far_c)
 
 
 def attend_last(side, qs, m_in, l_in, acc_in, unit, far_a):
@@ -425,8 +444,9 @@
     far_c = along(out_c, ahead(12), in_row(3))
     far_a = along(bundle_row(unit, r1, r2, r3, r4), ahead(4), in_row(1))
     qs = project_q(tokens, came, w_query, table)
-    state = attend_near(qs, unit, r1, r2, r3)
-    state = attend_middle(qs, *state, unit, r4, far_b, far_c)
+    state = attend_near(qs, unit, r1, r2)
+    state = attend_early(qs, *state, unit, far_b)
+    state = attend_middle(qs, *state, unit, r3, r4, far_c)
     xr = swap(attend_last(1, qs, *state, unit, far_a))
     xm = attend_last(0, qs, *state, unit, far_a)
 

time: 47.6 us -> 46.9 us (0.985)
  starting transfers between devices: 25.2 us -> 21.7 us
  waiting for transfers between devices: 7.32 us -> 10.4 us
    ppermute x7, starting transfers between devices: 13.5 us -> 10.1 us  [along(): return lax.ppermute(value, 'ctx', moves)]
    ppermute x7, waiting for transfers between devices: 4.07 us -> 7.13 us  [along(): return lax.ppermute(value, 'ctx', moves)]
    pallas_call x1, Pallas kernels: 2.17 us -> 1.25 us  [attend_middle(): call(middle_body, 'attend_middle', (state,) * 3, [VMEM] * 8, (VMEM,) * 3,...]
    pallas_call x1 -> x2, Pallas kernels: 2.06 us -> 2.72 us  [the longest x1 1.53 us: attend_near(): call(near_body, 'attend_near', (state, state, state), [VMEM] * 4, (VMEM,)...]
  transfers between devices with their start and end apart: 16 -> 16, of which waited for: 5 -> 7; matrix products, arithmetic and copies ran while one was open for 0% -> 0% of each run, Pallas kernels for 25% -> 25%
where the time goes in v8:
time: 46.9 us; the launch traced here: 46.8 us
  starting transfers between devices  21.7 us (46%)
  Pallas kernels  14.5 us (31%)
  waiting for transfers between devices  10.4 us (22%)
    ppermute x6, starting transfers between devices, shift(): lax.ppermute(value, 'head', [(g, (g + step) % groups) for g in range(grou...  11 us
    ppermute x7, starting transfers between devices, along(): return lax.ppermute(value, 'ctx', moves)  10.1 us
    ppermute x7, waiting for transfers between devices, along(): return lax.ppermute(value, 'ctx', moves)  7.13 us
    pallas_call x1, Pallas kernels, project_q(): call(q_body, 'project_q', like(width // 2 // HD, CHIP, HD), [VMEM, VMEM,...  3.1 us
    ppermute x6, waiting for transfers between devices, shift(): lax.ppermute(value, 'head', [(g, (g + step) % groups) for g in range(grou...  2.95 us
    pallas_call x1, Pallas kernels, project_own(): call(own_body, 'project_own', (like(ROWS, 2 * HD), like(ROWS, depth), lik...  2.35 us
    pallas_call x2, Pallas kernels, attend_last(): call(body, 'attend_last', like(ROWS, heads * HD), [VMEM] * 6, VMEM, [pltp...  2 us
    pallas_call x3, Pallas kernels, project_out(): call(body, 'project_out', (like(ROWS, half, dtype=dtype),) * len(parts),...  1.62 us
  transfers between devices with their start and end apart: 16, of which 7 were waited for; matrix products, arithmetic and copies ran while one was open for 0% of the time, Pallas kernels for 25%

profile of v8, /device:TPU:0, one launch (start us, length us, event | category | flops | bytes accessed | tf_op | source)
XLA Modules:
  0.0 46.8 jit_solution(12827490982793192260)
XLA Ops:
  0.5 2.3 %project_own.1 = (bf16[128,256]{1,0:T(8,128)(2,1)S(1)}, bf16[128,4096]{1,0:T(8,128)(2,1)S(1)}, bf16[4096,256]{1,0:T(8,128)(2,1)S(1)}, s32[1,128]{1,0:T(1,128)S(1)}, f32[256,128]{1,0:T(8,128)S(1)}) custom-call(bf16[128,4096]{1,0:T(8,128)(2,1)} %tok.1, bf16[4096,256]{1,0:T(8,128)(2,1)} %wk.1, bf16[4096,256]{1,0:T(8,128)(2,1)} %wv.1, s32[1,128]{1,0:T(1,128)} %bitcast.4, ...), custom_call_target="tpu_custom_call" | custom-call | flops 268435456 | bytes 3145728 | tf_op jit(solution)/shard_map/project_own/pallas_call | solution.py:124
  3.4 1.6 %collective-permute-start.2 = (bf16[264,256]{1,0:T(8,128)(2,1)S(1)}, bf16[264,256]{1,0:T(8,128)(2,1)S(1)}, u32[]{:S(2)}, u32[]{:S(2)}) collective-permute-start(bf16[264,256]{1,0:T(8,128)(2,1)S(1)} %project_unit.1.unit), channel_id=1, source_target_pairs={{0,8},{4,36},{8,16},{12,44},{16,24},{20,52},{24,32},{28,60},{32,40... | collective-permute-start | bytes 405512 | tf_op jit(solution)/shard_map/ppermute | solution.py:421
  5.0 2.7 %collective-permute-start.3 = (bf16[264,256]{1,0:T(8,128)(2,1)S(1)}, bf16[264,256]{1,0:T(8,128)(2,1)S(1)}, u32[]{:S(2)}, u32[]{:S(2)}) collective-permute-start(bf16[264,256]{1,0:T(8,128)(2,1)S(1)} %project_unit.1.unit), channel_id=1, source_target_pairs={{0,16},{4,68},{8,24},{12,76},{16,32},{20,84},{24,40},{28,92},{32,4... | collective-permute-start | bytes 405512 | tf_op jit(solution)/shard_map/ppermute | solution.py:421
  7.8 2.4 %collective-permute-start.5 = (bf16[264,256]{1,0:T(8,128)(2,1)S(1)}, bf16[264,256]{1,0:T(8,128)(2,1)S(1)}, u32[]{:S(2)}, u32[]{:S(2)}) collective-permute-start(bf16[264,256]{1,0:T(8,128)(2,1)S(1)} %project_unit.1.unit), channel_id=1, source_target_pairs={{0,24},{4,100},{8,32},{12,108},{16,40},{20,116},{24,48},{28,124},{... | collective-permute-start | bytes 405512 | tf_op jit(solution)/shard_map/ppermute | solution.py:421
  10.2 1.6 %collective-permute-start.6 = (bf16[264,256]{1,0:T(8,128)(2,1)S(1)}, bf16[264,256]{1,0:T(8,128)(2,1)S(1)}, u32[]{:S(2)}, u32[]{:S(2)}) collective-permute-start(bf16[264,256]{1,0:T(8,128)(2,1)S(1)} %project_unit.1.unit), channel_id=1, source_target_pairs={{0,32},{4,28},{8,40},{12,4},{16,48},{20,12},{24,56},{28,20},{32,64... | collective-permute-start | bytes 405512 | tf_op jit(solution)/shard_map/ppermute | solution.py:421
  11.8 1.2 %collective-permute-done.2.r1 = bf16[264,256]{1,0:T(8,128)(2,1)S(1)} collective-permute-done((bf16[264,256]{1,0:T(8,128)(2,1)S(1)}, bf16[264,256]{1,0:T(8,128)(2,1)S(1)}, u32[]{:S(2)}, u32[]{:S(2)}) %collective-permute-start.2) | collective-permute-done | bytes 135200 | tf_op jit(solution)/shard_map/ppermute | solution.py:421
  13.0 2.5 %collective-permute-done.3.r2 = bf16[264,256]{1,0:T(8,128)(2,1)S(1)} collective-permute-done((bf16[264,256]{1,0:T(8,128)(2,1)S(1)}, bf16[264,256]{1,0:T(8,128)(2,1)S(1)}, u32[]{:S(2)}, u32[]{:S(2)}) %collective-permute-start.3) | collective-permute-done | bytes 135200 | tf_op jit(solution)/shard_map/ppermute | solution.py:421
  15.8 1.2 %collective-permute-start.7 = (bf16[528,256]{1,0:T(8,128)(2,1)S(1)}, bf16[528,256]{1,0:T(8,128)(2,1)S(1)}, u32[]{:S(2)}, u32[]{:S(2)}) collective-permute-start(bf16[528,256]{1,0:T(8,128)(2,1)S(1)} %get-tuple-element.49), channel_id=1, source_target_pairs={{0,96},{4,28},{8,104},{12,4},{16,112},{20,12},{24,120},{28,20},{32... | collective-permute-start | bytes 811016 | tf_op jit(solution)/shard_map/ppermute | solution.py:421
  18.0 3.1 %project_q.1.qs = bf16[4,256,128]{2,1,0:T(8,128)(2,1)S(1)} custom-call(bf16[128,4096]{1,0:T(8,128)(2,1)S(1)} %get-tuple-element.34.tok, bf16[128,4096]{1,0:T(8,128)(2,1)S(1)} %collective-permute-done.came, bf16[4096,1024]{1,0:T(8,128)(2,1)} %wq.1, f32[256,128]{1,0:T(8,128)S(1)} %get-tuple-element.38.table), custom_call_target="tpu_custom_call" | custom-call | flops 1073741824 | bytes 6291456 | tf_op jit(solution)/shard_map/project_q/pallas_call | solution.py:187
  21.1 1.5 %attend_near.1 = (f32[4,256,128]{2,1,0:T(8,128)S(1)}, f32[4,256,128]{2,1,0:T(8,128)S(1)}, f32[4,256,128]{2,1,0:T(8,128)S(1)}) custom-call(bf16[4,256,128]{2,1,0:T(8,128)(2,1)S(1)} %project_q.1.qs, bf16[264,256]{1,0:T(8,128)(2,1)S(1)} %project_unit.1.unit, bf16[264,256]{1,0:T(8,128)(2,1)S(1)} %collective-permute-done.2.r1, ...), custom_call_target="tpu_custom_call" | custom-call | flops 402653184 | bytes 1048576 | tf_op jit(solution)/shard_map/attend_near/pallas_call | solution.py:301
  22.6 1.1 %collective-permute-done.4.far_b = bf16[528,256]{1,0:T(8,128)(2,1)S(1)} collective-permute-done((bf16[528,256]{1,0:T(8,128)(2,1)S(1)}, bf16[528,256]{1,0:T(8,128)(2,1)S(1)}, u32[]{:S(2)}, u32[]{:S(2)}) %collective-permute-start.4) | collective-permute-done | bytes 270368 | tf_op jit(solution)/shard_map/ppermute | solution.py:421
  23.7 1.2 %attend_early.1 = (f32[4,256,128]{2,1,0:T(8,128)S(1)}, f32[4,256,128]{2,1,0:T(8,128)S(1)}, f32[4,256,128]{2,1,0:T(8,128)S(1)}) custom-call(bf16[4,256,128]{2,1,0:T(8,128)(2,1)S(1)} %project_q.1.qs, f32[4,256,128]{2,1,0:T(8,128)S(1)} %get-tuple-element.42.m_in, f32[4,256,128]{2,1,0:T(8,128)S(1)} %get-tuple-element.43.l_in, ...), custom_call_target="tpu_custom_call" | custom-call | flops 2147483648 | bytes 1048576 | tf_op jit(solution)/shard_map/attend_early/pallas_call | solution.py:318
  24.9 1.3 %attend_middle.1 = (f32[4,256,128]{2,1,0:T(8,128)S(1)}, f32[4,256,128]{2,1,0:T(8,128)S(1)}, f32[4,256,128]{2,1,0:T(8,128)S(1)}) custom-call(bf16[4,256,128]{2,1,0:T(8,128)(2,1)S(1)} %project_q.1.qs, f32[4,256,128]{2,1,0:T(8,128)S(1)} %get-tuple-element.46.m_in, f32[4,256,128]{2,1,0:T(8,128)S(1)} %get-tuple-element.47.l_in, ...), custom_call_target="tpu_custom_call" | custom-call | flops 2147483648 | bytes 1048576 | tf_op jit(solution)/shard_map/attend_middle/pallas_call | solution.py:338
  26.2 1.8 %collective-permute-done.8.far_a = bf16[792,256]{1,0:T(8,128)(2,1)S(1)} collective-permute-done((bf16[792,256]{1,0:T(8,128)(2,1)S(1)}, bf16[792,256]{1,0:T(8,128)(2,1)S(1)}, u32[]{:S(2)}, u32[]{:S(2)}) %collective-permute-start.8) | collective-permute-done | bytes 405536 | tf_op jit(solution)/shard_map/ppermute | solution.py:421
  28.0 1.0 %attend_last.3 = bf16[128,512]{1,0:T(8,128)(2,1)S(1)} custom-call(bf16[4,256,128]{2,1,0:T(8,128)(2,1)S(1)} %project_q.1.qs, f32[4,256,128]{2,1,0:T(8,128)S(1)} %get-tuple-element.50.m_in, f32[4,256,128]{2,1,0:T(8,128)S(1)} %get-tuple-element.51.l_in, f32[4,256,128]{2,1,0:T(8,128)S(1)} %get-tuple-element.52.acc_in, bf16[264,256]{1,0:T(8,128)(2,1)S(1)} %project_unit.1.unit, ...), custom_call_target="tpu_custom_call" | custom-call | flops 201326592 | bytes 1048576 | tf_op jit(solution)/shard_map/attend_last/pallas_call | solution.py:359
  29.1 1.0 %attend_last.2.xm = bf16[128,512]{1,0:T(8,128)(2,1)S(1)} custom-call(bf16[4,256,128]{2,1,0:T(8,128)(2,1)S(1)} %project_q.1.qs, f32[4,256,128]{2,1,0:T(8,128)S(1)} %get-tuple-element.50.m_in, f32[4,256,128]{2,1,0:T(8,128)S(1)} %get-tuple-element.51.l_in, f32[4,256,128]{2,1,0:T(8,128)S(1)} %get-tuple-element.52.acc_in, bf16[264,256]{1,0:T(8,128)(2,1)S(1)} %project_unit.1.unit, ...), custom_call_target="tpu_custom_call" | custom-call | flops 201326592 | bytes 1048576 | tf_op jit(solution)/shard_map/attend_last/pallas_call | solution.py:359
  30.9 2.0 %collective-permute-start.10 = (bf16[128,512]{1,0:T(8,128)(2,1)S(1)}, bf16[128,512]{1,0:T(8,128)(2,1)S(1)}, u32[]{:S(2)}, u32[]{:S(2)}) collective-permute-start(bf16[128,512]{1,0:T(8,128)(2,1)S(1)} %get-tuple-element.57), channel_id=1, source_target_pairs={{0,1},{1,2},{2,3},{3,0},{4,5},{5,6},{6,7},{7,4},{8,9},{9,10},{10,1... | collective-permute-start | bytes 393224 | tf_op jit(solution)/shard_map/ppermute | solution.py:454
  32.8 2.4 %collective-permute-start.11 = (bf16[128,512]{1,0:T(8,128)(2,1)S(1)}, bf16[128,512]{1,0:T(8,128)(2,1)S(1)}, u32[]{:S(2)}, u32[]{:S(2)}) collective-permute-start(bf16[128,512]{1,0:T(8,128)(2,1)S(1)} %get-tuple-element.58), channel_id=1, source_target_pairs={{0,3},{1,0},{2,1},{3,2},{4,7},{5,4},{6,5},{7,6},{8,11},{9,8},{10,9... | collective-permute-start | bytes 393224 | tf_op jit(solution)/shard_map/ppermute | solution.py:454
  35.8 3.2 %collective-permute-start.14 = (bf16[128,512]{1,0:T(8,128)(2,1)S(1)}, bf16[128,512]{1,0:T(8,128)(2,1)S(1)}, u32[]{:S(2)}, u32[]{:S(2)}) collective-permute-start(bf16[128,512]{1,0:T(8,128)(2,1)S(1)} %get-tuple-element.61), channel_id=1, source_target_pairs={{0,3},{1,0},{2,1},{3,2},{4,7},{5,4},{6,5},{7,6},{8,11},{9,8},{10,9... | collective-permute-start | bytes 393224 | tf_op jit(solution)/shard_map/ppermute | solution.py:454
  39.0 0.7 %project_out.3 = (f32[128,512]{1,0:T(8,128)S(1)}, f32[128,512]{1,0:T(8,128)S(1)}, f32[128,512]{1,0:T(8,128)S(1)}, f32[128,512]{1,0:T(8,128)S(1)}) custom-call(bf16[128,512]{1,0:T(8,128)(2,1)S(1)} %attend_last.2.xm, bf16[128,512]{1,0:T(8,128)(2,1)S(1)} %collective-permute-done.9.xr, bf16[1024,4096]{1,0:T(8,128)(2,1)S(1)} %bitcast.2), custom_call_target="tpu_custom_call" | custom-call | flops 536870912 | bytes 4194304 | tf_op jit(solution)/shard_map/project_out/pallas_call | solution.py:382
  39.8 1.2 %collective-permute-start.12 = (bf16[128,512]{1,0:T(8,128)(2,1)S(1)}, bf16[128,512]{1,0:T(8,128)(2,1)S(1)}, u32[]{:S(2)}, u32[]{:S(2)}) collective-permute-start(bf16[128,512]{1,0:T(8,128)(2,1)S(1)} %get-tuple-element.59), channel_id=1, source_target_pairs={{0,1},{1,2},{2,3},{3,0},{4,5},{5,6},{6,7},{7,4},{8,9},{9,10},{10,1... | collective-permute-start | bytes 393224 | tf_op jit(solution)/shard_map/ppermute | solution.py:454
  41.0 2.1 %collective-permute-start.15 = (bf16[128,512]{1,0:T(8,128)(2,1)S(1)}, bf16[128,512]{1,0:T(8,128)(2,1)S(1)}, u32[]{:S(2)}, u32[]{:S(2)}) collective-permute-start(bf16[128,512]{1,0:T(8,128)(2,1)S(1)} %get-tuple-element.62), channel_id=1, source_target_pairs={{0,3},{1,0},{2,1},{3,2},{4,7},{5,4},{6,5},{7,6},{8,11},{9,8},{10,9... | collective-permute-start | bytes 393224 | tf_op jit(solution)/shard_map/ppermute | solution.py:454
  43.1 2.9 %collective-permute-done.12.left_a = bf16[128,512]{1,0:T(8,128)(2,1)S(1)} collective-permute-done((bf16[128,512]{1,0:T(8,128)(2,1)S(1)}, bf16[128,512]{1,0:T(8,128)(2,1)S(1)}, u32[]{:S(2)}, u32[]{:S(2)}) %collective-permute-start.12) | collective-permute-done | bytes 131104 | tf_op jit(solution)/shard_map/ppermute | solution.py:454
  46.0 0.8 %add_total.1 = bf16[128,1024]{1,0:T(8,128)(2,1)} custom-call(f32[128,512]{1,0:T(8,128)S(1)} %get-tuple-element.53.own_a, f32[128,512]{1,0:T(8,128)S(1)} %get-tuple-element.54.own_b, bf16[128,512]{1,0:T(8,128)(2,1)S(1)} %collective-permute-done.12.left_a, bf16[128,512]{1,0:T(8,128)(2,1)S(1)} %collective-permute-done.13.left_b, ...), custom_call_target="tpu_custom_call" | custom-call | bytes 1048576 | tf_op jit(solution)/shard_map/add_total/pallas_call | solution.py:408
  (28 shorter events, 3.8 us)
Async XLA Ops:
  0.0 2.9 %collective-permute-start = (bf16[128,4096]{1,0:T(8,128)(2,1)}, bf16[128,4096]{1,0:T(8,128)(2,1)S(1)}, u32[]{:S(2)}, u32[]{:S(2)}) collective-permute-start(bf16[128,4096]{1,0:T(8,128)(2,1)} %tok.1), channel_id=1, source_target_pairs={{0,4},{4,0},{8,12},{12,8},{16,20},{20,16},{24,28},{28,24},{32,36},... | collective-permute-start | bytes 3145736 | tf_op jit(solution)/shard_map/ppermute | solution.py:417
  0.0 2.9 %collective-permute-start.1 = (s32[1,128]{1,0:T(1,128)}, s32[1,128]{1,0:T(1,128)S(1)}, u32[]{:S(2)}, u32[]{:S(2)}) collective-permute-start(s32[1,128]{1,0:T(1,128)} %bitcast.3), channel_id=1, source_target_pairs={{0,4},{4,0},{8,12},{12,8},{16,20},{20,16},{24,28},{28,24},{32,36},... | collective-permute-start | bytes 1544 | tf_op jit(solution)/shard_map/ppermute | solution.py:417
  3.4 9.6 %collective-permute-start.2 = (bf16[264,256]{1,0:T(8,128)(2,1)S(1)}, bf16[264,256]{1,0:T(8,128)(2,1)S(1)}, u32[]{:S(2)}, u32[]{:S(2)}) collective-permute-start(bf16[264,256]{1,0:T(8,128)(2,1)S(1)} %project_unit.1.unit), channel_id=1, source_target_pairs={{0,8},{4,36},{8,16},{12,44},{16,24},{20,52},{24,32},{28,60},{32,40... | collective-permute-start | bytes 405512 | tf_op jit(solution)/shard_map/ppermute | solution.py:421
  5.0 10.4 %collective-permute-start.3 = (bf16[264,256]{1,0:T(8,128)(2,1)S(1)}, bf16[264,256]{1,0:T(8,128)(2,1)S(1)}, u32[]{:S(2)}, u32[]{:S(2)}) collective-permute-start(bf16[264,256]{1,0:T(8,128)(2,1)S(1)} %project_unit.1.unit), channel_id=1, source_target_pairs={{0,16},{4,68},{8,24},{12,76},{16,32},{20,84},{24,40},{28,92},{32,4... | collective-permute-start | bytes 405512 | tf_op jit(solution)/shard_map/ppermute | solution.py:421
  7.8 9.2 %collective-permute-start.5 = (bf16[264,256]{1,0:T(8,128)(2,1)S(1)}, bf16[264,256]{1,0:T(8,128)(2,1)S(1)}, u32[]{:S(2)}, u32[]{:S(2)}) collective-permute-start(bf16[264,256]{1,0:T(8,128)(2,1)S(1)} %project_unit.1.unit), channel_id=1, source_target_pairs={{0,24},{4,100},{8,32},{12,108},{16,40},{20,116},{24,48},{28,124},{... | collective-permute-start | bytes 405512 | tf_op jit(solution)/shard_map/ppermute | solution.py:421
  10.2 7.3 %collective-permute-start.6 = (bf16[264,256]{1,0:T(8,128)(2,1)S(1)}, bf16[264,256]{1,0:T(8,128)(2,1)S(1)}, u32[]{:S(2)}, u32[]{:S(2)}) collective-permute-start(bf16[264,256]{1,0:T(8,128)(2,1)S(1)} %project_unit.1.unit), channel_id=1, source_target_pairs={{0,32},{4,28},{8,40},{12,4},{16,48},{20,12},{24,56},{28,20},{32,64... | collective-permute-start | bytes 405512 | tf_op jit(solution)/shard_map/ppermute | solution.py:421
  15.6 8.1 %collective-permute-start.4 = (bf16[528,256]{1,0:T(8,128)(2,1)S(1)}, bf16[528,256]{1,0:T(8,128)(2,1)S(1)}, u32[]{:S(2)}, u32[]{:S(2)}) collective-permute-start(bf16[528,256]{1,0:T(8,128)(2,1)S(1)} %get-tuple-element.45), channel_id=1, source_target_pairs={{0,64},{4,20},{8,72},{12,28},{16,80},{20,4},{24,88},{28,12},{32,96... | collective-permute-start | bytes 811016 | tf_op jit(solution)/shard_map/ppermute | solution.py:421
  15.8 9.1 %collective-permute-start.7 = (bf16[528,256]{1,0:T(8,128)(2,1)S(1)}, bf16[528,256]{1,0:T(8,128)(2,1)S(1)}, u32[]{:S(2)}, u32[]{:S(2)}) collective-permute-start(bf16[528,256]{1,0:T(8,128)(2,1)S(1)} %get-tuple-element.49), channel_id=1, source_target_pairs={{0,96},{4,28},{8,104},{12,4},{16,112},{20,12},{24,120},{28,20},{32... | collective-permute-start | bytes 811016 | tf_op jit(solution)/shard_map/ppermute | solution.py:421
  17.6 10.3 %collective-permute-start.8 = (bf16[792,256]{1,0:T(8,128)(2,1)S(1)}, bf16[792,256]{1,0:T(8,128)(2,1)S(1)}, u32[]{:S(2)}, u32[]{:S(2)}) collective-permute-start(bf16[792,256]{1,0:T(8,128)(2,1)S(1)} %bundle_row.1), channel_id=1, source_target_pairs={{0,32},{4,12},{8,40},{12,20},{16,48},{20,28},{24,56},{28,4},{32,64... | collective-permute-start | bytes 1216520 | tf_op jit(solution)/shard_map/ppermute | solution.py:421
  23.7 6.7 %slice-start = ((s8[8388608]{0:T(1024)(128)(4,1)}), s8[4194304]{0:T(1024)(128)(4,1)S(1)}, s32[]{:S(2)}) async-start(s8[8388608]{0:T(1024)(128)(4,1)} %bitcast.1), calls=%async_computation | async-start | bytes 8388608
  24.9 5.5 %slice-start.1 = ((s8[8388608]{0:T(1024)(128)(4,1)}), s8[4194304]{0:T(1024)(128)(4,1)S(1)}, s32[]{:S(2)}) async-start(s8[8388608]{0:T(1024)(128)(4,1)} %bitcast.1), calls=%async_computation.1 | async-start | bytes 8388608
  29.0 1.4 %collective-permute-start.9 = (bf16[128,512]{1,0:T(8,128)(2,1)S(1)}, bf16[128,512]{1,0:T(8,128)(2,1)S(1)}, u32[]{:S(2)}, u32[]{:S(2)}) collective-permute-start(bf16[128,512]{1,0:T(8,128)(2,1)S(1)} %attend_last.3), channel_id=1, source_target_pairs={{0,4},{4,0},{8,12},{12,8},{16,20},{20,16},{24,28},{28,24},{32,36},... | collective-permute-start | bytes 393224 | tf_op jit(solution)/shard_map/ppermute | solution.py:417
  30.9 8.9 %collective-permute-start.10 = (bf16[128,512]{1,0:T(8,128)(2,1)S(1)}, bf16[128,512]{1,0:T(8,128)(2,1)S(1)}, u32[]{:S(2)}, u32[]{:S(2)}) collective-permute-start(bf16[128,512]{1,0:T(8,128)(2,1)S(1)} %get-tuple-element.57), channel_id=1, source_target_pairs={{0,1},{1,2},{2,3},{3,0},{4,5},{5,6},{6,7},{7,4},{8,9},{9,10},{10,1... | collective-permute-start | bytes 393224 | tf_op jit(solution)/shard_map/ppermute | solution.py:454
  32.8 6.9 %collective-permute-start.11 = (bf16[128,512]{1,0:T(8,128)(2,1)S(1)}, bf16[128,512]{1,0:T(8,128)(2,1)S(1)}, u32[]{:S(2)}, u32[]{:S(2)}) collective-permute-start(bf16[128,512]{1,0:T(8,128)(2,1)S(1)} %get-tuple-element.58), channel_id=1, source_target_pairs={{0,3},{1,0},{2,1},{3,2},{4,7},{5,4},{6,5},{7,6},{8,11},{9,8},{10,9... | collective-permute-start | bytes 393224 | tf_op jit(solution)/shard_map/ppermute | solution.py:454
  35.7 7.4 %collective-permute-start.13 = (bf16[128,512]{1,0:T(8,128)(2,1)S(1)}, bf16[128,512]{1,0:T(8,128)(2,1)S(1)}, u32[]{:S(2)}, u32[]{:S(2)}) collective-permute-start(bf16[128,512]{1,0:T(8,128)(2,1)S(1)} %get-tuple-element.60), channel_id=1, source_target_pairs={{0,1},{1,2},{2,3},{3,0},{4,5},{5,6},{6,7},{7,4},{8,9},{9,10},{10,1... | collective-permute-start | bytes 393224 | tf_op jit(solution)/shard_map/ppermute | solution.py:454
  35.8 7.3 %collective-permute-start.14 = (bf16[128,512]{1,0:T(8,128)(2,1)S(1)}, bf16[128,512]{1,0:T(8,128)(2,1)S(1)}, u32[]{:S(2)}, u32[]{:S(2)}) collective-permute-start(bf16[128,512]{1,0:T(8,128)(2,1)S(1)} %get-tuple-element.61), channel_id=1, source_target_pairs={{0,3},{1,0},{2,1},{3,2},{4,7},{5,4},{6,5},{7,6},{8,11},{9,8},{10,9... | collective-permute-start | bytes 393224 | tf_op jit(solution)/shard_map/ppermute | solution.py:454
  39.8 6.2 %collective-permute-start.12 = (bf16[128,512]{1,0:T(8,128)(2,1)S(1)}, bf16[128,512]{1,0:T(8,128)(2,1)S(1)}, u32[]{:S(2)}, u32[]{:S(2)}) collective-permute-start(bf16[128,512]{1,0:T(8,128)(2,1)S(1)} %get-tuple-element.59), channel_id=1, source_target_pairs={{0,1},{1,2},{2,3},{3,0},{4,5},{5,6},{6,7},{7,4},{8,9},{9,10},{10,1... | collective-permute-start | bytes 393224 | tf_op jit(solution)/shard_map/ppermute | solution.py:454
  41.0 5.0 %collective-permute-start.15 = (bf16[128,512]{1,0:T(8,128)(2,1)S(1)}, bf16[128,512]{1,0:T(8,128)(2,1)S(1)}, u32[]{:S(2)}, u32[]{:S(2)}) collective-permute-start(bf16[128,512]{1,0:T(8,128)(2,1)S(1)} %get-tuple-element.62), channel_id=1, source_target_pairs={{0,3},{1,0},{2,1},{3,2},{4,7},{5,4},{6,5},{7,6},{8,11},{9,8},{10,9... | collective-permute-start | bytes 393224 | tf_op jit(solution)/shard_map/ppermute | solution.py:454

commit v9 on v8

--- a/solution.py
+++ b/solution.py
@@ -417,7 +417,11 @@
         return lax.ppermute(value, "ctx", [(r, r ^ 1) for r in range(ranks)])
 
     def along(value, even, odd):
-        moves = [(r, 2 * (odd if r % 2 else even)(r // 2) + r % 2) for r in range(ranks)]
+        moves = []
+        for r in range(ranks):
+            step = odd if r % 2 else even
+            if step is not None:
+                moves.append((r, 2 * step(r // 2) + r % 2))
         return lax.ppermute(value, "ctx", moves)
 
     def ahead(step):
@@ -441,7 +445,7 @@
     r1, r2, came = lax.optimization_barrier((r1, r2, came))
     out_b, out_c = bundle_pairs(unit, r1, r2)
     far_b = along(out_b, ahead(8), in_row(2))
-    far_c = along(out_c, ahead(12), in_row(3))
+    far_c = along(out_c, None, in_row(3))
     far_a = along(bundle_row(unit, r1, r2, r3, r4), ahead(4), in_row(1))
     qs = project_q(tokens, came, w_query, table)
     state = attend_near(qs, unit, r1, r2)

time: 46.9 us -> 47 us (level)
  waiting for transfers between devices: 10.4 us -> 11 us
  starting transfers between devices: 21.7 us -> 21.1 us
    ppermute x7, starting transfers between devices: 10.1 us -> 9.52 us  [along(): return lax.ppermute(value, 'ctx', moves)]
    ppermute x7, waiting for transfers between devices: 7.13 us -> 7.73 us  [along(): return lax.ppermute(value, 'ctx', moves)]
where the time goes in v9:
time: 47 us; the launch traced here: 46.8 us
  starting transfers between devices  21.1 us (45%)
  Pallas kernels  14.5 us (31%)
  waiting for transfers between devices  11 us (23%)
    ppermute x6, starting transfers between devices, shift(): lax.ppermute(value, 'head', [(g, (g + step) % groups) for g in range(grou...  11 us
    ppermute x7, starting transfers between devices, along(): return lax.ppermute(value, 'ctx', moves)  9.52 us
    ppermute x7, waiting for transfers between devices, along(): return lax.ppermute(value, 'ctx', moves)  7.73 us
    pallas_call x1, Pallas kernels, project_q(): call(q_body, 'project_q', like(width // 2 // HD, CHIP, HD), [VMEM, VMEM,...  3.1 us
    ppermute x6, waiting for transfers between devices, shift(): lax.ppermute(value, 'head', [(g, (g + step) % groups) for g in range(grou...  2.95 us
    pallas_call x1, Pallas kernels, project_own(): call(own_body, 'project_own', (like(ROWS, 2 * HD), like(ROWS, depth), lik...  2.35 us
    pallas_call x2, Pallas kernels, attend_last(): call(body, 'attend_last', like(ROWS, heads * HD), [VMEM] * 6, VMEM, [pltp...  2 us
    pallas_call x3, Pallas kernels, project_out(): call(body, 'project_out', (like(ROWS, half, dtype=dtype),) * len(parts),...  1.62 us
  transfers between devices with their start and end apart: 16, of which 7 were waited for; matrix products, arithmetic and copies ran while one was open for 0% of the time, Pallas kernels for 25%

profile of v9, /device:TPU:0, one launch (start us, length us, event | category | flops | bytes accessed | tf_op | source)
XLA Modules:
  0.0 46.8 jit_solution(16419428294459953059)
XLA Ops:
  0.5 2.3 %project_own.1 = (bf16[128,256]{1,0:T(8,128)(2,1)S(1)}, bf16[128,4096]{1,0:T(8,128)(2,1)S(1)}, bf16[4096,256]{1,0:T(8,128)(2,1)S(1)}, s32[1,128]{1,0:T(1,128)S(1)}, f32[256,128]{1,0:T(8,128)S(1)}) custom-call(bf16[128,4096]{1,0:T(8,128)(2,1)} %tok.1, bf16[4096,256]{1,0:T(8,128)(2,1)} %wk.1, bf16[4096,256]{1,0:T(8,128)(2,1)} %wv.1, s32[1,128]{1,0:T(1,128)} %bitcast.4, ...), custom_call_target="tpu_custom_call" | custom-call | flops 268435456 | bytes 3145728 | tf_op jit(solution)/shard_map/project_own/pallas_call | solution.py:124
  3.4 1.6 %collective-permute-start.2 = (bf16[264,256]{1,0:T(8,128)(2,1)S(1)}, bf16[264,256]{1,0:T(8,128)(2,1)S(1)}, u32[]{:S(2)}, u32[]{:S(2)}) collective-permute-start(bf16[264,256]{1,0:T(8,128)(2,1)S(1)} %project_unit.1.unit), channel_id=1, source_target_pairs={{0,8},{4,36},{8,16},{12,44},{16,24},{20,52},{24,32},{28,60},{32,40... | collective-permute-start | bytes 405512 | tf_op jit(solution)/shard_map/ppermute | solution.py:425
  5.0 2.7 %collective-permute-start.3 = (bf16[264,256]{1,0:T(8,128)(2,1)S(1)}, bf16[264,256]{1,0:T(8,128)(2,1)S(1)}, u32[]{:S(2)}, u32[]{:S(2)}) collective-permute-start(bf16[264,256]{1,0:T(8,128)(2,1)S(1)} %project_unit.1.unit), channel_id=1, source_target_pairs={{0,16},{4,68},{8,24},{12,76},{16,32},{20,84},{24,40},{28,92},{32,4... | collective-permute-start | bytes 405512 | tf_op jit(solution)/shard_map/ppermute | solution.py:425
  7.8 2.4 %collective-permute-start.5 = (bf16[264,256]{1,0:T(8,128)(2,1)S(1)}, bf16[264,256]{1,0:T(8,128)(2,1)S(1)}, u32[]{:S(2)}, u32[]{:S(2)}) collective-permute-start(bf16[264,256]{1,0:T(8,128)(2,1)S(1)} %project_unit.1.unit), channel_id=1, source_target_pairs={{0,24},{4,100},{8,32},{12,108},{16,40},{20,116},{24,48},{28,124},{... | collective-permute-start | bytes 405512 | tf_op jit(solution)/shard_map/ppermute | solution.py:425
  10.2 1.6 %collective-permute-start.6 = (bf16[264,256]{1,0:T(8,128)(2,1)S(1)}, bf16[264,256]{1,0:T(8,128)(2,1)S(1)}, u32[]{:S(2)}, u32[]{:S(2)}) collective-permute-start(bf16[264,256]{1,0:T(8,128)(2,1)S(1)} %project_unit.1.unit), channel_id=1, source_target_pairs={{0,32},{4,28},{8,40},{12,4},{16,48},{20,12},{24,56},{28,20},{32,64... | collective-permute-start | bytes 405512 | tf_op jit(solution)/shard_map/ppermute | solution.py:425
  11.8 1.2 %collective-permute-done.2.r1 = bf16[264,256]{1,0:T(8,128)(2,1)S(1)} collective-permute-done((bf16[264,256]{1,0:T(8,128)(2,1)S(1)}, bf16[264,256]{1,0:T(8,128)(2,1)S(1)}, u32[]{:S(2)}, u32[]{:S(2)}) %collective-permute-start.2) | collective-permute-done | bytes 135200 | tf_op jit(solution)/shard_map/ppermute | solution.py:425
  13.0 2.5 %collective-permute-done.3.r2 = bf16[264,256]{1,0:T(8,128)(2,1)S(1)} collective-permute-done((bf16[264,256]{1,0:T(8,128)(2,1)S(1)}, bf16[264,256]{1,0:T(8,128)(2,1)S(1)}, u32[]{:S(2)}, u32[]{:S(2)}) %collective-permute-start.3) | collective-permute-done | bytes 135200 | tf_op jit(solution)/shard_map/ppermute | solution.py:425
  16.5 1.1 %collective-permute-done.6.r4.after = bf16[264,256]{1,0:T(8,128)(2,1)S(1)} collective-permute-done((bf16[264,256]{1,0:T(8,128)(2,1)S(1)}, bf16[264,256]{1,0:T(8,128)(2,1)S(1)}, u32[]{:S(2)}, u32[]{:S(2)}) %collective-permute-start.6) | collective-permute-done | bytes 135200 | tf_op jit(solution)/shard_map/ppermute | solution.py:425
  17.9 3.1 %project_q.1.qs = bf16[4,256,128]{2,1,0:T(8,128)(2,1)S(1)} custom-call(bf16[128,4096]{1,0:T(8,128)(2,1)S(1)} %get-tuple-element.34.tok, bf16[128,4096]{1,0:T(8,128)(2,1)S(1)} %collective-permute-done.came, bf16[4096,1024]{1,0:T(8,128)(2,1)} %wq.1, f32[256,128]{1,0:T(8,128)S(1)} %get-tuple-element.38.table), custom_call_target="tpu_custom_call" | custom-call | flops 1073741824 | bytes 6291456 | tf_op jit(solution)/shard_map/project_q/pallas_call | solution.py:187
  21.0 1.5 %attend_near.1 = (f32[4,256,128]{2,1,0:T(8,128)S(1)}, f32[4,256,128]{2,1,0:T(8,128)S(1)}, f32[4,256,128]{2,1,0:T(8,128)S(1)}) custom-call(bf16[4,256,128]{2,1,0:T(8,128)(2,1)S(1)} %project_q.1.qs, bf16[264,256]{1,0:T(8,128)(2,1)S(1)} %project_unit.1.unit, bf16[264,256]{1,0:T(8,128)(2,1)S(1)} %collective-permute-done.2.r1, ...), custom_call_target="tpu_custom_call" | custom-call | flops 402653184 | bytes 1048576 | tf_op jit(solution)/shard_map/attend_near/pallas_call | solution.py:301
  22.5 1.2 %collective-permute-done.4.far_b = bf16[528,256]{1,0:T(8,128)(2,1)S(1)} collective-permute-done((bf16[528,256]{1,0:T(8,128)(2,1)S(1)}, bf16[528,256]{1,0:T(8,128)(2,1)S(1)}, u32[]{:S(2)}, u32[]{:S(2)}) %collective-permute-start.4) | collective-permute-done | bytes 270368 | tf_op jit(solution)/shard_map/ppermute | solution.py:425
  23.7 1.2 %attend_early.1 = (f32[4,256,128]{2,1,0:T(8,128)S(1)}, f32[4,256,128]{2,1,0:T(8,128)S(1)}, f32[4,256,128]{2,1,0:T(8,128)S(1)}) custom-call(bf16[4,256,128]{2,1,0:T(8,128)(2,1)S(1)} %project_q.1.qs, f32[4,256,128]{2,1,0:T(8,128)S(1)} %get-tuple-element.42.m_in, f32[4,256,128]{2,1,0:T(8,128)S(1)} %get-tuple-element.43.l_in, ...), custom_call_target="tpu_custom_call" | custom-call | flops 2147483648 | bytes 1048576 | tf_op jit(solution)/shard_map/attend_early/pallas_call | solution.py:318
  24.9 1.3 %attend_middle.1 = (f32[4,256,128]{2,1,0:T(8,128)S(1)}, f32[4,256,128]{2,1,0:T(8,128)S(1)}, f32[4,256,128]{2,1,0:T(8,128)S(1)}) custom-call(bf16[4,256,128]{2,1,0:T(8,128)(2,1)S(1)} %project_q.1.qs, f32[4,256,128]{2,1,0:T(8,128)S(1)} %get-tuple-element.46.m_in, f32[4,256,128]{2,1,0:T(8,128)S(1)} %get-tuple-element.47.l_in, ...), custom_call_target="tpu_custom_call" | custom-call | flops 2147483648 | bytes 1048576 | tf_op jit(solution)/shard_map/attend_middle/pallas_call | solution.py:338
  26.2 1.8 %collective-permute-done.8.far_a = bf16[792,256]{1,0:T(8,128)(2,1)S(1)} collective-permute-done((bf16[792,256]{1,0:T(8,128)(2,1)S(1)}, bf16[792,256]{1,0:T(8,128)(2,1)S(1)}, u32[]{:S(2)}, u32[]{:S(2)}) %collective-permute-start.8) | collective-permute-done | bytes 405536 | tf_op jit(solution)/shard_map/ppermute | solution.py:425
  28.0 1.0 %attend_last.3 = bf16[128,512]{1,0:T(8,128)(2,1)S(1)} custom-call(bf16[4,256,128]{2,1,0:T(8,128)(2,1)S(1)} %project_q.1.qs, f32[4,256,128]{2,1,0:T(8,128)S(1)} %get-tuple-element.50.m_in, f32[4,256,128]{2,1,0:T(8,128)S(1)} %get-tuple-element.51.l_in, f32[4,256,128]{2,1,0:T(8,128)S(1)} %get-tuple-element.52.acc_in, bf16[264,256]{1,0:T(8,128)(2,1)S(1)} %project_unit.1.unit, ...), custom_call_target="tpu_custom_call" | custom-call | flops 201326592 | bytes 1048576 | tf_op jit(solution)/shard_map/attend_last/pallas_call | solution.py:359
  29.1 1.0 %attend_last.2.xm = bf16[128,512]{1,0:T(8,128)(2,1)S(1)} custom-call(bf16[4,256,128]{2,1,0:T(8,128)(2,1)S(1)} %project_q.1.qs, f32[4,256,128]{2,1,0:T(8,128)S(1)} %get-tuple-element.50.m_in, f32[4,256,128]{2,1,0:T(8,128)S(1)} %get-tuple-element.51.l_in, f32[4,256,128]{2,1,0:T(8,128)S(1)} %get-tuple-element.52.acc_in, bf16[264,256]{1,0:T(8,128)(2,1)S(1)} %project_unit.1.unit, ...), custom_call_target="tpu_custom_call" | custom-call | flops 201326592 | bytes 1048576 | tf_op jit(solution)/shard_map/attend_last/pallas_call | solution.py:359
  30.9 2.0 %collective-permute-start.10 = (bf16[128,512]{1,0:T(8,128)(2,1)S(1)}, bf16[128,512]{1,0:T(8,128)(2,1)S(1)}, u32[]{:S(2)}, u32[]{:S(2)}) collective-permute-start(bf16[128,512]{1,0:T(8,128)(2,1)S(1)} %get-tuple-element.57), channel_id=1, source_target_pairs={{0,1},{1,2},{2,3},{3,0},{4,5},{5,6},{6,7},{7,4},{8,9},{9,10},{10,1... | collective-permute-start | bytes 393224 | tf_op jit(solution)/shard_map/ppermute | solution.py:458
  32.8 2.4 %collective-permute-start.11 = (bf16[128,512]{1,0:T(8,128)(2,1)S(1)}, bf16[128,512]{1,0:T(8,128)(2,1)S(1)}, u32[]{:S(2)}, u32[]{:S(2)}) collective-permute-start(bf16[128,512]{1,0:T(8,128)(2,1)S(1)} %get-tuple-element.58), channel_id=1, source_target_pairs={{0,3},{1,0},{2,1},{3,2},{4,7},{5,4},{6,5},{7,6},{8,11},{9,8},{10,9... | collective-permute-start | bytes 393224 | tf_op jit(solution)/shard_map/ppermute | solution.py:458
  35.8 3.2 %collective-permute-start.14 = (bf16[128,512]{1,0:T(8,128)(2,1)S(1)}, bf16[128,512]{1,0:T(8,128)(2,1)S(1)}, u32[]{:S(2)}, u32[]{:S(2)}) collective-permute-start(bf16[128,512]{1,0:T(8,128)(2,1)S(1)} %get-tuple-element.61), channel_id=1, source_target_pairs={{0,3},{1,0},{2,1},{3,2},{4,7},{5,4},{6,5},{7,6},{8,11},{9,8},{10,9... | collective-permute-start | bytes 393224 | tf_op jit(solution)/shard_map/ppermute | solution.py:458
  39.0 0.7 %project_out.3 = (f32[128,512]{1,0:T(8,128)S(1)}, f32[128,512]{1,0:T(8,128)S(1)}, f32[128,512]{1,0:T(8,128)S(1)}, f32[128,512]{1,0:T(8,128)S(1)}) custom-call(bf16[128,512]{1,0:T(8,128)(2,1)S(1)} %attend_last.2.xm, bf16[128,512]{1,0:T(8,128)(2,1)S(1)} %collective-permute-done.9.xr, bf16[1024,4096]{1,0:T(8,128)(2,1)S(1)} %bitcast.2), custom_call_target="tpu_custom_call" | custom-call | flops 536870912 | bytes 4194304 | tf_op jit(solution)/shard_map/project_out/pallas_call | solution.py:382
  39.8 1.2 %collective-permute-start.12 = (bf16[128,512]{1,0:T(8,128)(2,1)S(1)}, bf16[128,512]{1,0:T(8,128)(2,1)S(1)}, u32[]{:S(2)}, u32[]{:S(2)}) collective-permute-start(bf16[128,512]{1,0:T(8,128)(2,1)S(1)} %get-tuple-element.59), channel_id=1, source_target_pairs={{0,1},{1,2},{2,3},{3,0},{4,5},{5,6},{6,7},{7,4},{8,9},{9,10},{10,1... | collective-permute-start | bytes 393224 | tf_op jit(solution)/shard_map/ppermute | solution.py:458
  41.0 2.1 %collective-permute-start.15 = (bf16[128,512]{1,0:T(8,128)(2,1)S(1)}, bf16[128,512]{1,0:T(8,128)(2,1)S(1)}, u32[]{:S(2)}, u32[]{:S(2)}) collective-permute-start(bf16[128,512]{1,0:T(8,128)(2,1)S(1)} %get-tuple-element.62), channel_id=1, source_target_pairs={{0,3},{1,0},{2,1},{3,2},{4,7},{5,4},{6,5},{7,6},{8,11},{9,8},{10,9... | collective-permute-start | bytes 393224 | tf_op jit(solution)/shard_map/ppermute | solution.py:458
  43.1 2.9 %collective-permute-done.12.left_a = bf16[128,512]{1,0:T(8,128)(2,1)S(1)} collective-permute-done((bf16[128,512]{1,0:T(8,128)(2,1)S(1)}, bf16[128,512]{1,0:T(8,128)(2,1)S(1)}, u32[]{:S(2)}, u32[]{:S(2)}) %collective-permute-start.12) | collective-permute-done | bytes 131104 | tf_op jit(solution)/shard_map/ppermute | solution.py:458
  46.0 0.8 %add_total.1 = bf16[128,1024]{1,0:T(8,128)(2,1)} custom-call(f32[128,512]{1,0:T(8,128)S(1)} %get-tuple-element.53.own_a, f32[128,512]{1,0:T(8,128)S(1)} %get-tuple-element.54.own_b, bf16[128,512]{1,0:T(8,128)(2,1)S(1)} %collective-permute-done.12.left_a, bf16[128,512]{1,0:T(8,128)(2,1)S(1)} %collective-permute-done.13.left_b, ...), custom_call_target="tpu_custom_call" | custom-call | bytes 1048576 | tf_op jit(solution)/shard_map/add_total/pallas_call | solution.py:408
  (28 shorter events, 3.8 us)
Async XLA Ops:
  0.0 2.9 %collective-permute-start = (bf16[128,4096]{1,0:T(8,128)(2,1)}, bf16[128,4096]{1,0:T(8,128)(2,1)S(1)}, u32[]{:S(2)}, u32[]{:S(2)}) collective-permute-start(bf16[128,4096]{1,0:T(8,128)(2,1)} %tok.1), channel_id=1, source_target_pairs={{0,4},{4,0},{8,12},{12,8},{16,20},{20,16},{24,28},{28,24},{32,36},... | collective-permute-start | bytes 3145736 | tf_op jit(solution)/shard_map/ppermute | solution.py:417
  0.0 2.9 %collective-permute-start.1 = (s32[1,128]{1,0:T(1,128)}, s32[1,128]{1,0:T(1,128)S(1)}, u32[]{:S(2)}, u32[]{:S(2)}) collective-permute-start(s32[1,128]{1,0:T(1,128)} %bitcast.3), channel_id=1, source_target_pairs={{0,4},{4,0},{8,12},{12,8},{16,20},{20,16},{24,28},{28,24},{32,36},... | collective-permute-start | bytes 1544 | tf_op jit(solution)/shard_map/ppermute | solution.py:417
  3.4 9.6 %collective-permute-start.2 = (bf16[264,256]{1,0:T(8,128)(2,1)S(1)}, bf16[264,256]{1,0:T(8,128)(2,1)S(1)}, u32[]{:S(2)}, u32[]{:S(2)}) collective-permute-start(bf16[264,256]{1,0:T(8,128)(2,1)S(1)} %project_unit.1.unit), channel_id=1, source_target_pairs={{0,8},{4,36},{8,16},{12,44},{16,24},{20,52},{24,32},{28,60},{32,40... | collective-permute-start | bytes 405512 | tf_op jit(solution)/shard_map/ppermute | solution.py:425
  5.0 10.4 %collective-permute-start.3 = (bf16[264,256]{1,0:T(8,128)(2,1)S(1)}, bf16[264,256]{1,0:T(8,128)(2,1)S(1)}, u32[]{:S(2)}, u32[]{:S(2)}) collective-permute-start(bf16[264,256]{1,0:T(8,128)(2,1)S(1)} %project_unit.1.unit), channel_id=1, source_target_pairs={{0,16},{4,68},{8,24},{12,76},{16,32},{20,84},{24,40},{28,92},{32,4... | collective-permute-start | bytes 405512 | tf_op jit(solution)/shard_map/ppermute | solution.py:425
  7.8 8.7 %collective-permute-start.5 = (bf16[264,256]{1,0:T(8,128)(2,1)S(1)}, bf16[264,256]{1,0:T(8,128)(2,1)S(1)}, u32[]{:S(2)}, u32[]{:S(2)}) collective-permute-start(bf16[264,256]{1,0:T(8,128)(2,1)S(1)} %project_unit.1.unit), channel_id=1, source_target_pairs={{0,24},{4,100},{8,32},{12,108},{16,40},{20,116},{24,48},{28,124},{... | collective-permute-start | bytes 405512 | tf_op jit(solution)/shard_map/ppermute | solution.py:425
  10.2 7.3 %collective-permute-start.6 = (bf16[264,256]{1,0:T(8,128)(2,1)S(1)}, bf16[264,256]{1,0:T(8,128)(2,1)S(1)}, u32[]{:S(2)}, u32[]{:S(2)}) collective-permute-start(bf16[264,256]{1,0:T(8,128)(2,1)S(1)} %project_unit.1.unit), channel_id=1, source_target_pairs={{0,32},{4,28},{8,40},{12,4},{16,48},{20,12},{24,56},{28,20},{32,64... | collective-permute-start | bytes 405512 | tf_op jit(solution)/shard_map/ppermute | solution.py:425
  15.6 8.1 %collective-permute-start.4 = (bf16[528,256]{1,0:T(8,128)(2,1)S(1)}, bf16[528,256]{1,0:T(8,128)(2,1)S(1)}, u32[]{:S(2)}, u32[]{:S(2)}) collective-permute-start(bf16[528,256]{1,0:T(8,128)(2,1)S(1)} %get-tuple-element.45), channel_id=1, source_target_pairs={{0,64},{4,20},{8,72},{12,28},{16,80},{20,4},{24,88},{28,12},{32,96... | collective-permute-start | bytes 811016 | tf_op jit(solution)/shard_map/ppermute | solution.py:425
  15.8 9.1 %collective-permute-start.7 = (bf16[528,256]{1,0:T(8,128)(2,1)S(1)}, bf16[528,256]{1,0:T(8,128)(2,1)S(1)}, u32[]{:S(2)}, u32[]{:S(2)}) collective-permute-start(bf16[528,256]{1,0:T(8,128)(2,1)S(1)} %get-tuple-element.49), channel_id=1, source_target_pairs={{4,28},{12,4},{20,12},{28,20},{36,60},{44,36},{52,44},{60,52},{68,... | collective-permute-start | bytes 811016 | tf_op jit(solution)/shard_map/ppermute | solution.py:425
  17.6 10.3 %collective-permute-start.8 = (bf16[792,256]{1,0:T(8,128)(2,1)S(1)}, bf16[792,256]{1,0:T(8,128)(2,1)S(1)}, u32[]{:S(2)}, u32[]{:S(2)}) collective-permute-start(bf16[792,256]{1,0:T(8,128)(2,1)S(1)} %bundle_row.1), channel_id=1, source_target_pairs={{0,32},{4,12},{8,40},{12,20},{16,48},{20,28},{24,56},{28,4},{32,64... | collective-permute-start | bytes 1216520 | tf_op jit(solution)/shard_map/ppermute | solution.py:425
  23.7 6.7 %slice-start = ((s8[8388608]{0:T(1024)(128)(4,1)}), s8[4194304]{0:T(1024)(128)(4,1)S(1)}, s32[]{:S(2)}) async-start(s8[8388608]{0:T(1024)(128)(4,1)} %bitcast.1), calls=%async_computation | async-start | bytes 8388608
  24.9 5.5 %slice-start.1 = ((s8[8388608]{0:T(1024)(128)(4,1)}), s8[4194304]{0:T(1024)(128)(4,1)S(1)}, s32[]{:S(2)}) async-start(s8[8388608]{0:T(1024)(128)(4,1)} %bitcast.1), calls=%async_computation.1 | async-start | bytes 8388608
  29.0 1.4 %collective-permute-start.9 = (bf16[128,512]{1,0:T(8,128)(2,1)S(1)}, bf16[128,512]{1,0:T(8,128)(2,1)S(1)}, u32[]{:S(2)}, u32[]{:S(2)}) collective-permute-start(bf16[128,512]{1,0:T(8,128)(2,1)S(1)} %attend_last.3), channel_id=1, source_target_pairs={{0,4},{4,0},{8,12},{12,8},{16,20},{20,16},{24,28},{28,24},{32,36},... | collective-permute-start | bytes 393224 | tf_op jit(solution)/shard_map/ppermute | solution.py:417
  30.9 8.9 %collective-permute-start.10 = (bf16[128,512]{1,0:T(8,128)(2,1)S(1)}, bf16[128,512]{1,0:T(8,128)(2,1)S(1)}, u32[]{:S(2)}, u32[]{:S(2)}) collective-permute-start(bf16[128,512]{1,0:T(8,128)(2,1)S(1)} %get-tuple-element.57), channel_id=1, source_target_pairs={{0,1},{1,2},{2,3},{3,0},{4,5},{5,6},{6,7},{7,4},{8,9},{9,10},{10,1... | collective-permute-start | bytes 393224 | tf_op jit(solution)/shard_map/ppermute | solution.py:458
  32.8 6.9 %collective-permute-start.11 = (bf16[128,512]{1,0:T(8,128)(2,1)S(1)}, bf16[128,512]{1,0:T(8,128)(2,1)S(1)}, u32[]{:S(2)}, u32[]{:S(2)}) collective-permute-start(bf16[128,512]{1,0:T(8,128)(2,1)S(1)} %get-tuple-element.58), channel_id=1, source_target_pairs={{0,3},{1,0},{2,1},{3,2},{4,7},{5,4},{6,5},{7,6},{8,11},{9,8},{10,9... | collective-permute-start | bytes 393224 | tf_op jit(solution)/shard_map/ppermute | solution.py:458
  35.7 7.4 %collective-permute-start.13 = (bf16[128,512]{1,0:T(8,128)(2,1)S(1)}, bf16[128,512]{1,0:T(8,128)(2,1)S(1)}, u32[]{:S(2)}, u32[]{:S(2)}) collective-permute-start(bf16[128,512]{1,0:T(8,128)(2,1)S(1)} %get-tuple-element.60), channel_id=1, source_target_pairs={{0,1},{1,2},{2,3},{3,0},{4,5},{5,6},{6,7},{7,4},{8,9},{9,10},{10,1... | collective-permute-start | bytes 393224 | tf_op jit(solution)/shard_map/ppermute | solution.py:458
  35.8 7.3 %collective-permute-start.14 = (bf16[128,512]{1,0:T(8,128)(2,1)S(1)}, bf16[128,512]{1,0:T(8,128)(2,1)S(1)}, u32[]{:S(2)}, u32[]{:S(2)}) collective-permute-start(bf16[128,512]{1,0:T(8,128)(2,1)S(1)} %get-tuple-element.61), channel_id=1, source_target_pairs={{0,3},{1,0},{2,1},{3,2},{4,7},{5,4},{6,5},{7,6},{8,11},{9,8},{10,9... | collective-permute-start | bytes 393224 | tf_op jit(solution)/shard_map/ppermute | solution.py:458
  39.8 6.2 %collective-permute-start.12 = (bf16[128,512]{1,0:T(8,128)(2,1)S(1)}, bf16[128,512]{1,0:T(8,128)(2,1)S(1)}, u32[]{:S(2)}, u32[]{:S(2)}) collective-permute-start(bf16[128,512]{1,0:T(8,128)(2,1)S(1)} %get-tuple-element.59), channel_id=1, source_target_pairs={{0,1},{1,2},{2,3},{3,0},{4,5},{5,6},{6,7},{7,4},{8,9},{9,10},{10,1... | collective-permute-start | bytes 393224 | tf_op jit(solution)/shard_map/ppermute | solution.py:458
  41.0 5.0 %collective-permute-start.15 = (bf16[128,512]{1,0:T(8,128)(2,1)S(1)}, bf16[128,512]{1,0:T(8,128)(2,1)S(1)}, u32[]{:S(2)}, u32[]{:S(2)}) collective-permute-start(bf16[128,512]{1,0:T(8,128)(2,1)S(1)} %get-tuple-element.62), channel_id=1, source_target_pairs={{0,3},{1,0},{2,1},{3,2},{4,7},{5,4},{6,5},{7,6},{8,11},{9,8},{10,9... | collective-permute-start | bytes 393224 | tf_op jit(solution)/shard_map/ppermute | solution.py:458

commit v10 on v8

--- a/solution.py
+++ b/solution.py
@@ -363,49 +363,36 @@
     )(qs, m_in, l_in, acc_in, unit, far_a)
 
 
-def project_out(xm, xr, w_out, groups, parts, dtype):
+def project_out(xm, xr, w_out, groups, shifts, dtype):
     depth = xm.shape[1]
     width = w_out.shape[1] // groups
-    half = width // 2
 
     def body(xm, xr, w, *outs):
         core = core_index()
         own = pl.ds(pl.multiple_of(core * depth, depth), depth)
         other = pl.ds(pl.multiple_of((1 - core) * depth, depth), depth)
-        for (shift, side), out in zip(parts, outs):
+        for shift, out in zip(shifts, outs):
             group = lax.rem(lax.axis_index("head") + shift, groups)
-            cols = pl.ds(pl.multiple_of(group * width + side * half, half), half)
+            cols = pl.ds(pl.multiple_of(group * width, width), width)
             got = jnp.dot(xm[...], w[own, cols], preferred_element_type=F32)
             got += jnp.dot(xr[...], w[other, cols], preferred_element_type=F32)
             out[...] = got.astype(dtype)
 
     return call(
-        body, "project_out", (like(ROWS, half, dtype=dtype),) * len(parts), [VMEM] * 3,
-        (VMEM,) * len(parts), limit=4,
-        flops=2 * ROWS * 2 * depth * half * len(parts), moved=len(parts),
+        body, "project_out", (like(ROWS, width, dtype=dtype),) * len(shifts), [VMEM] * 3,
+        (VMEM,) * len(shifts), limit=4,
+        flops=2 * ROWS * 2 * depth * width * len(shifts), moved=2 * len(shifts),
     )(xm, xr, w_out)
 
 
-def add_body(a, b, p, q, out_a, out_b):
-    out_a[...] = (a[...] + p[...].astype(F32)).astype(BF16)
-    out_b[...] = (b[...] + q[...].astype(F32)).astype(BF16)
-
-
-def add_passing(a, b, p, q):
-    out = like(*p.shape)
-    return call(add_body, "add_passing", (out, out), [VMEM] * 4, (VMEM,) * 2, limit=2)(a, b, p, q)
-
-
-def total_body(own_a, own_b, left_a, left_b, right_a, right_b, out):
-    half = own_a.shape[1]
-    for at, pieces in ((0, (own_a, left_a, right_a)), (half, (own_b, left_b, right_b))):
-        total = pieces[0][...] + pieces[1][...].astype(F32) + pieces[2][...].astype(F32)
-        out[:, at : at + half] = total.astype(BF16)
-
-
-def add_total(*pieces):
-    rows, half = pieces[0].shape
-    return call(total_body, "add_total", like(rows, 2 * half), [VMEM] * 6, VMEM, limit=2)(*pieces)
+def total_body(own, first, second, third, out):
+    total = own[...] + first[...].astype(F32)
+    total += second[...].astype(F32) + third[...].astype(F32)
+    out[...] = total.astype(BF16)
+
+
+def add_total(own, *came):
+    return call(total_body, "add_total", like(*own.shape), [VMEM] * 4, VMEM, limit=2)(own, *came)
 
 
 def shards(tokens, w_query, w_key, w_value, w_out, doc_ids):
@@ -453,14 +440,12 @@
     def shift(value, step):
         return lax.ppermute(value, "head", [(g, (g + step) % groups) for g in range(groups)])
 
-    a2, b2 = project_out(xm, xr, w_out, groups, ((2, 0), (2, 1)), BF16)
-    pass_a, pass_b = shift(a2, 1), shift(b2, -1)
-    b1, a3 = project_out(xm, xr, w_out, groups, ((1, 1), (3, 0)), BF16)
-    left_b, right_a = shift(b1, 1), shift(a3, -1)
-    a1, b3, a0, b0 = project_out(xm, xr, w_out, groups, ((1, 0), (3, 1), (0, 0), (0, 1)), F32)
-    a1, b3 = add_passing(a1, b3, pass_a, pass_b)
-    left_a, right_b = shift(a1, 1), shift(b3, -1)
-    return add_total(a0, b0, left_a, left_b, right_a, right_b)
+    came = []
+    for step in (3, 1, 2):
+        (partial,) = project_out(xm, xr, w_out, groups, (step,), BF16)
+        came.append(shift(partial, step))
+    (own,) = project_out(xm, xr, w_out, groups, (0,), F32)
+    return add_total(own, *came)
 
 
 def solution(mesh):

time: 46.9 us -> 51.4 us (1.096)
  waiting for transfers between devices: 10.4 us -> 19.6 us
  starting transfers between devices: 21.7 us -> 16.9 us
    ppermute x6 -> x3, waiting for transfers between devices: 2.95 us -> 12.1 us  [shift(): lax.ppermute(value, 'head', [(g, (g + step) % groups) for g in range(grou...]
    ppermute x6 -> x3, starting transfers between devices: 11 us -> 6.12 us  [shift(): lax.ppermute(value, 'head', [(g, (g + step) % groups) for g in range(grou...]
  transfers between devices with their start and end apart: 16 -> 13, of which waited for: 7 -> 8; matrix products, arithmetic and copies ran while one was open for 0% -> 0% of each run, Pallas kernels for 25% -> 23%
where the time goes in v10:
time: 51.4 us; the launch traced here: 51.3 us
  waiting for transfers between devices  19.6 us (38%)
  starting transfers between devices  16.9 us (33%)
  Pallas kernels  14.7 us (29%)
    ppermute x3, waiting for transfers between devices, shift(): lax.ppermute(value, 'head', [(g, (g + step) % groups) for g in range(grou...  12.1 us
    ppermute x7, starting transfers between devices, along(): return lax.ppermute(value, 'ctx', moves)  10.2 us
    ppermute x7, waiting for transfers between devices, along(): return lax.ppermute(value, 'ctx', moves)  7.11 us
    ppermute x3, starting transfers between devices, shift(): lax.ppermute(value, 'head', [(g, (g + step) % groups) for g in range(grou...  6.12 us
    pallas_call x1, Pallas kernels, project_q(): call(q_body, 'project_q', like(width // 2 // HD, CHIP, HD), [VMEM, VMEM,...  3.1 us
    pallas_call x1, Pallas kernels, project_own(): call(own_body, 'project_own', (like(ROWS, 2 * HD), like(ROWS, depth), lik...  2.35 us
    pallas_call x2, Pallas kernels, attend_last(): call(body, 'attend_last', like(ROWS, heads * HD), [VMEM] * 6, VMEM, [pltp...  2 us
    pallas_call x4, Pallas kernels, project_out(): call(body, 'project_out', (like(ROWS, width, dtype=dtype),) * len(shifts)...  1.78 us
  transfers between devices with their start and end apart: 13, of which 8 were waited for; matrix products, arithmetic and copies ran while one was open for 0% of the time, Pallas kernels for 23%

profile of v10, /device:TPU:0, one launch (start us, length us, event | category | flops | bytes accessed | tf_op | source)
XLA Modules:
  0.0 51.3 jit_solution(6139456657232865951)
XLA Ops:
  0.0 0.5 collective-permute-start.1
  0.5 2.3 %project_own.1 = (bf16[128,256]{1,0:T(8,128)(2,1)S(1)}, bf16[128,4096]{1,0:T(8,128)(2,1)S(1)}, bf16[4096,256]{1,0:T(8,128)(2,1)S(1)}, s32[1,128]{1,0:T(1,128)S(1)}, f32[256,128]{1,0:T(8,128)S(1)}) custom-call(bf16[128,4096]{1,0:T(8,128)(2,1)} %tok.1, bf16[4096,256]{1,0:T(8,128)(2,1)} %wk.1, bf16[4096,256]{1,0:T(8,128)(2,1)} %wv.1, s32[1,128]{1,0:T(1,128)} %bitcast.4, ...), custom_call_target="tpu_custom_call" | custom-call | flops 268435456 | bytes 3145728 | tf_op jit(solution)/shard_map/project_own/pallas_call | solution.py:124
  2.9 0.5 %project_unit.1.unit = bf16[264,256]{1,0:T(8,128)(2,1)S(1)} custom-call(bf16[128,256]{1,0:T(8,128)(2,1)S(1)} %get-tuple-element.25.half, bf16[128,4096]{1,0:T(8,128)(2,1)S(1)} %collective-permute-done.came, bf16[4096,256]{1,0:T(8,128)(2,1)S(1)} %get-tuple-element.26.w, s32[1,128]{1,0:T(1,128)S(1)} %get-tuple-element.27.docs, ...), custom_call_target="tpu_custom_call" | custom-call | flops 268435456 | bytes 1048576 | tf_op jit(solution)/shard_map/project_unit/pallas_call | solution.py:153
  3.4 1.6 %collective-permute-start.2 = (bf16[264,256]{1,0:T(8,128)(2,1)S(1)}, bf16[264,256]{1,0:T(8,128)(2,1)S(1)}, u32[]{:S(2)}, u32[]{:S(2)}) collective-permute-start(bf16[264,256]{1,0:T(8,128)(2,1)S(1)} %project_unit.1.unit), channel_id=1, source_target_pairs={{0,8},{4,36},{8,16},{12,44},{16,24},{20,52},{24,32},{28,60},{32,40... | collective-permute-start | bytes 405512 | tf_op jit(solution)/shard_map/ppermute | solution.py:408
  5.1 2.7 %collective-permute-start.3 = (bf16[264,256]{1,0:T(8,128)(2,1)S(1)}, bf16[264,256]{1,0:T(8,128)(2,1)S(1)}, u32[]{:S(2)}, u32[]{:S(2)}) collective-permute-start(bf16[264,256]{1,0:T(8,128)(2,1)S(1)} %project_unit.1.unit), channel_id=1, source_target_pairs={{0,16},{4,68},{8,24},{12,76},{16,32},{20,84},{24,40},{28,92},{32,4... | collective-permute-start | bytes 405512 | tf_op jit(solution)/shard_map/ppermute | solution.py:408
  7.8 2.4 %collective-permute-start.5 = (bf16[264,256]{1,0:T(8,128)(2,1)S(1)}, bf16[264,256]{1,0:T(8,128)(2,1)S(1)}, u32[]{:S(2)}, u32[]{:S(2)}) collective-permute-start(bf16[264,256]{1,0:T(8,128)(2,1)S(1)} %project_unit.1.unit), channel_id=1, source_target_pairs={{0,24},{4,100},{8,32},{12,108},{16,40},{20,116},{24,48},{28,124},{... | collective-permute-start | bytes 405512 | tf_op jit(solution)/shard_map/ppermute | solution.py:408
  10.2 1.6 %collective-permute-start.6 = (bf16[264,256]{1,0:T(8,128)(2,1)S(1)}, bf16[264,256]{1,0:T(8,128)(2,1)S(1)}, u32[]{:S(2)}, u32[]{:S(2)}) collective-permute-start(bf16[264,256]{1,0:T(8,128)(2,1)S(1)} %project_unit.1.unit), channel_id=1, source_target_pairs={{0,32},{4,28},{8,40},{12,4},{16,48},{20,12},{24,56},{28,20},{32,64... | collective-permute-start | bytes 405512 | tf_op jit(solution)/shard_map/ppermute | solution.py:408
  11.8 1.2 %collective-permute-done.2.r1 = bf16[264,256]{1,0:T(8,128)(2,1)S(1)} collective-permute-done((bf16[264,256]{1,0:T(8,128)(2,1)S(1)}, bf16[264,256]{1,0:T(8,128)(2,1)S(1)}, u32[]{:S(2)}, u32[]{:S(2)}) %collective-permute-start.2) | collective-permute-done | bytes 135200 | tf_op jit(solution)/shard_map/ppermute | solution.py:408
  13.0 2.5 %collective-permute-done.3.r2 = bf16[264,256]{1,0:T(8,128)(2,1)S(1)} collective-permute-done((bf16[264,256]{1,0:T(8,128)(2,1)S(1)}, bf16[264,256]{1,0:T(8,128)(2,1)S(1)}, u32[]{:S(2)}, u32[]{:S(2)}) %collective-permute-start.3) | collective-permute-done | bytes 135200 | tf_op jit(solution)/shard_map/ppermute | solution.py:408
  15.8 1.2 %collective-permute-start.7 = (bf16[528,256]{1,0:T(8,128)(2,1)S(1)}, bf16[528,256]{1,0:T(8,128)(2,1)S(1)}, u32[]{:S(2)}, u32[]{:S(2)}) collective-permute-start(bf16[528,256]{1,0:T(8,128)(2,1)S(1)} %get-tuple-element.39), channel_id=1, source_target_pairs={{0,96},{4,28},{8,104},{12,4},{16,112},{20,12},{24,120},{28,20},{32... | collective-permute-start | bytes 811016 | tf_op jit(solution)/shard_map/ppermute | solution.py:408
  17.0 0.6 %collective-permute-done.6.r4.after = bf16[264,256]{1,0:T(8,128)(2,1)S(1)} collective-permute-done((bf16[264,256]{1,0:T(8,128)(2,1)S(1)}, bf16[264,256]{1,0:T(8,128)(2,1)S(1)}, u32[]{:S(2)}, u32[]{:S(2)}) %collective-permute-start.6) | collective-permute-done | bytes 135200 | tf_op jit(solution)/shard_map/ppermute | solution.py:408
  18.0 3.1 %project_q.1.qs = bf16[4,256,128]{2,1,0:T(8,128)(2,1)S(1)} custom-call(bf16[128,4096]{1,0:T(8,128)(2,1)S(1)} %get-tuple-element.24.tok, bf16[128,4096]{1,0:T(8,128)(2,1)S(1)} %collective-permute-done.came, bf16[4096,1024]{1,0:T(8,128)(2,1)} %wq.1, f32[256,128]{1,0:T(8,128)S(1)} %get-tuple-element.28.table), custom_call_target="tpu_custom_call" | custom-call | flops 1073741824 | bytes 6291456 | tf_op jit(solution)/shard_map/project_q/pallas_call | solution.py:187
  21.1 1.5 %attend_near.1 = (f32[4,256,128]{2,1,0:T(8,128)S(1)}, f32[4,256,128]{2,1,0:T(8,128)S(1)}, f32[4,256,128]{2,1,0:T(8,128)S(1)}) custom-call(bf16[4,256,128]{2,1,0:T(8,128)(2,1)S(1)} %project_q.1.qs, bf16[264,256]{1,0:T(8,128)(2,1)S(1)} %project_unit.1.unit, bf16[264,256]{1,0:T(8,128)(2,1)S(1)} %collective-permute-done.2.r1, ...), custom_call_target="tpu_custom_call" | custom-call | flops 402653184 | bytes 1048576 | tf_op jit(solution)/shard_map/attend_near/pallas_call | solution.py:301
  22.6 1.1 %collective-permute-done.4.far_b = bf16[528,256]{1,0:T(8,128)(2,1)S(1)} collective-permute-done((bf16[528,256]{1,0:T(8,128)(2,1)S(1)}, bf16[528,256]{1,0:T(8,128)(2,1)S(1)}, u32[]{:S(2)}, u32[]{:S(2)}) %collective-permute-start.4) | collective-permute-done | bytes 270368 | tf_op jit(solution)/shard_map/ppermute | solution.py:408
  23.7 1.2 %attend_early.1 = (f32[4,256,128]{2,1,0:T(8,128)S(1)}, f32[4,256,128]{2,1,0:T(8,128)S(1)}, f32[4,256,128]{2,1,0:T(8,128)S(1)}) custom-call(bf16[4,256,128]{2,1,0:T(8,128)(2,1)S(1)} %project_q.1.qs, f32[4,256,128]{2,1,0:T(8,128)S(1)} %get-tuple-element.32.m_in, f32[4,256,128]{2,1,0:T(8,128)S(1)} %get-tuple-element.33.l_in, ...), custom_call_target="tpu_custom_call" | custom-call | flops 2147483648 | bytes 1048576 | tf_op jit(solution)/shard_map/attend_early/pallas_call | solution.py:318
  24.9 1.3 %attend_middle.1 = (f32[4,256,128]{2,1,0:T(8,128)S(1)}, f32[4,256,128]{2,1,0:T(8,128)S(1)}, f32[4,256,128]{2,1,0:T(8,128)S(1)}) custom-call(bf16[4,256,128]{2,1,0:T(8,128)(2,1)S(1)} %project_q.1.qs, f32[4,256,128]{2,1,0:T(8,128)S(1)} %get-tuple-element.36.m_in, f32[4,256,128]{2,1,0:T(8,128)S(1)} %get-tuple-element.37.l_in, ...), custom_call_target="tpu_custom_call" | custom-call | flops 2147483648 | bytes 1048576 | tf_op jit(solution)/shard_map/attend_middle/pallas_call | solution.py:338
  26.2 1.8 %collective-permute-done.8.far_a = bf16[792,256]{1,0:T(8,128)(2,1)S(1)} collective-permute-done((bf16[792,256]{1,0:T(8,128)(2,1)S(1)}, bf16[792,256]{1,0:T(8,128)(2,1)S(1)}, u32[]{:S(2)}, u32[]{:S(2)}) %collective-permute-start.8) | collective-permute-done | bytes 405536 | tf_op jit(solution)/shard_map/ppermute | solution.py:408
  27.9 1.0 %attend_last.3 = bf16[128,512]{1,0:T(8,128)(2,1)S(1)} custom-call(bf16[4,256,128]{2,1,0:T(8,128)(2,1)S(1)} %project_q.1.qs, f32[4,256,128]{2,1,0:T(8,128)S(1)} %get-tuple-element.40.m_in, f32[4,256,128]{2,1,0:T(8,128)S(1)} %get-tuple-element.41.l_in, f32[4,256,128]{2,1,0:T(8,128)S(1)} %get-tuple-element.42.acc_in, bf16[264,256]{1,0:T(8,128)(2,1)S(1)} %project_unit.1.unit, ...), custom_call_target="tpu_custom_call" | custom-call | flops 201326592 | bytes 1048576 | tf_op jit(solution)/shard_map/attend_last/pallas_call | solution.py:359
  29.0 1.0 %attend_last.2.xm = bf16[128,512]{1,0:T(8,128)(2,1)S(1)} custom-call(bf16[4,256,128]{2,1,0:T(8,128)(2,1)S(1)} %project_q.1.qs, f32[4,256,128]{2,1,0:T(8,128)S(1)} %get-tuple-element.40.m_in, f32[4,256,128]{2,1,0:T(8,128)S(1)} %get-tuple-element.41.l_in, f32[4,256,128]{2,1,0:T(8,128)S(1)} %get-tuple-element.42.acc_in, bf16[264,256]{1,0:T(8,128)(2,1)S(1)} %project_unit.1.unit, ...), custom_call_target="tpu_custom_call" | custom-call | flops 201326592 | bytes 1048576 | tf_op jit(solution)/shard_map/attend_last/pallas_call | solution.py:359
  30.8 4.1 %collective-permute-start.10 = (bf16[128,1024]{1,0:T(8,128)(2,1)S(1)}, bf16[128,1024]{1,0:T(8,128)(2,1)S(1)}, u32[]{:S(2)}, u32[]{:S(2)}) collective-permute-start(bf16[128,1024]{1,0:T(8,128)(2,1)S(1)} %project_out.5), channel_id=1, source_target_pairs={{0,3},{1,0},{2,1},{3,2},{4,7},{5,4},{6,5},{7,6},{8,11},{9,8},{10,9... | collective-permute-start | bytes 786440 | tf_op jit(solution)/shard_map/ppermute | solution.py:441
  36.0 1.9 %collective-permute-start.12 = (bf16[128,1024]{1,0:T(8,128)(2,1)S(1)}, bf16[128,1024]{1,0:T(8,128)(2,1)S(1)}, u32[]{:S(2)}, u32[]{:S(2)}) collective-permute-start(bf16[128,1024]{1,0:T(8,128)(2,1)S(1)} %project_out.7), channel_id=1, source_target_pairs={{0,2},{1,3},{2,0},{3,1},{4,6},{5,7},{6,4},{7,5},{8,10},{9,11},{10,... | collective-permute-start | bytes 786440 | tf_op jit(solution)/shard_map/ppermute | solution.py:441
  38.3 8.2 %collective-permute-done.10.first = bf16[128,1024]{1,0:T(8,128)(2,1)S(1)} collective-permute-done((bf16[128,1024]{1,0:T(8,128)(2,1)S(1)}, bf16[128,1024]{1,0:T(8,128)(2,1)S(1)}, u32[]{:S(2)}, u32[]{:S(2)}) %collective-permute-start.10) | collective-permute-done | bytes 262176 | tf_op jit(solution)/shard_map/ppermute | solution.py:441
  46.5 3.9 %collective-permute-done.11.second = bf16[128,1024]{1,0:T(8,128)(2,1)S(1)} collective-permute-done((bf16[128,1024]{1,0:T(8,128)(2,1)S(1)}, bf16[128,1024]{1,0:T(8,128)(2,1)S(1)}, u32[]{:S(2)}, u32[]{:S(2)}) %collective-permute-start.11) | collective-permute-done | bytes 262176 | tf_op jit(solution)/shard_map/ppermute | solution.py:441
  50.5 0.8 %add_total.1 = bf16[128,1024]{1,0:T(8,128)(2,1)} custom-call(f32[128,1024]{1,0:T(8,128)S(1)} %project_out.4.own, bf16[128,1024]{1,0:T(8,128)(2,1)S(1)} %collective-permute-done.10.first, bf16[128,1024]{1,0:T(8,128)(2,1)S(1)} %collective-permute-done.11.second, bf16[128,1024]{1,0:T(8,128)(2,1)S(1)} %collective-permute-done.12.third), custom_call_target="tpu_custom_call" | custom-call | bytes 1048576 | tf_op jit(solution)/shard_map/add_total/pallas_call | solution.py:395
  (22 shorter events, 3.0 us)
Async XLA Ops:
  0.0 2.9 %collective-permute-start = (bf16[128,4096]{1,0:T(8,128)(2,1)}, bf16[128,4096]{1,0:T(8,128)(2,1)S(1)}, u32[]{:S(2)}, u32[]{:S(2)}) collective-permute-start(bf16[128,4096]{1,0:T(8,128)(2,1)} %tok.1), channel_id=1, source_target_pairs={{0,4},{4,0},{8,12},{12,8},{16,20},{20,16},{24,28},{28,24},{32,36},... | collective-permute-start | bytes 3145736 | tf_op jit(solution)/shard_map/ppermute | solution.py:404
  0.0 2.9 %collective-permute-start.1 = (s32[1,128]{1,0:T(1,128)}, s32[1,128]{1,0:T(1,128)S(1)}, u32[]{:S(2)}, u32[]{:S(2)}) collective-permute-start(s32[1,128]{1,0:T(1,128)} %bitcast.3), channel_id=1, source_target_pairs={{0,4},{4,0},{8,12},{12,8},{16,20},{20,16},{24,28},{28,24},{32,36},... | collective-permute-start | bytes 1544 | tf_op jit(solution)/shard_map/ppermute | solution.py:404
  3.4 9.6 %collective-permute-start.2 = (bf16[264,256]{1,0:T(8,128)(2,1)S(1)}, bf16[264,256]{1,0:T(8,128)(2,1)S(1)}, u32[]{:S(2)}, u32[]{:S(2)}) collective-permute-start(bf16[264,256]{1,0:T(8,128)(2,1)S(1)} %project_unit.1.unit), channel_id=1, source_target_pairs={{0,8},{4,36},{8,16},{12,44},{16,24},{20,52},{24,32},{28,60},{32,40... | collective-permute-start | bytes 405512 | tf_op jit(solution)/shard_map/ppermute | solution.py:408
  5.1 10.4 %collective-permute-start.3 = (bf16[264,256]{1,0:T(8,128)(2,1)S(1)}, bf16[264,256]{1,0:T(8,128)(2,1)S(1)}, u32[]{:S(2)}, u32[]{:S(2)}) collective-permute-start(bf16[264,256]{1,0:T(8,128)(2,1)S(1)} %project_unit.1.unit), channel_id=1, source_target_pairs={{0,16},{4,68},{8,24},{12,76},{16,32},{20,84},{24,40},{28,92},{32,4... | collective-permute-start | bytes 405512 | tf_op jit(solution)/shard_map/ppermute | solution.py:408
  7.8 9.2 %collective-permute-start.5 = (bf16[264,256]{1,0:T(8,128)(2,1)S(1)}, bf16[264,256]{1,0:T(8,128)(2,1)S(1)}, u32[]{:S(2)}, u32[]{:S(2)}) collective-permute-start(bf16[264,256]{1,0:T(8,128)(2,1)S(1)} %project_unit.1.unit), channel_id=1, source_target_pairs={{0,24},{4,100},{8,32},{12,108},{16,40},{20,116},{24,48},{28,124},{... | collective-permute-start | bytes 405512 | tf_op jit(solution)/shard_map/ppermute | solution.py:408
  10.2 7.3 %collective-permute-start.6 = (bf16[264,256]{1,0:T(8,128)(2,1)S(1)}, bf16[264,256]{1,0:T(8,128)(2,1)S(1)}, u32[]{:S(2)}, u32[]{:S(2)}) collective-permute-start(bf16[264,256]{1,0:T(8,128)(2,1)S(1)} %project_unit.1.unit), channel_id=1, source_target_pairs={{0,32},{4,28},{8,40},{12,4},{16,48},{20,12},{24,56},{28,20},{32,64... | collective-permute-start | bytes 405512 | tf_op jit(solution)/shard_map/ppermute | solution.py:408
  15.6 8.1 %collective-permute-start.4 = (bf16[528,256]{1,0:T(8,128)(2,1)S(1)}, bf16[528,256]{1,0:T(8,128)(2,1)S(1)}, u32[]{:S(2)}, u32[]{:S(2)}) collective-permute-start(bf16[528,256]{1,0:T(8,128)(2,1)S(1)} %get-tuple-element.35), channel_id=1, source_target_pairs={{0,64},{4,20},{8,72},{12,28},{16,80},{20,4},{24,88},{28,12},{32,96... | collective-permute-start | bytes 811016 | tf_op jit(solution)/shard_map/ppermute | solution.py:408
  15.8 9.1 %collective-permute-start.7 = (bf16[528,256]{1,0:T(8,128)(2,1)S(1)}, bf16[528,256]{1,0:T(8,128)(2,1)S(1)}, u32[]{:S(2)}, u32[]{:S(2)}) collective-permute-start(bf16[528,256]{1,0:T(8,128)(2,1)S(1)} %get-tuple-element.39), channel_id=1, source_target_pairs={{0,96},{4,28},{8,104},{12,4},{16,112},{20,12},{24,120},{28,20},{32... | collective-permute-start | bytes 811016 | tf_op jit(solution)/shard_map/ppermute | solution.py:408
  17.6 10.3 %collective-permute-start.8 = (bf16[792,256]{1,0:T(8,128)(2,1)S(1)}, bf16[792,256]{1,0:T(8,128)(2,1)S(1)}, u32[]{:S(2)}, u32[]{:S(2)}) collective-permute-start(bf16[792,256]{1,0:T(8,128)(2,1)S(1)} %bundle_row.1), channel_id=1, source_target_pairs={{0,32},{4,12},{8,40},{12,20},{16,48},{20,28},{24,56},{28,4},{32,64... | collective-permute-start | bytes 1216520 | tf_op jit(solution)/shard_map/ppermute | solution.py:408
  23.7 6.7 %slice-start = ((s8[8388608]{0:T(1024)(128)(4,1)}), s8[4194304]{0:T(1024)(128)(4,1)S(1)}, s32[]{:S(2)}) async-start(s8[8388608]{0:T(1024)(128)(4,1)} %bitcast.1), calls=%async_computation | async-start | bytes 8388608
  24.9 5.5 %slice-start.1 = ((s8[8388608]{0:T(1024)(128)(4,1)}), s8[4194304]{0:T(1024)(128)(4,1)S(1)}, s32[]{:S(2)}) async-start(s8[8388608]{0:T(1024)(128)(4,1)} %bitcast.1), calls=%async_computation.1 | async-start | bytes 8388608
  29.0 1.4 %collective-permute-start.9 = (bf16[128,512]{1,0:T(8,128)(2,1)S(1)}, bf16[128,512]{1,0:T(8,128)(2,1)S(1)}, u32[]{:S(2)}, u32[]{:S(2)}) collective-permute-start(bf16[128,512]{1,0:T(8,128)(2,1)S(1)} %attend_last.3), channel_id=1, source_target_pairs={{0,4},{4,0},{8,12},{12,8},{16,20},{20,16},{24,28},{28,24},{32,36},... | collective-permute-start | bytes 393224 | tf_op jit(solution)/shard_map/ppermute | solution.py:404
  30.8 15.7 %collective-permute-start.10 = (bf16[128,1024]{1,0:T(8,128)(2,1)S(1)}, bf16[128,1024]{1,0:T(8,128)(2,1)S(1)}, u32[]{:S(2)}, u32[]{:S(2)}) collective-permute-start(bf16[128,1024]{1,0:T(8,128)(2,1)S(1)} %project_out.5), channel_id=1, source_target_pairs={{0,3},{1,0},{2,1},{3,2},{4,7},{5,4},{6,5},{7,6},{8,11},{9,8},{10,9... | collective-permute-start | bytes 786440 | tf_op jit(solution)/shard_map/ppermute | solution.py:441
  35.4 15.0 %collective-permute-start.11 = (bf16[128,1024]{1,0:T(8,128)(2,1)S(1)}, bf16[128,1024]{1,0:T(8,128)(2,1)S(1)}, u32[]{:S(2)}, u32[]{:S(2)}) collective-permute-start(bf16[128,1024]{1,0:T(8,128)(2,1)S(1)} %project_out.6), channel_id=1, source_target_pairs={{0,1},{1,2},{2,3},{3,0},{4,5},{5,6},{6,7},{7,4},{8,9},{9,10},{10,1... | collective-permute-start | bytes 786440 | tf_op jit(solution)/shard_map/ppermute | solution.py:441
  36.0 14.5 %collective-permute-start.12 = (bf16[128,1024]{1,0:T(8,128)(2,1)S(1)}, bf16[128,1024]{1,0:T(8,128)(2,1)S(1)}, u32[]{:S(2)}, u32[]{:S(2)}) collective-permute-start(bf16[128,1024]{1,0:T(8,128)(2,1)S(1)} %project_out.7), channel_id=1, source_target_pairs={{0,2},{1,3},{2,0},{3,1},{4,6},{5,7},{6,4},{7,5},{8,10},{9,11},{10,... | collective-permute-start | bytes 786440 | tf_op jit(solution)/shard_map/ppermute | solution.py:441

commit v11 on v8

--- a/solution.py
+++ b/solution.py
@@ -1,3 +1,4 @@
+import functools
 import math
 
 import jax
@@ -159,10 +160,10 @@
 Q_PARTS = 4
 
 
-def q_body(tok, came, wq, table, out, wq_s, sems):
-    half = wq.shape[1] // 2
+def q_body(side, tok, came, wq, table, out, wq_s, sems):
+    half = wq_s.shape[1]
     part = wq.shape[0] // Q_PARTS
-    cols = pl.ds(pl.multiple_of(core_index() * half, half), half)
+    cols = pl.ds(pl.multiple_of((2 * core_index() + side) * half, half), half)
     copies = []
     for i in range(Q_PARTS):
         rows = pl.ds(i * part, part)
@@ -182,12 +183,12 @@
             out[h, span, :] = rot(got[side][:, h * HD : (h + 1) * HD]).astype(BF16)
 
 
-def project_q(tokens, came, w_query, table):
+def project_q(tokens, came, w_query, table, side):
     depth, width = w_query.shape
     return call(
-        q_body, "project_q", like(width // 2 // HD, CHIP, HD), [VMEM, VMEM, HBM, VMEM], VMEM,
-        [pltpu.VMEM((depth, width // 2), BF16), pltpu.SemaphoreType.DMA((Q_PARTS,))],
-        limit=8, flops=2 * CHIP * depth * width // 2, moved=6,
+        functools.partial(q_body, side), "project_q", like(width // 4 // HD, CHIP, HD), [VMEM, VMEM, HBM, VMEM], VMEM,
+        [pltpu.VMEM((depth, width // 4), BF16), pltpu.SemaphoreType.DMA((Q_PARTS,))],
+        limit=8, flops=2 * CHIP * depth * width // 4, moved=3,
     )(tokens, came, w_query, table)
 
 
@@ -206,19 +207,16 @@
         out[i * UNIT : (i + 1) * UNIT, :] = slots[skip + i]
 
 
-def pairs_body(unit, r1, r2, out_b, out_c, slots):
-    for i, src in enumerate((unit, r1, r2)):
-        slots[i] = src[...]
-    fill(out_b, slots, 2, 0)
-    fill(out_c, slots, 1, 0)
-
-
-def bundle_pairs(unit, r1, r2):
-    pair = like(2 * UNIT, 2 * HD)
-    return call(
-        pairs_body, "bundle_pairs", (pair, pair), [VMEM] * 3, (VMEM,) * 2,
+def bundle_pair(unit, r1, r2, late, after):
+    def body(unit, r1, r2, after, out, slots):
+        for i, src in enumerate((unit, r1, r2)):
+            slots[i] = src[...]
+        fill(out, slots, late, 0)
+
+    return call(
+        body, "bundle_pair", like(2 * UNIT, 2 * HD), [VMEM] * 4, VMEM,
         [pltpu.VMEM((3, UNIT, 2 * HD), BF16)], limit=2,
-    )(unit, r1, r2)
+    )(unit, r1, r2, after)
 
 
 def row_body(unit, r1, r2, r3, after, out_a, slots):
@@ -276,14 +274,20 @@
     return [src[i * UNIT : (i + 1) * UNIT, :] for i in range(src.shape[0] // UNIT)]
 
 
-def near_body(qs, unit, r1, r2, m_s, l_s, acc):
+def query_of(halves):
+    per = halves[0].shape[0]
+    return lambda h: halves[h // per][h % per]
+
+
+def near_body(qa, qb, unit, r1, r2, m_s, l_s, acc):
+    query = query_of((qa, qb))
     tags, q_tag = tags_of(unit)
     rows = lax.broadcasted_iota(jnp.int32, (CHIP, CHIP), 0)
     cols = lax.broadcasted_iota(jnp.int32, (CHIP, CHIP), 1)
     bias = jnp.where((tags[0:1, :] == q_tag) & (cols <= rows), 0.0, -1e30)
     keys, values = unit[:CHIP, :HD], with_ones(unit[:CHIP, HD:])
-    for h in range(qs.shape[0]):
-        s = lax.dot_general(qs[h], keys, CONTRACT, preferred_element_type=F32)
+    for h in range(m_s.shape[0]):
+        s = lax.dot_general(query(h), keys, CONTRACT, preferred_element_type=F32)
         s = s * SCALE + bias
         top = jnp.max(s, axis=1, keepdims=True)
         got = jnp.dot(jnp.exp2(s - top).astype(BF16), values, preferred_element_type=F32)
@@ -292,64 +296,65 @@
         acc[h] = got[:, :HD]
     state = (m_s, l_s, acc)
     units = [src[...] for src in (r1, r2)]
-    add_units(lambda h: qs[h], units, NEAR, q_tag, lambda h: [ref[h] for ref in state], state)
+    add_units(query, units, NEAR, q_tag, lambda h: [ref[h] for ref in state], state)
 
 
 def attend_near(qs, unit, r1, r2):
-    heads = qs.shape[0]
+    heads = 2 * qs[0].shape[0]
     state = like(heads, CHIP, HD, dtype=F32)
     return call(
-        near_body, "attend_near", (state, state, state), [VMEM] * 4, (VMEM,) * 3, limit=8,
+        near_body, "attend_near", (state, state, state), [VMEM] * 5, (VMEM,) * 3, limit=8,
         flops=12 * heads * CHIP * CHIP * HD, exps=3 * heads * CHIP * CHIP,
-    )(qs, unit, r1, r2)
-
-
-def early_body(qs, m_in, l_in, acc_in, unit, far_b, m_s, l_s, acc):
+    )(*qs, unit, r1, r2)
+
+
+def early_body(qa, qb, m_in, l_in, acc_in, unit, far_b, m_s, l_s, acc):
     before = (m_in, l_in, acc_in)
     add_units(
-        lambda h: qs[h], parts(far_b), EARLY, tags_of(unit)[1],
+        query_of((qa, qb)), parts(far_b), EARLY, tags_of(unit)[1],
         lambda h: [ref[h] for ref in before], (m_s, l_s, acc),
     )
 
 
 def attend_early(qs, m_in, l_in, acc_in, unit, far_b):
-    heads = qs.shape[0]
+    heads = 2 * qs[0].shape[0]
     state = like(heads, CHIP, HD, dtype=F32)
     return call(
-        early_body, "attend_early", (state,) * 3, [VMEM] * 6, (VMEM,) * 3, limit=8,
+        early_body, "attend_early", (state,) * 3, [VMEM] * 7, (VMEM,) * 3, limit=8,
         flops=64 * heads * CHIP * CHIP * HD, exps=2 * heads * CHIP * CHIP,
-    )(qs, m_in, l_in, acc_in, unit, far_b)
-
-
-def middle_body(qs, m_in, l_in, acc_in, unit, r3, r4, far_c, m_s, l_s, acc):
+    )(*qs, m_in, l_in, acc_in, unit, far_b)
+
+
+def middle_body(qa, qb, m_in, l_in, acc_in, unit, r3, r4, far_c, m_s, l_s, acc):
     before = (m_in, l_in, acc_in)
     even = core_index() == 0
     third, fourth = parts(far_c)
     units = [jnp.where(even, r3[...], third), jnp.where(even, r4[...], fourth)]
     add_units(
-        lambda h: qs[h], units, MIDDLE, tags_of(unit)[1],
+        query_of((qa, qb)), units, MIDDLE, tags_of(unit)[1],
         lambda h: [ref[h] for ref in before], (m_s, l_s, acc),
     )
 
 
 def attend_middle(qs, m_in, l_in, acc_in, unit, r3, r4, far_c):
-    heads = qs.shape[0]
+    heads = 2 * qs[0].shape[0]
     state = like(heads, CHIP, HD, dtype=F32)
     return call(
-        middle_body, "attend_middle", (state,) * 3, [VMEM] * 8, (VMEM,) * 3, limit=8,
-        flops=64 * heads * CHIP * CHIP * HD, exps=2 * heads * CHIP * CHIP,
-    )(qs, m_in, l_in, acc_in, unit, r3, r4, far_c)
+        middle_body, "attend_middle", (state,) * 3, [VMEM] * 9, (VMEM,) * 3, limit=8,
+        flops=8 * heads * CHIP * CHIP * HD, exps=2 * heads * CHIP * CHIP,
+    )(*qs, m_in, l_in, acc_in, unit, r3, r4, far_c)
 
 
 def attend_last(side, qs, m_in, l_in, acc_in, unit, far_a):
-    heads = qs.shape[0]
-
-    def body(qs, m_in, l_in, acc_in, unit, far_a, out, tag_s, m_s, l_s, acc):
+    heads = 2 * qs[0].shape[0]
+
+    def body(qa, qb, m_in, l_in, acc_in, unit, far_a, out, tag_s, m_s, l_s, acc):
         rows = halves()[side]
+        per = qa.shape[0]
         before = (m_in, l_in, acc_in)
         tag_s[...] = jnp.broadcast_to(tags_of(unit)[1], (CHIP, HD))
         add_units(
-            lambda h: qs[h, rows, :], parts(far_a), LAST, tag_s[rows, :][:, 0:1],
+            lambda h: (qa, qb)[h // per][h % per, rows, :], parts(far_a), LAST, tag_s[rows, :][:, 0:1],
             lambda h: [ref[h, rows, :] for ref in before], (m_s, l_s, acc),
         )
         for h in range(heads):
@@ -357,10 +362,10 @@
 
     state = pltpu.VMEM((heads, ROWS, HD), F32)
     return call(
-        body, "attend_last", like(ROWS, heads * HD), [VMEM] * 6, VMEM,
+        body, "attend_last", like(ROWS, heads * HD), [VMEM] * 7, VMEM,
         [pltpu.VMEM((CHIP, HD), F32), state, state, state],
         limit=8, flops=4 * heads * ROWS * 3 * CHIP * HD, exps=heads * ROWS * 3 * CHIP,
-    )(qs, m_in, l_in, acc_in, unit, far_a)
+    )(*qs, m_in, l_in, acc_in, unit, far_a)
 
 
 def project_out(xm, xr, w_out, groups, parts, dtype):
@@ -438,12 +443,13 @@
     r2 = along(unit, ahead(2), ahead(8))
     r3 = along(unit, ahead(3), ahead(12))
     r4 = along(unit, ahead(4), in_row(3))
-    r1, r2, came = lax.optimization_barrier((r1, r2, came))
-    out_b, out_c = bundle_pairs(unit, r1, r2)
-    far_b = along(out_b, ahead(8), in_row(2))
-    far_c = along(out_c, ahead(12), in_row(3))
-    far_a = along(bundle_row(unit, r1, r2, r3, r4), ahead(4), in_row(1))
-    qs = project_q(tokens, came, w_query, table)
+    qs = project_q(tokens, came, w_query, table, 0)
+    r1, r2, came, qs = lax.optimization_barrier((r1, r2, came, qs))
+    far_b = along(bundle_pair(unit, r1, r2, 2, unit), ahead(8), in_row(2))
+    out_a = bundle_row(unit, r1, r2, r3, r4)
+    far_a = along(out_a, ahead(4), in_row(1))
+    far_c = along(bundle_pair(unit, r1, r2, 1, out_a), ahead(12), in_row(3))
+    qs = (qs, project_q(tokens, came, w_query, table, 1))
     state = attend_near(qs, unit, r1, r2)
     state = attend_early(qs, *state, unit, far_b)
     state = attend_middle(qs, *state, unit, r3, r4, far_c)

time: 46.9 us -> 47.1 us (level)
  waiting for transfers between devices: 10.4 us -> 7.21 us
  starting transfers between devices: 21.7 us -> 23.6 us
  Pallas kernels: 14.5 us -> 15.9 us
    ppermute x7, waiting for transfers between devices: 7.13 us -> 3.79 us  [along(): return lax.ppermute(value, 'ctx', moves)]
    ppermute x7, starting transfers between devices: 10.1 us -> 12 us  [along(): return lax.ppermute(value, 'ctx', moves)]
    pallas_call x7 -> x9, Pallas kernels: 9.14 us -> 10.5 us  [the longest x2 4.41 us: project_q(): call(functools.partial(q_body, side), 'project_q', like(width // 4 // HD,...]
  transfers between devices with their start and end apart: 16 -> 16, of which waited for: 7 -> 7; matrix products, arithmetic and copies ran while one was open for 0% -> 0% of each run, Pallas kernels for 25% -> 28%
where the time goes in v11:
time: 47.1 us; the launch traced here: 46.9 us
  starting transfers between devices  23.6 us (50%)
  Pallas kernels  15.9 us (34%)
  waiting for transfers between devices  7.21 us (15%)
    ppermute x7, starting transfers between devices, along(): return lax.ppermute(value, 'ctx', moves)  12 us
    ppermute x6, starting transfers between devices, shift(): lax.ppermute(value, 'head', [(g, (g + step) % groups) for g in range(grou...  11 us
    pallas_call x2, Pallas kernels, project_q(): call(functools.partial(q_body, side), 'project_q', like(width // 4 // HD,...  4.41 us
    ppermute x7, waiting for transfers between devices, along(): return lax.ppermute(value, 'ctx', moves)  3.79 us
    ppermute x6, waiting for transfers between devices, shift(): lax.ppermute(value, 'head', [(g, (g + step) % groups) for g in range(grou...  3.05 us
    pallas_call x1, Pallas kernels, project_own(): call(own_body, 'project_own', (like(ROWS, 2 * HD), like(ROWS, depth), lik...  2.35 us
    pallas_call x2, Pallas kernels, attend_last(): call(body, 'attend_last', like(ROWS, heads * HD), [VMEM] * 7, VMEM, [pltp...  1.94 us
    pallas_call x3, Pallas kernels, project_out(): call(body, 'project_out', (like(ROWS, half, dtype=dtype),) * len(parts),...  1.64 us
  transfers between devices with their start and end apart: 16, of which 7 were waited for; matrix products, arithmetic and copies ran while one was open for 0% of the time, Pallas kernels for 28%

profile of v11, /device:TPU:0, one launch (start us, length us, event | category | flops | bytes accessed | tf_op | source)
XLA Modules:
  0.0 46.9 jit_solution(1020002909979341906)
XLA Ops:
  0.5 2.4 %project_own.1 = (bf16[128,256]{1,0:T(8,128)(2,1)S(1)}, bf16[128,4096]{1,0:T(8,128)(2,1)S(1)}, bf16[4096,256]{1,0:T(8,128)(2,1)S(1)}, s32[1,128]{1,0:T(1,128)S(1)}, f32[256,128]{1,0:T(8,128)S(1)}) custom-call(bf16[128,4096]{1,0:T(8,128)(2,1)} %tok.1, bf16[4096,256]{1,0:T(8,128)(2,1)} %wk.1, bf16[4096,256]{1,0:T(8,128)(2,1)} %wv.1, s32[1,128]{1,0:T(1,128)} %bitcast.4, ...), custom_call_target="tpu_custom_call" | custom-call | flops 268435456 | bytes 3145728 | tf_op jit(solution)/shard_map/project_own/pallas_call | solution.py:125
  3.4 1.6 %collective-permute-start.2 = (bf16[264,256]{1,0:T(8,128)(2,1)S(1)}, bf16[264,256]{1,0:T(8,128)(2,1)S(1)}, u32[]{:S(2)}, u32[]{:S(2)}) collective-permute-start(bf16[264,256]{1,0:T(8,128)(2,1)S(1)} %project_unit.1.unit.after), channel_id=1, source_target_pairs={{0,8},{4,36},{8,16},{12,44},{16,24},{20,52},{24,32},{28,60},{32,40... | collective-permute-start | bytes 405512 | tf_op jit(solution)/shard_map/ppermute | solution.py:426
  5.1 2.7 %collective-permute-start.3 = (bf16[264,256]{1,0:T(8,128)(2,1)S(1)}, bf16[264,256]{1,0:T(8,128)(2,1)S(1)}, u32[]{:S(2)}, u32[]{:S(2)}) collective-permute-start(bf16[264,256]{1,0:T(8,128)(2,1)S(1)} %project_unit.1.unit.after), channel_id=1, source_target_pairs={{0,16},{4,68},{8,24},{12,76},{16,32},{20,84},{24,40},{28,92},{32,4... | collective-permute-start | bytes 405512 | tf_op jit(solution)/shard_map/ppermute | solution.py:426
  7.8 2.4 %collective-permute-start.5 = (bf16[264,256]{1,0:T(8,128)(2,1)S(1)}, bf16[264,256]{1,0:T(8,128)(2,1)S(1)}, u32[]{:S(2)}, u32[]{:S(2)}) collective-permute-start(bf16[264,256]{1,0:T(8,128)(2,1)S(1)} %project_unit.1.unit.after), channel_id=1, source_target_pairs={{0,24},{4,100},{8,32},{12,108},{16,40},{20,116},{24,48},{28,124},{... | collective-permute-start | bytes 405512 | tf_op jit(solution)/shard_map/ppermute | solution.py:426
  10.2 1.6 %collective-permute-start.6 = (bf16[264,256]{1,0:T(8,128)(2,1)S(1)}, bf16[264,256]{1,0:T(8,128)(2,1)S(1)}, u32[]{:S(2)}, u32[]{:S(2)}) collective-permute-start(bf16[264,256]{1,0:T(8,128)(2,1)S(1)} %project_unit.1.unit.after), channel_id=1, source_target_pairs={{0,32},{4,28},{8,40},{12,4},{16,48},{20,12},{24,56},{28,20},{32,64... | collective-permute-start | bytes 405512 | tf_op jit(solution)/shard_map/ppermute | solution.py:426
  11.8 2.2 %project_q.2.qa = bf16[2,256,128]{2,1,0:T(8,128)(2,1)S(1)} custom-call(bf16[128,4096]{1,0:T(8,128)(2,1)S(1)} %get-tuple-element.37.tok, bf16[128,4096]{1,0:T(8,128)(2,1)S(1)} %collective-permute-done.came, bf16[4096,1024]{1,0:T(8,128)(2,1)} %wq.3, f32[256,128]{1,0:T(8,128)S(1)} %get-tuple-element.36.table), custom_call_target="tpu_custom_call" | custom-call | flops 536870912 | bytes 3145728 | tf_op jit(solution)/shard_map/project_q/pallas_call | solution.py:188
  14.0 1.5 %collective-permute-done.3.r2 = bf16[264,256]{1,0:T(8,128)(2,1)S(1)} collective-permute-done((bf16[264,256]{1,0:T(8,128)(2,1)S(1)}, bf16[264,256]{1,0:T(8,128)(2,1)S(1)}, u32[]{:S(2)}, u32[]{:S(2)}) %collective-permute-start.3) | collective-permute-done | bytes 135200 | tf_op jit(solution)/shard_map/ppermute | solution.py:426
  16.2 1.3 %collective-permute-done.6.after.r4 = bf16[264,256]{1,0:T(8,128)(2,1)S(1)} collective-permute-done((bf16[264,256]{1,0:T(8,128)(2,1)S(1)}, bf16[264,256]{1,0:T(8,128)(2,1)S(1)}, u32[]{:S(2)}, u32[]{:S(2)}) %collective-permute-start.6) | collective-permute-done | bytes 135200 | tf_op jit(solution)/shard_map/ppermute | solution.py:426
  17.9 3.2 %collective-permute-start.7 = (bf16[528,256]{1,0:T(8,128)(2,1)S(1)}, bf16[528,256]{1,0:T(8,128)(2,1)S(1)}, u32[]{:S(2)}, u32[]{:S(2)}) collective-permute-start(bf16[528,256]{1,0:T(8,128)(2,1)S(1)} %bundle_pair.3), channel_id=1, source_target_pairs={{0,96},{4,28},{8,104},{12,4},{16,112},{20,12},{24,120},{28,20},{32... | collective-permute-start | bytes 811016 | tf_op jit(solution)/shard_map/ppermute | solution.py:426
  21.1 2.2 %project_q.3.qb = bf16[2,256,128]{2,1,0:T(8,128)(2,1)S(1)} custom-call(bf16[128,4096]{1,0:T(8,128)(2,1)S(1)} %get-tuple-element.37.tok, bf16[128,4096]{1,0:T(8,128)(2,1)S(1)} %collective-permute-done.came, bf16[4096,1024]{1,0:T(8,128)(2,1)} %wq.3, f32[256,128]{1,0:T(8,128)S(1)} %get-tuple-element.36.table), custom_call_target="tpu_custom_call" | custom-call | flops 536870912 | bytes 3145728 | tf_op jit(solution)/shard_map/project_q/pallas_call | solution.py:188
  23.3 1.6 %attend_near.1 = (f32[4,256,128]{2,1,0:T(8,128)S(1)}, f32[4,256,128]{2,1,0:T(8,128)S(1)}, f32[4,256,128]{2,1,0:T(8,128)S(1)}) custom-call(bf16[2,256,128]{2,1,0:T(8,128)(2,1)S(1)} %project_q.2.qa, bf16[2,256,128]{2,1,0:T(8,128)(2,1)S(1)} %project_q.3.qb, bf16[264,256]{1,0:T(8,128)(2,1)S(1)} %project_unit.1.unit.after, ...), custom_call_target="tpu_custom_call" | custom-call | flops 402653184 | bytes 1048576 | tf_op jit(solution)/shard_map/attend_near/pallas_call | solution.py:305
  24.9 1.2 %attend_early.1 = (f32[4,256,128]{2,1,0:T(8,128)S(1)}, f32[4,256,128]{2,1,0:T(8,128)S(1)}, f32[4,256,128]{2,1,0:T(8,128)S(1)}) custom-call(bf16[2,256,128]{2,1,0:T(8,128)(2,1)S(1)} %project_q.2.qa, bf16[2,256,128]{2,1,0:T(8,128)(2,1)S(1)} %project_q.3.qb, f32[4,256,128]{2,1,0:T(8,128)S(1)} %get-tuple-element.42.m_in, ...), custom_call_target="tpu_custom_call" | custom-call | flops 2147483648 | bytes 1048576 | tf_op jit(solution)/shard_map/attend_early/pallas_call | solution.py:322
  26.2 1.2 %attend_middle.1 = (f32[4,256,128]{2,1,0:T(8,128)S(1)}, f32[4,256,128]{2,1,0:T(8,128)S(1)}, f32[4,256,128]{2,1,0:T(8,128)S(1)}) custom-call(bf16[2,256,128]{2,1,0:T(8,128)(2,1)S(1)} %project_q.2.qa, bf16[2,256,128]{2,1,0:T(8,128)(2,1)S(1)} %project_q.3.qb, f32[4,256,128]{2,1,0:T(8,128)S(1)} %get-tuple-element.45.m_in, ...), custom_call_target="tpu_custom_call" | custom-call | flops 268435456 | bytes 1048576 | tf_op jit(solution)/shard_map/attend_middle/pallas_call | solution.py:342
  27.4 0.5 %collective-permute-done.8.far_a = bf16[792,256]{1,0:T(8,128)(2,1)S(1)} collective-permute-done((bf16[792,256]{1,0:T(8,128)(2,1)S(1)}, bf16[792,256]{1,0:T(8,128)(2,1)S(1)}, u32[]{:S(2)}, u32[]{:S(2)}) %collective-permute-start.8) | collective-permute-done | bytes 405536 | tf_op jit(solution)/shard_map/ppermute | solution.py:426
  27.9 1.0 %attend_last.3 = bf16[128,512]{1,0:T(8,128)(2,1)S(1)} custom-call(bf16[2,256,128]{2,1,0:T(8,128)(2,1)S(1)} %project_q.2.qa, bf16[2,256,128]{2,1,0:T(8,128)(2,1)S(1)} %project_q.3.qb, f32[4,256,128]{2,1,0:T(8,128)S(1)} %get-tuple-element.48.m_in, f32[4,256,128]{2,1,0:T(8,128)S(1)} %get-tuple-element.49.l_in, f32[4,256,128]{2,1,0:T(8,128)S(1)} %get-tuple-element.50.acc_in, ...), custom_call_target="tpu_custom_call" | custom-call | flops 201326592 | bytes 1048576 | tf_op jit(solution)/shard_map/attend_last/pallas_call | solution.py:364
  29.0 1.0 %attend_last.2.xm = bf16[128,512]{1,0:T(8,128)(2,1)S(1)} custom-call(bf16[2,256,128]{2,1,0:T(8,128)(2,1)S(1)} %project_q.2.qa, bf16[2,256,128]{2,1,0:T(8,128)(2,1)S(1)} %project_q.3.qb, f32[4,256,128]{2,1,0:T(8,128)S(1)} %get-tuple-element.48.m_in, f32[4,256,128]{2,1,0:T(8,128)S(1)} %get-tuple-element.49.l_in, f32[4,256,128]{2,1,0:T(8,128)S(1)} %get-tuple-element.50.acc_in, ...), custom_call_target="tpu_custom_call" | custom-call | flops 201326592 | bytes 1048576 | tf_op jit(solution)/shard_map/attend_last/pallas_call | solution.py:364
  30.8 2.1 %collective-permute-start.10 = (bf16[128,512]{1,0:T(8,128)(2,1)S(1)}, bf16[128,512]{1,0:T(8,128)(2,1)S(1)}, u32[]{:S(2)}, u32[]{:S(2)}) collective-permute-start(bf16[128,512]{1,0:T(8,128)(2,1)S(1)} %get-tuple-element.55), channel_id=1, source_target_pairs={{0,1},{1,2},{2,3},{3,0},{4,5},{5,6},{6,7},{7,4},{8,9},{9,10},{10,1... | collective-permute-start | bytes 393224 | tf_op jit(solution)/shard_map/ppermute | solution.py:460
  33.0 2.2 %collective-permute-start.11 = (bf16[128,512]{1,0:T(8,128)(2,1)S(1)}, bf16[128,512]{1,0:T(8,128)(2,1)S(1)}, u32[]{:S(2)}, u32[]{:S(2)}) collective-permute-start(bf16[128,512]{1,0:T(8,128)(2,1)S(1)} %get-tuple-element.56), channel_id=1, source_target_pairs={{0,3},{1,0},{2,1},{3,2},{4,7},{5,4},{6,5},{7,6},{8,11},{9,8},{10,9... | collective-permute-start | bytes 393224 | tf_op jit(solution)/shard_map/ppermute | solution.py:460
  35.7 3.2 %collective-permute-start.14 = (bf16[128,512]{1,0:T(8,128)(2,1)S(1)}, bf16[128,512]{1,0:T(8,128)(2,1)S(1)}, u32[]{:S(2)}, u32[]{:S(2)}) collective-permute-start(bf16[128,512]{1,0:T(8,128)(2,1)S(1)} %get-tuple-element.59), channel_id=1, source_target_pairs={{0,3},{1,0},{2,1},{3,2},{4,7},{5,4},{6,5},{7,6},{8,11},{9,8},{10,9... | collective-permute-start | bytes 393224 | tf_op jit(solution)/shard_map/ppermute | solution.py:460
  39.0 0.7 %project_out.3 = (f32[128,512]{1,0:T(8,128)S(1)}, f32[128,512]{1,0:T(8,128)S(1)}, f32[128,512]{1,0:T(8,128)S(1)}, f32[128,512]{1,0:T(8,128)S(1)}) custom-call(bf16[128,512]{1,0:T(8,128)(2,1)S(1)} %attend_last.2.xm, bf16[128,512]{1,0:T(8,128)(2,1)S(1)} %collective-permute-done.9.xr, bf16[1024,4096]{1,0:T(8,128)(2,1)S(1)} %bitcast.2), custom_call_target="tpu_custom_call" | custom-call | flops 536870912 | bytes 4194304 | tf_op jit(solution)/shard_map/project_out/pallas_call | solution.py:387
  39.8 1.4 %collective-permute-start.12 = (bf16[128,512]{1,0:T(8,128)(2,1)S(1)}, bf16[128,512]{1,0:T(8,128)(2,1)S(1)}, u32[]{:S(2)}, u32[]{:S(2)}) collective-permute-start(bf16[128,512]{1,0:T(8,128)(2,1)S(1)} %get-tuple-element.57), channel_id=1, source_target_pairs={{0,1},{1,2},{2,3},{3,0},{4,5},{5,6},{6,7},{7,4},{8,9},{9,10},{10,1... | collective-permute-start | bytes 393224 | tf_op jit(solution)/shard_map/ppermute | solution.py:460
  41.1 1.9 %collective-permute-start.15 = (bf16[128,512]{1,0:T(8,128)(2,1)S(1)}, bf16[128,512]{1,0:T(8,128)(2,1)S(1)}, u32[]{:S(2)}, u32[]{:S(2)}) collective-permute-start(bf16[128,512]{1,0:T(8,128)(2,1)S(1)} %get-tuple-element.60), channel_id=1, source_target_pairs={{0,3},{1,0},{2,1},{3,2},{4,7},{5,4},{6,5},{7,6},{8,11},{9,8},{10,9... | collective-permute-start | bytes 393224 | tf_op jit(solution)/shard_map/ppermute | solution.py:460
  43.1 2.9 %collective-permute-done.12.left_a = bf16[128,512]{1,0:T(8,128)(2,1)S(1)} collective-permute-done((bf16[128,512]{1,0:T(8,128)(2,1)S(1)}, bf16[128,512]{1,0:T(8,128)(2,1)S(1)}, u32[]{:S(2)}, u32[]{:S(2)}) %collective-permute-start.12) | collective-permute-done | bytes 131104 | tf_op jit(solution)/shard_map/ppermute | solution.py:460
  46.1 0.8 %add_total.1 = bf16[128,1024]{1,0:T(8,128)(2,1)} custom-call(f32[128,512]{1,0:T(8,128)S(1)} %get-tuple-element.51.own_a, f32[128,512]{1,0:T(8,128)S(1)} %get-tuple-element.52.own_b, bf16[128,512]{1,0:T(8,128)(2,1)S(1)} %collective-permute-done.12.left_a, bf16[128,512]{1,0:T(8,128)(2,1)S(1)} %collective-permute-done.13.left_b, ...), custom_call_target="tpu_custom_call" | custom-call | bytes 1048576 | tf_op jit(solution)/shard_map/add_total/pallas_call | solution.py:413
  (30 shorter events, 3.7 us)
Async XLA Ops:
  0.0 2.9 %collective-permute-start = (bf16[128,4096]{1,0:T(8,128)(2,1)}, bf16[128,4096]{1,0:T(8,128)(2,1)S(1)}, u32[]{:S(2)}, u32[]{:S(2)}) collective-permute-start(bf16[128,4096]{1,0:T(8,128)(2,1)} %tok.1), channel_id=1, source_target_pairs={{0,4},{4,0},{8,12},{12,8},{16,20},{20,16},{24,28},{28,24},{32,36},... | collective-permute-start | bytes 3145736 | tf_op jit(solution)/shard_map/ppermute | solution.py:422
  0.0 2.9 %collective-permute-start.1 = (s32[1,128]{1,0:T(1,128)}, s32[1,128]{1,0:T(1,128)S(1)}, u32[]{:S(2)}, u32[]{:S(2)}) collective-permute-start(s32[1,128]{1,0:T(1,128)} %bitcast.3), channel_id=1, source_target_pairs={{0,4},{4,0},{8,12},{12,8},{16,20},{20,16},{24,28},{28,24},{32,36},... | collective-permute-start | bytes 1544 | tf_op jit(solution)/shard_map/ppermute | solution.py:422
  3.4 10.6 %collective-permute-start.2 = (bf16[264,256]{1,0:T(8,128)(2,1)S(1)}, bf16[264,256]{1,0:T(8,128)(2,1)S(1)}, u32[]{:S(2)}, u32[]{:S(2)}) collective-permute-start(bf16[264,256]{1,0:T(8,128)(2,1)S(1)} %project_unit.1.unit.after), channel_id=1, source_target_pairs={{0,8},{4,36},{8,16},{12,44},{16,24},{20,52},{24,32},{28,60},{32,40... | collective-permute-start | bytes 405512 | tf_op jit(solution)/shard_map/ppermute | solution.py:426
  5.1 10.5 %collective-permute-start.3 = (bf16[264,256]{1,0:T(8,128)(2,1)S(1)}, bf16[264,256]{1,0:T(8,128)(2,1)S(1)}, u32[]{:S(2)}, u32[]{:S(2)}) collective-permute-start(bf16[264,256]{1,0:T(8,128)(2,1)S(1)} %project_unit.1.unit.after), channel_id=1, source_target_pairs={{0,16},{4,68},{8,24},{12,76},{16,32},{20,84},{24,40},{28,92},{32,4... | collective-permute-start | bytes 405512 | tf_op jit(solution)/shard_map/ppermute | solution.py:426
  7.8 8.4 %collective-permute-start.5 = (bf16[264,256]{1,0:T(8,128)(2,1)S(1)}, bf16[264,256]{1,0:T(8,128)(2,1)S(1)}, u32[]{:S(2)}, u32[]{:S(2)}) collective-permute-start(bf16[264,256]{1,0:T(8,128)(2,1)S(1)} %project_unit.1.unit.after), channel_id=1, source_target_pairs={{0,24},{4,100},{8,32},{12,108},{16,40},{20,116},{24,48},{28,124},{... | collective-permute-start | bytes 405512 | tf_op jit(solution)/shard_map/ppermute | solution.py:426
  10.2 7.3 %collective-permute-start.6 = (bf16[264,256]{1,0:T(8,128)(2,1)S(1)}, bf16[264,256]{1,0:T(8,128)(2,1)S(1)}, u32[]{:S(2)}, u32[]{:S(2)}) collective-permute-start(bf16[264,256]{1,0:T(8,128)(2,1)S(1)} %project_unit.1.unit.after), channel_id=1, source_target_pairs={{0,32},{4,28},{8,40},{12,4},{16,48},{20,12},{24,56},{28,20},{32,64... | collective-permute-start | bytes 405512 | tf_op jit(solution)/shard_map/ppermute | solution.py:426
  15.6 9.3 %collective-permute-start.4 = (bf16[528,256]{1,0:T(8,128)(2,1)S(1)}, bf16[528,256]{1,0:T(8,128)(2,1)S(1)}, u32[]{:S(2)}, u32[]{:S(2)}) collective-permute-start(bf16[528,256]{1,0:T(8,128)(2,1)S(1)} %bundle_pair.2), channel_id=1, source_target_pairs={{0,64},{4,20},{8,72},{12,28},{16,80},{20,4},{24,88},{28,12},{32,96... | collective-permute-start | bytes 811016 | tf_op jit(solution)/shard_map/ppermute | solution.py:426
  17.6 10.3 %collective-permute-start.8 = (bf16[792,256]{1,0:T(8,128)(2,1)S(1)}, bf16[792,256]{1,0:T(8,128)(2,1)S(1)}, u32[]{:S(2)}, u32[]{:S(2)}) collective-permute-start(bf16[792,256]{1,0:T(8,128)(2,1)S(1)} %bundle_row.1.after), channel_id=1, source_target_pairs={{0,32},{4,12},{8,40},{12,20},{16,48},{20,28},{24,56},{28,4},{32,64... | collective-permute-start | bytes 1216520 | tf_op jit(solution)/shard_map/ppermute | solution.py:426
  17.9 8.3 %collective-permute-start.7 = (bf16[528,256]{1,0:T(8,128)(2,1)S(1)}, bf16[528,256]{1,0:T(8,128)(2,1)S(1)}, u32[]{:S(2)}, u32[]{:S(2)}) collective-permute-start(bf16[528,256]{1,0:T(8,128)(2,1)S(1)} %bundle_pair.3), channel_id=1, source_target_pairs={{0,96},{4,28},{8,104},{12,4},{16,112},{20,12},{24,120},{28,20},{32... | collective-permute-start | bytes 811016 | tf_op jit(solution)/shard_map/ppermute | solution.py:426
  23.3 7.1 %slice-start = ((s8[8388608]{0:T(1024)(128)(4,1)}), s8[4194304]{0:T(1024)(128)(4,1)S(1)}, s32[]{:S(2)}) async-start(s8[8388608]{0:T(1024)(128)(4,1)} %bitcast.1), calls=%async_computation | async-start | bytes 8388608
  24.9 5.4 %slice-start.1 = ((s8[8388608]{0:T(1024)(128)(4,1)}), s8[4194304]{0:T(1024)(128)(4,1)S(1)}, s32[]{:S(2)}) async-start(s8[8388608]{0:T(1024)(128)(4,1)} %bitcast.1), calls=%async_computation.1 | async-start | bytes 8388608
  28.9 1.4 %collective-permute-start.9 = (bf16[128,512]{1,0:T(8,128)(2,1)S(1)}, bf16[128,512]{1,0:T(8,128)(2,1)S(1)}, u32[]{:S(2)}, u32[]{:S(2)}) collective-permute-start(bf16[128,512]{1,0:T(8,128)(2,1)S(1)} %attend_last.3), channel_id=1, source_target_pairs={{0,4},{4,0},{8,12},{12,8},{16,20},{20,16},{24,28},{28,24},{32,36},... | collective-permute-start | bytes 393224 | tf_op jit(solution)/shard_map/ppermute | solution.py:422
  30.8 8.8 %collective-permute-start.10 = (bf16[128,512]{1,0:T(8,128)(2,1)S(1)}, bf16[128,512]{1,0:T(8,128)(2,1)S(1)}, u32[]{:S(2)}, u32[]{:S(2)}) collective-permute-start(bf16[128,512]{1,0:T(8,128)(2,1)S(1)} %get-tuple-element.55), channel_id=1, source_target_pairs={{0,1},{1,2},{2,3},{3,0},{4,5},{5,6},{6,7},{7,4},{8,9},{9,10},{10,1... | collective-permute-start | bytes 393224 | tf_op jit(solution)/shard_map/ppermute | solution.py:460
  33.0 6.7 %collective-permute-start.11 = (bf16[128,512]{1,0:T(8,128)(2,1)S(1)}, bf16[128,512]{1,0:T(8,128)(2,1)S(1)}, u32[]{:S(2)}, u32[]{:S(2)}) collective-permute-start(bf16[128,512]{1,0:T(8,128)(2,1)S(1)} %get-tuple-element.56), channel_id=1, source_target_pairs={{0,3},{1,0},{2,1},{3,2},{4,7},{5,4},{6,5},{7,6},{8,11},{9,8},{10,9... | collective-permute-start | bytes 393224 | tf_op jit(solution)/shard_map/ppermute | solution.py:460
  35.6 7.4 %collective-permute-start.13 = (bf16[128,512]{1,0:T(8,128)(2,1)S(1)}, bf16[128,512]{1,0:T(8,128)(2,1)S(1)}, u32[]{:S(2)}, u32[]{:S(2)}) collective-permute-start(bf16[128,512]{1,0:T(8,128)(2,1)S(1)} %get-tuple-element.58), channel_id=1, source_target_pairs={{0,1},{1,2},{2,3},{3,0},{4,5},{5,6},{6,7},{7,4},{8,9},{9,10},{10,1... | collective-permute-start | bytes 393224 | tf_op jit(solution)/shard_map/ppermute | solution.py:460
  35.7 7.3 %collective-permute-start.14 = (bf16[128,512]{1,0:T(8,128)(2,1)S(1)}, bf16[128,512]{1,0:T(8,128)(2,1)S(1)}, u32[]{:S(2)}, u32[]{:S(2)}) collective-permute-start(bf16[128,512]{1,0:T(8,128)(2,1)S(1)} %get-tuple-element.59), channel_id=1, source_target_pairs={{0,3},{1,0},{2,1},{3,2},{4,7},{5,4},{6,5},{7,6},{8,11},{9,8},{10,9... | collective-permute-start | bytes 393224 | tf_op jit(solution)/shard_map/ppermute | solution.py:460
  39.8 6.2 %collective-permute-start.12 = (bf16[128,512]{1,0:T(8,128)(2,1)S(1)}, bf16[128,512]{1,0:T(8,128)(2,1)S(1)}, u32[]{:S(2)}, u32[]{:S(2)}) collective-permute-start(bf16[128,512]{1,0:T(8,128)(2,1)S(1)} %get-tuple-element.57), channel_id=1, source_target_pairs={{0,1},{1,2},{2,3},{3,0},{4,5},{5,6},{6,7},{7,4},{8,9},{9,10},{10,1... | collective-permute-start | bytes 393224 | tf_op jit(solution)/shard_map/ppermute | solution.py:460
  41.1 5.0 %collective-permute-start.15 = (bf16[128,512]{1,0:T(8,128)(2,1)S(1)}, bf16[128,512]{1,0:T(8,128)(2,1)S(1)}, u32[]{:S(2)}, u32[]{:S(2)}) collective-permute-start(bf16[128,512]{1,0:T(8,128)(2,1)S(1)} %get-tuple-element.60), channel_id=1, source_target_pairs={{0,3},{1,0},{2,1},{3,2},{4,7},{5,4},{6,5},{7,6},{8,11},{9,8},{10,9... | collective-permute-start | bytes 393224 | tf_op jit(solution)/shard_map/ppermute | solution.py:460

commit v12 on v8

--- a/solution.py
+++ b/solution.py
@@ -156,38 +156,21 @@
     )(half, came, w, docs, docs_came, table)
 
 
-Q_PARTS = 4
-
-
-def q_body(tok, came, wq, table, out, wq_s, sems):
+def q_body(tok, came, wq, table, out):
     half = wq.shape[1] // 2
-    part = wq.shape[0] // Q_PARTS
     cols = pl.ds(pl.multiple_of(core_index() * half, half), half)
-    copies = []
-    for i in range(Q_PARTS):
-        rows = pl.ds(i * part, part)
-        copies += started([
-            pltpu.make_async_copy(wq.at[rows, cols], wq_s.at[rows, :], sems.at[i])
-        ])
-    got = [None, None]
-    for i in range(Q_PARTS):
-        copies[i].wait()
-        rows = slice(i * part, (i + 1) * part)
-        for side, src in enumerate((tok, came)):
-            more = jnp.dot(src[:, rows], wq_s[rows, :], preferred_element_type=F32)
-            got[side] = more if i == 0 else got[side] + more
-    for side, span in enumerate(halves()):
+    for span, src in zip(halves(), (tok, came)):
+        got = jnp.dot(src[...], wq[:, cols], preferred_element_type=F32)
         rot = rotation(table[span, :])
         for h in range(half // HD):
-            out[h, span, :] = rot(got[side][:, h * HD : (h + 1) * HD]).astype(BF16)
+            out[h, span, :] = rot(got[:, h * HD : (h + 1) * HD]).astype(BF16)
 
 
 def project_q(tokens, came, w_query, table):
     depth, width = w_query.shape
     return call(
-        q_body, "project_q", like(width // 2 // HD, CHIP, HD), [VMEM, VMEM, HBM, VMEM], VMEM,
-        [pltpu.VMEM((depth, width // 2), BF16), pltpu.SemaphoreType.DMA((Q_PARTS,))],
-        limit=8, flops=2 * CHIP * depth * width // 2, moved=6,
+        q_body, "project_q", like(width // 2 // HD, CHIP, HD), [VMEM] * 4, VMEM,
+        limit=4, flops=2 * CHIP * depth * width // 2, moved=6,
     )(tokens, came, w_query, table)
 
 
@@ -206,19 +189,16 @@
         out[i * UNIT : (i + 1) * UNIT, :] = slots[skip + i]
 
 
-def pairs_body(unit, r1, r2, out_b, out_c, slots):
-    for i, src in enumerate((unit, r1, r2)):
-        slots[i] = src[...]
-    fill(out_b, slots, 2, 0)
-    fill(out_c, slots, 1, 0)
-
-
-def bundle_pairs(unit, r1, r2):
-    pair = like(2 * UNIT, 2 * HD)
-    return call(
-        pairs_body, "bundle_pairs", (pair, pair), [VMEM] * 3, (VMEM,) * 2,
+def bundle_pair(unit, r1, r2, late, after):
+    def body(unit, r1, r2, after, out, slots):
+        for i, src in enumerate((unit, r1, r2)):
+            slots[i] = src[...]
+        fill(out, slots, late, 0)
+
+    return call(
+        body, "bundle_pair", like(2 * UNIT, 2 * HD), [VMEM] * 4, VMEM,
         [pltpu.VMEM((3, UNIT, 2 * HD), BF16)], limit=2,
-    )(unit, r1, r2)
+    )(unit, r1, r2, after)
 
 
 def row_body(unit, r1, r2, r3, after, out_a, slots):
@@ -337,7 +317,7 @@
     state = like(heads, CHIP, HD, dtype=F32)
     return call(
         middle_body, "attend_middle", (state,) * 3, [VMEM] * 8, (VMEM,) * 3, limit=8,
-        flops=64 * heads * CHIP * CHIP * HD, exps=2 * heads * CHIP * CHIP,
+        flops=8 * heads * CHIP * CHIP * HD, exps=2 * heads * CHIP * CHIP,
     )(qs, m_in, l_in, acc_in, unit, r3, r4, far_c)
 
 
@@ -428,9 +408,9 @@
 
     docs = doc_ids.reshape(1, -1)
     came, docs_came = swap(tokens), swap(docs)
-    tokens, w_key, w_value, w_query, table, docs = (
+    tokens, w_key, w_value, table, docs = (
         pltpu.with_memory_space_constraint(a, pltpu.HBM)
-        for a in (tokens, w_key, w_value, w_query, table, docs)
+        for a in (tokens, w_key, w_value, table, docs)
     )
     half, tokens, w_kv, docs, table = project_own(tokens, w_key, w_value, docs, table)
     unit = project_unit(half, came, w_kv, docs, docs_came, table)
@@ -439,10 +419,10 @@
     r3 = along(unit, ahead(3), ahead(12))
     r4 = along(unit, ahead(4), in_row(3))
     r1, r2, came = lax.optimization_barrier((r1, r2, came))
-    out_b, out_c = bundle_pairs(unit, r1, r2)
-    far_b = along(out_b, ahead(8), in_row(2))
-    far_c = along(out_c, ahead(12), in_row(3))
-    far_a = along(bundle_row(unit, r1, r2, r3, r4), ahead(4), in_row(1))
+    far_b = along(bundle_pair(unit, r1, r2, 2, unit), ahead(8), in_row(2))
+    out_a = bundle_row(unit, r1, r2, r3, r4)
+    far_a = along(out_a, ahead(4), in_row(1))
+    far_c = along(bundle_pair(unit, r1, r2, 1, out_a), ahead(12), in_row(3))
     qs = project_q(tokens, came, w_query, table)
     state = attend_near(qs, unit, r1, r2)
     state = attend_early(qs, *state, unit, far_b)

time: 46.9 us -> 47.2 us (level)
  starting transfers between devices: 21.7 us -> 23.4 us
  Pallas kernels: 14.5 us -> 13.1 us
    ppermute x7, starting transfers between devices: 10.1 us -> 11.9 us  [along(): return lax.ppermute(value, 'ctx', moves)]
    pallas_call x2 -> x3, Pallas kernels: 3.16 us -> 1.5 us  [the longest x1 1.41 us: project_q(): call(q_body, 'project_q', like(width // 2 // HD, CHIP, HD), [VMEM] * 4, V...]
  transfers between devices with their start and end apart: 16 -> 16, of which waited for: 7 -> 8; matrix products, arithmetic and copies ran while one was open for 0% -> 0% of each run, Pallas kernels for 25% -> 22%
where the time goes in v12:
time: 47.2 us; the launch traced here: 47.1 us
  starting transfers between devices  23.4 us (50%)
  Pallas kernels  13.1 us (28%)
  waiting for transfers between devices  10.4 us (22%)
    ppermute x7, starting transfers between devices, along(): return lax.ppermute(value, 'ctx', moves)  11.9 us
    ppermute x6, starting transfers between devices, shift(): lax.ppermute(value, 'head', [(g, (g + step) % groups) for g in range(grou...  11 us
    ppermute x7, waiting for transfers between devices, along(): return lax.ppermute(value, 'ctx', moves)  7.1 us
    ppermute x6, waiting for transfers between devices, shift(): lax.ppermute(value, 'head', [(g, (g + step) % groups) for g in range(grou...  2.95 us
    pallas_call x1, Pallas kernels, project_own(): call(own_body, 'project_own', (like(ROWS, 2 * HD), like(ROWS, depth), lik...  2.5 us
    pallas_call x2, Pallas kernels, attend_last(): call(body, 'attend_last', like(ROWS, heads * HD), [VMEM] * 6, VMEM, [pltp...  1.96 us
    pallas_call x3, Pallas kernels, project_out(): call(body, 'project_out', (like(ROWS, half, dtype=dtype),) * len(parts),...  1.62 us
    pallas_call x1, Pallas kernels, attend_near(): call(near_body, 'attend_near', (state, state, state), [VMEM] * 4, (VMEM,)...  1.57 us
  transfers between devices with their start and end apart: 16, of which 8 were waited for; matrix products, arithmetic and copies ran while one was open for 0% of the time, Pallas kernels for 22%

profile of v12, /device:TPU:0, one launch (start us, length us, event | category | flops | bytes accessed | tf_op | source)
XLA Modules:
  0.0 47.1 jit_solution(13621639047788063108)
XLA Ops:
  0.5 2.5 %project_own.1 = (bf16[128,256]{1,0:T(8,128)(2,1)S(1)}, bf16[128,4096]{1,0:T(8,128)(2,1)S(1)}, bf16[4096,256]{1,0:T(8,128)(2,1)S(1)}, s32[1,128]{1,0:T(1,128)S(1)}, f32[256,128]{1,0:T(8,128)S(1)}) custom-call(bf16[128,4096]{1,0:T(8,128)(2,1)} %tok.1, bf16[4096,256]{1,0:T(8,128)(2,1)} %wk.1, bf16[4096,256]{1,0:T(8,128)(2,1)} %wv.1, s32[1,128]{1,0:T(1,128)} %bitcast.4, ...), custom_call_target="tpu_custom_call" | custom-call | flops 268435456 | bytes 3145728 | tf_op jit(solution)/shard_map/project_own/pallas_call | solution.py:124
  3.6 1.6 %collective-permute-start.2 = (bf16[264,256]{1,0:T(8,128)(2,1)S(1)}, bf16[264,256]{1,0:T(8,128)(2,1)S(1)}, u32[]{:S(2)}, u32[]{:S(2)}) collective-permute-start(bf16[264,256]{1,0:T(8,128)(2,1)S(1)} %project_unit.1.unit.after), channel_id=1, source_target_pairs={{0,8},{4,36},{8,16},{12,44},{16,24},{20,52},{24,32},{28,60},{32,40... | collective-permute-start | bytes 405512 | tf_op jit(solution)/shard_map/ppermute | solution.py:401
  5.2 2.7 %collective-permute-start.3 = (bf16[264,256]{1,0:T(8,128)(2,1)S(1)}, bf16[264,256]{1,0:T(8,128)(2,1)S(1)}, u32[]{:S(2)}, u32[]{:S(2)}) collective-permute-start(bf16[264,256]{1,0:T(8,128)(2,1)S(1)} %project_unit.1.unit.after), channel_id=1, source_target_pairs={{0,16},{4,68},{8,24},{12,76},{16,32},{20,84},{24,40},{28,92},{32,4... | collective-permute-start | bytes 405512 | tf_op jit(solution)/shard_map/ppermute | solution.py:401
  8.0 2.4 %collective-permute-start.5 = (bf16[264,256]{1,0:T(8,128)(2,1)S(1)}, bf16[264,256]{1,0:T(8,128)(2,1)S(1)}, u32[]{:S(2)}, u32[]{:S(2)}) collective-permute-start(bf16[264,256]{1,0:T(8,128)(2,1)S(1)} %project_unit.1.unit.after), channel_id=1, source_target_pairs={{0,24},{4,100},{8,32},{12,108},{16,40},{20,116},{24,48},{28,124},{... | collective-permute-start | bytes 405512 | tf_op jit(solution)/shard_map/ppermute | solution.py:401
  10.4 1.6 %collective-permute-start.6 = (bf16[264,256]{1,0:T(8,128)(2,1)S(1)}, bf16[264,256]{1,0:T(8,128)(2,1)S(1)}, u32[]{:S(2)}, u32[]{:S(2)}) collective-permute-start(bf16[264,256]{1,0:T(8,128)(2,1)S(1)} %project_unit.1.unit.after), channel_id=1, source_target_pairs={{0,32},{4,28},{8,40},{12,4},{16,48},{20,12},{24,56},{28,20},{32,64... | collective-permute-start | bytes 405512 | tf_op jit(solution)/shard_map/ppermute | solution.py:401
  12.0 1.2 %collective-permute-done.2.r1 = bf16[264,256]{1,0:T(8,128)(2,1)S(1)} collective-permute-done((bf16[264,256]{1,0:T(8,128)(2,1)S(1)}, bf16[264,256]{1,0:T(8,128)(2,1)S(1)}, u32[]{:S(2)}, u32[]{:S(2)}) %collective-permute-start.2) | collective-permute-done | bytes 135200 | tf_op jit(solution)/shard_map/ppermute | solution.py:401
  13.1 2.7 %collective-permute-done.3.r2 = bf16[264,256]{1,0:T(8,128)(2,1)S(1)} collective-permute-done((bf16[264,256]{1,0:T(8,128)(2,1)S(1)}, bf16[264,256]{1,0:T(8,128)(2,1)S(1)}, u32[]{:S(2)}, u32[]{:S(2)}) %collective-permute-start.3) | collective-permute-done | bytes 135200 | tf_op jit(solution)/shard_map/ppermute | solution.py:401
  16.4 1.3 %collective-permute-done.6.after.r4 = bf16[264,256]{1,0:T(8,128)(2,1)S(1)} collective-permute-done((bf16[264,256]{1,0:T(8,128)(2,1)S(1)}, bf16[264,256]{1,0:T(8,128)(2,1)S(1)}, u32[]{:S(2)}, u32[]{:S(2)}) %collective-permute-start.6) | collective-permute-done | bytes 135200 | tf_op jit(solution)/shard_map/ppermute | solution.py:401
  17.8 1.2 %collective-permute-start.8 = (bf16[792,256]{1,0:T(8,128)(2,1)S(1)}, bf16[792,256]{1,0:T(8,128)(2,1)S(1)}, u32[]{:S(2)}, u32[]{:S(2)}) collective-permute-start(bf16[792,256]{1,0:T(8,128)(2,1)S(1)} %bundle_row.1.after), channel_id=1, source_target_pairs={{0,32},{4,12},{8,40},{12,20},{16,48},{20,28},{24,56},{28,4},{32,64... | collective-permute-start | bytes 1216520 | tf_op jit(solution)/shard_map/ppermute | solution.py:401
  19.0 2.2 %collective-permute-start.7 = (bf16[528,256]{1,0:T(8,128)(2,1)S(1)}, bf16[528,256]{1,0:T(8,128)(2,1)S(1)}, u32[]{:S(2)}, u32[]{:S(2)}) collective-permute-start(bf16[528,256]{1,0:T(8,128)(2,1)S(1)} %bundle_pair.3), channel_id=1, source_target_pairs={{0,96},{4,28},{8,104},{12,4},{16,112},{20,12},{24,120},{28,20},{32... | collective-permute-start | bytes 811016 | tf_op jit(solution)/shard_map/ppermute | solution.py:401
  21.2 1.4 %project_q.1.qs = bf16[4,256,128]{2,1,0:T(8,128)(2,1)S(1)} custom-call(bf16[128,4096]{1,0:T(8,128)(2,1)S(1)} %get-tuple-element.32.tok, bf16[128,4096]{1,0:T(8,128)(2,1)S(1)} %collective-permute-done.came, bf16[4096,1024]{1,0:T(8,128)(2,1)S(1)} %copy-done, f32[256,128]{1,0:T(8,128)S(1)} %get-tuple-element.36.table), custom_call_target="tpu_custom_call" | custom-call | flops 1073741824 | bytes 6291456 | tf_op jit(solution)/shard_map/project_q/pallas_call | solution.py:171
  22.7 1.6 %attend_near.1 = (f32[4,256,128]{2,1,0:T(8,128)S(1)}, f32[4,256,128]{2,1,0:T(8,128)S(1)}, f32[4,256,128]{2,1,0:T(8,128)S(1)}) custom-call(bf16[4,256,128]{2,1,0:T(8,128)(2,1)S(1)} %project_q.1.qs, bf16[264,256]{1,0:T(8,128)(2,1)S(1)} %project_unit.1.unit.after, bf16[264,256]{1,0:T(8,128)(2,1)S(1)} %collective-permute-done.2.r1, ...), custom_call_target="tpu_custom_call" | custom-call | flops 402653184 | bytes 1048576 | tf_op jit(solution)/shard_map/attend_near/pallas_call | solution.py:281
  24.2 1.2 %attend_early.1 = (f32[4,256,128]{2,1,0:T(8,128)S(1)}, f32[4,256,128]{2,1,0:T(8,128)S(1)}, f32[4,256,128]{2,1,0:T(8,128)S(1)}) custom-call(bf16[4,256,128]{2,1,0:T(8,128)(2,1)S(1)} %project_q.1.qs, f32[4,256,128]{2,1,0:T(8,128)S(1)} %get-tuple-element.40.m_in, f32[4,256,128]{2,1,0:T(8,128)S(1)} %get-tuple-element.41.l_in, ...), custom_call_target="tpu_custom_call" | custom-call | flops 2147483648 | bytes 1048576 | tf_op jit(solution)/shard_map/attend_early/pallas_call | solution.py:298
  25.6 1.2 %attend_middle.1 = (f32[4,256,128]{2,1,0:T(8,128)S(1)}, f32[4,256,128]{2,1,0:T(8,128)S(1)}, f32[4,256,128]{2,1,0:T(8,128)S(1)}) custom-call(bf16[4,256,128]{2,1,0:T(8,128)(2,1)S(1)} %project_q.1.qs, f32[4,256,128]{2,1,0:T(8,128)S(1)} %get-tuple-element.43.m_in, f32[4,256,128]{2,1,0:T(8,128)S(1)} %get-tuple-element.44.l_in, ...), custom_call_target="tpu_custom_call" | custom-call | flops 268435456 | bytes 1048576 | tf_op jit(solution)/shard_map/attend_middle/pallas_call | solution.py:318
  26.8 1.4 %collective-permute-done.8.far_a = bf16[792,256]{1,0:T(8,128)(2,1)S(1)} collective-permute-done((bf16[792,256]{1,0:T(8,128)(2,1)S(1)}, bf16[792,256]{1,0:T(8,128)(2,1)S(1)}, u32[]{:S(2)}, u32[]{:S(2)}) %collective-permute-start.8) | collective-permute-done | bytes 405536 | tf_op jit(solution)/shard_map/ppermute | solution.py:401
  28.2 1.0 %attend_last.3 = bf16[128,512]{1,0:T(8,128)(2,1)S(1)} custom-call(bf16[4,256,128]{2,1,0:T(8,128)(2,1)S(1)} %project_q.1.qs, f32[4,256,128]{2,1,0:T(8,128)S(1)} %get-tuple-element.46.m_in, f32[4,256,128]{2,1,0:T(8,128)S(1)} %get-tuple-element.47.l_in, f32[4,256,128]{2,1,0:T(8,128)S(1)} %get-tuple-element.48.acc_in, ...), custom_call_target="tpu_custom_call" | custom-call | flops 201326592 | bytes 1048576 | tf_op jit(solution)/shard_map/attend_last/pallas_call | solution.py:339
  29.3 1.0 %attend_last.2.xm = bf16[128,512]{1,0:T(8,128)(2,1)S(1)} custom-call(bf16[4,256,128]{2,1,0:T(8,128)(2,1)S(1)} %project_q.1.qs, f32[4,256,128]{2,1,0:T(8,128)S(1)} %get-tuple-element.46.m_in, f32[4,256,128]{2,1,0:T(8,128)S(1)} %get-tuple-element.47.l_in, f32[4,256,128]{2,1,0:T(8,128)S(1)} %get-tuple-element.48.acc_in, ...), custom_call_target="tpu_custom_call" | custom-call | flops 201326592 | bytes 1048576 | tf_op jit(solution)/shard_map/attend_last/pallas_call | solution.py:339
  31.1 2.0 %collective-permute-start.10 = (bf16[128,512]{1,0:T(8,128)(2,1)S(1)}, bf16[128,512]{1,0:T(8,128)(2,1)S(1)}, u32[]{:S(2)}, u32[]{:S(2)}) collective-permute-start(bf16[128,512]{1,0:T(8,128)(2,1)S(1)} %get-tuple-element.53), channel_id=1, source_target_pairs={{0,1},{1,2},{2,3},{3,0},{4,5},{5,6},{6,7},{7,4},{8,9},{9,10},{10,1... | collective-permute-start | bytes 393224 | tf_op jit(solution)/shard_map/ppermute | solution.py:434
  33.1 2.4 %collective-permute-start.11 = (bf16[128,512]{1,0:T(8,128)(2,1)S(1)}, bf16[128,512]{1,0:T(8,128)(2,1)S(1)}, u32[]{:S(2)}, u32[]{:S(2)}) collective-permute-start(bf16[128,512]{1,0:T(8,128)(2,1)S(1)} %get-tuple-element.54), channel_id=1, source_target_pairs={{0,3},{1,0},{2,1},{3,2},{4,7},{5,4},{6,5},{7,6},{8,11},{9,8},{10,9... | collective-permute-start | bytes 393224 | tf_op jit(solution)/shard_map/ppermute | solution.py:434
  36.0 3.2 %collective-permute-start.14 = (bf16[128,512]{1,0:T(8,128)(2,1)S(1)}, bf16[128,512]{1,0:T(8,128)(2,1)S(1)}, u32[]{:S(2)}, u32[]{:S(2)}) collective-permute-start(bf16[128,512]{1,0:T(8,128)(2,1)S(1)} %get-tuple-element.57), channel_id=1, source_target_pairs={{0,3},{1,0},{2,1},{3,2},{4,7},{5,4},{6,5},{7,6},{8,11},{9,8},{10,9... | collective-permute-start | bytes 393224 | tf_op jit(solution)/shard_map/ppermute | solution.py:434
  40.1 1.2 %collective-permute-start.12 = (bf16[128,512]{1,0:T(8,128)(2,1)S(1)}, bf16[128,512]{1,0:T(8,128)(2,1)S(1)}, u32[]{:S(2)}, u32[]{:S(2)}) collective-permute-start(bf16[128,512]{1,0:T(8,128)(2,1)S(1)} %get-tuple-element.55), channel_id=1, source_target_pairs={{0,1},{1,2},{2,3},{3,0},{4,5},{5,6},{6,7},{7,4},{8,9},{9,10},{10,1... | collective-permute-start | bytes 393224 | tf_op jit(solution)/shard_map/ppermute | solution.py:434
  41.3 2.1 %collective-permute-start.15 = (bf16[128,512]{1,0:T(8,128)(2,1)S(1)}, bf16[128,512]{1,0:T(8,128)(2,1)S(1)}, u32[]{:S(2)}, u32[]{:S(2)}) collective-permute-start(bf16[128,512]{1,0:T(8,128)(2,1)S(1)} %get-tuple-element.58), channel_id=1, source_target_pairs={{0,3},{1,0},{2,1},{3,2},{4,7},{5,4},{6,5},{7,6},{8,11},{9,8},{10,9... | collective-permute-start | bytes 393224 | tf_op jit(solution)/shard_map/ppermute | solution.py:434
  43.4 2.9 %collective-permute-done.12.left_a = bf16[128,512]{1,0:T(8,128)(2,1)S(1)} collective-permute-done((bf16[128,512]{1,0:T(8,128)(2,1)S(1)}, bf16[128,512]{1,0:T(8,128)(2,1)S(1)}, u32[]{:S(2)}, u32[]{:S(2)}) %collective-permute-start.12) | collective-permute-done | bytes 131104 | tf_op jit(solution)/shard_map/ppermute | solution.py:434
  46.3 0.8 %add_total.1 = bf16[128,1024]{1,0:T(8,128)(2,1)} custom-call(f32[128,512]{1,0:T(8,128)S(1)} %get-tuple-element.49.own_a, f32[128,512]{1,0:T(8,128)S(1)} %get-tuple-element.50.own_b, bf16[128,512]{1,0:T(8,128)(2,1)S(1)} %collective-permute-done.12.left_a, bf16[128,512]{1,0:T(8,128)(2,1)S(1)} %collective-permute-done.13.left_b, ...), custom_call_target="tpu_custom_call" | custom-call | bytes 1048576 | tf_op jit(solution)/shard_map/add_total/pallas_call | solution.py:388
  (31 shorter events, 4.0 us)
Async XLA Ops:
  0.0 3.0 %collective-permute-start = (bf16[128,4096]{1,0:T(8,128)(2,1)}, bf16[128,4096]{1,0:T(8,128)(2,1)S(1)}, u32[]{:S(2)}, u32[]{:S(2)}) collective-permute-start(bf16[128,4096]{1,0:T(8,128)(2,1)} %tok.1), channel_id=1, source_target_pairs={{0,4},{4,0},{8,12},{12,8},{16,20},{20,16},{24,28},{28,24},{32,36},... | collective-permute-start | bytes 3145736 | tf_op jit(solution)/shard_map/ppermute | solution.py:397
  0.0 3.0 %collective-permute-start.1 = (s32[1,128]{1,0:T(1,128)}, s32[1,128]{1,0:T(1,128)S(1)}, u32[]{:S(2)}, u32[]{:S(2)}) collective-permute-start(s32[1,128]{1,0:T(1,128)} %bitcast.3), channel_id=1, source_target_pairs={{0,4},{4,0},{8,12},{12,8},{16,20},{20,16},{24,28},{28,24},{32,36},... | collective-permute-start | bytes 1544 | tf_op jit(solution)/shard_map/ppermute | solution.py:397
  0.5 20.7 %copy-start = (bf16[4096,1024]{1,0:T(8,128)(2,1)S(1)}, bf16[4096,1024]{1,0:T(8,128)(2,1)}, u32[]{:S(2)}) copy-start(bf16[4096,1024]{1,0:T(8,128)(2,1)} %wq.1) | copy-start | bytes 25165828
  3.6 9.5 %collective-permute-start.2 = (bf16[264,256]{1,0:T(8,128)(2,1)S(1)}, bf16[264,256]{1,0:T(8,128)(2,1)S(1)}, u32[]{:S(2)}, u32[]{:S(2)}) collective-permute-start(bf16[264,256]{1,0:T(8,128)(2,1)S(1)} %project_unit.1.unit.after), channel_id=1, source_target_pairs={{0,8},{4,36},{8,16},{12,44},{16,24},{20,52},{24,32},{28,60},{32,40... | collective-permute-start | bytes 405512 | tf_op jit(solution)/shard_map/ppermute | solution.py:401
  5.2 10.6 %collective-permute-start.3 = (bf16[264,256]{1,0:T(8,128)(2,1)S(1)}, bf16[264,256]{1,0:T(8,128)(2,1)S(1)}, u32[]{:S(2)}, u32[]{:S(2)}) collective-permute-start(bf16[264,256]{1,0:T(8,128)(2,1)S(1)} %project_unit.1.unit.after), channel_id=1, source_target_pairs={{0,16},{4,68},{8,24},{12,76},{16,32},{20,84},{24,40},{28,92},{32,4... | collective-permute-start | bytes 405512 | tf_op jit(solution)/shard_map/ppermute | solution.py:401
  8.0 8.4 %collective-permute-start.5 = (bf16[264,256]{1,0:T(8,128)(2,1)S(1)}, bf16[264,256]{1,0:T(8,128)(2,1)S(1)}, u32[]{:S(2)}, u32[]{:S(2)}) collective-permute-start(bf16[264,256]{1,0:T(8,128)(2,1)S(1)} %project_unit.1.unit.after), channel_id=1, source_target_pairs={{0,24},{4,100},{8,32},{12,108},{16,40},{20,116},{24,48},{28,124},{... | collective-permute-start | bytes 405512 | tf_op jit(solution)/shard_map/ppermute | solution.py:401
  10.4 7.3 %collective-permute-start.6 = (bf16[264,256]{1,0:T(8,128)(2,1)S(1)}, bf16[264,256]{1,0:T(8,128)(2,1)S(1)}, u32[]{:S(2)}, u32[]{:S(2)}) collective-permute-start(bf16[264,256]{1,0:T(8,128)(2,1)S(1)} %project_unit.1.unit.after), channel_id=1, source_target_pairs={{0,32},{4,28},{8,40},{12,4},{16,48},{20,12},{24,56},{28,20},{32,64... | collective-permute-start | bytes 405512 | tf_op jit(solution)/shard_map/ppermute | solution.py:401
  15.9 8.4 %collective-permute-start.4 = (bf16[528,256]{1,0:T(8,128)(2,1)S(1)}, bf16[528,256]{1,0:T(8,128)(2,1)S(1)}, u32[]{:S(2)}, u32[]{:S(2)}) collective-permute-start(bf16[528,256]{1,0:T(8,128)(2,1)S(1)} %bundle_pair.2), channel_id=1, source_target_pairs={{0,64},{4,20},{8,72},{12,28},{16,80},{20,4},{24,88},{28,12},{32,96... | collective-permute-start | bytes 811016 | tf_op jit(solution)/shard_map/ppermute | solution.py:401
  17.8 10.4 %collective-permute-start.8 = (bf16[792,256]{1,0:T(8,128)(2,1)S(1)}, bf16[792,256]{1,0:T(8,128)(2,1)S(1)}, u32[]{:S(2)}, u32[]{:S(2)}) collective-permute-start(bf16[792,256]{1,0:T(8,128)(2,1)S(1)} %bundle_row.1.after), channel_id=1, source_target_pairs={{0,32},{4,12},{8,40},{12,20},{16,48},{20,28},{24,56},{28,4},{32,64... | collective-permute-start | bytes 1216520 | tf_op jit(solution)/shard_map/ppermute | solution.py:401
  19.0 6.5 %collective-permute-start.7 = (bf16[528,256]{1,0:T(8,128)(2,1)S(1)}, bf16[528,256]{1,0:T(8,128)(2,1)S(1)}, u32[]{:S(2)}, u32[]{:S(2)}) collective-permute-start(bf16[528,256]{1,0:T(8,128)(2,1)S(1)} %bundle_pair.3), channel_id=1, source_target_pairs={{0,96},{4,28},{8,104},{12,4},{16,112},{20,12},{24,120},{28,20},{32... | collective-permute-start | bytes 811016 | tf_op jit(solution)/shard_map/ppermute | solution.py:401
  22.6 8.0 %slice-start = ((s8[8388608]{0:T(1024)(128)(4,1)}), s8[4194304]{0:T(1024)(128)(4,1)S(1)}, s32[]{:S(2)}) async-start(s8[8388608]{0:T(1024)(128)(4,1)} %bitcast.1), calls=%async_computation | async-start | bytes 8388608
  24.2 6.4 %slice-start.1 = ((s8[8388608]{0:T(1024)(128)(4,1)}), s8[4194304]{0:T(1024)(128)(4,1)S(1)}, s32[]{:S(2)}) async-start(s8[8388608]{0:T(1024)(128)(4,1)} %bitcast.1), calls=%async_computation.1 | async-start | bytes 8388608
  29.2 1.4 %collective-permute-start.9 = (bf16[128,512]{1,0:T(8,128)(2,1)S(1)}, bf16[128,512]{1,0:T(8,128)(2,1)S(1)}, u32[]{:S(2)}, u32[]{:S(2)}) collective-permute-start(bf16[128,512]{1,0:T(8,128)(2,1)S(1)} %attend_last.3), channel_id=1, source_target_pairs={{0,4},{4,0},{8,12},{12,8},{16,20},{20,16},{24,28},{28,24},{32,36},... | collective-permute-start | bytes 393224 | tf_op jit(solution)/shard_map/ppermute | solution.py:397
  31.1 8.9 %collective-permute-start.10 = (bf16[128,512]{1,0:T(8,128)(2,1)S(1)}, bf16[128,512]{1,0:T(8,128)(2,1)S(1)}, u32[]{:S(2)}, u32[]{:S(2)}) collective-permute-start(bf16[128,512]{1,0:T(8,128)(2,1)S(1)} %get-tuple-element.53), channel_id=1, source_target_pairs={{0,1},{1,2},{2,3},{3,0},{4,5},{5,6},{6,7},{7,4},{8,9},{9,10},{10,1... | collective-permute-start | bytes 393224 | tf_op jit(solution)/shard_map/ppermute | solution.py:434
  33.1 6.9 %collective-permute-start.11 = (bf16[128,512]{1,0:T(8,128)(2,1)S(1)}, bf16[128,512]{1,0:T(8,128)(2,1)S(1)}, u32[]{:S(2)}, u32[]{:S(2)}) collective-permute-start(bf16[128,512]{1,0:T(8,128)(2,1)S(1)} %get-tuple-element.54), channel_id=1, source_target_pairs={{0,3},{1,0},{2,1},{3,2},{4,7},{5,4},{6,5},{7,6},{8,11},{9,8},{10,9... | collective-permute-start | bytes 393224 | tf_op jit(solution)/shard_map/ppermute | solution.py:434
  36.0 7.4 %collective-permute-start.13 = (bf16[128,512]{1,0:T(8,128)(2,1)S(1)}, bf16[128,512]{1,0:T(8,128)(2,1)S(1)}, u32[]{:S(2)}, u32[]{:S(2)}) collective-permute-start(bf16[128,512]{1,0:T(8,128)(2,1)S(1)} %get-tuple-element.56), channel_id=1, source_target_pairs={{0,1},{1,2},{2,3},{3,0},{4,5},{5,6},{6,7},{7,4},{8,9},{9,10},{10,1... | collective-permute-start | bytes 393224 | tf_op jit(solution)/shard_map/ppermute | solution.py:434
  36.0 7.3 %collective-permute-start.14 = (bf16[128,512]{1,0:T(8,128)(2,1)S(1)}, bf16[128,512]{1,0:T(8,128)(2,1)S(1)}, u32[]{:S(2)}, u32[]{:S(2)}) collective-permute-start(bf16[128,512]{1,0:T(8,128)(2,1)S(1)} %get-tuple-element.57), channel_id=1, source_target_pairs={{0,3},{1,0},{2,1},{3,2},{4,7},{5,4},{6,5},{7,6},{8,11},{9,8},{10,9... | collective-permute-start | bytes 393224 | tf_op jit(solution)/shard_map/ppermute | solution.py:434
  40.1 6.2 %collective-permute-start.12 = (bf16[128,512]{1,0:T(8,128)(2,1)S(1)}, bf16[128,512]{1,0:T(8,128)(2,1)S(1)}, u32[]{:S(2)}, u32[]{:S(2)}) collective-permute-start(bf16[128,512]{1,0:T(8,128)(2,1)S(1)} %get-tuple-element.55), channel_id=1, source_target_pairs={{0,1},{1,2},{2,3},{3,0},{4,5},{5,6},{6,7},{7,4},{8,9},{9,10},{10,1... | collective-permute-start | bytes 393224 | tf_op jit(solution)/shard_map/ppermute | solution.py:434
  41.3 5.0 %collective-permute-start.15 = (bf16[128,512]{1,0:T(8,128)(2,1)S(1)}, bf16[128,512]{1,0:T(8,128)(2,1)S(1)}, u32[]{:S(2)}, u32[]{:S(2)}) collective-permute-start(bf16[128,512]{1,0:T(8,128)(2,1)S(1)} %get-tuple-element.58), channel_id=1, source_target_pairs={{0,3},{1,0},{2,1},{3,2},{4,7},{5,4},{6,5},{7,6},{8,11},{9,8},{10,9... | collective-permute-start | bytes 393224 | tf_op jit(solution)/shard_map/ppermute | solution.py:434

commit v13 on v12

--- a/solution.py
+++ b/solution.py
@@ -397,7 +397,11 @@
         return lax.ppermute(value, "ctx", [(r, r ^ 1) for r in range(ranks)])
 
     def along(value, even, odd):
-        moves = [(r, 2 * (odd if r % 2 else even)(r // 2) + r % 2) for r in range(ranks)]
+        moves = []
+        for r in range(ranks):
+            step = odd if r % 2 else even
+            if step is not None:
+                moves.append((r, 2 * step(r // 2) + r % 2))
         return lax.ppermute(value, "ctx", moves)
 
     def ahead(step):
@@ -422,7 +426,7 @@
     far_b = along(bundle_pair(unit, r1, r2, 2, unit), ahead(8), in_row(2))
     out_a = bundle_row(unit, r1, r2, r3, r4)
     far_a = along(out_a, ahead(4), in_row(1))
-    far_c = along(bundle_pair(unit, r1, r2, 1, out_a), ahead(12), in_row(3))
+    far_c = along(bundle_pair(unit, r1, r2, 1, out_a), None, in_row(3))
     qs = project_q(tokens, came, w_query, table)
     state = attend_near(qs, unit, r1, r2)
     state = attend_early(qs, *state, unit, far_b)

time: 47.2 us -> 47.2 us (level)
  starting transfers between devices: 23.4 us -> 21.9 us
  waiting for transfers between devices: 10.4 us -> 11.9 us
    ppermute x7, starting transfers between devices: 11.9 us -> 10.4 us  [along(): return lax.ppermute(value, 'ctx', moves)]
    ppermute x7, waiting for transfers between devices: 7.1 us -> 8.58 us  [along(): return lax.ppermute(value, 'ctx', moves)]
where the time goes in v13:
time: 47.2 us; the launch traced here: 47.1 us
  starting transfers between devices  21.9 us (46%)
  Pallas kernels  13.1 us (28%)
  waiting for transfers between devices  11.9 us (25%)
    ppermute x6, starting transfers between devices, shift(): lax.ppermute(value, 'head', [(g, (g + step) % groups) for g in range(grou...  11 us
    ppermute x7, starting transfers between devices, along(): return lax.ppermute(value, 'ctx', moves)  10.4 us
    ppermute x7, waiting for transfers between devices, along(): return lax.ppermute(value, 'ctx', moves)  8.58 us
    ppermute x6, waiting for transfers between devices, shift(): lax.ppermute(value, 'head', [(g, (g + step) % groups) for g in range(grou...  2.95 us
    pallas_call x1, Pallas kernels, project_own(): call(own_body, 'project_own', (like(ROWS, 2 * HD), like(ROWS, depth), lik...  2.5 us
    pallas_call x2, Pallas kernels, attend_last(): call(body, 'attend_last', like(ROWS, heads * HD), [VMEM] * 6, VMEM, [pltp...  1.96 us
    pallas_call x3, Pallas kernels, project_out(): call(body, 'project_out', (like(ROWS, half, dtype=dtype),) * len(parts),...  1.62 us
    pallas_call x1, Pallas kernels, attend_near(): call(near_body, 'attend_near', (state, state, state), [VMEM] * 4, (VMEM,)...  1.57 us
  transfers between devices with their start and end apart: 16, of which 8 were waited for; matrix products, arithmetic and copies ran while one was open for 0% of the time, Pallas kernels for 22%

profile of v13, /device:TPU:0, one launch (start us, length us, event | category | flops | bytes accessed | tf_op | source)
XLA Modules:
  0.0 47.1 jit_solution(9857729949700239248)
XLA Ops:
  0.5 2.5 %project_own.1 = (bf16[128,256]{1,0:T(8,128)(2,1)S(1)}, bf16[128,4096]{1,0:T(8,128)(2,1)S(1)}, bf16[4096,256]{1,0:T(8,128)(2,1)S(1)}, s32[1,128]{1,0:T(1,128)S(1)}, f32[256,128]{1,0:T(8,128)S(1)}) custom-call(bf16[128,4096]{1,0:T(8,128)(2,1)} %tok.1, bf16[4096,256]{1,0:T(8,128)(2,1)} %wk.1, bf16[4096,256]{1,0:T(8,128)(2,1)} %wv.1, s32[1,128]{1,0:T(1,128)} %bitcast.4, ...), custom_call_target="tpu_custom_call" | custom-call | flops 268435456 | bytes 3145728 | tf_op jit(solution)/shard_map/project_own/pallas_call | solution.py:124
  3.6 1.6 %collective-permute-start.2 = (bf16[264,256]{1,0:T(8,128)(2,1)S(1)}, bf16[264,256]{1,0:T(8,128)(2,1)S(1)}, u32[]{:S(2)}, u32[]{:S(2)}) collective-permute-start(bf16[264,256]{1,0:T(8,128)(2,1)S(1)} %project_unit.1.unit.after), channel_id=1, source_target_pairs={{0,8},{4,36},{8,16},{12,44},{16,24},{20,52},{24,32},{28,60},{32,40... | collective-permute-start | bytes 405512 | tf_op jit(solution)/shard_map/ppermute | solution.py:405
  5.2 2.7 %collective-permute-start.3 = (bf16[264,256]{1,0:T(8,128)(2,1)S(1)}, bf16[264,256]{1,0:T(8,128)(2,1)S(1)}, u32[]{:S(2)}, u32[]{:S(2)}) collective-permute-start(bf16[264,256]{1,0:T(8,128)(2,1)S(1)} %project_unit.1.unit.after), channel_id=1, source_target_pairs={{0,16},{4,68},{8,24},{12,76},{16,32},{20,84},{24,40},{28,92},{32,4... | collective-permute-start | bytes 405512 | tf_op jit(solution)/shard_map/ppermute | solution.py:405
  8.0 2.4 %collective-permute-start.5 = (bf16[264,256]{1,0:T(8,128)(2,1)S(1)}, bf16[264,256]{1,0:T(8,128)(2,1)S(1)}, u32[]{:S(2)}, u32[]{:S(2)}) collective-permute-start(bf16[264,256]{1,0:T(8,128)(2,1)S(1)} %project_unit.1.unit.after), channel_id=1, source_target_pairs={{0,24},{4,100},{8,32},{12,108},{16,40},{20,116},{24,48},{28,124},{... | collective-permute-start | bytes 405512 | tf_op jit(solution)/shard_map/ppermute | solution.py:405
  10.4 1.6 %collective-permute-start.6 = (bf16[264,256]{1,0:T(8,128)(2,1)S(1)}, bf16[264,256]{1,0:T(8,128)(2,1)S(1)}, u32[]{:S(2)}, u32[]{:S(2)}) collective-permute-start(bf16[264,256]{1,0:T(8,128)(2,1)S(1)} %project_unit.1.unit.after), channel_id=1, source_target_pairs={{0,32},{4,28},{8,40},{12,4},{16,48},{20,12},{24,56},{28,20},{32,64... | collective-permute-start | bytes 405512 | tf_op jit(solution)/shard_map/ppermute | solution.py:405
  12.0 1.2 %collective-permute-done.2.r1 = bf16[264,256]{1,0:T(8,128)(2,1)S(1)} collective-permute-done((bf16[264,256]{1,0:T(8,128)(2,1)S(1)}, bf16[264,256]{1,0:T(8,128)(2,1)S(1)}, u32[]{:S(2)}, u32[]{:S(2)}) %collective-permute-start.2) | collective-permute-done | bytes 135200 | tf_op jit(solution)/shard_map/ppermute | solution.py:405
  13.1 2.7 %collective-permute-done.3.r2 = bf16[264,256]{1,0:T(8,128)(2,1)S(1)} collective-permute-done((bf16[264,256]{1,0:T(8,128)(2,1)S(1)}, bf16[264,256]{1,0:T(8,128)(2,1)S(1)}, u32[]{:S(2)}, u32[]{:S(2)}) %collective-permute-start.3) | collective-permute-done | bytes 135200 | tf_op jit(solution)/shard_map/ppermute | solution.py:405
  16.4 1.3 %collective-permute-done.6.after.r4 = bf16[264,256]{1,0:T(8,128)(2,1)S(1)} collective-permute-done((bf16[264,256]{1,0:T(8,128)(2,1)S(1)}, bf16[264,256]{1,0:T(8,128)(2,1)S(1)}, u32[]{:S(2)}, u32[]{:S(2)}) %collective-permute-start.6) | collective-permute-done | bytes 135200 | tf_op jit(solution)/shard_map/ppermute | solution.py:405
  17.8 1.2 %collective-permute-start.8 = (bf16[792,256]{1,0:T(8,128)(2,1)S(1)}, bf16[792,256]{1,0:T(8,128)(2,1)S(1)}, u32[]{:S(2)}, u32[]{:S(2)}) collective-permute-start(bf16[792,256]{1,0:T(8,128)(2,1)S(1)} %bundle_row.1.after), channel_id=1, source_target_pairs={{0,32},{4,12},{8,40},{12,20},{16,48},{20,28},{24,56},{28,4},{32,64... | collective-permute-start | bytes 1216520 | tf_op jit(solution)/shard_map/ppermute | solution.py:405
  19.7 1.4 %project_q.1.qs = bf16[4,256,128]{2,1,0:T(8,128)(2,1)S(1)} custom-call(bf16[128,4096]{1,0:T(8,128)(2,1)S(1)} %get-tuple-element.32.tok, bf16[128,4096]{1,0:T(8,128)(2,1)S(1)} %collective-permute-done.came, bf16[4096,1024]{1,0:T(8,128)(2,1)S(1)} %copy-done, f32[256,128]{1,0:T(8,128)S(1)} %get-tuple-element.36.table), custom_call_target="tpu_custom_call" | custom-call | flops 1073741824 | bytes 6291456 | tf_op jit(solution)/shard_map/project_q/pallas_call | solution.py:171
  21.2 1.6 %attend_near.1 = (f32[4,256,128]{2,1,0:T(8,128)S(1)}, f32[4,256,128]{2,1,0:T(8,128)S(1)}, f32[4,256,128]{2,1,0:T(8,128)S(1)}) custom-call(bf16[4,256,128]{2,1,0:T(8,128)(2,1)S(1)} %project_q.1.qs, bf16[264,256]{1,0:T(8,128)(2,1)S(1)} %project_unit.1.unit.after, bf16[264,256]{1,0:T(8,128)(2,1)S(1)} %collective-permute-done.2.r1, ...), custom_call_target="tpu_custom_call" | custom-call | flops 402653184 | bytes 1048576 | tf_op jit(solution)/shard_map/attend_near/pallas_call | solution.py:281
  22.8 1.2 %collective-permute-done.4.far_b = bf16[528,256]{1,0:T(8,128)(2,1)S(1)} collective-permute-done((bf16[528,256]{1,0:T(8,128)(2,1)S(1)}, bf16[528,256]{1,0:T(8,128)(2,1)S(1)}, u32[]{:S(2)}, u32[]{:S(2)}) %collective-permute-start.4) | collective-permute-done | bytes 270368 | tf_op jit(solution)/shard_map/ppermute | solution.py:405
  24.0 1.2 %attend_early.1 = (f32[4,256,128]{2,1,0:T(8,128)S(1)}, f32[4,256,128]{2,1,0:T(8,128)S(1)}, f32[4,256,128]{2,1,0:T(8,128)S(1)}) custom-call(bf16[4,256,128]{2,1,0:T(8,128)(2,1)S(1)} %project_q.1.qs, f32[4,256,128]{2,1,0:T(8,128)S(1)} %get-tuple-element.40.m_in, f32[4,256,128]{2,1,0:T(8,128)S(1)} %get-tuple-element.41.l_in, ...), custom_call_target="tpu_custom_call" | custom-call | flops 2147483648 | bytes 1048576 | tf_op jit(solution)/shard_map/attend_early/pallas_call | solution.py:298
  25.3 1.2 %attend_middle.1 = (f32[4,256,128]{2,1,0:T(8,128)S(1)}, f32[4,256,128]{2,1,0:T(8,128)S(1)}, f32[4,256,128]{2,1,0:T(8,128)S(1)}) custom-call(bf16[4,256,128]{2,1,0:T(8,128)(2,1)S(1)} %project_q.1.qs, f32[4,256,128]{2,1,0:T(8,128)S(1)} %get-tuple-element.43.m_in, f32[4,256,128]{2,1,0:T(8,128)S(1)} %get-tuple-element.44.l_in, ...), custom_call_target="tpu_custom_call" | custom-call | flops 268435456 | bytes 1048576 | tf_op jit(solution)/shard_map/attend_middle/pallas_call | solution.py:318
  26.5 1.7 %collective-permute-done.8.far_a = bf16[792,256]{1,0:T(8,128)(2,1)S(1)} collective-permute-done((bf16[792,256]{1,0:T(8,128)(2,1)S(1)}, bf16[792,256]{1,0:T(8,128)(2,1)S(1)}, u32[]{:S(2)}, u32[]{:S(2)}) %collective-permute-start.8) | collective-permute-done | bytes 405536 | tf_op jit(solution)/shard_map/ppermute | solution.py:405
  28.2 1.0 %attend_last.3 = bf16[128,512]{1,0:T(8,128)(2,1)S(1)} custom-call(bf16[4,256,128]{2,1,0:T(8,128)(2,1)S(1)} %project_q.1.qs, f32[4,256,128]{2,1,0:T(8,128)S(1)} %get-tuple-element.46.m_in, f32[4,256,128]{2,1,0:T(8,128)S(1)} %get-tuple-element.47.l_in, f32[4,256,128]{2,1,0:T(8,128)S(1)} %get-tuple-element.48.acc_in, ...), custom_call_target="tpu_custom_call" | custom-call | flops 201326592 | bytes 1048576 | tf_op jit(solution)/shard_map/attend_last/pallas_call | solution.py:339
  29.3 1.0 %attend_last.2.xm = bf16[128,512]{1,0:T(8,128)(2,1)S(1)} custom-call(bf16[4,256,128]{2,1,0:T(8,128)(2,1)S(1)} %project_q.1.qs, f32[4,256,128]{2,1,0:T(8,128)S(1)} %get-tuple-element.46.m_in, f32[4,256,128]{2,1,0:T(8,128)S(1)} %get-tuple-element.47.l_in, f32[4,256,128]{2,1,0:T(8,128)S(1)} %get-tuple-element.48.acc_in, ...), custom_call_target="tpu_custom_call" | custom-call | flops 201326592 | bytes 1048576 | tf_op jit(solution)/shard_map/attend_last/pallas_call | solution.py:339
  31.1 2.0 %collective-permute-start.10 = (bf16[128,512]{1,0:T(8,128)(2,1)S(1)}, bf16[128,512]{1,0:T(8,128)(2,1)S(1)}, u32[]{:S(2)}, u32[]{:S(2)}) collective-permute-start(bf16[128,512]{1,0:T(8,128)(2,1)S(1)} %get-tuple-element.53), channel_id=1, source_target_pairs={{0,1},{1,2},{2,3},{3,0},{4,5},{5,6},{6,7},{7,4},{8,9},{9,10},{10,1... | collective-permute-start | bytes 393224 | tf_op jit(solution)/shard_map/ppermute | solution.py:438
  33.1 2.4 %collective-permute-start.11 = (bf16[128,512]{1,0:T(8,128)(2,1)S(1)}, bf16[128,512]{1,0:T(8,128)(2,1)S(1)}, u32[]{:S(2)}, u32[]{:S(2)}) collective-permute-start(bf16[128,512]{1,0:T(8,128)(2,1)S(1)} %get-tuple-element.54), channel_id=1, source_target_pairs={{0,3},{1,0},{2,1},{3,2},{4,7},{5,4},{6,5},{7,6},{8,11},{9,8},{10,9... | collective-permute-start | bytes 393224 | tf_op jit(solution)/shard_map/ppermute | solution.py:438
  36.0 3.2 %collective-permute-start.14 = (bf16[128,512]{1,0:T(8,128)(2,1)S(1)}, bf16[128,512]{1,0:T(8,128)(2,1)S(1)}, u32[]{:S(2)}, u32[]{:S(2)}) collective-permute-start(bf16[128,512]{1,0:T(8,128)(2,1)S(1)} %get-tuple-element.57), channel_id=1, source_target_pairs={{0,3},{1,0},{2,1},{3,2},{4,7},{5,4},{6,5},{7,6},{8,11},{9,8},{10,9... | collective-permute-start | bytes 393224 | tf_op jit(solution)/shard_map/ppermute | solution.py:438
  40.1 1.2 %collective-permute-start.12 = (bf16[128,512]{1,0:T(8,128)(2,1)S(1)}, bf16[128,512]{1,0:T(8,128)(2,1)S(1)}, u32[]{:S(2)}, u32[]{:S(2)}) collective-permute-start(bf16[128,512]{1,0:T(8,128)(2,1)S(1)} %get-tuple-element.55), channel_id=1, source_target_pairs={{0,1},{1,2},{2,3},{3,0},{4,5},{5,6},{6,7},{7,4},{8,9},{9,10},{10,1... | collective-permute-start | bytes 393224 | tf_op jit(solution)/shard_map/ppermute | solution.py:438
  41.3 2.1 %collective-permute-start.15 = (bf16[128,512]{1,0:T(8,128)(2,1)S(1)}, bf16[128,512]{1,0:T(8,128)(2,1)S(1)}, u32[]{:S(2)}, u32[]{:S(2)}) collective-permute-start(bf16[128,512]{1,0:T(8,128)(2,1)S(1)} %get-tuple-element.58), channel_id=1, source_target_pairs={{0,3},{1,0},{2,1},{3,2},{4,7},{5,4},{6,5},{7,6},{8,11},{9,8},{10,9... | collective-permute-start | bytes 393224 | tf_op jit(solution)/shard_map/ppermute | solution.py:438
  43.4 2.9 %collective-permute-done.12.left_a = bf16[128,512]{1,0:T(8,128)(2,1)S(1)} collective-permute-done((bf16[128,512]{1,0:T(8,128)(2,1)S(1)}, bf16[128,512]{1,0:T(8,128)(2,1)S(1)}, u32[]{:S(2)}, u32[]{:S(2)}) %collective-permute-start.12) | collective-permute-done | bytes 131104 | tf_op jit(solution)/shard_map/ppermute | solution.py:438
  46.3 0.8 %add_total.1 = bf16[128,1024]{1,0:T(8,128)(2,1)} custom-call(f32[128,512]{1,0:T(8,128)S(1)} %get-tuple-element.49.own_a, f32[128,512]{1,0:T(8,128)S(1)} %get-tuple-element.50.own_b, bf16[128,512]{1,0:T(8,128)(2,1)S(1)} %collective-permute-done.12.left_a, bf16[128,512]{1,0:T(8,128)(2,1)S(1)} %collective-permute-done.13.left_b, ...), custom_call_target="tpu_custom_call" | custom-call | bytes 1048576 | tf_op jit(solution)/shard_map/add_total/pallas_call | solution.py:388
  (31 shorter events, 4.6 us)
Async XLA Ops:
  0.0 3.0 %collective-permute-start = (bf16[128,4096]{1,0:T(8,128)(2,1)}, bf16[128,4096]{1,0:T(8,128)(2,1)S(1)}, u32[]{:S(2)}, u32[]{:S(2)}) collective-permute-start(bf16[128,4096]{1,0:T(8,128)(2,1)} %tok.1), channel_id=1, source_target_pairs={{0,4},{4,0},{8,12},{12,8},{16,20},{20,16},{24,28},{28,24},{32,36},... | collective-permute-start | bytes 3145736 | tf_op jit(solution)/shard_map/ppermute | solution.py:397
  0.0 3.0 %collective-permute-start.1 = (s32[1,128]{1,0:T(1,128)}, s32[1,128]{1,0:T(1,128)S(1)}, u32[]{:S(2)}, u32[]{:S(2)}) collective-permute-start(s32[1,128]{1,0:T(1,128)} %bitcast.3), channel_id=1, source_target_pairs={{0,4},{4,0},{8,12},{12,8},{16,20},{20,16},{24,28},{28,24},{32,36},... | collective-permute-start | bytes 1544 | tf_op jit(solution)/shard_map/ppermute | solution.py:397
  0.5 19.2 %copy-start = (bf16[4096,1024]{1,0:T(8,128)(2,1)S(1)}, bf16[4096,1024]{1,0:T(8,128)(2,1)}, u32[]{:S(2)}) copy-start(bf16[4096,1024]{1,0:T(8,128)(2,1)} %wq.1) | copy-start | bytes 25165828
  3.6 9.5 %collective-permute-start.2 = (bf16[264,256]{1,0:T(8,128)(2,1)S(1)}, bf16[264,256]{1,0:T(8,128)(2,1)S(1)}, u32[]{:S(2)}, u32[]{:S(2)}) collective-permute-start(bf16[264,256]{1,0:T(8,128)(2,1)S(1)} %project_unit.1.unit.after), channel_id=1, source_target_pairs={{0,8},{4,36},{8,16},{12,44},{16,24},{20,52},{24,32},{28,60},{32,40... | collective-permute-start | bytes 405512 | tf_op jit(solution)/shard_map/ppermute | solution.py:405
  5.2 10.6 %collective-permute-start.3 = (bf16[264,256]{1,0:T(8,128)(2,1)S(1)}, bf16[264,256]{1,0:T(8,128)(2,1)S(1)}, u32[]{:S(2)}, u32[]{:S(2)}) collective-permute-start(bf16[264,256]{1,0:T(8,128)(2,1)S(1)} %project_unit.1.unit.after), channel_id=1, source_target_pairs={{0,16},{4,68},{8,24},{12,76},{16,32},{20,84},{24,40},{28,92},{32,4... | collective-permute-start | bytes 405512 | tf_op jit(solution)/shard_map/ppermute | solution.py:405
  8.0 8.4 %collective-permute-start.5 = (bf16[264,256]{1,0:T(8,128)(2,1)S(1)}, bf16[264,256]{1,0:T(8,128)(2,1)S(1)}, u32[]{:S(2)}, u32[]{:S(2)}) collective-permute-start(bf16[264,256]{1,0:T(8,128)(2,1)S(1)} %project_unit.1.unit.after), channel_id=1, source_target_pairs={{0,24},{4,100},{8,32},{12,108},{16,40},{20,116},{24,48},{28,124},{... | collective-permute-start | bytes 405512 | tf_op jit(solution)/shard_map/ppermute | solution.py:405
  10.4 7.3 %collective-permute-start.6 = (bf16[264,256]{1,0:T(8,128)(2,1)S(1)}, bf16[264,256]{1,0:T(8,128)(2,1)S(1)}, u32[]{:S(2)}, u32[]{:S(2)}) collective-permute-start(bf16[264,256]{1,0:T(8,128)(2,1)S(1)} %project_unit.1.unit.after), channel_id=1, source_target_pairs={{0,32},{4,28},{8,40},{12,4},{16,48},{20,12},{24,56},{28,20},{32,64... | collective-permute-start | bytes 405512 | tf_op jit(solution)/shard_map/ppermute | solution.py:405
  15.9 8.1 %collective-permute-start.4 = (bf16[528,256]{1,0:T(8,128)(2,1)S(1)}, bf16[528,256]{1,0:T(8,128)(2,1)S(1)}, u32[]{:S(2)}, u32[]{:S(2)}) collective-permute-start(bf16[528,256]{1,0:T(8,128)(2,1)S(1)} %bundle_pair.2), channel_id=1, source_target_pairs={{0,64},{4,20},{8,72},{12,28},{16,80},{20,4},{24,88},{28,12},{32,96... | collective-permute-start | bytes 811016 | tf_op jit(solution)/shard_map/ppermute | solution.py:405
  17.8 10.4 %collective-permute-start.8 = (bf16[792,256]{1,0:T(8,128)(2,1)S(1)}, bf16[792,256]{1,0:T(8,128)(2,1)S(1)}, u32[]{:S(2)}, u32[]{:S(2)}) collective-permute-start(bf16[792,256]{1,0:T(8,128)(2,1)S(1)} %bundle_row.1.after), channel_id=1, source_target_pairs={{0,32},{4,12},{8,40},{12,20},{16,48},{20,28},{24,56},{28,4},{32,64... | collective-permute-start | bytes 1216520 | tf_op jit(solution)/shard_map/ppermute | solution.py:405
  19.0 6.2 %collective-permute-start.7 = (bf16[528,256]{1,0:T(8,128)(2,1)S(1)}, bf16[528,256]{1,0:T(8,128)(2,1)S(1)}, u32[]{:S(2)}, u32[]{:S(2)}) collective-permute-start(bf16[528,256]{1,0:T(8,128)(2,1)S(1)} %bundle_pair.3), channel_id=1, source_target_pairs={{4,28},{12,4},{20,12},{28,20},{36,60},{44,36},{52,44},{60,52},{68,... | collective-permute-start | bytes 811016 | tf_op jit(solution)/shard_map/ppermute | solution.py:405
  21.2 9.5 %slice-start = ((s8[8388608]{0:T(1024)(128)(4,1)}), s8[4194304]{0:T(1024)(128)(4,1)S(1)}, s32[]{:S(2)}) async-start(s8[8388608]{0:T(1024)(128)(4,1)} %bitcast.1), calls=%async_computation | async-start | bytes 8388608
  24.0 6.7 %slice-start.1 = ((s8[8388608]{0:T(1024)(128)(4,1)}), s8[4194304]{0:T(1024)(128)(4,1)S(1)}, s32[]{:S(2)}) async-start(s8[8388608]{0:T(1024)(128)(4,1)} %bitcast.1), calls=%async_computation.1 | async-start | bytes 8388608
  29.2 1.4 %collective-permute-start.9 = (bf16[128,512]{1,0:T(8,128)(2,1)S(1)}, bf16[128,512]{1,0:T(8,128)(2,1)S(1)}, u32[]{:S(2)}, u32[]{:S(2)}) collective-permute-start(bf16[128,512]{1,0:T(8,128)(2,1)S(1)} %attend_last.3), channel_id=1, source_target_pairs={{0,4},{4,0},{8,12},{12,8},{16,20},{20,16},{24,28},{28,24},{32,36},... | collective-permute-start | bytes 393224 | tf_op jit(solution)/shard_map/ppermute | solution.py:397
  31.1 8.9 %collective-permute-start.10 = (bf16[128,512]{1,0:T(8,128)(2,1)S(1)}, bf16[128,512]{1,0:T(8,128)(2,1)S(1)}, u32[]{:S(2)}, u32[]{:S(2)}) collective-permute-start(bf16[128,512]{1,0:T(8,128)(2,1)S(1)} %get-tuple-element.53), channel_id=1, source_target_pairs={{0,1},{1,2},{2,3},{3,0},{4,5},{5,6},{6,7},{7,4},{8,9},{9,10},{10,1... | collective-permute-start | bytes 393224 | tf_op jit(solution)/shard_map/ppermute | solution.py:438
  33.1 6.9 %collective-permute-start.11 = (bf16[128,512]{1,0:T(8,128)(2,1)S(1)}, bf16[128,512]{1,0:T(8,128)(2,1)S(1)}, u32[]{:S(2)}, u32[]{:S(2)}) collective-permute-start(bf16[128,512]{1,0:T(8,128)(2,1)S(1)} %get-tuple-element.54), channel_id=1, source_target_pairs={{0,3},{1,0},{2,1},{3,2},{4,7},{5,4},{6,5},{7,6},{8,11},{9,8},{10,9... | collective-permute-start | bytes 393224 | tf_op jit(solution)/shard_map/ppermute | solution.py:438
  36.0 7.4 %collective-permute-start.13 = (bf16[128,512]{1,0:T(8,128)(2,1)S(1)}, bf16[128,512]{1,0:T(8,128)(2,1)S(1)}, u32[]{:S(2)}, u32[]{:S(2)}) collective-permute-start(bf16[128,512]{1,0:T(8,128)(2,1)S(1)} %get-tuple-element.56), channel_id=1, source_target_pairs={{0,1},{1,2},{2,3},{3,0},{4,5},{5,6},{6,7},{7,4},{8,9},{9,10},{10,1... | collective-permute-start | bytes 393224 | tf_op jit(solution)/shard_map/ppermute | solution.py:438
  36.0 7.3 %collective-permute-start.14 = (bf16[128,512]{1,0:T(8,128)(2,1)S(1)}, bf16[128,512]{1,0:T(8,128)(2,1)S(1)}, u32[]{:S(2)}, u32[]{:S(2)}) collective-permute-start(bf16[128,512]{1,0:T(8,128)(2,1)S(1)} %get-tuple-element.57), channel_id=1, source_target_pairs={{0,3},{1,0},{2,1},{3,2},{4,7},{5,4},{6,5},{7,6},{8,11},{9,8},{10,9... | collective-permute-start | bytes 393224 | tf_op jit(solution)/shard_map/ppermute | solution.py:438
  40.1 6.2 %collective-permute-start.12 = (bf16[128,512]{1,0:T(8,128)(2,1)S(1)}, bf16[128,512]{1,0:T(8,128)(2,1)S(1)}, u32[]{:S(2)}, u32[]{:S(2)}) collective-permute-start(bf16[128,512]{1,0:T(8,128)(2,1)S(1)} %get-tuple-element.55), channel_id=1, source_target_pairs={{0,1},{1,2},{2,3},{3,0},{4,5},{5,6},{6,7},{7,4},{8,9},{9,10},{10,1... | collective-permute-start | bytes 393224 | tf_op jit(solution)/shard_map/ppermute | solution.py:438
  41.3 5.0 %collective-permute-start.15 = (bf16[128,512]{1,0:T(8,128)(2,1)S(1)}, bf16[128,512]{1,0:T(8,128)(2,1)S(1)}, u32[]{:S(2)}, u32[]{:S(2)}) collective-permute-start(bf16[128,512]{1,0:T(8,128)(2,1)S(1)} %get-tuple-element.58), channel_id=1, source_target_pairs={{0,3},{1,0},{2,1},{3,2},{4,7},{5,4},{6,5},{7,6},{8,11},{9,8},{10,9... | collective-permute-start | bytes 393224 | tf_op jit(solution)/shard_map/ppermute | solution.py:438

commit v14 on v13

--- a/solution.py
+++ b/solution.py
@@ -176,9 +176,9 @@
 
 NONE = 99
 NEAR = ((1, 2), (4, 8))
-EARLY = ((8, 9), (2, 6))
+EARLY = ((5, 6, 7), (1, 5, 9))
 MIDDLE = ((3, 4), (3, 7))
-LAST = ((5, 6, 7), (1, 5, 9))
+LAST = ((8, 9), (2, 6))
 
 
 def fill(out, slots, late, even):
@@ -423,16 +423,16 @@
     r3 = along(unit, ahead(3), ahead(12))
     r4 = along(unit, ahead(4), in_row(3))
     r1, r2, came = lax.optimization_barrier((r1, r2, came))
-    far_b = along(bundle_pair(unit, r1, r2, 2, unit), ahead(8), in_row(2))
     out_a = bundle_row(unit, r1, r2, r3, r4)
+    far_b = along(bundle_pair(unit, r1, r2, 2, out_a), ahead(8), in_row(2))
     far_a = along(out_a, ahead(4), in_row(1))
     far_c = along(bundle_pair(unit, r1, r2, 1, out_a), None, in_row(3))
     qs = project_q(tokens, came, w_query, table)
     state = attend_near(qs, unit, r1, r2)
-    state = attend_early(qs, *state, unit, far_b)
     state = attend_middle(qs, *state, unit, r3, r4, far_c)
-    xr = swap(attend_last(1, qs, *state, unit, far_a))
-    xm = attend_last(0, qs, *state, unit, far_a)
+    state = attend_early(qs, *state, unit, far_a)
+    xr = swap(attend_last(1, qs, *state, unit, far_b))
+    xm = attend_last(0, qs, *state, unit, far_b)
 
     def shift(value, step):
         return lax.ppermute(value, "head", [(g, (g + step) % groups) for g in range(groups)])

time: 47.2 us -> 50.3 us (1.066)
  starting transfers between devices: 21.9 us -> 23.7 us
  waiting for transfers between devices: 11.9 us -> 13.2 us
    ppermute x7, starting transfers between devices: 10.4 us -> 12.1 us  [along(): return lax.ppermute(value, 'ctx', moves)]
    ppermute x7, waiting for transfers between devices: 8.58 us -> 9.71 us  [along(): return lax.ppermute(value, 'ctx', moves)]
  transfers between devices with their start and end apart: 16 -> 16, of which waited for: 8 -> 5; matrix products, arithmetic and copies ran while one was open for 0% -> 0% of each run, Pallas kernels for 22% -> 21%
where the time goes in v14:
time: 50.3 us; the launch traced here: 50.2 us
  starting transfers between devices  23.7 us (47%)
  waiting for transfers between devices  13.2 us (26%)
  Pallas kernels  13.1 us (26%)
    ppermute x7, starting transfers between devices, along(): return lax.ppermute(value, 'ctx', moves)  12.1 us
    ppermute x6, starting transfers between devices, shift(): lax.ppermute(value, 'head', [(g, (g + step) % groups) for g in range(grou...  11 us
    ppermute x7, waiting for transfers between devices, along(): return lax.ppermute(value, 'ctx', moves)  9.71 us
    ppermute x6, waiting for transfers between devices, shift(): lax.ppermute(value, 'head', [(g, (g + step) % groups) for g in range(grou...  2.95 us
    pallas_call x1, Pallas kernels, project_own(): call(own_body, 'project_own', (like(ROWS, 2 * HD), like(ROWS, depth), lik...  2.5 us
    pallas_call x3, Pallas kernels, project_out(): call(body, 'project_out', (like(ROWS, half, dtype=dtype),) * len(parts),...  1.7 us
    pallas_call x1, Pallas kernels, attend_near(): call(near_body, 'attend_near', (state, state, state), [VMEM] * 4, (VMEM,)...  1.6 us
    pallas_call x2, Pallas kernels, attend_last(): call(body, 'attend_last', like(ROWS, heads * HD), [VMEM] * 6, VMEM, [pltp...  1.57 us
  transfers between devices with their start and end apart: 16, of which 5 were waited for; matrix products, arithmetic and copies ran while one was open for 0% of the time, Pallas kernels for 21%

profile of v14, /device:TPU:0, one launch (start us, length us, event | category | flops | bytes accessed | tf_op | source)
XLA Modules:
  0.0 50.2 jit_solution(6222238820333996222)
XLA Ops:
  0.5 2.5 %project_own.1 = (bf16[128,256]{1,0:T(8,128)(2,1)S(1)}, bf16[128,4096]{1,0:T(8,128)(2,1)S(1)}, bf16[4096,256]{1,0:T(8,128)(2,1)S(1)}, s32[1,128]{1,0:T(1,128)S(1)}, f32[256,128]{1,0:T(8,128)S(1)}) custom-call(bf16[128,4096]{1,0:T(8,128)(2,1)} %tok.1, bf16[4096,256]{1,0:T(8,128)(2,1)} %wk.1, bf16[4096,256]{1,0:T(8,128)(2,1)} %wv.1, s32[1,128]{1,0:T(1,128)} %bitcast.4, ...), custom_call_target="tpu_custom_call" | custom-call | flops 268435456 | bytes 3145728 | tf_op jit(solution)/shard_map/project_own/pallas_call | solution.py:124
  3.6 3.2 %collective-permute-start.3 = (bf16[264,256]{1,0:T(8,128)(2,1)S(1)}, bf16[264,256]{1,0:T(8,128)(2,1)S(1)}, u32[]{:S(2)}, u32[]{:S(2)}) collective-permute-start(bf16[264,256]{1,0:T(8,128)(2,1)S(1)} %project_unit.1.unit), channel_id=1, source_target_pairs={{0,16},{4,68},{8,24},{12,76},{16,32},{20,84},{24,40},{28,92},{32,4... | collective-permute-start | bytes 405512 | tf_op jit(solution)/shard_map/ppermute | solution.py:405
  7.4 1.6 %collective-permute-start.5 = (bf16[264,256]{1,0:T(8,128)(2,1)S(1)}, bf16[264,256]{1,0:T(8,128)(2,1)S(1)}, u32[]{:S(2)}, u32[]{:S(2)}) collective-permute-start(bf16[264,256]{1,0:T(8,128)(2,1)S(1)} %project_unit.1.unit), channel_id=1, source_target_pairs={{0,32},{4,28},{8,40},{12,4},{16,48},{20,12},{24,56},{28,20},{32,64... | collective-permute-start | bytes 405512 | tf_op jit(solution)/shard_map/ppermute | solution.py:405
  8.9 3.7 %collective-permute-start.4 = (bf16[264,256]{1,0:T(8,128)(2,1)S(1)}, bf16[264,256]{1,0:T(8,128)(2,1)S(1)}, u32[]{:S(2)}, u32[]{:S(2)}) collective-permute-start(bf16[264,256]{1,0:T(8,128)(2,1)S(1)} %project_unit.1.unit), channel_id=1, source_target_pairs={{0,24},{4,100},{8,32},{12,108},{16,40},{20,116},{24,48},{28,124},{... | collective-permute-start | bytes 405512 | tf_op jit(solution)/shard_map/ppermute | solution.py:405
  12.6 3.1 %collective-permute-done.2.r1 = bf16[264,256]{1,0:T(8,128)(2,1)S(1)} collective-permute-done((bf16[264,256]{1,0:T(8,128)(2,1)S(1)}, bf16[264,256]{1,0:T(8,128)(2,1)S(1)}, u32[]{:S(2)}, u32[]{:S(2)}) %collective-permute-start.2) | collective-permute-done | bytes 135200 | tf_op jit(solution)/shard_map/ppermute | solution.py:405
  15.7 2.0 %collective-permute-done.5.after.r4 = bf16[264,256]{1,0:T(8,128)(2,1)S(1)} collective-permute-done((bf16[264,256]{1,0:T(8,128)(2,1)S(1)}, bf16[264,256]{1,0:T(8,128)(2,1)S(1)}, u32[]{:S(2)}, u32[]{:S(2)}) %collective-permute-start.5) | collective-permute-done | bytes 135200 | tf_op jit(solution)/shard_map/ppermute | solution.py:405
  17.8 0.6 %collective-permute-start.7 = (bf16[792,256]{1,0:T(8,128)(2,1)S(1)}, bf16[792,256]{1,0:T(8,128)(2,1)S(1)}, u32[]{:S(2)}, u32[]{:S(2)}) collective-permute-start(bf16[792,256]{1,0:T(8,128)(2,1)S(1)} %bundle_row.1.after), channel_id=1, source_target_pairs={{0,32},{4,12},{8,40},{12,20},{16,48},{20,28},{24,56},{28,4},{32,64... | collective-permute-start | bytes 1216520 | tf_op jit(solution)/shard_map/ppermute | solution.py:405
  18.5 0.7 %collective-permute-start.6 = (bf16[528,256]{1,0:T(8,128)(2,1)S(1)}, bf16[528,256]{1,0:T(8,128)(2,1)S(1)}, u32[]{:S(2)}, u32[]{:S(2)}) collective-permute-start(bf16[528,256]{1,0:T(8,128)(2,1)S(1)} %bundle_pair.2), channel_id=1, source_target_pairs={{4,28},{12,4},{20,12},{28,20},{36,60},{44,36},{52,44},{60,52},{68,... | collective-permute-start | bytes 811016 | tf_op jit(solution)/shard_map/ppermute | solution.py:405
  19.2 1.8 %collective-permute-start.8 = (bf16[528,256]{1,0:T(8,128)(2,1)S(1)}, bf16[528,256]{1,0:T(8,128)(2,1)S(1)}, u32[]{:S(2)}, u32[]{:S(2)}) collective-permute-start(bf16[528,256]{1,0:T(8,128)(2,1)S(1)} %bundle_pair.3), channel_id=1, source_target_pairs={{0,64},{4,20},{8,72},{12,28},{16,80},{20,4},{24,88},{28,12},{32,96... | collective-permute-start | bytes 811016 | tf_op jit(solution)/shard_map/ppermute | solution.py:405
  21.0 1.4 %project_q.1.qs = bf16[4,256,128]{2,1,0:T(8,128)(2,1)S(1)} custom-call(bf16[128,4096]{1,0:T(8,128)(2,1)S(1)} %get-tuple-element.32.tok, bf16[128,4096]{1,0:T(8,128)(2,1)S(1)} %collective-permute-done.came, bf16[4096,1024]{1,0:T(8,128)(2,1)S(1)} %copy-done, f32[256,128]{1,0:T(8,128)S(1)} %get-tuple-element.36.table), custom_call_target="tpu_custom_call" | custom-call | flops 1073741824 | bytes 6291456 | tf_op jit(solution)/shard_map/project_q/pallas_call | solution.py:171
  22.4 1.6 %attend_near.1 = (f32[4,256,128]{2,1,0:T(8,128)S(1)}, f32[4,256,128]{2,1,0:T(8,128)S(1)}, f32[4,256,128]{2,1,0:T(8,128)S(1)}) custom-call(bf16[4,256,128]{2,1,0:T(8,128)(2,1)S(1)} %project_q.1.qs, bf16[264,256]{1,0:T(8,128)(2,1)S(1)} %project_unit.1.unit, bf16[264,256]{1,0:T(8,128)(2,1)S(1)} %collective-permute-done.2.r1, ...), custom_call_target="tpu_custom_call" | custom-call | flops 402653184 | bytes 1048576 | tf_op jit(solution)/shard_map/attend_near/pallas_call | solution.py:281
  24.0 1.2 %attend_middle.1 = (f32[4,256,128]{2,1,0:T(8,128)S(1)}, f32[4,256,128]{2,1,0:T(8,128)S(1)}, f32[4,256,128]{2,1,0:T(8,128)S(1)}) custom-call(bf16[4,256,128]{2,1,0:T(8,128)(2,1)S(1)} %project_q.1.qs, f32[4,256,128]{2,1,0:T(8,128)S(1)} %get-tuple-element.40.m_in, f32[4,256,128]{2,1,0:T(8,128)S(1)} %get-tuple-element.41.l_in, ...), custom_call_target="tpu_custom_call" | custom-call | flops 268435456 | bytes 1048576 | tf_op jit(solution)/shard_map/attend_middle/pallas_call | solution.py:318
  25.3 4.6 %collective-permute-done.7.far_b = bf16[792,256]{1,0:T(8,128)(2,1)S(1)} collective-permute-done((bf16[792,256]{1,0:T(8,128)(2,1)S(1)}, bf16[792,256]{1,0:T(8,128)(2,1)S(1)}, u32[]{:S(2)}, u32[]{:S(2)}) %collective-permute-start.7) | collective-permute-done | bytes 405536 | tf_op jit(solution)/shard_map/ppermute | solution.py:405
  29.9 1.5 %attend_early.1 = (f32[4,256,128]{2,1,0:T(8,128)S(1)}, f32[4,256,128]{2,1,0:T(8,128)S(1)}, f32[4,256,128]{2,1,0:T(8,128)S(1)}) custom-call(bf16[4,256,128]{2,1,0:T(8,128)(2,1)S(1)} %project_q.1.qs, f32[4,256,128]{2,1,0:T(8,128)S(1)} %get-tuple-element.43.m_in, f32[4,256,128]{2,1,0:T(8,128)S(1)} %get-tuple-element.44.l_in, ...), custom_call_target="tpu_custom_call" | custom-call | flops 2147483648 | bytes 1048576 | tf_op jit(solution)/shard_map/attend_early/pallas_call | solution.py:298
  31.4 0.8 %attend_last.3 = bf16[128,512]{1,0:T(8,128)(2,1)S(1)} custom-call(bf16[4,256,128]{2,1,0:T(8,128)(2,1)S(1)} %project_q.1.qs, f32[4,256,128]{2,1,0:T(8,128)S(1)} %get-tuple-element.46.m_in, f32[4,256,128]{2,1,0:T(8,128)S(1)} %get-tuple-element.47.l_in, f32[4,256,128]{2,1,0:T(8,128)S(1)} %get-tuple-element.48.acc_in, bf16[264,256]{1,0:T(8,128)(2,1)S(1)} %project_unit.1.unit, ...), custom_call_target="tpu_custom_call" | custom-call | flops 201326592 | bytes 1048576 | tf_op jit(solution)/shard_map/attend_last/pallas_call | solution.py:339
  32.3 0.8 %attend_last.2.xm = bf16[128,512]{1,0:T(8,128)(2,1)S(1)} custom-call(bf16[4,256,128]{2,1,0:T(8,128)(2,1)S(1)} %project_q.1.qs, f32[4,256,128]{2,1,0:T(8,128)S(1)} %get-tuple-element.46.m_in, f32[4,256,128]{2,1,0:T(8,128)S(1)} %get-tuple-element.47.l_in, f32[4,256,128]{2,1,0:T(8,128)S(1)} %get-tuple-element.48.acc_in, bf16[264,256]{1,0:T(8,128)(2,1)S(1)} %project_unit.1.unit, ...), custom_call_target="tpu_custom_call" | custom-call | flops 201326592 | bytes 1048576 | tf_op jit(solution)/shard_map/attend_last/pallas_call | solution.py:339
  34.1 2.0 %collective-permute-start.10 = (bf16[128,512]{1,0:T(8,128)(2,1)S(1)}, bf16[128,512]{1,0:T(8,128)(2,1)S(1)}, u32[]{:S(2)}, u32[]{:S(2)}) collective-permute-start(bf16[128,512]{1,0:T(8,128)(2,1)S(1)} %get-tuple-element.53), channel_id=1, source_target_pairs={{0,1},{1,2},{2,3},{3,0},{4,5},{5,6},{6,7},{7,4},{8,9},{9,10},{10,1... | collective-permute-start | bytes 393224 | tf_op jit(solution)/shard_map/ppermute | solution.py:438
  36.1 2.4 %collective-permute-start.11 = (bf16[128,512]{1,0:T(8,128)(2,1)S(1)}, bf16[128,512]{1,0:T(8,128)(2,1)S(1)}, u32[]{:S(2)}, u32[]{:S(2)}) collective-permute-start(bf16[128,512]{1,0:T(8,128)(2,1)S(1)} %get-tuple-element.54), channel_id=1, source_target_pairs={{0,3},{1,0},{2,1},{3,2},{4,7},{5,4},{6,5},{7,6},{8,11},{9,8},{10,9... | collective-permute-start | bytes 393224 | tf_op jit(solution)/shard_map/ppermute | solution.py:438
  39.1 3.2 %collective-permute-start.14 = (bf16[128,512]{1,0:T(8,128)(2,1)S(1)}, bf16[128,512]{1,0:T(8,128)(2,1)S(1)}, u32[]{:S(2)}, u32[]{:S(2)}) collective-permute-start(bf16[128,512]{1,0:T(8,128)(2,1)S(1)} %get-tuple-element.57), channel_id=1, source_target_pairs={{0,3},{1,0},{2,1},{3,2},{4,7},{5,4},{6,5},{7,6},{8,11},{9,8},{10,9... | collective-permute-start | bytes 393224 | tf_op jit(solution)/shard_map/ppermute | solution.py:438
  42.3 0.8 %project_out.3 = (f32[128,512]{1,0:T(8,128)S(1)}, f32[128,512]{1,0:T(8,128)S(1)}, f32[128,512]{1,0:T(8,128)S(1)}, f32[128,512]{1,0:T(8,128)S(1)}) custom-call(bf16[128,512]{1,0:T(8,128)(2,1)S(1)} %attend_last.2.xm, bf16[128,512]{1,0:T(8,128)(2,1)S(1)} %collective-permute-done.9.xr, bf16[1024,4096]{1,0:T(8,128)(2,1)S(1)} %bitcast.2), custom_call_target="tpu_custom_call" | custom-call | flops 536870912 | bytes 4194304 | tf_op jit(solution)/shard_map/project_out/pallas_call | solution.py:362
  43.1 1.1 %collective-permute-start.12 = (bf16[128,512]{1,0:T(8,128)(2,1)S(1)}, bf16[128,512]{1,0:T(8,128)(2,1)S(1)}, u32[]{:S(2)}, u32[]{:S(2)}) collective-permute-start(bf16[128,512]{1,0:T(8,128)(2,1)S(1)} %get-tuple-element.55), channel_id=1, source_target_pairs={{0,1},{1,2},{2,3},{3,0},{4,5},{5,6},{6,7},{7,4},{8,9},{9,10},{10,1... | collective-permute-start | bytes 393224 | tf_op jit(solution)/shard_map/ppermute | solution.py:438
  44.2 2.2 %collective-permute-start.15 = (bf16[128,512]{1,0:T(8,128)(2,1)S(1)}, bf16[128,512]{1,0:T(8,128)(2,1)S(1)}, u32[]{:S(2)}, u32[]{:S(2)}) collective-permute-start(bf16[128,512]{1,0:T(8,128)(2,1)S(1)} %get-tuple-element.58), channel_id=1, source_target_pairs={{0,3},{1,0},{2,1},{3,2},{4,7},{5,4},{6,5},{7,6},{8,11},{9,8},{10,9... | collective-permute-start | bytes 393224 | tf_op jit(solution)/shard_map/ppermute | solution.py:438
  46.4 2.9 %collective-permute-done.12.left_a = bf16[128,512]{1,0:T(8,128)(2,1)S(1)} collective-permute-done((bf16[128,512]{1,0:T(8,128)(2,1)S(1)}, bf16[128,512]{1,0:T(8,128)(2,1)S(1)}, u32[]{:S(2)}, u32[]{:S(2)}) %collective-permute-start.12) | collective-permute-done | bytes 131104 | tf_op jit(solution)/shard_map/ppermute | solution.py:438
  49.4 0.8 %add_total.1 = bf16[128,1024]{1,0:T(8,128)(2,1)} custom-call(f32[128,512]{1,0:T(8,128)S(1)} %get-tuple-element.49.own_a, f32[128,512]{1,0:T(8,128)S(1)} %get-tuple-element.50.own_b, bf16[128,512]{1,0:T(8,128)(2,1)S(1)} %collective-permute-done.12.left_a, bf16[128,512]{1,0:T(8,128)(2,1)S(1)} %collective-permute-done.13.left_b, ...), custom_call_target="tpu_custom_call" | custom-call | bytes 1048576 | tf_op jit(solution)/shard_map/add_total/pallas_call | solution.py:388
  (31 shorter events, 3.6 us)
Async XLA Ops:
  0.0 3.0 %collective-permute-start = (bf16[128,4096]{1,0:T(8,128)(2,1)}, bf16[128,4096]{1,0:T(8,128)(2,1)S(1)}, u32[]{:S(2)}, u32[]{:S(2)}) collective-permute-start(bf16[128,4096]{1,0:T(8,128)(2,1)} %tok.1), channel_id=1, source_target_pairs={{0,4},{4,0},{8,12},{12,8},{16,20},{20,16},{24,28},{28,24},{32,36},... | collective-permute-start | bytes 3145736 | tf_op jit(solution)/shard_map/ppermute | solution.py:397
  0.0 3.0 %collective-permute-start.1 = (s32[1,128]{1,0:T(1,128)}, s32[1,128]{1,0:T(1,128)S(1)}, u32[]{:S(2)}, u32[]{:S(2)}) collective-permute-start(s32[1,128]{1,0:T(1,128)} %bitcast.3), channel_id=1, source_target_pairs={{0,4},{4,0},{8,12},{12,8},{16,20},{20,16},{24,28},{28,24},{32,36},... | collective-permute-start | bytes 1544 | tf_op jit(solution)/shard_map/ppermute | solution.py:397
  0.5 20.5 %copy-start = (bf16[4096,1024]{1,0:T(8,128)(2,1)S(1)}, bf16[4096,1024]{1,0:T(8,128)(2,1)}, u32[]{:S(2)}) copy-start(bf16[4096,1024]{1,0:T(8,128)(2,1)} %wq.1) | copy-start | bytes 25165828
  3.6 9.0 %collective-permute-start.3 = (bf16[264,256]{1,0:T(8,128)(2,1)S(1)}, bf16[264,256]{1,0:T(8,128)(2,1)S(1)}, u32[]{:S(2)}, u32[]{:S(2)}) collective-permute-start(bf16[264,256]{1,0:T(8,128)(2,1)S(1)} %project_unit.1.unit), channel_id=1, source_target_pairs={{0,16},{4,68},{8,24},{12,76},{16,32},{20,84},{24,40},{28,92},{32,4... | collective-permute-start | bytes 405512 | tf_op jit(solution)/shard_map/ppermute | solution.py:405
  6.8 8.9 %collective-permute-start.2 = (bf16[264,256]{1,0:T(8,128)(2,1)S(1)}, bf16[264,256]{1,0:T(8,128)(2,1)S(1)}, u32[]{:S(2)}, u32[]{:S(2)}) collective-permute-start(bf16[264,256]{1,0:T(8,128)(2,1)S(1)} %project_unit.1.unit), channel_id=1, source_target_pairs={{0,8},{4,36},{8,16},{12,44},{16,24},{20,52},{24,32},{28,60},{32,40... | collective-permute-start | bytes 405512 | tf_op jit(solution)/shard_map/ppermute | solution.py:405
  7.4 10.3 %collective-permute-start.5 = (bf16[264,256]{1,0:T(8,128)(2,1)S(1)}, bf16[264,256]{1,0:T(8,128)(2,1)S(1)}, u32[]{:S(2)}, u32[]{:S(2)}) collective-permute-start(bf16[264,256]{1,0:T(8,128)(2,1)S(1)} %project_unit.1.unit), channel_id=1, source_target_pairs={{0,32},{4,28},{8,40},{12,4},{16,48},{20,12},{24,56},{28,20},{32,64... | collective-permute-start | bytes 405512 | tf_op jit(solution)/shard_map/ppermute | solution.py:405
  8.9 8.8 %collective-permute-start.4 = (bf16[264,256]{1,0:T(8,128)(2,1)S(1)}, bf16[264,256]{1,0:T(8,128)(2,1)S(1)}, u32[]{:S(2)}, u32[]{:S(2)}) collective-permute-start(bf16[264,256]{1,0:T(8,128)(2,1)S(1)} %project_unit.1.unit), channel_id=1, source_target_pairs={{0,24},{4,100},{8,32},{12,108},{16,40},{20,116},{24,48},{28,124},{... | collective-permute-start | bytes 405512 | tf_op jit(solution)/shard_map/ppermute | solution.py:405
  17.8 12.1 %collective-permute-start.7 = (bf16[792,256]{1,0:T(8,128)(2,1)S(1)}, bf16[792,256]{1,0:T(8,128)(2,1)S(1)}, u32[]{:S(2)}, u32[]{:S(2)}) collective-permute-start(bf16[792,256]{1,0:T(8,128)(2,1)S(1)} %bundle_row.1.after), channel_id=1, source_target_pairs={{0,32},{4,12},{8,40},{12,20},{16,48},{20,28},{24,56},{28,4},{32,64... | collective-permute-start | bytes 1216520 | tf_op jit(solution)/shard_map/ppermute | solution.py:405
  18.5 5.6 %collective-permute-start.6 = (bf16[528,256]{1,0:T(8,128)(2,1)S(1)}, bf16[528,256]{1,0:T(8,128)(2,1)S(1)}, u32[]{:S(2)}, u32[]{:S(2)}) collective-permute-start(bf16[528,256]{1,0:T(8,128)(2,1)S(1)} %bundle_pair.2), channel_id=1, source_target_pairs={{4,28},{12,4},{20,12},{28,20},{36,60},{44,36},{52,44},{60,52},{68,... | collective-permute-start | bytes 811016 | tf_op jit(solution)/shard_map/ppermute | solution.py:405
  19.2 12.2 %collective-permute-start.8 = (bf16[528,256]{1,0:T(8,128)(2,1)S(1)}, bf16[528,256]{1,0:T(8,128)(2,1)S(1)}, u32[]{:S(2)}, u32[]{:S(2)}) collective-permute-start(bf16[528,256]{1,0:T(8,128)(2,1)S(1)} %bundle_pair.3), channel_id=1, source_target_pairs={{0,64},{4,20},{8,72},{12,28},{16,80},{20,4},{24,88},{28,12},{32,96... | collective-permute-start | bytes 811016 | tf_op jit(solution)/shard_map/ppermute | solution.py:405
  24.0 9.6 %slice-start = ((s8[8388608]{0:T(1024)(128)(4,1)}), s8[4194304]{0:T(1024)(128)(4,1)S(1)}, s32[]{:S(2)}) async-start(s8[8388608]{0:T(1024)(128)(4,1)} %bitcast.1), calls=%async_computation | async-start | bytes 8388608
  29.9 3.8 %slice-start.1 = ((s8[8388608]{0:T(1024)(128)(4,1)}), s8[4194304]{0:T(1024)(128)(4,1)S(1)}, s32[]{:S(2)}) async-start(s8[8388608]{0:T(1024)(128)(4,1)} %bitcast.1), calls=%async_computation.1 | async-start | bytes 8388608
  32.2 1.4 %collective-permute-start.9 = (bf16[128,512]{1,0:T(8,128)(2,1)S(1)}, bf16[128,512]{1,0:T(8,128)(2,1)S(1)}, u32[]{:S(2)}, u32[]{:S(2)}) collective-permute-start(bf16[128,512]{1,0:T(8,128)(2,1)S(1)} %attend_last.3), channel_id=1, source_target_pairs={{0,4},{4,0},{8,12},{12,8},{16,20},{20,16},{24,28},{28,24},{32,36},... | collective-permute-start | bytes 393224 | tf_op jit(solution)/shard_map/ppermute | solution.py:397
  34.1 8.9 %collective-permute-start.10 = (bf16[128,512]{1,0:T(8,128)(2,1)S(1)}, bf16[128,512]{1,0:T(8,128)(2,1)S(1)}, u32[]{:S(2)}, u32[]{:S(2)}) collective-permute-start(bf16[128,512]{1,0:T(8,128)(2,1)S(1)} %get-tuple-element.53), channel_id=1, source_target_pairs={{0,1},{1,2},{2,3},{3,0},{4,5},{5,6},{6,7},{7,4},{8,9},{9,10},{10,1... | collective-permute-start | bytes 393224 | tf_op jit(solution)/shard_map/ppermute | solution.py:438
  36.1 6.9 %collective-permute-start.11 = (bf16[128,512]{1,0:T(8,128)(2,1)S(1)}, bf16[128,512]{1,0:T(8,128)(2,1)S(1)}, u32[]{:S(2)}, u32[]{:S(2)}) collective-permute-start(bf16[128,512]{1,0:T(8,128)(2,1)S(1)} %get-tuple-element.54), channel_id=1, source_target_pairs={{0,3},{1,0},{2,1},{3,2},{4,7},{5,4},{6,5},{7,6},{8,11},{9,8},{10,9... | collective-permute-start | bytes 393224 | tf_op jit(solution)/shard_map/ppermute | solution.py:438
  39.0 7.5 %collective-permute-start.13 = (bf16[128,512]{1,0:T(8,128)(2,1)S(1)}, bf16[128,512]{1,0:T(8,128)(2,1)S(1)}, u32[]{:S(2)}, u32[]{:S(2)}) collective-permute-start(bf16[128,512]{1,0:T(8,128)(2,1)S(1)} %get-tuple-element.56), channel_id=1, source_target_pairs={{0,1},{1,2},{2,3},{3,0},{4,5},{5,6},{6,7},{7,4},{8,9},{9,10},{10,1... | collective-permute-start | bytes 393224 | tf_op jit(solution)/shard_map/ppermute | solution.py:438
  39.1 7.4 %collective-permute-start.14 = (bf16[128,512]{1,0:T(8,128)(2,1)S(1)}, bf16[128,512]{1,0:T(8,128)(2,1)S(1)}, u32[]{:S(2)}, u32[]{:S(2)}) collective-permute-start(bf16[128,512]{1,0:T(8,128)(2,1)S(1)} %get-tuple-element.57), channel_id=1, source_target_pairs={{0,3},{1,0},{2,1},{3,2},{4,7},{5,4},{6,5},{7,6},{8,11},{9,8},{10,9... | collective-permute-start | bytes 393224 | tf_op jit(solution)/shard_map/ppermute | solution.py:438
  43.1 6.2 %collective-permute-start.12 = (bf16[128,512]{1,0:T(8,128)(2,1)S(1)}, bf16[128,512]{1,0:T(8,128)(2,1)S(1)}, u32[]{:S(2)}, u32[]{:S(2)}) collective-permute-start(bf16[128,512]{1,0:T(8,128)(2,1)S(1)} %get-tuple-element.55), channel_id=1, source_target_pairs={{0,1},{1,2},{2,3},{3,0},{4,5},{5,6},{6,7},{7,4},{8,9},{9,10},{10,1... | collective-permute-start | bytes 393224 | tf_op jit(solution)/shard_map/ppermute | solution.py:438
  44.2 5.1 %collective-permute-start.15 = (bf16[128,512]{1,0:T(8,128)(2,1)S(1)}, bf16[128,512]{1,0:T(8,128)(2,1)S(1)}, u32[]{:S(2)}, u32[]{:S(2)}) collective-permute-start(bf16[128,512]{1,0:T(8,128)(2,1)S(1)} %get-tuple-element.58), channel_id=1, source_target_pairs={{0,3},{1,0},{2,1},{3,2},{4,7},{5,4},{6,5},{7,6},{8,11},{9,8},{10,9... | collective-permute-start | bytes 393224 | tf_op jit(solution)/shard_map/ppermute | solution.py:438

commit v15 on v12

--- a/solution.py
+++ b/solution.py
@@ -189,16 +189,19 @@
         out[i * UNIT : (i + 1) * UNIT, :] = slots[skip + i]
 
 
-def bundle_pair(unit, r1, r2, late, after):
-    def body(unit, r1, r2, after, out, slots):
-        for i, src in enumerate((unit, r1, r2)):
-            slots[i] = src[...]
-        fill(out, slots, late, 0)
-
-    return call(
-        body, "bundle_pair", like(2 * UNIT, 2 * HD), [VMEM] * 4, VMEM,
+def pairs_body(unit, r1, r2, out_b, out_c, slots):
+    for i, src in enumerate((unit, r1, r2)):
+        slots[i] = src[...]
+    fill(out_b, slots, 2, 0)
+    fill(out_c, slots, 1, 0)
+
+
+def bundle_pairs(unit, r1, r2):
+    pair = like(2 * UNIT, 2 * HD)
+    return call(
+        pairs_body, "bundle_pairs", (pair, pair), [VMEM] * 3, (VMEM,) * 2,
         [pltpu.VMEM((3, UNIT, 2 * HD), BF16)], limit=2,
-    )(unit, r1, r2, after)
+    )(unit, r1, r2)
 
 
 def row_body(unit, r1, r2, r3, after, out_a, slots):
@@ -317,7 +320,7 @@
     state = like(heads, CHIP, HD, dtype=F32)
     return call(
         middle_body, "attend_middle", (state,) * 3, [VMEM] * 8, (VMEM,) * 3, limit=8,
-        flops=8 * heads * CHIP * CHIP * HD, exps=2 * heads * CHIP * CHIP,
+        flops=64 * heads * CHIP * CHIP * HD, exps=2 * heads * CHIP * CHIP,
     )(qs, m_in, l_in, acc_in, unit, r3, r4, far_c)
 
 
@@ -419,10 +422,10 @@
     r3 = along(unit, ahead(3), ahead(12))
     r4 = along(unit, ahead(4), in_row(3))
     r1, r2, came = lax.optimization_barrier((r1, r2, came))
-    far_b = along(bundle_pair(unit, r1, r2, 2, unit), ahead(8), in_row(2))
-    out_a = bundle_row(unit, r1, r2, r3, r4)
-    far_a = along(out_a, ahead(4), in_row(1))
-    far_c = along(bundle_pair(unit, r1, r2, 1, out_a), ahead(12), in_row(3))
+    out_b, out_c = bundle_pairs(unit, r1, r2)
+    far_b = along(out_b, ahead(8), in_row(2))
+    far_c = along(out_c, ahead(12), in_row(3))
+    far_a = along(bundle_row(unit, r1, r2, r3, r4), ahead(4), in_row(1))
     qs = project_q(tokens, came, w_query, table)
     state = attend_near(qs, unit, r1, r2)
     state = attend_early(qs, *state, unit, far_b)

time: 47.2 us -> 47.2 us (level)
  waiting for transfers between devices: 10.4 us -> 11.7 us
  starting transfers between devices: 23.4 us -> 22.4 us
    ppermute x7, waiting for transfers between devices: 7.1 us -> 8.37 us  [along(): return lax.ppermute(value, 'ctx', moves)]
    ppermute x7, starting transfers between devices: 11.9 us -> 10.8 us  [along(): return lax.ppermute(value, 'ctx', moves)]
  transfers between devices with their start and end apart: 16 -> 16, of which waited for: 8 -> 7; matrix products, arithmetic and copies ran while one was open for 0% -> 0% of each run, Pallas kernels for 22% -> 21%
where the time goes in v15:
time: 47.2 us; the launch traced here: 47.1 us
  starting transfers between devices  22.4 us (47%)
  Pallas kernels  12.9 us (27%)
  waiting for transfers between devices  11.7 us (25%)
    ppermute x6, starting transfers between devices, shift(): lax.ppermute(value, 'head', [(g, (g + step) % groups) for g in range(grou...  11 us
    ppermute x7, starting transfers between devices, along(): return lax.ppermute(value, 'ctx', moves)  10.8 us
    ppermute x7, waiting for transfers between devices, along(): return lax.ppermute(value, 'ctx', moves)  8.37 us
    ppermute x6, waiting for transfers between devices, shift(): lax.ppermute(value, 'head', [(g, (g + step) % groups) for g in range(grou...  2.95 us
    pallas_call x1, Pallas kernels, project_own(): call(own_body, 'project_own', (like(ROWS, 2 * HD), like(ROWS, depth), lik...  2.5 us
    pallas_call x2, Pallas kernels, attend_last(): call(body, 'attend_last', like(ROWS, heads * HD), [VMEM] * 6, VMEM, [pltp...  2 us
    pallas_call x3, Pallas kernels, project_out(): call(body, 'project_out', (like(ROWS, half, dtype=dtype),) * len(parts),...  1.64 us
    pallas_call x1, Pallas kernels, attend_near(): call(near_body, 'attend_near', (state, state, state), [VMEM] * 4, (VMEM,)...  1.49 us
  transfers between devices with their start and end apart: 16, of which 7 were waited for; matrix products, arithmetic and copies ran while one was open for 0% of the time, Pallas kernels for 21%

profile of v15, /device:TPU:0, one launch (start us, length us, event | category | flops | bytes accessed | tf_op | source)
XLA Modules:
  0.0 47.1 jit_solution(16996685686269370168)
XLA Ops:
  0.5 2.5 %project_own.1 = (bf16[128,256]{1,0:T(8,128)(2,1)S(1)}, bf16[128,4096]{1,0:T(8,128)(2,1)S(1)}, bf16[4096,256]{1,0:T(8,128)(2,1)S(1)}, s32[1,128]{1,0:T(1,128)S(1)}, f32[256,128]{1,0:T(8,128)S(1)}) custom-call(bf16[128,4096]{1,0:T(8,128)(2,1)} %tok.1, bf16[4096,256]{1,0:T(8,128)(2,1)} %wk.1, bf16[4096,256]{1,0:T(8,128)(2,1)} %wv.1, s32[1,128]{1,0:T(1,128)} %bitcast.4, ...), custom_call_target="tpu_custom_call" | custom-call | flops 268435456 | bytes 3145728 | tf_op jit(solution)/shard_map/project_own/pallas_call | solution.py:124
  3.6 1.6 %collective-permute-start.2 = (bf16[264,256]{1,0:T(8,128)(2,1)S(1)}, bf16[264,256]{1,0:T(8,128)(2,1)S(1)}, u32[]{:S(2)}, u32[]{:S(2)}) collective-permute-start(bf16[264,256]{1,0:T(8,128)(2,1)S(1)} %project_unit.1.unit), channel_id=1, source_target_pairs={{0,8},{4,36},{8,16},{12,44},{16,24},{20,52},{24,32},{28,60},{32,40... | collective-permute-start | bytes 405512 | tf_op jit(solution)/shard_map/ppermute | solution.py:404
  5.2 2.7 %collective-permute-start.3 = (bf16[264,256]{1,0:T(8,128)(2,1)S(1)}, bf16[264,256]{1,0:T(8,128)(2,1)S(1)}, u32[]{:S(2)}, u32[]{:S(2)}) collective-permute-start(bf16[264,256]{1,0:T(8,128)(2,1)S(1)} %project_unit.1.unit), channel_id=1, source_target_pairs={{0,16},{4,68},{8,24},{12,76},{16,32},{20,84},{24,40},{28,92},{32,4... | collective-permute-start | bytes 405512 | tf_op jit(solution)/shard_map/ppermute | solution.py:404
  8.0 2.4 %collective-permute-start.5 = (bf16[264,256]{1,0:T(8,128)(2,1)S(1)}, bf16[264,256]{1,0:T(8,128)(2,1)S(1)}, u32[]{:S(2)}, u32[]{:S(2)}) collective-permute-start(bf16[264,256]{1,0:T(8,128)(2,1)S(1)} %project_unit.1.unit), channel_id=1, source_target_pairs={{0,24},{4,100},{8,32},{12,108},{16,40},{20,116},{24,48},{28,124},{... | collective-permute-start | bytes 405512 | tf_op jit(solution)/shard_map/ppermute | solution.py:404
  10.4 1.6 %collective-permute-start.6 = (bf16[264,256]{1,0:T(8,128)(2,1)S(1)}, bf16[264,256]{1,0:T(8,128)(2,1)S(1)}, u32[]{:S(2)}, u32[]{:S(2)}) collective-permute-start(bf16[264,256]{1,0:T(8,128)(2,1)S(1)} %project_unit.1.unit), channel_id=1, source_target_pairs={{0,32},{4,28},{8,40},{12,4},{16,48},{20,12},{24,56},{28,20},{32,64... | collective-permute-start | bytes 405512 | tf_op jit(solution)/shard_map/ppermute | solution.py:404
  12.0 1.2 %collective-permute-done.2.r1 = bf16[264,256]{1,0:T(8,128)(2,1)S(1)} collective-permute-done((bf16[264,256]{1,0:T(8,128)(2,1)S(1)}, bf16[264,256]{1,0:T(8,128)(2,1)S(1)}, u32[]{:S(2)}, u32[]{:S(2)}) %collective-permute-start.2) | collective-permute-done | bytes 135200 | tf_op jit(solution)/shard_map/ppermute | solution.py:404
  13.1 2.7 %collective-permute-done.3.r2 = bf16[264,256]{1,0:T(8,128)(2,1)S(1)} collective-permute-done((bf16[264,256]{1,0:T(8,128)(2,1)S(1)}, bf16[264,256]{1,0:T(8,128)(2,1)S(1)}, u32[]{:S(2)}, u32[]{:S(2)}) %collective-permute-start.3) | collective-permute-done | bytes 135200 | tf_op jit(solution)/shard_map/ppermute | solution.py:404
  16.0 1.2 %collective-permute-start.7 = (bf16[528,256]{1,0:T(8,128)(2,1)S(1)}, bf16[528,256]{1,0:T(8,128)(2,1)S(1)}, u32[]{:S(2)}, u32[]{:S(2)}) collective-permute-start(bf16[528,256]{1,0:T(8,128)(2,1)S(1)} %get-tuple-element.49), channel_id=1, source_target_pairs={{0,96},{4,28},{8,104},{12,4},{16,112},{20,12},{24,120},{28,20},{32... | collective-permute-start | bytes 811016 | tf_op jit(solution)/shard_map/ppermute | solution.py:404
  17.8 1.2 %collective-permute-start.8 = (bf16[792,256]{1,0:T(8,128)(2,1)S(1)}, bf16[792,256]{1,0:T(8,128)(2,1)S(1)}, u32[]{:S(2)}, u32[]{:S(2)}) collective-permute-start(bf16[792,256]{1,0:T(8,128)(2,1)S(1)} %bundle_row.1), channel_id=1, source_target_pairs={{0,32},{4,12},{8,40},{12,20},{16,48},{20,28},{24,56},{28,4},{32,64... | collective-permute-start | bytes 1216520 | tf_op jit(solution)/shard_map/ppermute | solution.py:404
  19.0 1.4 %project_q.1.qs = bf16[4,256,128]{2,1,0:T(8,128)(2,1)S(1)} custom-call(bf16[128,4096]{1,0:T(8,128)(2,1)S(1)} %get-tuple-element.34.tok, bf16[128,4096]{1,0:T(8,128)(2,1)S(1)} %collective-permute-done.came, bf16[4096,1024]{1,0:T(8,128)(2,1)S(1)} %copy-done, f32[256,128]{1,0:T(8,128)S(1)} %get-tuple-element.38.table), custom_call_target="tpu_custom_call" | custom-call | flops 1073741824 | bytes 6291456 | tf_op jit(solution)/shard_map/project_q/pallas_call | solution.py:171
  20.4 1.5 %attend_near.1 = (f32[4,256,128]{2,1,0:T(8,128)S(1)}, f32[4,256,128]{2,1,0:T(8,128)S(1)}, f32[4,256,128]{2,1,0:T(8,128)S(1)}) custom-call(bf16[4,256,128]{2,1,0:T(8,128)(2,1)S(1)} %project_q.1.qs, bf16[264,256]{1,0:T(8,128)(2,1)S(1)} %project_unit.1.unit, bf16[264,256]{1,0:T(8,128)(2,1)S(1)} %collective-permute-done.2.r1, ...), custom_call_target="tpu_custom_call" | custom-call | flops 402653184 | bytes 1048576 | tf_op jit(solution)/shard_map/attend_near/pallas_call | solution.py:284
  21.9 2.1 %collective-permute-done.4.far_b = bf16[528,256]{1,0:T(8,128)(2,1)S(1)} collective-permute-done((bf16[528,256]{1,0:T(8,128)(2,1)S(1)}, bf16[528,256]{1,0:T(8,128)(2,1)S(1)}, u32[]{:S(2)}, u32[]{:S(2)}) %collective-permute-start.4) | collective-permute-done | bytes 270368 | tf_op jit(solution)/shard_map/ppermute | solution.py:404
  24.0 1.2 %attend_early.1 = (f32[4,256,128]{2,1,0:T(8,128)S(1)}, f32[4,256,128]{2,1,0:T(8,128)S(1)}, f32[4,256,128]{2,1,0:T(8,128)S(1)}) custom-call(bf16[4,256,128]{2,1,0:T(8,128)(2,1)S(1)} %project_q.1.qs, f32[4,256,128]{2,1,0:T(8,128)S(1)} %get-tuple-element.42.m_in, f32[4,256,128]{2,1,0:T(8,128)S(1)} %get-tuple-element.43.l_in, ...), custom_call_target="tpu_custom_call" | custom-call | flops 2147483648 | bytes 1048576 | tf_op jit(solution)/shard_map/attend_early/pallas_call | solution.py:301
  25.2 1.2 %attend_middle.1 = (f32[4,256,128]{2,1,0:T(8,128)S(1)}, f32[4,256,128]{2,1,0:T(8,128)S(1)}, f32[4,256,128]{2,1,0:T(8,128)S(1)}) custom-call(bf16[4,256,128]{2,1,0:T(8,128)(2,1)S(1)} %project_q.1.qs, f32[4,256,128]{2,1,0:T(8,128)S(1)} %get-tuple-element.46.m_in, f32[4,256,128]{2,1,0:T(8,128)S(1)} %get-tuple-element.47.l_in, ...), custom_call_target="tpu_custom_call" | custom-call | flops 2147483648 | bytes 1048576 | tf_op jit(solution)/shard_map/attend_middle/pallas_call | solution.py:321
  26.4 1.8 %collective-permute-done.8.far_a = bf16[792,256]{1,0:T(8,128)(2,1)S(1)} collective-permute-done((bf16[792,256]{1,0:T(8,128)(2,1)S(1)}, bf16[792,256]{1,0:T(8,128)(2,1)S(1)}, u32[]{:S(2)}, u32[]{:S(2)}) %collective-permute-start.8) | collective-permute-done | bytes 405536 | tf_op jit(solution)/shard_map/ppermute | solution.py:404
  28.3 1.0 %attend_last.3 = bf16[128,512]{1,0:T(8,128)(2,1)S(1)} custom-call(bf16[4,256,128]{2,1,0:T(8,128)(2,1)S(1)} %project_q.1.qs, f32[4,256,128]{2,1,0:T(8,128)S(1)} %get-tuple-element.50.m_in, f32[4,256,128]{2,1,0:T(8,128)S(1)} %get-tuple-element.51.l_in, f32[4,256,128]{2,1,0:T(8,128)S(1)} %get-tuple-element.52.acc_in, bf16[264,256]{1,0:T(8,128)(2,1)S(1)} %project_unit.1.unit, ...), custom_call_target="tpu_custom_call" | custom-call | flops 201326592 | bytes 1048576 | tf_op jit(solution)/shard_map/attend_last/pallas_call | solution.py:342
  29.4 1.0 %attend_last.2.xm = bf16[128,512]{1,0:T(8,128)(2,1)S(1)} custom-call(bf16[4,256,128]{2,1,0:T(8,128)(2,1)S(1)} %project_q.1.qs, f32[4,256,128]{2,1,0:T(8,128)S(1)} %get-tuple-element.50.m_in, f32[4,256,128]{2,1,0:T(8,128)S(1)} %get-tuple-element.51.l_in, f32[4,256,128]{2,1,0:T(8,128)S(1)} %get-tuple-element.52.acc_in, bf16[264,256]{1,0:T(8,128)(2,1)S(1)} %project_unit.1.unit, ...), custom_call_target="tpu_custom_call" | custom-call | flops 201326592 | bytes 1048576 | tf_op jit(solution)/shard_map/attend_last/pallas_call | solution.py:342
  31.2 2.0 %collective-permute-start.10 = (bf16[128,512]{1,0:T(8,128)(2,1)S(1)}, bf16[128,512]{1,0:T(8,128)(2,1)S(1)}, u32[]{:S(2)}, u32[]{:S(2)}) collective-permute-start(bf16[128,512]{1,0:T(8,128)(2,1)S(1)} %get-tuple-element.57), channel_id=1, source_target_pairs={{0,1},{1,2},{2,3},{3,0},{4,5},{5,6},{6,7},{7,4},{8,9},{9,10},{10,1... | collective-permute-start | bytes 393224 | tf_op jit(solution)/shard_map/ppermute | solution.py:437
  33.1 2.4 %collective-permute-start.11 = (bf16[128,512]{1,0:T(8,128)(2,1)S(1)}, bf16[128,512]{1,0:T(8,128)(2,1)S(1)}, u32[]{:S(2)}, u32[]{:S(2)}) collective-permute-start(bf16[128,512]{1,0:T(8,128)(2,1)S(1)} %get-tuple-element.58), channel_id=1, source_target_pairs={{0,3},{1,0},{2,1},{3,2},{4,7},{5,4},{6,5},{7,6},{8,11},{9,8},{10,9... | collective-permute-start | bytes 393224 | tf_op jit(solution)/shard_map/ppermute | solution.py:437
  36.1 3.2 %collective-permute-start.14 = (bf16[128,512]{1,0:T(8,128)(2,1)S(1)}, bf16[128,512]{1,0:T(8,128)(2,1)S(1)}, u32[]{:S(2)}, u32[]{:S(2)}) collective-permute-start(bf16[128,512]{1,0:T(8,128)(2,1)S(1)} %get-tuple-element.61), channel_id=1, source_target_pairs={{0,3},{1,0},{2,1},{3,2},{4,7},{5,4},{6,5},{7,6},{8,11},{9,8},{10,9... | collective-permute-start | bytes 393224 | tf_op jit(solution)/shard_map/ppermute | solution.py:437
  40.1 1.2 %collective-permute-start.12 = (bf16[128,512]{1,0:T(8,128)(2,1)S(1)}, bf16[128,512]{1,0:T(8,128)(2,1)S(1)}, u32[]{:S(2)}, u32[]{:S(2)}) collective-permute-start(bf16[128,512]{1,0:T(8,128)(2,1)S(1)} %get-tuple-element.59), channel_id=1, source_target_pairs={{0,1},{1,2},{2,3},{3,0},{4,5},{5,6},{6,7},{7,4},{8,9},{9,10},{10,1... | collective-permute-start | bytes 393224 | tf_op jit(solution)/shard_map/ppermute | solution.py:437
  41.3 2.1 %collective-permute-start.15 = (bf16[128,512]{1,0:T(8,128)(2,1)S(1)}, bf16[128,512]{1,0:T(8,128)(2,1)S(1)}, u32[]{:S(2)}, u32[]{:S(2)}) collective-permute-start(bf16[128,512]{1,0:T(8,128)(2,1)S(1)} %get-tuple-element.62), channel_id=1, source_target_pairs={{0,3},{1,0},{2,1},{3,2},{4,7},{5,4},{6,5},{7,6},{8,11},{9,8},{10,9... | collective-permute-start | bytes 393224 | tf_op jit(solution)/shard_map/ppermute | solution.py:437
  43.4 2.9 %collective-permute-done.12.left_a = bf16[128,512]{1,0:T(8,128)(2,1)S(1)} collective-permute-done((bf16[128,512]{1,0:T(8,128)(2,1)S(1)}, bf16[128,512]{1,0:T(8,128)(2,1)S(1)}, u32[]{:S(2)}, u32[]{:S(2)}) %collective-permute-start.12) | collective-permute-done | bytes 131104 | tf_op jit(solution)/shard_map/ppermute | solution.py:437
  46.4 0.8 %add_total.1 = bf16[128,1024]{1,0:T(8,128)(2,1)} custom-call(f32[128,512]{1,0:T(8,128)S(1)} %get-tuple-element.53.own_a, f32[128,512]{1,0:T(8,128)S(1)} %get-tuple-element.54.own_b, bf16[128,512]{1,0:T(8,128)(2,1)S(1)} %collective-permute-done.12.left_a, bf16[128,512]{1,0:T(8,128)(2,1)S(1)} %collective-permute-done.13.left_b, ...), custom_call_target="tpu_custom_call" | custom-call | bytes 1048576 | tf_op jit(solution)/shard_map/add_total/pallas_call | solution.py:391
  (30 shorter events, 4.1 us)
Async XLA Ops:
  0.0 3.0 %collective-permute-start = (bf16[128,4096]{1,0:T(8,128)(2,1)}, bf16[128,4096]{1,0:T(8,128)(2,1)S(1)}, u32[]{:S(2)}, u32[]{:S(2)}) collective-permute-start(bf16[128,4096]{1,0:T(8,128)(2,1)} %tok.1), channel_id=1, source_target_pairs={{0,4},{4,0},{8,12},{12,8},{16,20},{20,16},{24,28},{28,24},{32,36},... | collective-permute-start | bytes 3145736 | tf_op jit(solution)/shard_map/ppermute | solution.py:400
  0.0 3.0 %collective-permute-start.1 = (s32[1,128]{1,0:T(1,128)}, s32[1,128]{1,0:T(1,128)S(1)}, u32[]{:S(2)}, u32[]{:S(2)}) collective-permute-start(s32[1,128]{1,0:T(1,128)} %bitcast.3), channel_id=1, source_target_pairs={{0,4},{4,0},{8,12},{12,8},{16,20},{20,16},{24,28},{28,24},{32,36},... | collective-permute-start | bytes 1544 | tf_op jit(solution)/shard_map/ppermute | solution.py:400
  0.5 18.5 %copy-start = (bf16[4096,1024]{1,0:T(8,128)(2,1)S(1)}, bf16[4096,1024]{1,0:T(8,128)(2,1)}, u32[]{:S(2)}) copy-start(bf16[4096,1024]{1,0:T(8,128)(2,1)} %wq.1) | copy-start | bytes 25165828
  3.6 9.5 %collective-permute-start.2 = (bf16[264,256]{1,0:T(8,128)(2,1)S(1)}, bf16[264,256]{1,0:T(8,128)(2,1)S(1)}, u32[]{:S(2)}, u32[]{:S(2)}) collective-permute-start(bf16[264,256]{1,0:T(8,128)(2,1)S(1)} %project_unit.1.unit), channel_id=1, source_target_pairs={{0,8},{4,36},{8,16},{12,44},{16,24},{20,52},{24,32},{28,60},{32,40... | collective-permute-start | bytes 405512 | tf_op jit(solution)/shard_map/ppermute | solution.py:404
  5.2 10.6 %collective-permute-start.3 = (bf16[264,256]{1,0:T(8,128)(2,1)S(1)}, bf16[264,256]{1,0:T(8,128)(2,1)S(1)}, u32[]{:S(2)}, u32[]{:S(2)}) collective-permute-start(bf16[264,256]{1,0:T(8,128)(2,1)S(1)} %project_unit.1.unit), channel_id=1, source_target_pairs={{0,16},{4,68},{8,24},{12,76},{16,32},{20,84},{24,40},{28,92},{32,4... | collective-permute-start | bytes 405512 | tf_op jit(solution)/shard_map/ppermute | solution.py:404
  8.0 9.2 %collective-permute-start.5 = (bf16[264,256]{1,0:T(8,128)(2,1)S(1)}, bf16[264,256]{1,0:T(8,128)(2,1)S(1)}, u32[]{:S(2)}, u32[]{:S(2)}) collective-permute-start(bf16[264,256]{1,0:T(8,128)(2,1)S(1)} %project_unit.1.unit), channel_id=1, source_target_pairs={{0,24},{4,100},{8,32},{12,108},{16,40},{20,116},{24,48},{28,124},{... | collective-permute-start | bytes 405512 | tf_op jit(solution)/shard_map/ppermute | solution.py:404
  10.4 7.3 %collective-permute-start.6 = (bf16[264,256]{1,0:T(8,128)(2,1)S(1)}, bf16[264,256]{1,0:T(8,128)(2,1)S(1)}, u32[]{:S(2)}, u32[]{:S(2)}) collective-permute-start(bf16[264,256]{1,0:T(8,128)(2,1)S(1)} %project_unit.1.unit), channel_id=1, source_target_pairs={{0,32},{4,28},{8,40},{12,4},{16,48},{20,12},{24,56},{28,20},{32,64... | collective-permute-start | bytes 405512 | tf_op jit(solution)/shard_map/ppermute | solution.py:404
  15.9 8.1 %collective-permute-start.4 = (bf16[528,256]{1,0:T(8,128)(2,1)S(1)}, bf16[528,256]{1,0:T(8,128)(2,1)S(1)}, u32[]{:S(2)}, u32[]{:S(2)}) collective-permute-start(bf16[528,256]{1,0:T(8,128)(2,1)S(1)} %get-tuple-element.45), channel_id=1, source_target_pairs={{0,64},{4,20},{8,72},{12,28},{16,80},{20,4},{24,88},{28,12},{32,96... | collective-permute-start | bytes 811016 | tf_op jit(solution)/shard_map/ppermute | solution.py:404
  16.0 9.2 %collective-permute-start.7 = (bf16[528,256]{1,0:T(8,128)(2,1)S(1)}, bf16[528,256]{1,0:T(8,128)(2,1)S(1)}, u32[]{:S(2)}, u32[]{:S(2)}) collective-permute-start(bf16[528,256]{1,0:T(8,128)(2,1)S(1)} %get-tuple-element.49), channel_id=1, source_target_pairs={{0,96},{4,28},{8,104},{12,4},{16,112},{20,12},{24,120},{28,20},{32... | collective-permute-start | bytes 811016 | tf_op jit(solution)/shard_map/ppermute | solution.py:404
  17.8 10.5 %collective-permute-start.8 = (bf16[792,256]{1,0:T(8,128)(2,1)S(1)}, bf16[792,256]{1,0:T(8,128)(2,1)S(1)}, u32[]{:S(2)}, u32[]{:S(2)}) collective-permute-start(bf16[792,256]{1,0:T(8,128)(2,1)S(1)} %bundle_row.1), channel_id=1, source_target_pairs={{0,32},{4,12},{8,40},{12,20},{16,48},{20,28},{24,56},{28,4},{32,64... | collective-permute-start | bytes 1216520 | tf_op jit(solution)/shard_map/ppermute | solution.py:404
  24.0 6.7 %slice-start = ((s8[8388608]{0:T(1024)(128)(4,1)}), s8[4194304]{0:T(1024)(128)(4,1)S(1)}, s32[]{:S(2)}) async-start(s8[8388608]{0:T(1024)(128)(4,1)} %bitcast.1), calls=%async_computation | async-start | bytes 8388608
  25.2 5.5 %slice-start.1 = ((s8[8388608]{0:T(1024)(128)(4,1)}), s8[4194304]{0:T(1024)(128)(4,1)S(1)}, s32[]{:S(2)}) async-start(s8[8388608]{0:T(1024)(128)(4,1)} %bitcast.1), calls=%async_computation.1 | async-start | bytes 8388608
  29.3 1.4 %collective-permute-start.9 = (bf16[128,512]{1,0:T(8,128)(2,1)S(1)}, bf16[128,512]{1,0:T(8,128)(2,1)S(1)}, u32[]{:S(2)}, u32[]{:S(2)}) collective-permute-start(bf16[128,512]{1,0:T(8,128)(2,1)S(1)} %attend_last.3), channel_id=1, source_target_pairs={{0,4},{4,0},{8,12},{12,8},{16,20},{20,16},{24,28},{28,24},{32,36},... | collective-permute-start | bytes 393224 | tf_op jit(solution)/shard_map/ppermute | solution.py:400
  31.2 8.9 %collective-permute-start.10 = (bf16[128,512]{1,0:T(8,128)(2,1)S(1)}, bf16[128,512]{1,0:T(8,128)(2,1)S(1)}, u32[]{:S(2)}, u32[]{:S(2)}) collective-permute-start(bf16[128,512]{1,0:T(8,128)(2,1)S(1)} %get-tuple-element.57), channel_id=1, source_target_pairs={{0,1},{1,2},{2,3},{3,0},{4,5},{5,6},{6,7},{7,4},{8,9},{9,10},{10,1... | collective-permute-start | bytes 393224 | tf_op jit(solution)/shard_map/ppermute | solution.py:437
  33.1 6.9 %collective-permute-start.11 = (bf16[128,512]{1,0:T(8,128)(2,1)S(1)}, bf16[128,512]{1,0:T(8,128)(2,1)S(1)}, u32[]{:S(2)}, u32[]{:S(2)}) collective-permute-start(bf16[128,512]{1,0:T(8,128)(2,1)S(1)} %get-tuple-element.58), channel_id=1, source_target_pairs={{0,3},{1,0},{2,1},{3,2},{4,7},{5,4},{6,5},{7,6},{8,11},{9,8},{10,9... | collective-permute-start | bytes 393224 | tf_op jit(solution)/shard_map/ppermute | solution.py:437
  36.0 7.4 %collective-permute-start.13 = (bf16[128,512]{1,0:T(8,128)(2,1)S(1)}, bf16[128,512]{1,0:T(8,128)(2,1)S(1)}, u32[]{:S(2)}, u32[]{:S(2)}) collective-permute-start(bf16[128,512]{1,0:T(8,128)(2,1)S(1)} %get-tuple-element.60), channel_id=1, source_target_pairs={{0,1},{1,2},{2,3},{3,0},{4,5},{5,6},{6,7},{7,4},{8,9},{9,10},{10,1... | collective-permute-start | bytes 393224 | tf_op jit(solution)/shard_map/ppermute | solution.py:437
  36.1 7.3 %collective-permute-start.14 = (bf16[128,512]{1,0:T(8,128)(2,1)S(1)}, bf16[128,512]{1,0:T(8,128)(2,1)S(1)}, u32[]{:S(2)}, u32[]{:S(2)}) collective-permute-start(bf16[128,512]{1,0:T(8,128)(2,1)S(1)} %get-tuple-element.61), channel_id=1, source_target_pairs={{0,3},{1,0},{2,1},{3,2},{4,7},{5,4},{6,5},{7,6},{8,11},{9,8},{10,9... | collective-permute-start | bytes 393224 | tf_op jit(solution)/shard_map/ppermute | solution.py:437
  40.1 6.2 %collective-permute-start.12 = (bf16[128,512]{1,0:T(8,128)(2,1)S(1)}, bf16[128,512]{1,0:T(8,128)(2,1)S(1)}, u32[]{:S(2)}, u32[]{:S(2)}) collective-permute-start(bf16[128,512]{1,0:T(8,128)(2,1)S(1)} %get-tuple-element.59), channel_id=1, source_target_pairs={{0,1},{1,2},{2,3},{3,0},{4,5},{5,6},{6,7},{7,4},{8,9},{9,10},{10,1... | collective-permute-start | bytes 393224 | tf_op jit(solution)/shard_map/ppermute | solution.py:437
  41.3 5.0 %collective-permute-start.15 = (bf16[128,512]{1,0:T(8,128)(2,1)S(1)}, bf16[128,512]{1,0:T(8,128)(2,1)S(1)}, u32[]{:S(2)}, u32[]{:S(2)}) collective-permute-start(bf16[128,512]{1,0:T(8,128)(2,1)S(1)} %get-tuple-element.62), channel_id=1, source_target_pairs={{0,3},{1,0},{2,1},{3,2},{4,7},{5,4},{6,5},{7,6},{8,11},{9,8},{10,9... | collective-permute-start | bytes 393224 | tf_op jit(solution)/shard_map/ppermute | solution.py:437
